TPU v7x, 128 devices: a whole 4x4x4 slice. The times are simulated.
128 devices in a mesh: role: 4 (over x), dp: 32 (over z, y, core).
Axes of the slice: x: 4, y: 4, z: 4, core: 2. Of those that a mesh axis runs over, the one named last changes fastest.
Arguments:
- wavlm_hidden: bfloat16 [64, 512, 1024], P('dp'), may hold values from -6 to 6
- whisper_hidden: bfloat16 [64, 512, 1280], P('dp'), may hold values from -6 to 6
- wavlm_qkv: bfloat16 [1024, 3072], P(None, 'dp'), may hold values from -8 to 8
- whisper_qkv: bfloat16 [1280, 3840], P(None, 'dp'), may hold values from -8 to 8
- wavlm_out: bfloat16 [1024, 1024], replicated, may hold values from -0.1875 to 0.1875
- whisper_out: bfloat16 [1280, 1280], replicated, may hold values from -0.15625 to 0.15625
- frames_valid: int32 [64], replicated, may hold values from 128 to 512, as said below
- slot_clip: int32 [64], replicated, may hold values from 0 to 63, each once
- latent: bfloat16 [2, 32, 128, 512], P(None, 'dp'), may hold values from -6 to 6
- wavlm_head: bfloat16 [512, 1024], replicated, may hold values from -0.25 to 0.25
- whisper_head: bfloat16 [512, 1280], replicated, may hold values from -0.25 to 0.25
Outputs:
- grad_wavlm_head: float32 [512, 1024], replicated
- grad_whisper_head: float32 [512, 1280], replicated
Inputs may be any that keep to these rules, and one draw needn't show every extreme that they name: `frames_valid`: a multiple of 4; some clip has all 512 frames valid. `slot_clip`: every clip stands in exactly one slot.
All inputs are finite; a program needn't handle non-finite values.
Results may differ from a plain program's by a relative error of at most 0.002.
Values may be sent and summed in bfloat16 or wider, within the bound.
No kernel may reach another device: no remote copies, remote signals or barrier semaphores. Data moves between devices by JAX's collectives and lax.ppermute only.
A program may use at most 128 MiB of HBM per device.

v0:
```python
import jax
import jax.numpy as jnp
from jax import lax
from jax.experimental import pallas as pl
from jax.experimental.pallas import tpu as pltpu
from jax.sharding import PartitionSpec as P


WAVLM_D = 1024
WHISPER_D = 1280
STU_D = 512
HEAD = 64
FRAMES = 512
POOL = 4
POOLED = 128
CLIPS = 64
ROLES = 4
A_HEADS = WAVLM_D // HEAD // ROLES
W_HEADS = WHISPER_D // HEAD // ROLES
A_COLS = A_HEADS * HEAD
W_COLS = W_HEADS * HEAD
OUT_COLS = 640
ROWS = 64

epsilon_norm = 1e-05
epsilon_cos = 1e-06


bf16 = jnp.bfloat16
f32 = jnp.float32


def dp_send(x, dz, dy, dc):
    pairs = []
    for i in range(32):
        z, y, c = i // 8, (i // 2) % 4, i % 2
        target = ((z + dz) % 4) * 8 + ((y + dy) % 4) * 2 + (c + dc) % 2
        pairs.append((i, target))
    return lax.ppermute(x, "dp", pairs)


def role_send(x, k):
    return lax.ppermute(x, "role", [(i, (i + k) % ROLES) for i in range(ROLES)])


def place_of(column):
    return column // 8, (column // 2) % 4, column % 2


def norm_kernel(wavlm, whisper, norm_a, norm_w, mean_a, mean_w):
    pool_mat = jnp.where(
        lax.broadcasted_iota(jnp.int32, (32, 128), 1) // POOL
        == lax.broadcasted_iota(jnp.int32, (32, 128), 0),
        1.0 / POOL,
        0.0,
    ).astype(bf16)
    for hidden, norm, mean in ((wavlm, norm_a, mean_a), (whisper, norm_w, mean_w)):
        rows = hidden[0].astype(f32)
        centred = rows - jnp.mean(rows, axis=-1, keepdims=True)
        variance = jnp.mean(centred * centred, axis=-1, keepdims=True)
        norm[0] = (centred * lax.rsqrt(variance + epsilon_norm)).astype(bf16)

        @pl.when(pl.program_id(1) == lax.axis_index("role"))
        def _():
            mean[...] = jnp.dot(pool_mat, hidden[0], preferred_element_type=f32)


def norms(wavlm, whisper):
    rows = lambda width: pl.BlockSpec((1, 128, width), lambda i, j: (i, j, 0))
    mean = lambda width: pl.BlockSpec((32, width), lambda i, j: (i, 0))
    return pl.pallas_call(
        norm_kernel,
        grid=(2, 4),
        out_shape=[
            jax.ShapeDtypeStruct(wavlm.shape, bf16),
            jax.ShapeDtypeStruct(whisper.shape, bf16),
            jax.ShapeDtypeStruct((ROWS, WAVLM_D), f32),
            jax.ShapeDtypeStruct((ROWS, WHISPER_D), f32),
        ],
        in_specs=[rows(WAVLM_D), rows(WHISPER_D)],
        out_specs=[rows(WAVLM_D), rows(WHISPER_D), mean(WAVLM_D), mean(WHISPER_D)],
        cost_estimate=pl.CostEstimate(
            flops=60_000_000, bytes_accessed=24_000_000, transcendentals=4096
        ),
        name="norms",
    )(wavlm, whisper)


def chunk_kernel(qkv_a, qkv_w, *refs):
    outs, chunks = refs[:4], refs[4]
    z = place_of(lax.axis_index("dp"))[0]
    for part in range(4):
        for t in range(2):
            lane = (2 * part + t) * 128
            chunks[part, 3 * t : 3 * t + 3] = qkv_a[:, lane : lane + 128].reshape(3, 32, 128)
        for t in range(10):
            if part < 3:
                chunks[part, 6 + t] = qkv_w[32 * part : 32 * part + 32, 128 * t : 128 * t + 128]
            else:
                chunks[part, 6 + t] = jnp.concatenate(
                    [qkv_w[96:120, 128 * t : 128 * t + 128], jnp.zeros((8, 128), bf16)], axis=0
                )
    for k in range(4):
        outs[k][...] = chunks[(z + k) % 4]


def weight_chunks(qkv_a, qkv_w):
    vmem = pl.BlockSpec(memory_space=pltpu.VMEM)
    return pl.pallas_call(
        chunk_kernel,
        out_shape=[jax.ShapeDtypeStruct((16, 32, 128), bf16)] * 4,
        in_specs=[vmem, vmem],
        out_specs=[vmem] * 4,
        scratch_shapes=[pltpu.VMEM((4, 16, 32, 128), bf16)],
        name="weight_chunks",
    )(qkv_a, qkv_w)


def share_kernel(*refs):
    parts, out = refs[:4], refs[4]
    role = lax.axis_index("role")
    z, y, c = place_of(lax.axis_index("dp"))
    row = lax.broadcasted_iota(jnp.int32, (32, 128), 0)
    sources = [(role + 4 * ((s - role + 6) % 3)) // 3 for s in range(3)]
    for g in range(4):
        if g < 3:
            column, width = 96 * (2 * y + c) + 32 * g + row, A_COLS
        else:
            column, width = 120 * (2 * y + c) + 32 * z + row, W_COLS
        source = jnp.where(
            column < width, sources[0], jnp.where(column < 2 * width, sources[1], sources[2])
        )
        groups = (g, g + 3) if g < 3 else range(6, 16)
        for group in groups:
            value = parts[0][group].astype(f32)
            for k in range(1, 4):
                value = jnp.where(
                    source == (z - k + 4) % 4, parts[k][group].astype(f32), value
                )
            value = value.astype(bf16)
            out[:, group] = jnp.broadcast_to(value[None], (16, 32, 128))


def shares(parts):
    vmem = pl.BlockSpec(memory_space=pltpu.VMEM)
    return pl.pallas_call(
        share_kernel,
        out_shape=jax.ShapeDtypeStruct((16, 16, 32, 128), bf16),
        in_specs=[vmem] * 4,
        out_specs=vmem,
        cost_estimate=pl.CostEstimate(flops=0, bytes_accessed=5_000_000, transcendentals=0),
        name="shares",
    )(*parts)


def spread_kernel(latent, out):
    out[...] = jnp.broadcast_to(latent[:, 0][None], (16, 2, 32, STU_D))


def spread(latent):
    return pl.pallas_call(
        spread_kernel,
        grid=(1,),
        out_shape=jax.ShapeDtypeStruct((16, 2, 32, STU_D), bf16),
        in_specs=[
            pl.BlockSpec((2, 1, 32, STU_D), lambda i: (0, 0, lax.axis_index("role"), 0))
        ],
        out_specs=pl.BlockSpec((16, 2, 32, STU_D), lambda i: (0, 0, 0, 0)),
        name="spread",
    )(latent)


def pick_kernel(slot_clip, rows, own, other, slots):
    column = lax.axis_index("dp")
    c = column % 2
    base = (column // 2) * 4

    def find(s, carry):
        local = slot_clip[s] - base

        @pl.when((local >= 0) & (local < 4))
        def _():
            slots[jnp.clip(local, 0, 3)] = s

        return carry

    lax.fori_loop(0, CLIPS, find, 0)
    for out, owner in ((own, c), (other, 1 - c)):
        for i in range(2):
            slot = slots[2 * owner + i]
            h, j = slot // 32, slot % 32
            value = rows[j // 2, h]
            hit = (j % 2 == c).astype(f32)
            out[i * 32 : i * 32 + 32] = jnp.where(hit > 0, value.astype(f32), 0.0).astype(bf16)


def pick(slot_clip, rows):
    vmem = pl.BlockSpec(memory_space=pltpu.VMEM)
    return pl.pallas_call(
        pick_kernel,
        out_shape=[jax.ShapeDtypeStruct((ROWS, STU_D), bf16)] * 2,
        in_specs=[pl.BlockSpec(memory_space=pltpu.SMEM), vmem],
        out_specs=[vmem] * 2,
        scratch_shapes=[pltpu.SMEM((4,), jnp.int32)],
        cost_estimate=pl.CostEstimate(flops=0, bytes_accessed=6_000_000, transcendentals=0),
        name="pick",
    )(slot_clip, rows)


def attend_kernel(frames_valid, *refs):
    pieces = refs[:2]
    norm_a, norm_w = refs[2:4]
    outs = refs[4:8]
    wt_a, wt_w, qkv_a, qkv_w, proj, att_a, att_w, pooled, sem_a, sem_w = refs[8:]
    role = lax.axis_index("role")
    column = lax.axis_index("dp")
    c = column % 2

    def fetch(p, carry):
        zs = p // 4
        for n, piece in enumerate(pieces):
            block = (p % 4) * 2 + (c + n) % 2
            for t in range(2):
                pltpu.make_async_copy(
                    piece.at[p, pl.ds(3 * t, 3)], wt_a.at[2 * zs + t, pl.ds(3 * block, 3)], sem_a
                ).start()
            pltpu.make_async_copy(
                piece.at[p, pl.ds(6, 10)], wt_w.at[:, block * 4 + zs], sem_w
            ).start()
        return carry

    lax.fori_loop(0, 16, fetch, 0)
    ones_row = jnp.where(
        lax.broadcasted_iota(jnp.int32, (16, FRAMES), 0) == 0, 1.0, 0.0
    ).astype(bf16)
    pool_mat = jnp.where(
        lax.broadcasted_iota(jnp.int32, (POOLED, FRAMES), 1) // POOL
        == lax.broadcasted_iota(jnp.int32, (POOLED, FRAMES), 0),
        1.0 / POOL,
        0.0,
    ).astype(bf16)
    nt = (((1,), (1,)), ((), ()))
    tn = (((0,), (0,)), ((), ()))

    def put(qkv, kind, clip, head, value):
        scale = jnp.where(kind == 0, HEAD ** (-0.5), 1.0).astype(f32)
        qkv[kind, clip, head] = (value.astype(bf16).astype(f32) * scale).astype(bf16)

    def attention(qkv, att, heads):
        def one(i, carry):
            clip = i // heads
            head = i % heads
            valid = frames_valid[column * 2 + clip]
            query = qkv[0, clip, head]
            key = qkv[1, clip, head]
            value = qkv[2, clip, head]
            rows = lax.broadcasted_iota(jnp.int32, (16, FRAMES), 0)
            frame = lax.broadcasted_iota(jnp.int32, (16, FRAMES), 1)
            bias = jnp.where((rows == 0) & (frame >= valid), -1e30, 0.0).astype(bf16)
            key_x = jnp.concatenate([key, bias], axis=0)
            query_x = jnp.concatenate([query, ones_row], axis=0)
            value_x = jnp.concatenate([value, ones_row], axis=0)
            scores = lax.dot_general(key_x, query_x, tn, preferred_element_type=f32)
            top = jnp.max(scores, axis=0, keepdims=True)
            raised = jnp.exp(scores - top).astype(bf16)
            mixed = jnp.dot(value_x, raised, preferred_element_type=f32)
            total = mixed[HEAD : HEAD + 1]
            att[clip, head] = (mixed[:HEAD] * (1.0 / total)).astype(bf16)
            return carry

        lax.fori_loop(0, 2 * heads, one, 0)

    pltpu.make_async_copy(wt_a, wt_a, sem_a).wait()
    for clip in range(2):
        for s in range(3):
            kind = (s - role + 6) % 3
            lhs = jnp.concatenate(
                [wt_a[t, 8 * s : 8 * s + 8].reshape(A_COLS, 128) for t in range(8)], axis=1
            )
            value = lax.dot_general(lhs, norm_a[clip], nt, preferred_element_type=f32)
            for h in range(A_HEADS):
                put(qkv_a, kind, clip, h, value[h * HEAD : (h + 1) * HEAD])
    attention(qkv_a, att_a, A_HEADS)
    for clip in range(2):
        rows = att_a[clip].reshape(A_COLS, FRAMES)
        mean = lax.dot_general(pool_mat, rows, nt, preferred_element_type=f32).astype(bf16)
        pooled[:, clip * 32 : clip * 32 + 32, :A_COLS] = mean.reshape(ROLES, 32, A_COLS)

    pltpu.make_async_copy(wt_w, wt_w, sem_w).wait()
    for clip in range(2):
        for b in range(4):
            lhs = jnp.concatenate(
                [wt_w[t, 8 * b : 8 * b + 8].reshape(256, 128) for t in range(10)], axis=1
            )
            proj[256 * b : 256 * b + 256] = lax.dot_general(
                lhs, norm_w[clip], nt, preferred_element_type=f32
            )
        for s in range(3):
            kind = (s - role + 6) % 3
            for h in range(W_HEADS):
                start = s * W_COLS + h * HEAD
                parts = []
                while start < s * W_COLS + (h + 1) * HEAD:
                    block, inner = start // 120, start % 120
                    take = min(120 - inner, s * W_COLS + (h + 1) * HEAD - start)
                    parts.append(proj[block * 128 + inner : block * 128 + inner + take])
                    start += take
                value = parts[0] if len(parts) == 1 else jnp.concatenate(parts, axis=0)
                put(qkv_w, kind, clip, h, value)
    attention(qkv_w, att_w, W_HEADS)
    for clip in range(2):
        rows = att_w[clip].reshape(W_COLS, FRAMES)
        mean = lax.dot_general(pool_mat, rows, nt, preferred_element_type=f32).astype(bf16)
        mean = jnp.concatenate([mean, jnp.zeros((POOLED, 64), bf16)], axis=1)
        pooled[:, clip * 32 : clip * 32 + 32, A_COLS:] = mean.reshape(ROLES, 32, 384)
    for k in range(ROLES):
        outs[k][...] = pooled[(role + k) % ROLES]


def attend(frames_valid, pieces, norm_a, norm_w):
    vmem = pl.BlockSpec(memory_space=pltpu.VMEM)
    return pl.pallas_call(
        attend_kernel,
        out_shape=[jax.ShapeDtypeStruct((ROWS, OUT_COLS), bf16)] * ROLES,
        in_specs=[pl.BlockSpec(memory_space=pltpu.SMEM)]
        + [pl.BlockSpec(memory_space=pl.ANY)] * 2
        + [vmem, vmem],
        out_specs=[vmem] * ROLES,
        scratch_shapes=[
            pltpu.VMEM((8, 24, 32, 128), bf16),
            pltpu.VMEM((10, 32, 32, 128), bf16),
            pltpu.VMEM((3, 2, A_HEADS, HEAD, FRAMES), bf16),
            pltpu.VMEM((3, 2, W_HEADS, HEAD, FRAMES), bf16),
            pltpu.VMEM((1024, FRAMES), f32),
            pltpu.VMEM((2, A_HEADS, HEAD, FRAMES), bf16),
            pltpu.VMEM((2, W_HEADS, HEAD, FRAMES), bf16),
            pltpu.VMEM((ROLES, ROWS, OUT_COLS), bf16),
            pltpu.SemaphoreType.DMA,
            pltpu.SemaphoreType.DMA,
        ],
        cost_estimate=pl.CostEstimate(
            flops=8_000_000_000, bytes_accessed=12_000_000, transcendentals=5_000_000
        ),
        name="attend",
    )(frames_valid, *pieces, norm_a, norm_w)


def slope_kernel(frames_valid, *refs):
    parts = refs[:4]
    out_a, out_w, mean_a, mean_w, pred_a, pred_w = refs[4:10]
    outs = refs[10:14]
    grouped = refs[14]
    role = lax.axis_index("role")
    clip = lax.axis_index("dp") * 2
    row = lax.broadcasted_iota(jnp.int32, (ROWS, 1), 0)
    valid = jnp.where(row < 32, frames_valid[clip], frames_valid[clip + 1]) // POOL
    keep = (row % 32 + role * 32) < valid

    def slope_of(mean, out, pred, cols, first):
        width = mean.shape[-1]
        total = mean[...]
        extra = cols - 256
        left, right = [], []
        for k in range(ROLES):
            start = pl.multiple_of(((role - k + ROLES) % ROLES) * cols, 64)
            total = total + jnp.dot(
                parts[k][:, first : first + 256],
                out[pl.ds(start, 256), :],
                preferred_element_type=f32,
            )
            if extra:
                left.append(parts[k][:, first + 256 : first + cols])
                right.append(out[pl.ds(start + 256, extra), :])
        if extra:
            total = total + jnp.dot(
                jnp.concatenate(left, axis=1),
                jnp.concatenate(right, axis=0),
                preferred_element_type=f32,
            )
        target = total.astype(bf16).astype(f32)
        predicted = pred[...]
        pred_sq = jnp.sum(predicted * predicted, axis=-1, keepdims=True) + epsilon_cos
        targ_sq = jnp.sum(target * target, axis=-1, keepdims=True) + epsilon_cos
        pred_norm = jnp.sqrt(pred_sq)
        both = pred_norm * jnp.sqrt(targ_sq)
        cosine = jnp.sum(predicted * target, axis=-1, keepdims=True) / both
        slope = (cosine / (pred_norm * pred_norm)) * predicted - target / both
        slope = slope + (predicted - target) * (1.0 / width)
        return jnp.where(keep, slope, 0.0).astype(bf16)

    slope_a = slope_of(mean_a, out_a, pred_a, A_COLS, 0)
    for g in range(ROLES):
        grouped[g, :, :A_COLS] = slope_a[:, g * A_COLS : (g + 1) * A_COLS]
    slope_w = slope_of(mean_w, out_w, pred_w, W_COLS, A_COLS)
    for g in range(ROLES):
        grouped[g, :, A_COLS:] = jnp.concatenate(
            [slope_w[:, g * W_COLS : (g + 1) * W_COLS], jnp.zeros((ROWS, 64), bf16)], axis=1
        )
    for k in range(ROLES):
        outs[k][...] = grouped[(role + k) % ROLES]


def slopes(frames_valid, parts, out_a, out_w, mean_a, mean_w, pred_a, pred_w):
    vmem = pl.BlockSpec(memory_space=pltpu.VMEM)
    return pl.pallas_call(
        slope_kernel,
        out_shape=[jax.ShapeDtypeStruct((ROWS, OUT_COLS), bf16)] * ROLES,
        in_specs=[pl.BlockSpec(memory_space=pltpu.SMEM)] + [vmem] * 10,
        out_specs=[vmem] * ROLES,
        scratch_shapes=[pltpu.VMEM((ROLES, ROWS, OUT_COLS), bf16)],
        name="slopes",
    )(frames_valid, *parts, out_a, out_w, mean_a, mean_w, pred_a, pred_w)


def half_gradient(refs, half):
    start = pl.multiple_of(half * 256, 256)
    lat = jnp.concatenate([refs[k][:, pl.ds(start, 256)] for k in range(4)], axis=0)
    slo = jnp.concatenate([refs[4 + k][...] for k in range(4)], axis=0)
    grad = lax.dot_general(lat, slo, (((0,), (0,)), ((), ())), preferred_element_type=f32)
    return grad.reshape(16, 16, OUT_COLS)


def partner_kernel(*refs):
    refs[8][...] = half_gradient(refs, 1 - lax.axis_index("dp") % 2)


def keep_kernel(*refs):
    refs[9][...] = half_gradient(refs, lax.axis_index("dp") % 2) + refs[8][...]


def outer(kernel, *args):
    vmem = pl.BlockSpec(memory_space=pltpu.VMEM)
    return pl.pallas_call(
        kernel,
        out_shape=jax.ShapeDtypeStruct((16, 16, OUT_COLS), f32),
        in_specs=[vmem] * len(args),
        out_specs=vmem,
    )(*args)


def sum_kernel(x, out):
    total = jnp.sum(x[...], axis=0).astype(bf16)
    out[...] = jnp.broadcast_to(total[None], out.shape)


def reduce_parts(x):
    vmem = pl.BlockSpec(memory_space=pltpu.VMEM)
    return pl.pallas_call(
        sum_kernel,
        out_shape=jax.ShapeDtypeStruct((64, 16, OUT_COLS), bf16),
        in_specs=[vmem],
        out_specs=vmem,
        name="reduce_parts",
    )(x)


def place_kernel(own, other, out_a, out_w):
    for n, piece in enumerate((own, other)):
        core = (lax.axis_index("dp") + n) % 2
        blocks = []
        for g in range(ROLES):
            block = piece[g].reshape(64, OUT_COLS).astype(f32)
            out_a[core, :, g * A_COLS : (g + 1) * A_COLS] = block[:, :A_COLS]
            blocks.append(block[:, A_COLS : A_COLS + W_COLS])
        out_w[core] = jnp.concatenate(blocks, axis=1)


def place(own, other):
    spec = pl.BlockSpec((ROLES, 4, 16, OUT_COLS), lambda i: (0, i, 0, 0))
    return pl.pallas_call(
        place_kernel,
        grid=(4,),
        out_shape=[
            jax.ShapeDtypeStruct((2, 256, WAVLM_D), f32),
            jax.ShapeDtypeStruct((2, 256, WHISPER_D), f32),
        ],
        in_specs=[spec, spec],
        out_specs=[
            pl.BlockSpec((2, 64, WAVLM_D), lambda i: (0, i, 0)),
            pl.BlockSpec((2, 64, WHISPER_D), lambda i: (0, i, 0)),
        ],
        name="place",
    )(own, other)


PLANE = [[z * 8 + y * 2 + c for z in range(4) for y in range(4)] for c in range(2)]
SLICE = [[r * 32 + i for r in range(ROLES) for i in plane] for plane in PLANE]


def per_device(
    wavlm_hidden,
    whisper_hidden,
    wavlm_qkv,
    whisper_qkv,
    wavlm_out,
    whisper_out,
    frames_valid,
    slot_clip,
    latent,
    wavlm_head,
    whisper_head,
):
    chunks = weight_chunks(wavlm_qkv.T, whisper_qkv.T)
    chunks = [chunks[0]] + [dp_send(chunks[k], k, 0, 0) for k in (1, 2, 3)]
    lat_copies = spread(latent)
    all_lat = lax.all_to_all(
        lat_copies, "dp", split_axis=0, concat_axis=0, tiled=True, axis_index_groups=PLANE
    )
    copies = shares(chunks)
    own_weights = lax.all_to_all(
        copies, "dp", split_axis=0, concat_axis=0, tiled=True, axis_index_groups=PLANE
    )
    other_weights = dp_send(own_weights, 0, 0, 1)

    lat_own, lat_other = pick(slot_clip, all_lat)
    lat = lat_own + dp_send(lat_other, 0, 0, 1)
    lats = [lat] + [role_send(lat, k) for k in (1, 2, 3)]
    norm_a, norm_w, mean_a, mean_w = norms(wavlm_hidden, whisper_hidden)
    pred_a = jnp.dot(lat, wavlm_head, preferred_element_type=f32)
    pred_w = jnp.dot(lat, whisper_head, preferred_element_type=f32)
    ready = lax.optimization_barrier((other_weights, *lats, pred_a, pred_w))
    other_weights, lats, (pred_a, pred_w) = ready[0], ready[1:5], ready[5:]

    pooled = attend(frames_valid, (own_weights, other_weights), norm_a, norm_w)
    parts = [pooled[0]] + [role_send(pooled[k], k) for k in (1, 2, 3)]
    sloped = slopes(
        frames_valid, parts, wavlm_out, whisper_out, mean_a, mean_w, pred_a, pred_w
    )
    slos = [sloped[0]] + [role_send(sloped[k], k) for k in (1, 2, 3)]
    partner = outer(partner_kernel, *lats, *slos)
    halves = outer(keep_kernel, *lats, *slos, dp_send(partner, 0, 0, 1))
    arrived = lax.all_to_all(
        halves, "dp", split_axis=0, concat_axis=0, tiled=True, axis_index_groups=PLANE
    )
    summed = lax.all_to_all(
        reduce_parts(arrived),
        ("role", "dp"),
        split_axis=0,
        concat_axis=0,
        tiled=True,
        axis_index_groups=SLICE,
    ).reshape(ROLES, 16, 16, OUT_COLS)
    grad_a, grad_w = place(summed, dp_send(summed, 0, 0, 1))
    return grad_a.reshape(STU_D, WAVLM_D), grad_w.reshape(STU_D, WHISPER_D)


def solution(mesh):
    in_specs = (
        P("dp", None, None),
        P("dp", None, None),
        P(None, "dp"),
        P(None, "dp"),
        P(),
        P(),
        P(),
        P(),
        P(None, "dp", None, None),
        P(),
        P(),
    )
    out_specs = (P(), P())

    return jax.shard_map(
        per_device, mesh=mesh, in_specs=in_specs, out_specs=out_specs, check_vma=False
    )
```

profile of v0, /device:TPU:1, one launch (start us, length us, event | category | flops | bytes accessed | tf_op | source)
XLA Modules:
  0.0 209.1 jit_solution(13991151789452097051)
XLA Ops:
  0.6 0.0 copy-start
  0.6 2.0 weight_chunks.1
  2.7 2.5 %collective-permute-start = (bf16[16,32,128]{2,1,0:T(8,128)(2,1)}, bf16[16,32,128]{2,1,0:T(8,128)(2,1)S(1)}, u32[]{:S(2)}, u32[]{:S(2)}) collective-permute-start(bf16[16,32,128]{2,1,0:T(8,128)(2,1)} %get-tuple-element.30), channel_id=1, source_target_pairs={{0,8},{1,9},{2,10},{3,11},{4,12},{5,13},{6,14},{7,15},{8,16},{9,17... | collective-permute-start | bytes 393224 | tf_op jit(solution)/shard_map/ppermute | solution.py:39
  5.1 3.3 %collective-permute-start.1 = (bf16[16,32,128]{2,1,0:T(8,128)(2,1)}, bf16[16,32,128]{2,1,0:T(8,128)(2,1)S(1)}, u32[]{:S(2)}, u32[]{:S(2)}) collective-permute-start(bf16[16,32,128]{2,1,0:T(8,128)(2,1)} %get-tuple-element.31), channel_id=1, source_target_pairs={{0,16},{1,17},{2,18},{3,19},{4,20},{5,21},{6,22},{7,23},{8,24},{9,... | collective-permute-start | bytes 393224 | tf_op jit(solution)/shard_map/ppermute | solution.py:39
  8.4 0.7 collective-permute-start.2
  9.2 1.5 collective-permute-done.refs_1_
  10.7 3.7 %collective-permute-done.1.refs_2_ = bf16[16,32,128]{2,1,0:T(8,128)(2,1)S(1)} collective-permute-done((bf16[16,32,128]{2,1,0:T(8,128)(2,1)}, bf16[16,32,128]{2,1,0:T(8,128)(2,1)S(1)}, u32[]{:S(2)}, u32[]{:S(2)}) %collective-permute-start.1) | collective-permute-done | bytes 131104 | tf_op jit(solution)/shard_map/ppermute | solution.py:39
  14.4 0.0 collective-permute-done.2.refs_3_
  14.4 0.6 copy-done.13
  15.0 0.0 copy-done.14
  15.1 2.7 %shares.1 = bf16[16,16,32,128]{3,2,1,0:T(8,128)(2,1)} custom-call(bf16[16,32,128]{2,1,0:T(8,128)(2,1)} %get-tuple-element.29.refs_0_, bf16[16,32,128]{2,1,0:T(8,128)(2,1)} %copy-done.12, bf16[16,32,128]{2,1,0:T(8,128)(2,1)} %copy-done.13, bf16[16,32,128]{2,1,0:T(8,128)(2,1)} %copy-done.14), custom_call_target="tpu_custom_call" | custom-call | bytes 5000000 | tf_op jit(solution)/shard_map/shares/pallas_call | solution.py:146
  17.8 33.3 %all_to_all.20.refs_0_ = bf16[16,16,32,128]{3,2,1,0:T(8,128)(2,1)S(1)} all-to-all(bf16[16,16,32,128]{3,2,1,0:T(8,128)(2,1)} %shares.1), channel_id=1, replica_groups={{0,2,4,6,8,10,12,14,16,18,20,22,24,26,28,30},{1,3,5,7,9,11,13,15,17,19,..., dimensions={0} | all-to-all | bytes 4194304 | tf_op jit(solution)/shard_map/all_to_all | solution.py:510
  51.1 2.3 %collective-permute-start.3 = (bf16[16,16,32,128]{3,2,1,0:T(8,128)(2,1)S(1)}, bf16[16,16,32,128]{3,2,1,0:T(8,128)(2,1)}, u32[]{:S(2)}, u32[]{:S(2)}) collective-permute-start(bf16[16,16,32,128]{3,2,1,0:T(8,128)(2,1)S(1)} %all_to_all.20.refs_0_), channel_id=1, source_target_pairs={{0,1},{1,0},{2,3},{3,2},{4,5},{5,4},{6,7},{7,6},{8,9},{9,8},{10,11... | collective-permute-start | bytes 6291464 | tf_op jit(solution)/shard_map/ppermute | solution.py:39
  53.4 1.9 spread.1
  55.3 21.3 %all_to_all.21.rows = bf16[16,2,32,512]{3,2,1,0:T(8,128)(2,1)} all-to-all(bf16[16,2,32,512]{3,2,1,0:T(8,128)(2,1)} %spread.1), channel_id=1, replica_groups={{0,2,4,6,8,10,12,14,16,18,20,22,24,26,28,30},{1,3,5,7,9,11,13,15,17,19,..., dimensions={0} | all-to-all | bytes 2097152 | tf_op jit(solution)/shard_map/all_to_all | solution.py:506
  76.6 2.8 %pick.1 = (bf16[64,512]{1,0:T(8,128)(2,1)}, bf16[64,512]{1,0:T(8,128)(2,1)}) custom-call(s32[64]{0:T(128)} %slot_clip.1, bf16[16,2,32,512]{3,2,1,0:T(8,128)(2,1)} %all_to_all.21.rows), custom_call_target="tpu_custom_call" | custom-call | bytes 6000000 | tf_op jit(solution)/shard_map/pick/pallas_call | solution.py:199
  79.3 1.2 collective-permute-start.4
  80.5 9.2 %norms.1 = (bf16[2,512,1024]{2,1,0:T(8,128)(2,1)}, bf16[2,512,1280]{2,1,0:T(8,128)(2,1)}, f32[64,1024]{1,0:T(8,128)}, f32[64,1280]{1,0:T(8,128)}) custom-call(bf16[2,512,1024]{2,1,0:T(8,128)(2,1)} %wavlm.1, bf16[2,512,1280]{2,1,0:T(8,128)(2,1)} %whisper.1), custom_call_target="tpu_custom_call" | custom-call | flops 60000000 | bytes 24000000 | tf_op jit(solution)/shard_map/norms/pallas_call | solution.py:71
  89.8 0.0 collective-permute-done.4
  89.8 0.6 copy-done.19
  90.4 0.9 add.3.refs_0_
  91.2 0.0 copy-start.3
  91.3 2.7 %collective-permute-start.7 = (bf16[64,512]{1,0:T(8,128)(2,1)S(1)}, bf16[64,512]{1,0:T(8,128)(2,1)S(1)}, u32[]{:S(2)}, u32[]{:S(2)}) collective-permute-start(bf16[64,512]{1,0:T(8,128)(2,1)S(1)} %add.3.refs_0_), channel_id=1, source_target_pairs={{0,96},{32,0},{64,32},{96,64},{1,97},{33,1},{65,33},{97,65},{2,98}... | collective-permute-start | bytes 196616 | tf_op jit(solution)/shard_map/ppermute | solution.py:43
  94.0 0.5 collective-permute-start.6
  94.5 0.4 collective-permute-start.5
  94.9 1.1 fusion.1.refs_9_
  96.0 0.0 copy-done.4
  96.0 1.0 fusion.refs_8_
  97.0 0.0 collective-permute-done.7.refs_3_
  97.0 1.7 collective-permute-done.6.refs_2_
  98.7 2.0 collective-permute-done.5.refs_1_
  100.7 0.0 collective-permute-done.3.refs_1_
  100.7 0.6 copy-done.11
  101.3 22.4 %attend.1 = (bf16[64,640]{1,0:T(8,128)(2,1)}, bf16[64,640]{1,0:T(8,128)(2,1)}, bf16[64,640]{1,0:T(8,128)(2,1)}, bf16[64,640]{1,0:T(8,128)(2,1)}) custom-call(s32[64]{0:T(128)} %frames_valid.3, bf16[16,16,32,128]{3,2,1,0:T(8,128)(2,1)} %copy-done.2, bf16[16,16,32,128]{3,2,1,0:T(8,128)(2,1)} %collective-permute-done.3.refs_1_, ...), custom_call_target="tpu_custom_call" | custom-call | flops 8000000000 | bytes 12000000 | tf_op jit(solution)/shard_map/attend/pallas_call | solution.py:322
  123.7 0.0 copy-done.3
  123.7 0.1 collective-permute-start.8
  123.8 1.0 collective-permute-start.9
  124.8 1.7 collective-permute-start.10
  126.5 4.2 %collective-permute-done.8.refs_1_ = bf16[64,640]{1,0:T(8,128)(2,1)S(1)} collective-permute-done((bf16[64,640]{1,0:T(8,128)(2,1)}, bf16[64,640]{1,0:T(8,128)(2,1)S(1)}, u32[]{:S(2)}, u32[]{:S(2)}) %collective-permute-start.8) | collective-permute-done | bytes 81952 | tf_op jit(solution)/shard_map/ppermute | solution.py:43
  130.7 0.0 collective-permute-done.9.refs_2_
  130.7 0.0 collective-permute-done.10.refs_3_
  130.7 0.6 copy-done.15
  131.3 0.0 copy-done.16
  131.3 0.0 copy-done.17
  131.4 5.1 %slopes.1 = (bf16[64,640]{1,0:T(8,128)(2,1)}, bf16[64,640]{1,0:T(8,128)(2,1)}, bf16[64,640]{1,0:T(8,128)(2,1)}, bf16[64,640]{1,0:T(8,128)(2,1)}) custom-call(s32[64]{0:T(128)} %frames_valid.3, bf16[64,640]{1,0:T(8,128)(2,1)} %get-tuple-element.42.refs_0_, bf16[64,640]{1,0:T(8,128)(2,1)} %copy-done.15, bf16[64,640]{1,0:T(8,128)(2,1)} %copy-done.16, ...), custom_call_target="tpu_custom_call" | custom-call | tf_op jit(solution)/shard_map/slopes/pallas_call | solution.py:405
  136.5 1.1 collective-permute-start.11
  137.5 1.8 collective-permute-start.12
  139.4 0.6 collective-permute-start.13
  140.0 1.2 collective-permute-done.11.refs_5_
  141.2 1.3 collective-permute-done.12.refs_6_
  142.6 0.6 collective-permute-done.13.refs_7_
  143.2 0.0 copy-done.7
  143.2 0.6 copy-done.8
  143.8 2.3 %shard_map.122 = f32[16,16,640]{2,1,0:T(8,128)} custom-call(bf16[64,512]{1,0:T(8,128)(2,1)} %copy-done.3, bf16[64,512]{1,0:T(8,128)(2,1)} %copy-done.11, bf16[64,512]{1,0:T(8,128)(2,1)} %copy-done.10, bf16[64,512]{1,0:T(8,128)(2,1)} %copy-done.9, bf16[64,640]{1,0:T(8,128)(2,1)} %get-tuple-element.50.refs_4_, bf16[64,640]{1,0:T(8,128)(2,1)} %copy-done.6, ...), custom_call_target="tpu_custom_call" | custom-call | tf_op jit(solution)/shard_map/pallas_call | solution.py:433
  146.1 3.5 %collective-permute-start.14 = (f32[16,16,640]{2,1,0:T(8,128)}, f32[16,16,640]{2,1,0:T(8,128)S(1)}, u32[]{:S(2)}, u32[]{:S(2)}) collective-permute-start(f32[16,16,640]{2,1,0:T(8,128)} %shard_map.122), channel_id=1, source_target_pairs={{0,1},{1,0},{2,3},{3,2},{4,5},{5,4},{6,7},{7,6},{8,9},{9,8},{10,11... | collective-permute-start | bytes 1966088 | tf_op jit(solution)/shard_map/ppermute | solution.py:39
  149.6 1.9 collective-permute-done.14.refs_8_
  151.5 0.8 copy-done.5
  152.4 2.5 %shard_map.123 = f32[16,16,640]{2,1,0:T(8,128)} custom-call(bf16[64,512]{1,0:T(8,128)(2,1)} %copy-done.3, bf16[64,512]{1,0:T(8,128)(2,1)} %copy-done.11, bf16[64,512]{1,0:T(8,128)(2,1)} %copy-done.10, bf16[64,512]{1,0:T(8,128)(2,1)} %copy-done.9, bf16[64,640]{1,0:T(8,128)(2,1)} %get-tuple-element.50.refs_4_, bf16[64,640]{1,0:T(8,128)(2,1)} %copy-done.6, ...), custom_call_target="tpu_custom_call" | custom-call | tf_op jit(solution)/shard_map/pallas_call | solution.py:433
  154.9 16.9 %all_to_all.22.x = f32[16,16,640]{2,1,0:T(8,128)} all-to-all(f32[16,16,640]{2,1,0:T(8,128)} %shard_map.123), channel_id=1, replica_groups={{0,2,4,6,8,10,12,14,16,18,20,22,24,26,28,30},{1,3,5,7,9,11,13,15,17,19,..., dimensions={0} | all-to-all | bytes 1310720 | tf_op jit(solution)/shard_map/all_to_all | solution.py:532
  171.8 2.3 %reduce_parts.1 = bf16[64,16,640]{2,1,0:T(8,128)(2,1)} custom-call(f32[16,16,640]{2,1,0:T(8,128)} %all_to_all.22.x), custom_call_target="tpu_custom_call" | custom-call | tf_op jit(solution)/shard_map/reduce_parts/pallas_call | solution.py:448
  174.1 24.2 %all_to_all.23 = bf16[64,16,640]{2,1,0:T(8,128)(2,1)S(1)} all-to-all(bf16[64,16,640]{2,1,0:T(8,128)(2,1)} %reduce_parts.1), channel_id=1, replica_groups={{0,2,4,6,8,10,12,14,16,18,20,22,24,26,28,30,32,34,36,38,40,42,44,46,48,..., dimensions={0} | all-to-all | bytes 2621440 | tf_op jit(solution)/shard_map/all_to_all | solution.py:535
  198.3 3.5 %collective-permute-start.15 = (bf16[4,16,16,640]{3,2,1,0:T(8,128)(2,1)S(1)}, bf16[4,16,16,640]{3,2,1,0:T(8,128)(2,1)}, u32[]{:S(2)}, u32[]{:S(2)}) collective-permute-start(bf16[4,16,16,640]{3,2,1,0:T(8,128)(2,1)S(1)} %bitcast.9), channel_id=1, source_target_pairs={{0,1},{1,0},{2,3},{3,2},{4,5},{5,4},{6,7},{7,6},{8,9},{9,8},{10,11... | collective-permute-start | bytes 3932168 | tf_op jit(solution)/shard_map/ppermute | solution.py:39
  201.8 2.8 %collective-permute-done.15.other = bf16[4,16,16,640]{3,2,1,0:T(8,128)(2,1)} collective-permute-done((bf16[4,16,16,640]{3,2,1,0:T(8,128)(2,1)S(1)}, bf16[4,16,16,640]{3,2,1,0:T(8,128)(2,1)}, u32[]{:S(2)}, u32[]{:S(2)}) %collective-permute-start.15) | collective-permute-done | bytes 1310752 | tf_op jit(solution)/shard_map/ppermute | solution.py:39
  204.6 4.5 %place.1 = (f32[2,256,1024]{2,1,0:T(8,128)}, f32[2,256,1280]{2,1,0:T(8,128)}) custom-call(bf16[4,16,16,640]{3,2,1,0:T(8,128)(2,1)} %bitcast.10, bf16[4,16,16,640]{3,2,1,0:T(8,128)(2,1)} %collective-permute-done.15.other), custom_call_target="tpu_custom_call" | custom-call | tf_op jit(solution)/shard_map/place/pallas_call | solution.py:470
  (26 shorter events, 0.0 us)
Async XLA Ops:
  0.6 94.2 %copy-start = (bf16[512,1280]{1,0:T(8,128)(2,1)S(1)}, bf16[512,1280]{1,0:T(8,128)(2,1)}, u32[]{:S(2)}) copy-start(bf16[512,1280]{1,0:T(8,128)(2,1)} %param.21) | copy-start | bytes 3932164
  2.7 8.0 %collective-permute-start = (bf16[16,32,128]{2,1,0:T(8,128)(2,1)}, bf16[16,32,128]{2,1,0:T(8,128)(2,1)S(1)}, u32[]{:S(2)}, u32[]{:S(2)}) collective-permute-start(bf16[16,32,128]{2,1,0:T(8,128)(2,1)} %get-tuple-element.30), channel_id=1, source_target_pairs={{0,8},{1,9},{2,10},{3,11},{4,12},{5,13},{6,14},{7,15},{8,16},{9,17... | collective-permute-start | bytes 393224 | tf_op jit(solution)/shard_map/ppermute | solution.py:39
  5.1 9.2 %collective-permute-start.1 = (bf16[16,32,128]{2,1,0:T(8,128)(2,1)}, bf16[16,32,128]{2,1,0:T(8,128)(2,1)S(1)}, u32[]{:S(2)}, u32[]{:S(2)}) collective-permute-start(bf16[16,32,128]{2,1,0:T(8,128)(2,1)} %get-tuple-element.31), channel_id=1, source_target_pairs={{0,16},{1,17},{2,18},{3,19},{4,20},{5,21},{6,22},{7,23},{8,24},{9,... | collective-permute-start | bytes 393224 | tf_op jit(solution)/shard_map/ppermute | solution.py:39
  8.4 5.9 %collective-permute-start.2 = (bf16[16,32,128]{2,1,0:T(8,128)(2,1)}, bf16[16,32,128]{2,1,0:T(8,128)(2,1)S(1)}, u32[]{:S(2)}, u32[]{:S(2)}) collective-permute-start(bf16[16,32,128]{2,1,0:T(8,128)(2,1)} %get-tuple-element.32), channel_id=1, source_target_pairs={{0,24},{1,25},{2,26},{3,27},{4,28},{5,29},{6,30},{7,31},{8,0},{9,1... | collective-permute-start | bytes 393224 | tf_op jit(solution)/shard_map/ppermute | solution.py:39
  10.7 3.7 %copy-start.12 = (bf16[16,32,128]{2,1,0:T(8,128)(2,1)}, bf16[16,32,128]{2,1,0:T(8,128)(2,1)S(1)}, u32[]{:S(2)}) copy-start(bf16[16,32,128]{2,1,0:T(8,128)(2,1)S(1)} %collective-permute-done.refs_1_) | copy-start | bytes 393220
  14.4 0.7 copy-start.13
  14.4 0.7 copy-start.14
  51.1 28.3 %copy-start.2 = (bf16[16,16,32,128]{3,2,1,0:T(8,128)(2,1)}, bf16[16,16,32,128]{3,2,1,0:T(8,128)(2,1)S(1)}, u32[]{:S(2)}) copy-start(bf16[16,16,32,128]{3,2,1,0:T(8,128)(2,1)S(1)} %all_to_all.20.refs_0_) | copy-start | bytes 6291460
  51.1 49.6 %collective-permute-start.3 = (bf16[16,16,32,128]{3,2,1,0:T(8,128)(2,1)S(1)}, bf16[16,16,32,128]{3,2,1,0:T(8,128)(2,1)}, u32[]{:S(2)}, u32[]{:S(2)}) collective-permute-start(bf16[16,16,32,128]{3,2,1,0:T(8,128)(2,1)S(1)} %all_to_all.20.refs_0_), channel_id=1, source_target_pairs={{0,1},{1,0},{2,3},{3,2},{4,5},{5,4},{6,7},{7,6},{8,9},{9,8},{10,11... | collective-permute-start | bytes 6291464 | tf_op jit(solution)/shard_map/ppermute | solution.py:39
  79.3 11.0 %copy-start.18 = (bf16[64,512]{1,0:T(8,128)(2,1)S(1)}, bf16[64,512]{1,0:T(8,128)(2,1)}, u32[]{:S(2)}) copy-start(bf16[64,512]{1,0:T(8,128)(2,1)} %get-tuple-element.33) | copy-start | bytes 196612
  79.3 10.4 %collective-permute-start.4 = (bf16[64,512]{1,0:T(8,128)(2,1)}, bf16[64,512]{1,0:T(8,128)(2,1)S(1)}, u32[]{:S(2)}, u32[]{:S(2)}) collective-permute-start(bf16[64,512]{1,0:T(8,128)(2,1)} %get-tuple-element.34), channel_id=1, source_target_pairs={{0,1},{1,0},{2,3},{3,2},{4,5},{5,4},{6,7},{7,6},{8,9},{9,8},{10,11... | collective-permute-start | bytes 196616 | tf_op jit(solution)/shard_map/ppermute | solution.py:39
  89.7 6.2 %copy-start.4 = (bf16[512,1024]{1,0:T(8,128)(2,1)S(1)}, bf16[512,1024]{1,0:T(8,128)(2,1)}, u32[]{:S(2)}) copy-start(bf16[512,1024]{1,0:T(8,128)(2,1)} %param.20) | copy-start | bytes 3145732
  89.8 0.6 copy-start.19
  91.2 32.5 %copy-start.3 = (bf16[64,512]{1,0:T(8,128)(2,1)}, bf16[64,512]{1,0:T(8,128)(2,1)S(1)}, u32[]{:S(2)}) copy-start(bf16[64,512]{1,0:T(8,128)(2,1)S(1)} %add.3.refs_0_) | copy-start | bytes 196612
  91.3 5.7 %collective-permute-start.7 = (bf16[64,512]{1,0:T(8,128)(2,1)S(1)}, bf16[64,512]{1,0:T(8,128)(2,1)S(1)}, u32[]{:S(2)}, u32[]{:S(2)}) collective-permute-start(bf16[64,512]{1,0:T(8,128)(2,1)S(1)} %add.3.refs_0_), channel_id=1, source_target_pairs={{0,96},{32,0},{64,32},{96,64},{1,97},{33,1},{65,33},{97,65},{2,98}... | collective-permute-start | bytes 196616 | tf_op jit(solution)/shard_map/ppermute | solution.py:43
  94.0 4.7 %collective-permute-start.6 = (bf16[64,512]{1,0:T(8,128)(2,1)S(1)}, bf16[64,512]{1,0:T(8,128)(2,1)S(1)}, u32[]{:S(2)}, u32[]{:S(2)}) collective-permute-start(bf16[64,512]{1,0:T(8,128)(2,1)S(1)} %add.3.refs_0_), channel_id=1, source_target_pairs={{0,64},{32,96},{64,0},{96,32},{1,65},{33,97},{65,1},{97,33},{2,66}... | collective-permute-start | bytes 196616 | tf_op jit(solution)/shard_map/ppermute | solution.py:43
  94.5 6.3 %collective-permute-start.5 = (bf16[64,512]{1,0:T(8,128)(2,1)S(1)}, bf16[64,512]{1,0:T(8,128)(2,1)S(1)}, u32[]{:S(2)}, u32[]{:S(2)}) collective-permute-start(bf16[64,512]{1,0:T(8,128)(2,1)S(1)} %add.3.refs_0_), channel_id=1, source_target_pairs={{0,32},{32,64},{64,96},{96,0},{1,33},{33,65},{65,97},{97,1},{2,34}... | collective-permute-start | bytes 196616 | tf_op jit(solution)/shard_map/ppermute | solution.py:43
  97.0 26.8 %copy-start.9 = (bf16[64,512]{1,0:T(8,128)(2,1)}, bf16[64,512]{1,0:T(8,128)(2,1)S(1)}, u32[]{:S(2)}) copy-start(bf16[64,512]{1,0:T(8,128)(2,1)S(1)} %collective-permute-done.7.refs_3_) | copy-start | bytes 196612
  98.7 2.1 copy-start.10
  100.7 0.6 copy-start.11
  123.7 6.9 %collective-permute-start.8 = (bf16[64,640]{1,0:T(8,128)(2,1)}, bf16[64,640]{1,0:T(8,128)(2,1)S(1)}, u32[]{:S(2)}, u32[]{:S(2)}) collective-permute-start(bf16[64,640]{1,0:T(8,128)(2,1)} %get-tuple-element.43), channel_id=1, source_target_pairs={{0,32},{32,64},{64,96},{96,0},{1,33},{33,65},{65,97},{97,1},{2,34}... | collective-permute-start | bytes 245768 | tf_op jit(solution)/shard_map/ppermute | solution.py:43
  123.8 6.9 %collective-permute-start.9 = (bf16[64,640]{1,0:T(8,128)(2,1)}, bf16[64,640]{1,0:T(8,128)(2,1)S(1)}, u32[]{:S(2)}, u32[]{:S(2)}) collective-permute-start(bf16[64,640]{1,0:T(8,128)(2,1)} %get-tuple-element.44), channel_id=1, source_target_pairs={{0,64},{32,96},{64,0},{96,32},{1,65},{33,97},{65,1},{97,33},{2,66}... | collective-permute-start | bytes 245768 | tf_op jit(solution)/shard_map/ppermute | solution.py:43
  124.8 5.9 %collective-permute-start.10 = (bf16[64,640]{1,0:T(8,128)(2,1)}, bf16[64,640]{1,0:T(8,128)(2,1)S(1)}, u32[]{:S(2)}, u32[]{:S(2)}) collective-permute-start(bf16[64,640]{1,0:T(8,128)(2,1)} %get-tuple-element.45), channel_id=1, source_target_pairs={{0,96},{32,0},{64,32},{96,64},{1,97},{33,1},{65,33},{97,65},{2,98}... | collective-permute-start | bytes 245768 | tf_op jit(solution)/shard_map/ppermute | solution.py:43
  130.7 0.6 copy-start.15
  130.7 0.7 copy-start.16
  130.7 0.7 copy-start.17
  136.5 4.7 %collective-permute-start.11 = (bf16[64,640]{1,0:T(8,128)(2,1)}, bf16[64,640]{1,0:T(8,128)(2,1)S(1)}, u32[]{:S(2)}, u32[]{:S(2)}) collective-permute-start(bf16[64,640]{1,0:T(8,128)(2,1)} %get-tuple-element.51), channel_id=1, source_target_pairs={{0,32},{32,64},{64,96},{96,0},{1,33},{33,65},{65,97},{97,1},{2,34}... | collective-permute-start | bytes 245768 | tf_op jit(solution)/shard_map/ppermute | solution.py:43
  137.5 5.0 %collective-permute-start.12 = (bf16[64,640]{1,0:T(8,128)(2,1)}, bf16[64,640]{1,0:T(8,128)(2,1)S(1)}, u32[]{:S(2)}, u32[]{:S(2)}) collective-permute-start(bf16[64,640]{1,0:T(8,128)(2,1)} %get-tuple-element.52), channel_id=1, source_target_pairs={{0,64},{32,96},{64,0},{96,32},{1,65},{33,97},{65,1},{97,33},{2,66}... | collective-permute-start | bytes 245768 | tf_op jit(solution)/shard_map/ppermute | solution.py:43
  139.4 3.8 %collective-permute-start.13 = (bf16[64,640]{1,0:T(8,128)(2,1)}, bf16[64,640]{1,0:T(8,128)(2,1)S(1)}, u32[]{:S(2)}, u32[]{:S(2)}) collective-permute-start(bf16[64,640]{1,0:T(8,128)(2,1)} %get-tuple-element.53), channel_id=1, source_target_pairs={{0,96},{32,0},{64,32},{96,64},{1,97},{33,1},{65,33},{97,65},{2,98}... | collective-permute-start | bytes 245768 | tf_op jit(solution)/shard_map/ppermute | solution.py:43
  141.2 2.0 copy-start.6
  142.6 0.6 copy-start.7
  143.2 0.6 copy-start.8
  146.1 5.4 %collective-permute-start.14 = (f32[16,16,640]{2,1,0:T(8,128)}, f32[16,16,640]{2,1,0:T(8,128)S(1)}, u32[]{:S(2)}, u32[]{:S(2)}) collective-permute-start(f32[16,16,640]{2,1,0:T(8,128)} %shard_map.122), channel_id=1, source_target_pairs={{0,1},{1,0},{2,3},{3,2},{4,5},{5,4},{6,7},{7,6},{8,9},{9,8},{10,11... | collective-permute-start | bytes 1966088 | tf_op jit(solution)/shard_map/ppermute | solution.py:39
  151.5 0.8 copy-start.5
  198.3 6.3 %copy-start.1 = (bf16[64,16,640]{2,1,0:T(8,128)(2,1)}, bf16[64,16,640]{2,1,0:T(8,128)(2,1)S(1)}, u32[]{:S(2)}) copy-start(bf16[64,16,640]{2,1,0:T(8,128)(2,1)S(1)} %all_to_all.23) | copy-start | bytes 3932164
  198.3 6.3 %collective-permute-start.15 = (bf16[4,16,16,640]{3,2,1,0:T(8,128)(2,1)S(1)}, bf16[4,16,16,640]{3,2,1,0:T(8,128)(2,1)}, u32[]{:S(2)}, u32[]{:S(2)}) collective-permute-start(bf16[4,16,16,640]{3,2,1,0:T(8,128)(2,1)S(1)} %bitcast.9), channel_id=1, source_target_pairs={{0,1},{1,0},{2,3},{3,2},{4,5},{5,4},{6,7},{7,6},{8,9},{9,8},{10,11... | collective-permute-start | bytes 3932168 | tf_op jit(solution)/shard_map/ppermute | solution.py:39
where the time goes:
time: 210 us; the launch traced here: 209 us
  blocking collectives  95.7 us (46%)
  Pallas kernels  57.7 us (27%)
  starting transfers between devices  26.9 us (13%)
  waiting for transfers between devices  21 us (10%)
  local copies, waits for them, and re-layouts  4.08 us (2%)
  matrix products  2.11 us (1%)
    all_to_all x1, blocking collectives, per_device(): lax.all_to_all(copies, 'dp', split_axis=0, concat_axis=0, tiled=True, axi...  33.3 us
    all_to_all x1, blocking collectives, per_device(): lax.all_to_all(reduce_parts(arrived), ('role', 'dp'), split_axis=0, conca...  24.2 us
    pallas_call x1, Pallas kernels, attend(): pl.pallas_call(attend_kernel, out_shape=[jax.ShapeDtypeStruct((ROWS, OUT_...  22.4 us
    all_to_all x1, blocking collectives, per_device(): lax.all_to_all(lat_copies, 'dp', split_axis=0, concat_axis=0, tiled=True,...  21.3 us
    ppermute x7, starting transfers between devices, dp_send(): return lax.ppermute(x, 'dp', pairs)  17 us
    all_to_all x1, blocking collectives, per_device(): lax.all_to_all(halves, 'dp', split_axis=0, concat_axis=0, tiled=True, axi...  16.9 us
    ppermute x9, waiting for transfers between devices, role_send(): return lax.ppermute(x, 'role', [(i, (i + k) % ROLES) for i in range(ROLES)])  11.1 us
    ppermute x7, waiting for transfers between devices, dp_send(): return lax.ppermute(x, 'dp', pairs)  9.94 us
  transfers between devices with their start and end apart: 16, of which 10 were waited for; matrix products, arithmetic and copies ran while one was open for 1% of the time, Pallas kernels for 7%

commit v1 on v0

v1 whole, which is shorter than its diff:
```python
import jax
import jax.numpy as jnp
from jax import lax
from jax.experimental import pallas as pl
from jax.experimental.pallas import tpu as pltpu
from jax.sharding import PartitionSpec as P


WAVLM_D = 1024
WHISPER_D = 1280
STU_D = 512
HEAD = 64
FRAMES = 512
POOL = 4
POOLED = 128
CLIPS = 64
ROLES = 4
A_HEADS = WAVLM_D // HEAD // ROLES
W_HEADS = WHISPER_D // HEAD // ROLES
A_COLS = A_HEADS * HEAD
W_COLS = W_HEADS * HEAD
OUT_COLS = 640
ROWS = 64

epsilon_norm = 1e-05
epsilon_cos = 1e-06


bf16 = jnp.bfloat16
f32 = jnp.float32


def dp_send(x, dz, dy, dc):
    pairs = []
    for i in range(32):
        z, y, c = i // 8, (i // 2) % 4, i % 2
        target = ((z + dz) % 4) * 8 + ((y + dy) % 4) * 2 + (c + dc) % 2
        pairs.append((i, target))
    return lax.ppermute(x, "dp", pairs)


def role_send(x, k):
    return lax.ppermute(x, "role", [(i, (i + k) % ROLES) for i in range(ROLES)])


def place_of(column):
    return column // 8, (column // 2) % 4, column % 2


def norm_kernel(wavlm, whisper, norm_a, norm_w, mean_a, mean_w):
    pool_mat = jnp.where(
        lax.broadcasted_iota(jnp.int32, (32, 128), 1) // POOL
        == lax.broadcasted_iota(jnp.int32, (32, 128), 0),
        1.0 / POOL,
        0.0,
    ).astype(bf16)
    for hidden, norm, mean in ((wavlm, norm_a, mean_a), (whisper, norm_w, mean_w)):
        rows = hidden[0].astype(f32)
        centred = rows - jnp.mean(rows, axis=-1, keepdims=True)
        variance = jnp.mean(centred * centred, axis=-1, keepdims=True)
        norm[0] = (centred * lax.rsqrt(variance + epsilon_norm)).astype(bf16)

        @pl.when(pl.program_id(1) == lax.axis_index("role"))
        def _():
            mean[...] = jnp.dot(pool_mat, hidden[0], preferred_element_type=f32)


def norms(wavlm, whisper):
    rows = lambda width: pl.BlockSpec((1, 128, width), lambda i, j: (i, j, 0))
    mean = lambda width: pl.BlockSpec((32, width), lambda i, j: (i, 0))
    return pl.pallas_call(
        norm_kernel,
        grid=(2, 4),
        out_shape=[
            jax.ShapeDtypeStruct(wavlm.shape, bf16),
            jax.ShapeDtypeStruct(whisper.shape, bf16),
            jax.ShapeDtypeStruct((ROWS, WAVLM_D), f32),
            jax.ShapeDtypeStruct((ROWS, WHISPER_D), f32),
        ],
        in_specs=[rows(WAVLM_D), rows(WHISPER_D)],
        out_specs=[rows(WAVLM_D), rows(WHISPER_D), mean(WAVLM_D), mean(WHISPER_D)],
        cost_estimate=pl.CostEstimate(
            flops=60_000_000, bytes_accessed=24_000_000, transcendentals=4096
        ),
        name="norms",
    )(wavlm, whisper)


def chunk_kernel(qkv_a, qkv_w, *refs):
    outs, chunks = refs[:4], refs[4]
    z = place_of(lax.axis_index("dp"))[0]
    for part in range(4):
        for t in range(2):
            lane = (2 * part + t) * 128
            chunks[part, 3 * t : 3 * t + 3] = qkv_a[:, lane : lane + 128].reshape(3, 32, 128)
        for t in range(10):
            if part < 3:
                chunks[part, 6 + t] = qkv_w[32 * part : 32 * part + 32, 128 * t : 128 * t + 128]
            else:
                chunks[part, 6 + t] = jnp.concatenate(
                    [qkv_w[96:120, 128 * t : 128 * t + 128], jnp.zeros((8, 128), bf16)], axis=0
                )
    for k in range(4):
        outs[k][...] = chunks[(z + k) % 4]


def weight_chunks(qkv_a, qkv_w):
    vmem = pl.BlockSpec(memory_space=pltpu.VMEM)
    return pl.pallas_call(
        chunk_kernel,
        out_shape=[jax.ShapeDtypeStruct((16, 32, 128), bf16)] * 4,
        in_specs=[vmem, vmem],
        out_specs=[vmem] * 4,
        scratch_shapes=[pltpu.VMEM((4, 16, 32, 128), bf16)],
        name="weight_chunks",
    )(qkv_a, qkv_w)


def share_kernel(*refs):
    parts, latent, out = refs[:4], refs[4], refs[5]
    role = lax.axis_index("role")
    z, y, c = place_of(lax.axis_index("dp"))
    row = lax.broadcasted_iota(jnp.int32, (32, 128), 0)
    sources = [(role + 4 * ((s - role + 6) % 3)) // 3 for s in range(3)]
    for g in range(4):
        if g < 3:
            column, width = 96 * (2 * y + c) + 32 * g + row, A_COLS
        else:
            column, width = 120 * (2 * y + c) + 32 * z + row, W_COLS
        source = jnp.where(
            column < width, sources[0], jnp.where(column < 2 * width, sources[1], sources[2])
        )
        groups = (g, g + 3) if g < 3 else range(6, 16)
        for group in groups:
            value = parts[0][group].astype(f32)
            for k in range(1, 4):
                value = jnp.where(
                    source == (z - k + 4) % 4, parts[k][group].astype(f32), value
                )
            value = value.astype(bf16)
            out[:, group] = jnp.broadcast_to(value[None], (16, 32, 128))


    for h in range(2):
        for t in range(4):
            value = latent[h, 0, :, 128 * t : 128 * t + 128]
            out[:, 16 + 4 * h + t] = jnp.broadcast_to(value[None], (16, 32, 128))


def shares(parts, latent):
    whole = pl.BlockSpec((16, 32, 128), lambda i: (0, 0, 0))
    return pl.pallas_call(
        share_kernel,
        grid=(1,),
        out_shape=jax.ShapeDtypeStruct((16, 24, 32, 128), bf16),
        in_specs=[whole] * 4
        + [pl.BlockSpec((2, 1, 32, STU_D), lambda i: (0, 0, lax.axis_index("role"), 0))],
        out_specs=pl.BlockSpec((16, 24, 32, 128), lambda i: (0, 0, 0, 0)),
        name="shares",
    )(*parts, latent)


def pick_kernel(slot_clip, own, other, out, slots, rows, sem):
    column = lax.axis_index("dp")
    c = column % 2
    base = (column // 2) * 4

    def find(s, carry):
        local = slot_clip[s] - base

        @pl.when((local >= 0) & (local < 4))
        def _():
            slots[jnp.clip(local, 0, 3)] = s

        return carry

    lax.fori_loop(0, CLIPS, find, 0)
    for i in range(4):
        slot = slots[(2 * c + i) % 4]
        h, j = slot // 32, slot % 32
        groups = pl.ds(16 + 4 * h, 4)

        @pl.when(j % 2 == c)
        def _():
            pltpu.make_async_copy(own.at[j // 2, groups], rows.at[i], sem.at[i]).start()

        @pl.when(j % 2 != c)
        def _():
            pltpu.make_async_copy(other.at[j // 2, groups], rows.at[i], sem.at[i]).start()

    for i in range(4):
        pltpu.make_async_copy(rows.at[i], rows.at[i], sem.at[i]).wait()
        out[i * 32 : i * 32 + 32] = jnp.concatenate([rows[i, t] for t in range(4)], axis=1)


def pick(slot_clip, own, other):
    hbm = pl.BlockSpec(memory_space=pl.ANY)
    return pl.pallas_call(
        pick_kernel,
        out_shape=jax.ShapeDtypeStruct((2 * ROWS, STU_D), bf16),
        in_specs=[pl.BlockSpec(memory_space=pltpu.SMEM), hbm, hbm],
        out_specs=pl.BlockSpec(memory_space=pltpu.VMEM),
        scratch_shapes=[
            pltpu.SMEM((4,), jnp.int32),
            pltpu.VMEM((4, 4, 32, 128), bf16),
            pltpu.SemaphoreType.DMA((4,)),
        ],
        name="pick",
    )(slot_clip, own, other)


def attend_kernel(frames_valid, *refs):
    pieces = refs[:2]
    norm_a_hbm, norm_w_hbm, pooled = refs[2:5]
    norm_a, norm_w, wt_a, wt_w, qkv_a, qkv_w, proj, att_a, att_w = refs[5:14]
    score_refs, sems = refs[14:16], refs[16]
    sem_a, sem_w = sems.at[0], sems.at[1]
    copy_a = pltpu.make_async_copy(norm_a_hbm, norm_a, sems.at[2])
    copy_w = pltpu.make_async_copy(norm_w_hbm, norm_w, sems.at[3])
    role = lax.axis_index("role")
    column = lax.axis_index("dp")
    c = column % 2

    def fetch(p, carry):
        zs = p // 4
        for n, piece in enumerate(pieces):
            block = (p % 4) * 2 + (c + n) % 2
            for t in range(2):
                pltpu.make_async_copy(
                    piece.at[p, pl.ds(3 * t, 3)], wt_a.at[2 * zs + t, pl.ds(3 * block, 3)], sem_a
                ).start()
            pltpu.make_async_copy(
                piece.at[p, pl.ds(6, 10)], wt_w.at[:, block * 4 + zs], sem_w
            ).start()
        return carry

    lax.fori_loop(0, 16, fetch, 0)
    copy_a.start()
    copy_w.start()
    ones_row = jnp.where(
        lax.broadcasted_iota(jnp.int32, (16, FRAMES), 0) == 0, 1.0, 0.0
    ).astype(bf16)
    pool_mat = jnp.where(
        lax.broadcasted_iota(jnp.int32, (POOLED, FRAMES), 1) // POOL
        == lax.broadcasted_iota(jnp.int32, (POOLED, FRAMES), 0),
        1.0 / POOL,
        0.0,
    ).astype(bf16)
    nt = (((1,), (1,)), ((), ()))
    tn = (((0,), (0,)), ((), ()))

    def put(qkv, kind, clip, head, value):
        scale = jnp.where(kind == 0, HEAD ** (-0.5), 1.0).astype(f32)
        qkv[kind, clip, head] = (value.astype(bf16).astype(f32) * scale).astype(bf16)

    def attention(qkv, att, heads):
        rows = lax.broadcasted_iota(jnp.int32, (16, FRAMES), 0)
        frame = lax.broadcasted_iota(jnp.int32, (16, FRAMES), 1)

        bias = [
            jnp.where(
                (rows == 0) & (frame >= frames_valid[column * 2 + clip]), -1e30, 0.0
            ).astype(bf16)
            for clip in range(2)
        ]

        def score(item, scores):
            clip, head = item % 2, item // 2
            key_x = jnp.concatenate([qkv[1, clip, head], bias[clip]], axis=0)
            query_x = jnp.concatenate([qkv[0, clip, head], ones_row], axis=0)
            value = lax.dot_general(key_x, query_x, tn, preferred_element_type=f32)
            scores[...] = value
            return jnp.max(value, axis=0, keepdims=True)

        def mix(item, scores, top):
            clip, head = item % 2, item // 2
            value_x = jnp.concatenate([qkv[2, clip, head], ones_row], axis=0)
            raised = jnp.exp(scores[...] - top).astype(bf16)
            mixed = jnp.dot(value_x, raised, preferred_element_type=f32)
            total = mixed[HEAD : HEAD + 1]
            att[clip, head] = (mixed[:HEAD] * (1.0 / total)).astype(bf16)

        top = score(0, score_refs[0])
        for item in range(2 * heads):
            if item + 1 < 2 * heads:
                next_top = score(item + 1, score_refs[(item + 1) % 2])
            mix(item, score_refs[item % 2], top)
            top = next_top

    pltpu.make_async_copy(wt_a, wt_a, sem_a).wait()
    copy_a.wait()
    for clip in range(2):
        lhs = jnp.concatenate([wt_a[t].reshape(3 * A_COLS, 128) for t in range(8)], axis=1)
        value = lax.dot_general(lhs, norm_a[clip], nt, preferred_element_type=f32)
        for s in range(3):
            kind = (s - role + 6) % 3
            for h in range(A_HEADS):
                start = s * A_COLS + h * HEAD
                put(qkv_a, kind, clip, h, value[start : start + HEAD])
    attention(qkv_a, att_a, A_HEADS)
    for clip in range(2):
        rows = att_a[clip].reshape(A_COLS, FRAMES)
        mean = lax.dot_general(pool_mat, rows, nt, preferred_element_type=f32).astype(bf16)
        pooled[:, clip * 32 : clip * 32 + 32, :A_COLS] = mean.reshape(ROLES, 32, A_COLS)

    pltpu.make_async_copy(wt_w, wt_w, sem_w).wait()
    copy_w.wait()
    for clip in range(2):
        lhs = jnp.concatenate([wt_w[t].reshape(1024, 128) for t in range(10)], axis=1)
        proj[...] = lax.dot_general(lhs, norm_w[clip], nt, preferred_element_type=f32)
        for s in range(3):
            kind = (s - role + 6) % 3
            for h in range(W_HEADS):
                start = s * W_COLS + h * HEAD
                parts = []
                while start < s * W_COLS + (h + 1) * HEAD:
                    block, inner = start // 120, start % 120
                    take = min(120 - inner, s * W_COLS + (h + 1) * HEAD - start)
                    parts.append(proj[block * 128 + inner : block * 128 + inner + take])
                    start += take
                value = parts[0] if len(parts) == 1 else jnp.concatenate(parts, axis=0)
                put(qkv_w, kind, clip, h, value)
    attention(qkv_w, att_w, W_HEADS)
    for clip in range(2):
        rows = att_w[clip].reshape(W_COLS, FRAMES)
        mean = lax.dot_general(pool_mat, rows, nt, preferred_element_type=f32).astype(bf16)
        mean = jnp.concatenate([mean, jnp.zeros((POOLED, 64), bf16)], axis=1)
        pooled[:, clip * 32 : clip * 32 + 32, A_COLS:] = mean.reshape(ROLES, 32, 384)


def attend(frames_valid, pieces, norm_a, norm_w):
    vmem = pl.BlockSpec(memory_space=pltpu.VMEM)
    return pl.pallas_call(
        attend_kernel,
        out_shape=jax.ShapeDtypeStruct((ROLES, ROWS, OUT_COLS), bf16),
        in_specs=[pl.BlockSpec(memory_space=pltpu.SMEM)]
        + [pl.BlockSpec(memory_space=pl.ANY)] * 4,
        out_specs=vmem,
        scratch_shapes=[
            pltpu.VMEM((2, FRAMES, WAVLM_D), bf16),
            pltpu.VMEM((2, FRAMES, WHISPER_D), bf16),
            pltpu.VMEM((8, 24, 32, 128), bf16),
            pltpu.VMEM((10, 32, 32, 128), bf16),
            pltpu.VMEM((3, 2, A_HEADS, HEAD, FRAMES), bf16),
            pltpu.VMEM((3, 2, W_HEADS, HEAD, FRAMES), bf16),
            pltpu.VMEM((1024, FRAMES), f32),
            pltpu.VMEM((2, A_HEADS, HEAD, FRAMES), bf16),
            pltpu.VMEM((2, W_HEADS, HEAD, FRAMES), bf16),
            pltpu.VMEM((FRAMES, FRAMES), f32),
            pltpu.VMEM((FRAMES, FRAMES), f32),
            pltpu.SemaphoreType.DMA((4,)),
        ],
        cost_estimate=pl.CostEstimate(
            flops=8_000_000_000, bytes_accessed=12_000_000, transcendentals=5_000_000
        ),
        name="attend",
    )(frames_valid, *pieces, norm_a, norm_w)


def slope_kernel(frames_valid, parts, out_a_hbm, out_w_hbm, *refs):
    mean_a, mean_w, pred_a, pred_w, grouped, out_a, out_w, sems = refs
    copy_a = pltpu.make_async_copy(out_a_hbm, out_a, sems.at[0])
    copy_w = pltpu.make_async_copy(out_w_hbm, out_w, sems.at[1])
    copy_a.start()
    copy_w.start()
    role = lax.axis_index("role")
    clip = lax.axis_index("dp") * 2
    row = lax.broadcasted_iota(jnp.int32, (ROWS, 1), 0)
    valid = jnp.where(row < 32, frames_valid[clip], frames_valid[clip + 1]) // POOL
    keep = (row % 32 + role * 32) < valid

    def slope_of(mean, copy, out, pred, cols, first):
        width = mean.shape[-1]
        attended = jnp.concatenate(
            [parts[r, :, first : first + cols] for r in range(ROLES)], axis=1
        )
        copy.wait()
        total = mean[...] + jnp.dot(attended, out[...], preferred_element_type=f32)
        target = total.astype(bf16).astype(f32)
        predicted = pred[...]
        pred_sq = jnp.sum(predicted * predicted, axis=-1, keepdims=True) + epsilon_cos
        targ_sq = jnp.sum(target * target, axis=-1, keepdims=True) + epsilon_cos
        pred_norm = jnp.sqrt(pred_sq)
        both = pred_norm * jnp.sqrt(targ_sq)
        cosine = jnp.sum(predicted * target, axis=-1, keepdims=True) / both
        slope = (cosine / (pred_norm * pred_norm)) * predicted - target / both
        slope = slope + (predicted - target) * (1.0 / width)
        return jnp.where(keep, slope, 0.0).astype(bf16)

    slope_a = slope_of(mean_a, copy_a, out_a, pred_a, A_COLS, 0)
    for g in range(ROLES):
        grouped[g, :, :A_COLS] = slope_a[:, g * A_COLS : (g + 1) * A_COLS]
    slope_w = slope_of(mean_w, copy_w, out_w, pred_w, W_COLS, A_COLS)
    for g in range(ROLES):
        grouped[g, :, A_COLS:] = jnp.concatenate(
            [slope_w[:, g * W_COLS : (g + 1) * W_COLS], jnp.zeros((ROWS, 64), bf16)], axis=1
        )


def slopes(frames_valid, parts, out_a, out_w, mean_a, mean_w, pred_a, pred_w):
    vmem = pl.BlockSpec(memory_space=pltpu.VMEM)
    hbm = pl.BlockSpec(memory_space=pl.ANY)
    return pl.pallas_call(
        slope_kernel,
        out_shape=jax.ShapeDtypeStruct((ROLES, ROWS, OUT_COLS), bf16),
        in_specs=[pl.BlockSpec(memory_space=pltpu.SMEM), vmem, hbm, hbm] + [vmem] * 4,
        out_specs=vmem,
        scratch_shapes=[
            pltpu.VMEM((WAVLM_D, WAVLM_D), bf16),
            pltpu.VMEM((WHISPER_D, WHISPER_D), bf16),
            pltpu.SemaphoreType.DMA((2,)),
        ],
        name="slopes",
    )(frames_valid, parts, out_a, out_w, mean_a, mean_w, pred_a, pred_w)


def outer_kernel(*refs):
    lats, own, other, out = refs[:4], refs[4], refs[5], refs[6]
    role = lax.axis_index("role")
    start = pl.multiple_of((lax.axis_index("dp") % 2) * 256, 256)
    lat = jnp.concatenate([lats[k][:, pl.ds(start, 256)] for k in range(ROLES)], axis=0)
    rows = []
    for k in range(ROLES):
        source = (role - k + ROLES) % ROLES
        rows += [own[source], other[source]]
    grad = lax.dot_general(
        lat, jnp.concatenate(rows, axis=0), (((0,), (0,)), ((), ())), preferred_element_type=f32
    )
    out[...] = grad.reshape(16, 16, OUT_COLS)


def outer(lats, own, other):
    vmem = pl.BlockSpec(memory_space=pltpu.VMEM)
    return pl.pallas_call(
        outer_kernel,
        out_shape=jax.ShapeDtypeStruct((16, 16, OUT_COLS), f32),
        in_specs=[vmem] * 6,
        out_specs=vmem,
        name="outer",
    )(*lats, own, other)


def sum_kernel(x, out):
    total = jnp.sum(x[...], axis=0).astype(bf16)
    out[...] = jnp.broadcast_to(total[None], out.shape)


def reduce_parts(x):
    vmem = pl.BlockSpec(memory_space=pltpu.VMEM)
    return pl.pallas_call(
        sum_kernel,
        out_shape=jax.ShapeDtypeStruct((64, 16, OUT_COLS), bf16),
        in_specs=[vmem],
        out_specs=vmem,
        name="reduce_parts",
    )(x)


def place_kernel(piece, *refs):
    out_a, out_w = refs[-2:]
    blocks = []
    for g in range(ROLES):
        block = piece[g].reshape(128, OUT_COLS).astype(f32)
        out_a[0, :, g * A_COLS : (g + 1) * A_COLS] = block[:, :A_COLS]
        blocks.append(block[:, A_COLS : A_COLS + W_COLS])
    out_w[0] = jnp.concatenate(blocks, axis=1)


def place(piece, partner, held=()):
    half = lambda: (lax.axis_index("dp") + partner) % 2
    hbm = pl.BlockSpec(memory_space=pl.ANY)
    return pl.pallas_call(
        place_kernel,
        grid=(2,),
        out_shape=[
            jax.ShapeDtypeStruct((2, 256, WAVLM_D), f32),
            jax.ShapeDtypeStruct((2, 256, WHISPER_D), f32),
        ],
        in_specs=[pl.BlockSpec((ROLES, 8, 16, OUT_COLS), lambda i: (0, i, 0, 0))]
        + [hbm] * len(held),
        out_specs=[
            pl.BlockSpec((1, 128, WAVLM_D), lambda i: (half(), i, 0)),
            pl.BlockSpec((1, 128, WHISPER_D), lambda i: (half(), i, 0)),
        ],
        input_output_aliases={1: 0, 2: 1} if held else {},
        name="place_partner" if partner else "place_own",
    )(piece, *held)


PLANE = [[z * 8 + y * 2 + c for z in range(4) for y in range(4)] for c in range(2)]
SLICE = [[r * 32 + i for r in range(ROLES) for i in plane] for plane in PLANE]


def per_device(
    wavlm_hidden,
    whisper_hidden,
    wavlm_qkv,
    whisper_qkv,
    wavlm_out,
    whisper_out,
    frames_valid,
    slot_clip,
    latent,
    wavlm_head,
    whisper_head,
):
    chunks = weight_chunks(wavlm_qkv.T, whisper_qkv.T)
    chunks = [chunks[0]] + [dp_send(chunks[k], k, 0, 0) for k in (1, 2, 3)]
    copies = shares(chunks, latent)
    own_rows = lax.all_to_all(
        copies, "dp", split_axis=0, concat_axis=0, tiled=True, axis_index_groups=PLANE
    )
    other_rows = dp_send(own_rows, 0, 0, 1)
    norm_a, norm_w, mean_a, mean_w = norms(wavlm_hidden, whisper_hidden)

    pooled = attend(frames_valid, (own_rows, other_rows), norm_a, norm_w)
    parts = lax.all_to_all(pooled, "role", split_axis=0, concat_axis=0, tiled=True)
    lat = pick(slot_clip, own_rows, other_rows)
    lats = [lat] + [role_send(lat, k) for k in (1, 2, 3)]
    pred_a = jnp.dot(lat[:ROWS], wavlm_head, preferred_element_type=f32)
    pred_w = jnp.dot(lat[:ROWS], whisper_head, preferred_element_type=f32)
    sloped = slopes(
        frames_valid, parts, wavlm_out, whisper_out, mean_a, mean_w, pred_a, pred_w
    )
    slope_own = lax.all_to_all(sloped, "role", split_axis=0, concat_axis=0, tiled=True)
    slope_other = dp_send(slope_own, 0, 0, 1)
    halves = outer(lats, slope_own, slope_other)
    arrived = lax.all_to_all(
        halves, "dp", split_axis=0, concat_axis=0, tiled=True, axis_index_groups=PLANE
    )
    summed = lax.all_to_all(
        reduce_parts(arrived),
        ("role", "dp"),
        split_axis=0,
        concat_axis=0,
        tiled=True,
        axis_index_groups=SLICE,
    ).reshape(ROLES, 16, 16, OUT_COLS)
    partner = dp_send(summed, 0, 0, 1)
    held = place(summed, 0)
    grad_a, grad_w = place(partner, 1, held)
    return grad_a.reshape(STU_D, WAVLM_D), grad_w.reshape(STU_D, WHISPER_D)


def solution(mesh):
    in_specs = (
        P("dp", None, None),
        P("dp", None, None),
        P(None, "dp"),
        P(None, "dp"),
        P(),
        P(),
        P(),
        P(),
        P(None, "dp", None, None),
        P(),
        P(),
    )
    out_specs = (P(), P())

    return jax.shard_map(
        per_device, mesh=mesh, in_specs=in_specs, out_specs=out_specs, check_vma=False
    )
```

time: 210 us -> 188 us (0.90)
  waiting for transfers between devices: 21 us -> 12.2 us
  Pallas kernels: 57.7 us -> 49.3 us
  starting transfers between devices: 26.9 us -> 20.7 us
    all_to_all x1, blocking collectives: 33.3 us -> 44.7 us  [per_device(): lax.all_to_all(copies, 'dp', split_axis=0, concat_axis=0, tiled=True, axi...]
    all_to_all x1, blocking collectives: 21.3 us -> 10.6 us  [per_device(): lax.all_to_all(sloped, 'role', split_axis=0, concat_axis=0, tiled=True)]
    pallas_call x8 -> x7, Pallas kernels: 44.2 us -> 35.8 us  [the longest x1 16.1 us: attend(): pl.pallas_call(attend_kernel, out_shape=jax.ShapeDtypeStruct((ROLES, ROWS...]
    ppermute x9 -> x3, starting transfers between devices: 9.88 us -> 2.79 us  [role_send(): return lax.ppermute(x, 'role', [(i, (i + k) % ROLES) for i in range(ROLES)])]
    ppermute x9 -> x3, waiting for transfers between devices: 11.1 us -> 6.55 us  [role_send(): return lax.ppermute(x, 'role', [(i, (i + k) % ROLES) for i in range(ROLES)])]
    ppermute x7 -> x6, waiting for transfers between devices: 9.94 us -> 5.45 us  [dp_send(): return lax.ppermute(x, 'dp', pairs)]
    all_to_all x0 -> x1, starting transfers between devices: none -> 3.97 us  [per_device(): lax.all_to_all(pooled, 'role', split_axis=0, concat_axis=0, tiled=True)]
    ppermute x7 -> x6, starting transfers between devices: 17 us -> 14 us  [dp_send(): return lax.ppermute(x, 'dp', pairs)]
  transfers between devices with their start and end apart: 16 -> 10, of which waited for: 10 -> 7; matrix products, arithmetic and copies ran while one was open for 1% -> 2% of each run, Pallas kernels for 7% -> 8%
where the time goes in v1:
time: 188 us; the launch traced here: 187 us
  blocking collectives  97.5 us (52%)
  Pallas kernels  49.3 us (26%)
  starting transfers between devices  20.7 us (11%)
  waiting for transfers between devices  12.2 us (6%)
  matrix products  3.77 us (2%)
  local copies, waits for them, and re-layouts  2.79 us (1%)
    all_to_all x1, blocking collectives, per_device(): lax.all_to_all(copies, 'dp', split_axis=0, concat_axis=0, tiled=True, axi...  44.7 us
    all_to_all x1, blocking collectives, per_device(): lax.all_to_all(reduce_parts(arrived), ('role', 'dp'), split_axis=0, conca...  26.3 us
    pallas_call x1, Pallas kernels, attend(): pl.pallas_call(attend_kernel, out_shape=jax.ShapeDtypeStruct((ROLES, ROWS...  16.1 us
    all_to_all x1, blocking collectives, per_device(): lax.all_to_all(halves, 'dp', split_axis=0, concat_axis=0, tiled=True, axi...  15.8 us
    ppermute x6, starting transfers between devices, dp_send(): return lax.ppermute(x, 'dp', pairs)  14 us
    all_to_all x1, blocking collectives, per_device(): lax.all_to_all(sloped, 'role', split_axis=0, concat_axis=0, tiled=True)  10.6 us
    pallas_call x1, Pallas kernels, norms(): pl.pallas_call(norm_kernel, grid=(2, 4), out_shape=[jax.ShapeDtypeStruct(...  9.21 us
    ppermute x3, waiting for transfers between devices, role_send(): return lax.ppermute(x, 'role', [(i, (i + k) % ROLES) for i in range(ROLES)])  6.55 us
  transfers between devices with their start and end apart: 10, of which 7 were waited for; matrix products, arithmetic and copies ran while one was open for 2% of the time, Pallas kernels for 8%

profile of v1, /device:TPU:1, one launch (start us, length us, event | category | flops | bytes accessed | tf_op | source)
XLA Modules:
  0.0 187.0 jit_solution(7714424139141346536)
XLA Ops:
  0.6 0.0 copy-start
  0.6 2.0 %weight_chunks.1 = (bf16[16,32,128]{2,1,0:T(8,128)(2,1)}, bf16[16,32,128]{2,1,0:T(8,128)(2,1)}, bf16[16,32,128]{2,1,0:T(8,128)(2,1)}, bf16[16,32,128]{2,1,0:T(8,128)(2,1)}) custom-call(bf16[96,1024]{1,0:T(8,128)(2,1)} %bitcast.12, bf16[120,1280]{1,0:T(8,128)(2,1)} %bitcast.11), custom_call_target="tpu_custom_call" | custom-call | tf_op jit(solution)/shard_map/weight_chunks/pallas_call | solution.py:109
  2.7 2.5 %collective-permute-start = (bf16[16,32,128]{2,1,0:T(8,128)(2,1)}, bf16[16,32,128]{2,1,0:T(8,128)(2,1)S(1)}, u32[]{:S(2)}, u32[]{:S(2)}) collective-permute-start(bf16[16,32,128]{2,1,0:T(8,128)(2,1)} %get-tuple-element.15), channel_id=1, source_target_pairs={{0,8},{1,9},{2,10},{3,11},{4,12},{5,13},{6,14},{7,15},{8,16},{9,17... | collective-permute-start | bytes 393224 | tf_op jit(solution)/shard_map/ppermute | solution.py:39
  5.1 3.3 %collective-permute-start.1 = (bf16[16,32,128]{2,1,0:T(8,128)(2,1)}, bf16[16,32,128]{2,1,0:T(8,128)(2,1)S(1)}, u32[]{:S(2)}, u32[]{:S(2)}) collective-permute-start(bf16[16,32,128]{2,1,0:T(8,128)(2,1)} %get-tuple-element.16), channel_id=1, source_target_pairs={{0,16},{1,17},{2,18},{3,19},{4,20},{5,21},{6,22},{7,23},{8,24},{9,... | collective-permute-start | bytes 393224 | tf_op jit(solution)/shard_map/ppermute | solution.py:39
  8.4 0.7 collective-permute-start.2
  9.2 1.5 collective-permute-done.refs_1_
  10.7 0.0 copy-start.10
  10.7 3.7 %collective-permute-done.1.refs_2_ = bf16[16,32,128]{2,1,0:T(8,128)(2,1)S(1)} collective-permute-done((bf16[16,32,128]{2,1,0:T(8,128)(2,1)}, bf16[16,32,128]{2,1,0:T(8,128)(2,1)S(1)}, u32[]{:S(2)}, u32[]{:S(2)}) %collective-permute-start.1) | collective-permute-done | bytes 131104 | tf_op jit(solution)/shard_map/ppermute | solution.py:39
  14.4 0.0 copy-start.11
  14.4 0.0 collective-permute-done.2.refs_3_
  14.4 0.0 copy-start.12
  14.4 0.0 copy-done.10
  14.4 0.6 copy-done.11
  15.0 0.0 copy-done.12
  15.1 3.2 %shares.1 = bf16[16,24,32,128]{3,2,1,0:T(8,128)(2,1)} custom-call(bf16[16,32,128]{2,1,0:T(8,128)(2,1)} %get-tuple-element.14.refs_0_, bf16[16,32,128]{2,1,0:T(8,128)(2,1)} %copy-done.10, bf16[16,32,128]{2,1,0:T(8,128)(2,1)} %copy-done.11, bf16[16,32,128]{2,1,0:T(8,128)(2,1)} %copy-done.12, bf16[2,1,128,512]{3,2,1,0:T(8,128)(2,1)} %refs_4_.1), custom_call_target="tpu_custom_call" | custom-call | tf_op jit(solution)/shard_map/shares/pallas_call | solution.py:152
  18.3 44.7 %all_to_all.25.own.refs_0_ = bf16[16,24,32,128]{3,2,1,0:T(8,128)(2,1)} all-to-all(bf16[16,24,32,128]{3,2,1,0:T(8,128)(2,1)} %shares.1), channel_id=1, replica_groups={{0,2,4,6,8,10,12,14,16,18,20,22,24,26,28,30},{1,3,5,7,9,11,13,15,17,19,..., dimensions={0} | all-to-all | bytes 6291456 | tf_op jit(solution)/shard_map/all_to_all | solution.py:510
  63.0 2.3 %collective-permute-start.3 = (bf16[16,24,32,128]{3,2,1,0:T(8,128)(2,1)}, bf16[16,24,32,128]{3,2,1,0:T(8,128)(2,1)}, u32[]{:S(2)}, u32[]{:S(2)}) collective-permute-start(bf16[16,24,32,128]{3,2,1,0:T(8,128)(2,1)} %all_to_all.25.own.refs_0_), channel_id=1, source_target_pairs={{0,1},{1,0},{2,3},{3,2},{4,5},{5,4},{6,7},{7,6},{8,9},{9,8},{10,11... | collective-permute-start | bytes 9437192 | tf_op jit(solution)/shard_map/ppermute | solution.py:39
  65.2 9.2 %norms.1 = (bf16[2,512,1024]{2,1,0:T(8,128)(2,1)}, bf16[2,512,1280]{2,1,0:T(8,128)(2,1)}, f32[64,1024]{1,0:T(8,128)}, f32[64,1280]{1,0:T(8,128)}) custom-call(bf16[2,512,1024]{2,1,0:T(8,128)(2,1)} %wavlm.1, bf16[2,512,1280]{2,1,0:T(8,128)(2,1)} %whisper.1), custom_call_target="tpu_custom_call" | custom-call | flops 60000000 | bytes 24000000 | tf_op jit(solution)/shard_map/norms/pallas_call | solution.py:71
  74.4 0.0 collective-permute-done.3.other.refs_1_
  74.4 16.1 %attend.1 = bf16[4,64,640]{2,1,0:T(8,128)(2,1)} custom-call(s32[64]{0:T(128)} %frames_valid.3, bf16[16,24,32,128]{3,2,1,0:T(8,128)(2,1)} %all_to_all.25.own.refs_0_, bf16[16,24,32,128]{3,2,1,0:T(8,128)(2,1)} %collective-permute-done.3.other.refs_1_, bf16[2,512,1024]{2,1,0:T(8,128)(2,1)} %get-tuple-element.18.refs_2_, ...), custom_call_target="tpu_custom_call" | custom-call | flops 8000000000 | bytes 12000000 | tf_op jit(solution)/shard_map/attend/pallas_call | solution.py:333
  90.6 4.0 %all-to-all-start.1 = ((bf16[4,64,640]{2,1,0:T(8,128)(2,1)}), bf16[4,64,640]{2,1,0:T(8,128)(2,1)S(1)}, u32[]{:S(2)}, u32[]{:S(2)}) async-start(bf16[4,64,640]{2,1,0:T(8,128)(2,1)} %attend.1), calls=%async_computation.1 | async-start | bytes 655360 | tf_op jit(solution)/shard_map/all_to_all | solution.py:517
  94.5 0.0 copy-start.5
  94.5 3.1 %pick.1.refs_0_ = bf16[128,512]{1,0:T(8,128)(2,1)} custom-call(s32[64]{0:T(128)} %slot_clip.1, bf16[16,24,32,128]{3,2,1,0:T(8,128)(2,1)} %all_to_all.25.own.refs_0_, bf16[16,24,32,128]{3,2,1,0:T(8,128)(2,1)} %collective-permute-done.3.other.refs_1_), custom_call_target="tpu_custom_call" | custom-call | tf_op jit(solution)/shard_map/pick/pallas_call | solution.py:198
  97.7 0.0 copy-done
  97.7 1.9 %fusion.refs_3_ = f32[64,1280]{1,0:T(8,128)} fusion(bf16[512,1280]{1,0:T(8,128)(2,1)S(1)} %copy-done, bf16[128,512]{1,0:T(8,128)(2,1)} %pick.1.refs_0_), kind=kOutput, calls=%fused_computation | convolution fusion | flops 83886080 | bytes 1703936 | tf_op jit(solution)/shard_map/dot_general | solution.py:521
  99.6 0.0 copy-done.5
  99.6 1.9 fusion.2.refs_2_
  101.5 0.2 all-to-all-done.1.parts
  101.7 0.0 copy-start.2
  101.7 0.7 copy-done.2
  102.4 0.0 copy-start.4
  102.4 5.7 %slopes.1 = bf16[4,64,640]{2,1,0:T(8,128)(2,1)} custom-call(s32[64]{0:T(128)} %frames_valid.3, bf16[4,64,640]{2,1,0:T(8,128)(2,1)} %copy-done.2, bf16[1024,1024]{1,0:T(8,128)(2,1)} %out_a_hbm.1, bf16[1280,1280]{1,0:T(8,128)(2,1)} %out_w_hbm.1, f32[64,1024]{1,0:T(8,128)} %get-tuple-element.20.refs_0_, f32[64,1280]{1,0:T(8,128)} %get-tuple-element.21.refs_1_, ...), custom_call_target="tpu_custom_call" | custom-call | tf_op jit(solution)/shard_map/slopes/pallas_call | solution.py:403
  108.1 10.6 %all_to_all.26.refs_4_ = bf16[4,64,640]{2,1,0:T(8,128)(2,1)S(1)} all-to-all(bf16[4,64,640]{2,1,0:T(8,128)(2,1)} %slopes.1), channel_id=1, replica_groups=mesh['role'=4,'dp'=32] {'role'}, dimensions={0} | all-to-all | bytes 655360 | tf_op jit(solution)/shard_map/all_to_all | solution.py:525
  118.7 0.0 copy-start.3
  118.7 1.7 collective-permute-start.7
  120.4 0.0 copy-done.4
  120.4 0.3 collective-permute-start.4
  120.7 1.8 collective-permute-start.5
  122.5 0.7 collective-permute-start.6
  123.2 3.9 %collective-permute-done.4.refs_1_ = bf16[128,512]{1,0:T(8,128)(2,1)S(1)} collective-permute-done((bf16[128,512]{1,0:T(8,128)(2,1)S(1)}, bf16[128,512]{1,0:T(8,128)(2,1)S(1)}, u32[]{:S(2)}, u32[]{:S(2)}) %collective-permute-start.4) | collective-permute-done | bytes 131104 | tf_op jit(solution)/shard_map/ppermute | solution.py:43
  127.2 0.0 copy-start.7
  127.2 1.7 collective-permute-done.5.refs_2_
  128.9 0.0 copy-start.8
  128.9 0.9 collective-permute-done.6.refs_3_
  129.8 0.0 copy-start.9
  129.8 0.0 collective-permute-done.7.refs_5_
  129.8 0.0 copy-done.3
  129.8 0.0 copy-done.7
  129.8 0.0 copy-done.8
  129.8 0.6 copy-done.9
  130.4 0.0 copy-start.6
  130.4 0.7 copy-done.6
  131.2 2.6 %outer.1 = f32[16,16,640]{2,1,0:T(8,128)} custom-call(bf16[128,512]{1,0:T(8,128)(2,1)} %pick.1.refs_0_, bf16[128,512]{1,0:T(8,128)(2,1)} %copy-done.7, bf16[128,512]{1,0:T(8,128)(2,1)} %copy-done.8, bf16[128,512]{1,0:T(8,128)(2,1)} %copy-done.9, bf16[4,64,640]{2,1,0:T(8,128)(2,1)} %copy-done.3, bf16[4,64,640]{2,1,0:T(8,128)(2,1)} %copy-done.6), custom_call_target="tpu_custom_call" | custom-call | tf_op jit(solution)/shard_map/outer/pallas_call | solution.py:434
  133.7 15.8 %all_to_all.27.x = f32[16,16,640]{2,1,0:T(8,128)} all-to-all(f32[16,16,640]{2,1,0:T(8,128)} %outer.1), channel_id=1, replica_groups={{0,2,4,6,8,10,12,14,16,18,20,22,24,26,28,30},{1,3,5,7,9,11,13,15,17,19,..., dimensions={0} | all-to-all | bytes 1310720 | tf_op jit(solution)/shard_map/all_to_all | solution.py:528
  149.6 2.3 %reduce_parts.1 = bf16[64,16,640]{2,1,0:T(8,128)(2,1)} custom-call(f32[16,16,640]{2,1,0:T(8,128)} %all_to_all.27.x), custom_call_target="tpu_custom_call" | custom-call | tf_op jit(solution)/shard_map/reduce_parts/pallas_call | solution.py:450
  151.8 26.3 %all_to_all.28 = bf16[64,16,640]{2,1,0:T(8,128)(2,1)S(1)} all-to-all(bf16[64,16,640]{2,1,0:T(8,128)(2,1)} %reduce_parts.1), channel_id=1, replica_groups={{0,2,4,6,8,10,12,14,16,18,20,22,24,26,28,30,32,34,36,38,40,42,44,46,48,..., dimensions={0} | all-to-all | bytes 2621440 | tf_op jit(solution)/shard_map/all_to_all | solution.py:531
  178.2 0.0 copy-start.1
  178.2 3.5 %collective-permute-start.8 = (bf16[4,16,16,640]{3,2,1,0:T(8,128)(2,1)S(1)}, bf16[4,16,16,640]{3,2,1,0:T(8,128)(2,1)}, u32[]{:S(2)}, u32[]{:S(2)}) collective-permute-start(bf16[4,16,16,640]{3,2,1,0:T(8,128)(2,1)S(1)} %bitcast.7), channel_id=1, source_target_pairs={{0,1},{1,0},{2,3},{3,2},{4,5},{5,4},{6,7},{7,6},{8,9},{9,8},{10,11... | collective-permute-start | bytes 3932168 | tf_op jit(solution)/shard_map/ppermute | solution.py:39
  181.7 0.0 copy-done.1
  181.7 2.6 %place_own.1 = (f32[2,256,1024]{2,1,0:T(8,128)}, f32[2,256,1280]{2,1,0:T(8,128)}) custom-call(bf16[4,16,16,640]{3,2,1,0:T(8,128)(2,1)} %bitcast.8), custom_call_target="tpu_custom_call" | custom-call | tf_op jit(solution)/shard_map/place_own/pallas_call | solution.py:472
  184.2 0.2 collective-permute-done.8.piece
  184.5 2.6 %place_partner.1 = (f32[2,256,1024]{2,1,0:T(8,128)}, f32[2,256,1280]{2,1,0:T(8,128)}) custom-call(bf16[4,16,16,640]{3,2,1,0:T(8,128)(2,1)} %collective-permute-done.8.piece, f32[2,256,1024]{2,1,0:T(8,128)} %get-tuple-element.22.refs_0_, f32[2,256,1280]{2,1,0:T(8,128)} %get-tuple-element.23.refs_1_), custom_call_target="tpu_custom_call", output_to_operand_aliasing={{0}: (1, {}), {1}: (2, {})} | custom-call | tf_op jit(solution)/shard_map/place_partner/pallas_call | solution.py:472
Async XLA Ops:
  0.6 97.0 %copy-start = (bf16[512,1280]{1,0:T(8,128)(2,1)S(1)}, bf16[512,1280]{1,0:T(8,128)(2,1)}, u32[]{:S(2)}) copy-start(bf16[512,1280]{1,0:T(8,128)(2,1)} %param.21) | copy-start | bytes 3932164
  2.7 8.0 %collective-permute-start = (bf16[16,32,128]{2,1,0:T(8,128)(2,1)}, bf16[16,32,128]{2,1,0:T(8,128)(2,1)S(1)}, u32[]{:S(2)}, u32[]{:S(2)}) collective-permute-start(bf16[16,32,128]{2,1,0:T(8,128)(2,1)} %get-tuple-element.15), channel_id=1, source_target_pairs={{0,8},{1,9},{2,10},{3,11},{4,12},{5,13},{6,14},{7,15},{8,16},{9,17... | collective-permute-start | bytes 393224 | tf_op jit(solution)/shard_map/ppermute | solution.py:39
  5.1 9.2 %collective-permute-start.1 = (bf16[16,32,128]{2,1,0:T(8,128)(2,1)}, bf16[16,32,128]{2,1,0:T(8,128)(2,1)S(1)}, u32[]{:S(2)}, u32[]{:S(2)}) collective-permute-start(bf16[16,32,128]{2,1,0:T(8,128)(2,1)} %get-tuple-element.16), channel_id=1, source_target_pairs={{0,16},{1,17},{2,18},{3,19},{4,20},{5,21},{6,22},{7,23},{8,24},{9,... | collective-permute-start | bytes 393224 | tf_op jit(solution)/shard_map/ppermute | solution.py:39
  8.4 5.9 %collective-permute-start.2 = (bf16[16,32,128]{2,1,0:T(8,128)(2,1)}, bf16[16,32,128]{2,1,0:T(8,128)(2,1)S(1)}, u32[]{:S(2)}, u32[]{:S(2)}) collective-permute-start(bf16[16,32,128]{2,1,0:T(8,128)(2,1)} %get-tuple-element.17), channel_id=1, source_target_pairs={{0,24},{1,25},{2,26},{3,27},{4,28},{5,29},{6,30},{7,31},{8,0},{9,1... | collective-permute-start | bytes 393224 | tf_op jit(solution)/shard_map/ppermute | solution.py:39
  10.7 3.7 %copy-start.10 = (bf16[16,32,128]{2,1,0:T(8,128)(2,1)}, bf16[16,32,128]{2,1,0:T(8,128)(2,1)S(1)}, u32[]{:S(2)}) copy-start(bf16[16,32,128]{2,1,0:T(8,128)(2,1)S(1)} %collective-permute-done.refs_1_) | copy-start | bytes 393220
  14.4 0.6 copy-start.11
  14.4 0.7 copy-start.12
  63.0 11.5 %collective-permute-start.3 = (bf16[16,24,32,128]{3,2,1,0:T(8,128)(2,1)}, bf16[16,24,32,128]{3,2,1,0:T(8,128)(2,1)}, u32[]{:S(2)}, u32[]{:S(2)}) collective-permute-start(bf16[16,24,32,128]{3,2,1,0:T(8,128)(2,1)} %all_to_all.25.own.refs_0_), channel_id=1, source_target_pairs={{0,1},{1,0},{2,3},{3,2},{4,5},{5,4},{6,7},{7,6},{8,9},{9,8},{10,11... | collective-permute-start | bytes 9437192 | tf_op jit(solution)/shard_map/ppermute | solution.py:39
  90.6 11.1 %all-to-all-start.1 = ((bf16[4,64,640]{2,1,0:T(8,128)(2,1)}), bf16[4,64,640]{2,1,0:T(8,128)(2,1)S(1)}, u32[]{:S(2)}, u32[]{:S(2)}) async-start(bf16[4,64,640]{2,1,0:T(8,128)(2,1)} %attend.1), calls=%async_computation.1 | async-start | bytes 655360 | tf_op jit(solution)/shard_map/all_to_all | solution.py:517
  94.5 5.1 %copy-start.5 = (bf16[512,1024]{1,0:T(8,128)(2,1)S(1)}, bf16[512,1024]{1,0:T(8,128)(2,1)}, u32[]{:S(2)}) copy-start(bf16[512,1024]{1,0:T(8,128)(2,1)} %param.20) | copy-start | bytes 3145732
  101.7 0.7 copy-start.2
  102.4 18.0 %copy-start.4 = (bf16[128,512]{1,0:T(8,128)(2,1)S(1)}, bf16[128,512]{1,0:T(8,128)(2,1)}, u32[]{:S(2)}) copy-start(bf16[128,512]{1,0:T(8,128)(2,1)} %pick.1.refs_0_) | copy-start | bytes 393220
  118.7 11.1 %copy-start.3 = (bf16[4,64,640]{2,1,0:T(8,128)(2,1)}, bf16[4,64,640]{2,1,0:T(8,128)(2,1)S(1)}, u32[]{:S(2)}) copy-start(bf16[4,64,640]{2,1,0:T(8,128)(2,1)S(1)} %all_to_all.26.refs_4_) | copy-start | bytes 983044
  118.7 11.1 %collective-permute-start.7 = (bf16[4,64,640]{2,1,0:T(8,128)(2,1)S(1)}, bf16[4,64,640]{2,1,0:T(8,128)(2,1)S(1)}, u32[]{:S(2)}, u32[]{:S(2)}) collective-permute-start(bf16[4,64,640]{2,1,0:T(8,128)(2,1)S(1)} %all_to_all.26.refs_4_), channel_id=1, source_target_pairs={{0,1},{1,0},{2,3},{3,2},{4,5},{5,4},{6,7},{7,6},{8,9},{9,8},{10,11... | collective-permute-start | bytes 983048 | tf_op jit(solution)/shard_map/ppermute | solution.py:39
  120.4 6.7 %collective-permute-start.4 = (bf16[128,512]{1,0:T(8,128)(2,1)S(1)}, bf16[128,512]{1,0:T(8,128)(2,1)S(1)}, u32[]{:S(2)}, u32[]{:S(2)}) collective-permute-start(bf16[128,512]{1,0:T(8,128)(2,1)S(1)} %copy-done.4), channel_id=1, source_target_pairs={{0,32},{32,64},{64,96},{96,0},{1,33},{33,65},{65,97},{97,1},{2,34}... | collective-permute-start | bytes 393224 | tf_op jit(solution)/shard_map/ppermute | solution.py:43
  120.7 8.2 %collective-permute-start.5 = (bf16[128,512]{1,0:T(8,128)(2,1)S(1)}, bf16[128,512]{1,0:T(8,128)(2,1)S(1)}, u32[]{:S(2)}, u32[]{:S(2)}) collective-permute-start(bf16[128,512]{1,0:T(8,128)(2,1)S(1)} %copy-done.4), channel_id=1, source_target_pairs={{0,64},{32,96},{64,0},{96,32},{1,65},{33,97},{65,1},{97,33},{2,66}... | collective-permute-start | bytes 393224 | tf_op jit(solution)/shard_map/ppermute | solution.py:43
  122.5 7.3 %collective-permute-start.6 = (bf16[128,512]{1,0:T(8,128)(2,1)S(1)}, bf16[128,512]{1,0:T(8,128)(2,1)S(1)}, u32[]{:S(2)}, u32[]{:S(2)}) collective-permute-start(bf16[128,512]{1,0:T(8,128)(2,1)S(1)} %copy-done.4), channel_id=1, source_target_pairs={{0,96},{32,0},{64,32},{96,64},{1,97},{33,1},{65,33},{97,65},{2,98}... | collective-permute-start | bytes 393224 | tf_op jit(solution)/shard_map/ppermute | solution.py:43
  127.2 2.6 %copy-start.7 = (bf16[128,512]{1,0:T(8,128)(2,1)}, bf16[128,512]{1,0:T(8,128)(2,1)S(1)}, u32[]{:S(2)}) copy-start(bf16[128,512]{1,0:T(8,128)(2,1)S(1)} %collective-permute-done.4.refs_1_) | copy-start | bytes 393220
  128.9 0.9 copy-start.8
  129.8 0.6 copy-start.9
  130.4 0.7 copy-start.6
  178.2 3.5 %copy-start.1 = (bf16[64,16,640]{2,1,0:T(8,128)(2,1)}, bf16[64,16,640]{2,1,0:T(8,128)(2,1)S(1)}, u32[]{:S(2)}) copy-start(bf16[64,16,640]{2,1,0:T(8,128)(2,1)S(1)} %all_to_all.28) | copy-start | bytes 3932164
  178.2 6.3 %collective-permute-start.8 = (bf16[4,16,16,640]{3,2,1,0:T(8,128)(2,1)S(1)}, bf16[4,16,16,640]{3,2,1,0:T(8,128)(2,1)}, u32[]{:S(2)}, u32[]{:S(2)}) collective-permute-start(bf16[4,16,16,640]{3,2,1,0:T(8,128)(2,1)S(1)} %bitcast.7), channel_id=1, source_target_pairs={{0,1},{1,0},{2,3},{3,2},{4,5},{5,4},{6,7},{7,6},{8,9},{9,8},{10,11... | collective-permute-start | bytes 3932168 | tf_op jit(solution)/shard_map/ppermute | solution.py:39

commit v2 on v1

--- a/solution.py
+++ b/solution.py
@@ -92,12 +92,12 @@
     for part in range(4):
         for t in range(2):
             lane = (2 * part + t) * 128
-            chunks[part, 3 * t : 3 * t + 3] = qkv_a[:, lane : lane + 128].reshape(3, 32, 128)
+            chunks[part, 8 * t : 8 * t + 3] = qkv_a[:, lane : lane + 128].reshape(3, 32, 128)
         for t in range(10):
             if part < 3:
-                chunks[part, 6 + t] = qkv_w[32 * part : 32 * part + 32, 128 * t : 128 * t + 128]
+                chunks[part, 3 + t + 3 * (t // 5)] = qkv_w[32 * part : 32 * part + 32, 128 * t : 128 * t + 128]
             else:
-                chunks[part, 6 + t] = jnp.concatenate(
+                chunks[part, 3 + t + 3 * (t // 5)] = jnp.concatenate(
                     [qkv_w[96:120, 128 * t : 128 * t + 128], jnp.zeros((8, 128), bf16)], axis=0
                 )
     for k in range(4):
@@ -117,7 +117,7 @@
 
 
 def share_kernel(*refs):
-    parts, latent, out = refs[:4], refs[4], refs[5]
+    parts, latent, outs = refs[:4], refs[4], refs[5:]
     role = lax.axis_index("role")
     z, y, c = place_of(lax.axis_index("dp"))
     row = lax.broadcasted_iota(jnp.int32, (32, 128), 0)
@@ -130,37 +130,54 @@
         source = jnp.where(
             column < width, sources[0], jnp.where(column < 2 * width, sources[1], sources[2])
         )
-        groups = (g, g + 3) if g < 3 else range(6, 16)
-        for group in groups:
-            value = parts[0][group].astype(f32)
-            for k in range(1, 4):
-                value = jnp.where(
-                    source == (z - k + 4) % 4, parts[k][group].astype(f32), value
-                )
-            value = value.astype(bf16)
-            out[:, group] = jnp.broadcast_to(value[None], (16, 32, 128))
-
-
-    for h in range(2):
+        for half in range(2):
+            for group in (g,) if g < 3 else range(3, 8):
+                value = parts[0][8 * half + group].astype(f32)
+                for k in range(1, 4):
+                    other = parts[k][8 * half + group].astype(f32)
+                    value = jnp.where(source == (z - k + 4) % 4, other, value)
+                outs[half][group] = value.astype(bf16)
+    for half in range(2):
         for t in range(4):
-            value = latent[h, 0, :, 128 * t : 128 * t + 128]
-            out[:, 16 + 4 * h + t] = jnp.broadcast_to(value[None], (16, 32, 128))
+            outs[half][8 + t] = latent[half, 0, :, 128 * t : 128 * t + 128]
 
 
 def shares(parts, latent):
     whole = pl.BlockSpec((16, 32, 128), lambda i: (0, 0, 0))
+    half = pl.BlockSpec((12, 32, 128), lambda i: (0, 0, 0))
     return pl.pallas_call(
         share_kernel,
         grid=(1,),
-        out_shape=jax.ShapeDtypeStruct((16, 24, 32, 128), bf16),
+        out_shape=[jax.ShapeDtypeStruct((12, 32, 128), bf16)] * 2,
         in_specs=[whole] * 4
         + [pl.BlockSpec((2, 1, 32, STU_D), lambda i: (0, 0, lax.axis_index("role"), 0))],
-        out_specs=pl.BlockSpec((16, 24, 32, 128), lambda i: (0, 0, 0, 0)),
+        out_specs=[half] * 2,
         name="shares",
     )(*parts, latent)
 
 
-def pick_kernel(slot_clip, own, other, out, slots, rows, sem):
+def spread_line(first, second):
+    got = {}
+    for k in (1, 3, 2):
+        got[k] = dp_send(first, k, 0, 0), dp_send(second, 0, k, 0)
+    lines = [first] + [got[k][0] for k in (1, 2, 3)], [second] + [got[k][1] for k in (1, 2, 3)]
+    return jnp.stack(lines[0]), jnp.stack(lines[1])
+
+
+def spread_cross(first, second):
+    send_a = lambda x, k: dp_send(x, 0, k, 0)
+    send_b = lambda x, k: dp_send(x, k, 0, 0)
+    a1, b1 = send_a(first, 1), send_b(second, 1)
+    a3, b3 = send_a(first, 3), send_b(second, 3)
+    a2, b2 = send_a(a1[:2], 1), send_b(b1[:2], 1)
+    a2x, b2x = send_a(a3[2:], 3), send_b(b3[2:], 3)
+    return [first, a1, a3, a2, a2x, second, b1, b3, b2, b2x]
+
+
+CROSS = [(0, 0), (1, 0), (3, 0), (2, 0), (2, 2)]
+
+
+def pick_latents(slot_clip, rows, slots, out):
     column = lax.axis_index("dp")
     c = column % 2
     base = (column // 2) * 4
@@ -178,65 +195,44 @@
     for i in range(4):
         slot = slots[(2 * c + i) % 4]
         h, j = slot // 32, slot % 32
-        groups = pl.ds(16 + 4 * h, 4)
-
-        @pl.when(j % 2 == c)
-        def _():
-            pltpu.make_async_copy(own.at[j // 2, groups], rows.at[i], sem.at[i]).start()
-
-        @pl.when(j % 2 != c)
-        def _():
-            pltpu.make_async_copy(other.at[j // 2, groups], rows.at[i], sem.at[i]).start()
-
-    for i in range(4):
-        pltpu.make_async_copy(rows.at[i], rows.at[i], sem.at[i]).wait()
-        out[i * 32 : i * 32 + 32] = jnp.concatenate([rows[i, t] for t in range(4)], axis=1)
-
-
-def pick(slot_clip, own, other):
-    hbm = pl.BlockSpec(memory_space=pl.ANY)
-    return pl.pallas_call(
-        pick_kernel,
-        out_shape=jax.ShapeDtypeStruct((2 * ROWS, STU_D), bf16),
-        in_specs=[pl.BlockSpec(memory_space=pltpu.SMEM), hbm, hbm],
-        out_specs=pl.BlockSpec(memory_space=pltpu.VMEM),
-        scratch_shapes=[
-            pltpu.SMEM((4,), jnp.int32),
-            pltpu.VMEM((4, 4, 32, 128), bf16),
-            pltpu.SemaphoreType.DMA((4,)),
-        ],
-        name="pick",
-    )(slot_clip, own, other)
-
-
-def attend_kernel(frames_valid, *refs):
-    pieces = refs[:2]
-    norm_a_hbm, norm_w_hbm, pooled = refs[2:5]
-    norm_a, norm_w, wt_a, wt_w, qkv_a, qkv_w, proj, att_a, att_w = refs[5:14]
-    score_refs, sems = refs[14:16], refs[16]
-    sem_a, sem_w = sems.at[0], sems.at[1]
+        out[i * 32 : i * 32 + 32] = jnp.concatenate(
+            [rows[j, 12 * h + 8 + t] for t in range(4)], axis=1
+        )
+
+
+def attend_kernel(frames_valid, slot_clip, *refs):
+    pieces = refs[:20]
+    norm_a_hbm, norm_w_hbm, pooled, lat = refs[20:24]
+    norm_a, norm_w, rows_in, qkv_a, qkv_w, proj, att_a, att_w = refs[24:32]
+    score_refs, slots, sems = refs[32:34], refs[34], refs[35]
     copy_a = pltpu.make_async_copy(norm_a_hbm, norm_a, sems.at[2])
     copy_w = pltpu.make_async_copy(norm_w_hbm, norm_w, sems.at[3])
     role = lax.axis_index("role")
     column = lax.axis_index("dp")
-    c = column % 2
-
-    def fetch(p, carry):
-        zs = p // 4
+    z, y, c = place_of(column)
+    for first, count, sem in ((0, 3, sems.at[0]), (3, 9, sems.at[1])):
         for n, piece in enumerate(pieces):
-            block = (p % 4) * 2 + (c + n) % 2
-            for t in range(2):
+            core = (c + n // 10) % 2
+            half = (n % 10) // 5
+            far, entry = CROSS[n % 5]
+            for e in range(piece.shape[0]):
+                near = entry + e
+                dz, dy = (near, far) if half == 0 else (far, near)
+                device = ((z - dz) % 4) * 8 + ((y - dy) % 4) * 2 + core
                 pltpu.make_async_copy(
-                    piece.at[p, pl.ds(3 * t, 3)], wt_a.at[2 * zs + t, pl.ds(3 * block, 3)], sem_a
+                    piece.at[e, pl.ds(first, count)],
+                    rows_in.at[device, pl.ds(12 * half + first, count)],
+                    sem,
                 ).start()
-            pltpu.make_async_copy(
-                piece.at[p, pl.ds(6, 10)], wt_w.at[:, block * 4 + zs], sem_w
-            ).start()
-        return carry
-
-    lax.fori_loop(0, 16, fetch, 0)
-    copy_a.start()
+        if first == 0:
+            copy_a.start()
     copy_w.start()
+    wait_a = pltpu.make_async_copy(
+        rows_in.at[:, pl.ds(0, 6)], rows_in.at[:, pl.ds(0, 6)], sems.at[0]
+    )
+    wait_w = pltpu.make_async_copy(
+        rows_in.at[:, pl.ds(0, 18)], rows_in.at[:, pl.ds(0, 18)], sems.at[1]
+    )
     ones_row = jnp.where(
         lax.broadcasted_iota(jnp.int32, (16, FRAMES), 0) == 0, 1.0, 0.0
     ).astype(bf16)
@@ -287,10 +283,24 @@
             mix(item, score_refs[item % 2], top)
             top = next_top
 
-    pltpu.make_async_copy(wt_a, wt_a, sem_a).wait()
+    wait_a.wait()
     copy_a.wait()
     for clip in range(2):
-        lhs = jnp.concatenate([wt_a[t].reshape(3 * A_COLS, 128) for t in range(8)], axis=1)
+        lhs = jnp.concatenate(
+            [
+                jnp.concatenate(
+                    [
+                        rows_in[8 * (t // 2) + block, 12 * (t % 2) : 12 * (t % 2) + 3].reshape(
+                            96, 128
+                        )
+                        for block in range(8)
+                    ],
+                    axis=0,
+                )
+                for t in range(8)
+            ],
+            axis=1,
+        )
         value = lax.dot_general(lhs, norm_a[clip], nt, preferred_element_type=f32)
         for s in range(3):
             kind = (s - role + 6) % 3
@@ -303,10 +313,23 @@
         mean = lax.dot_general(pool_mat, rows, nt, preferred_element_type=f32).astype(bf16)
         pooled[:, clip * 32 : clip * 32 + 32, :A_COLS] = mean.reshape(ROLES, 32, A_COLS)
 
-    pltpu.make_async_copy(wt_w, wt_w, sem_w).wait()
+    wait_w.wait()
     copy_w.wait()
     for clip in range(2):
-        lhs = jnp.concatenate([wt_w[t].reshape(1024, 128) for t in range(10)], axis=1)
+        lhs = jnp.concatenate(
+            [
+                jnp.concatenate(
+                    [
+                        rows_in[8 * zs + block, 12 * (t // 5) + 3 + t % 5]
+                        for block in range(8)
+                        for zs in range(4)
+                    ],
+                    axis=0,
+                )
+                for t in range(10)
+            ],
+            axis=1,
+        )
         proj[...] = lax.dot_general(lhs, norm_w[clip], nt, preferred_element_type=f32)
         for s in range(3):
             kind = (s - role + 6) % 3
@@ -326,21 +349,24 @@
         mean = lax.dot_general(pool_mat, rows, nt, preferred_element_type=f32).astype(bf16)
         mean = jnp.concatenate([mean, jnp.zeros((POOLED, 64), bf16)], axis=1)
         pooled[:, clip * 32 : clip * 32 + 32, A_COLS:] = mean.reshape(ROLES, 32, 384)
-
-
-def attend(frames_valid, pieces, norm_a, norm_w):
+    pick_latents(slot_clip, rows_in, slots, lat)
+
+
+def attend(frames_valid, slot_clip, pieces, norm_a, norm_w):
     vmem = pl.BlockSpec(memory_space=pltpu.VMEM)
     return pl.pallas_call(
         attend_kernel,
-        out_shape=jax.ShapeDtypeStruct((ROLES, ROWS, OUT_COLS), bf16),
-        in_specs=[pl.BlockSpec(memory_space=pltpu.SMEM)]
-        + [pl.BlockSpec(memory_space=pl.ANY)] * 4,
-        out_specs=vmem,
+        out_shape=[
+            jax.ShapeDtypeStruct((ROLES, ROWS, OUT_COLS), bf16),
+            jax.ShapeDtypeStruct((2 * ROWS, STU_D), bf16),
+        ],
+        in_specs=[pl.BlockSpec(memory_space=pltpu.SMEM)] * 2
+        + [pl.BlockSpec(memory_space=pl.ANY)] * 22,
+        out_specs=[vmem] * 2,
         scratch_shapes=[
             pltpu.VMEM((2, FRAMES, WAVLM_D), bf16),
             pltpu.VMEM((2, FRAMES, WHISPER_D), bf16),
-            pltpu.VMEM((8, 24, 32, 128), bf16),
-            pltpu.VMEM((10, 32, 32, 128), bf16),
+            pltpu.VMEM((32, 24, 32, 128), bf16),
             pltpu.VMEM((3, 2, A_HEADS, HEAD, FRAMES), bf16),
             pltpu.VMEM((3, 2, W_HEADS, HEAD, FRAMES), bf16),
             pltpu.VMEM((1024, FRAMES), f32),
@@ -348,13 +374,14 @@
             pltpu.VMEM((2, W_HEADS, HEAD, FRAMES), bf16),
             pltpu.VMEM((FRAMES, FRAMES), f32),
             pltpu.VMEM((FRAMES, FRAMES), f32),
+            pltpu.SMEM((4,), jnp.int32),
             pltpu.SemaphoreType.DMA((4,)),
         ],
         cost_estimate=pl.CostEstimate(
             flops=8_000_000_000, bytes_accessed=12_000_000, transcendentals=5_000_000
         ),
         name="attend",
-    )(frames_valid, *pieces, norm_a, norm_w)
+    )(frames_valid, slot_clip, *pieces, norm_a, norm_w)
 
 
 def slope_kernel(frames_valid, parts, out_a_hbm, out_w_hbm, *refs):
@@ -414,6 +441,21 @@
     )(frames_valid, parts, out_a, out_w, mean_a, mean_w, pred_a, pred_w)
 
 
+def pass_kernel(x, out):
+    out[...] = x[...]
+
+
+def passed(x):
+    vmem = pl.BlockSpec(memory_space=pltpu.VMEM)
+    return pl.pallas_call(
+        pass_kernel,
+        out_shape=jax.ShapeDtypeStruct(x.shape, x.dtype),
+        in_specs=[vmem],
+        out_specs=vmem,
+        name="passed",
+    )(x)
+
+
 def outer_kernel(*refs):
     lats, own, other, out = refs[:4], refs[4], refs[5], refs[6]
     role = lax.axis_index("role")
@@ -506,23 +548,22 @@
 ):
     chunks = weight_chunks(wavlm_qkv.T, whisper_qkv.T)
     chunks = [chunks[0]] + [dp_send(chunks[k], k, 0, 0) for k in (1, 2, 3)]
-    copies = shares(chunks, latent)
-    own_rows = lax.all_to_all(
-        copies, "dp", split_axis=0, concat_axis=0, tiled=True, axis_index_groups=PLANE
-    )
-    other_rows = dp_send(own_rows, 0, 0, 1)
+    first, second = shares(chunks, latent)
+    first, second = spread_line(first, second)
+    pieces = spread_cross(first, second)
+    pieces = pieces + [dp_send(x, 0, 0, 1) for x in pieces]
     norm_a, norm_w, mean_a, mean_w = norms(wavlm_hidden, whisper_hidden)
 
-    pooled = attend(frames_valid, (own_rows, other_rows), norm_a, norm_w)
+    pooled, lat = attend(frames_valid, slot_clip, pieces, norm_a, norm_w)
     parts = lax.all_to_all(pooled, "role", split_axis=0, concat_axis=0, tiled=True)
-    lat = pick(slot_clip, own_rows, other_rows)
-    lats = [lat] + [role_send(lat, k) for k in (1, 2, 3)]
     pred_a = jnp.dot(lat[:ROWS], wavlm_head, preferred_element_type=f32)
     pred_w = jnp.dot(lat[:ROWS], whisper_head, preferred_element_type=f32)
     sloped = slopes(
         frames_valid, parts, wavlm_out, whisper_out, mean_a, mean_w, pred_a, pred_w
     )
     slope_own = lax.all_to_all(sloped, "role", split_axis=0, concat_axis=0, tiled=True)
+    lat = passed(lat)
+    lats = [lat] + [role_send(lat, k) for k in (1, 2, 3)]
     slope_other = dp_send(slope_own, 0, 0, 1)
     halves = outer(lats, slope_own, slope_other)
     arrived = lax.all_to_all(

time: 188 us -> 193 us (1.027)
  blocking collectives: 97.5 us -> 50 us
  starting transfers between devices: 20.7 us -> 50.1 us
  waiting for transfers between devices: 12.2 us -> 35.5 us
  Pallas kernels: 49.3 us -> 46.4 us
    all_to_all x1 -> x0, blocking collectives: 44.7 us -> none  [per_device(): lax.all_to_all(copies, 'dp', split_axis=0, concat_axis=0, tiled=True, axi...]
    ppermute x6 -> x29, starting transfers between devices: 14 us -> 43.9 us  [dp_send(): return lax.ppermute(x, 'dp', pairs)]
    ppermute x6 -> x29, waiting for transfers between devices: 5.45 us -> 23 us  [dp_send(): return lax.ppermute(x, 'dp', pairs)]
    all_to_all x1, waiting for transfers between devices: 0.24 us -> 3.8 us  [per_device(): lax.all_to_all(pooled, 'role', split_axis=0, concat_axis=0, tiled=True)]
    pallas_call x3, Pallas kernels: 22.5 us -> 19.6 us  [the longest x1 16.2 us: attend(): pl.pallas_call(attend_kernel, out_shape=[jax.ShapeDtypeStruct((ROLES, ROW...]
    all_to_all x1, blocking collectives: 26.3 us -> 23.9 us  [per_device(): lax.all_to_all(reduce_parts(arrived), ('role', 'dp'), split_axis=0, conca...]
    ppermute x3, waiting for transfers between devices: 6.55 us -> 8.75 us  [role_send(): return lax.ppermute(x, 'role', [(i, (i + k) % ROLES) for i in range(ROLES)])]
  transfers between devices with their start and end apart: 10 -> 33, of which waited for: 7 -> 13; matrix products, arithmetic and copies ran while one was open for 2% -> 3% of each run, Pallas kernels for 8% -> 7%
where the time goes in v2:
time: 193 us; the launch traced here: 192 us
  starting transfers between devices  50.1 us (26%)
  blocking collectives  50 us (26%)
  Pallas kernels  46.4 us (24%)
  waiting for transfers between devices  35.5 us (18%)
  local copies, waits for them, and re-layouts  4.5 us (2%)
  matrix products  2.94 us (2%)
    ppermute x29, starting transfers between devices, dp_send(): return lax.ppermute(x, 'dp', pairs)  43.9 us
    all_to_all x1, blocking collectives, per_device(): lax.all_to_all(reduce_parts(arrived), ('role', 'dp'), split_axis=0, conca...  23.9 us
    ppermute x29, waiting for transfers between devices, dp_send(): return lax.ppermute(x, 'dp', pairs)  23 us
    all_to_all x1, blocking collectives, per_device(): lax.all_to_all(halves, 'dp', split_axis=0, concat_axis=0, tiled=True, axi...  16.7 us
    pallas_call x1, Pallas kernels, attend(): pl.pallas_call(attend_kernel, out_shape=[jax.ShapeDtypeStruct((ROLES, ROW...  16.2 us
    all_to_all x1, blocking collectives, per_device(): lax.all_to_all(sloped, 'role', split_axis=0, concat_axis=0, tiled=True)  9.31 us
    pallas_call x1, Pallas kernels, norms(): pl.pallas_call(norm_kernel, grid=(2, 4), out_shape=[jax.ShapeDtypeStruct(...  9.19 us
    ppermute x3, waiting for transfers between devices, role_send(): return lax.ppermute(x, 'role', [(i, (i + k) % ROLES) for i in range(ROLES)])  8.75 us
  transfers between devices with their start and end apart: 33, of which 13 were waited for; matrix products, arithmetic and copies ran while one was open for 3% of the time, Pallas kernels for 7%

profile of v2, /device:TPU:1, one launch (start us, length us, event | category | flops | bytes accessed | tf_op | source)
XLA Modules:
  0.0 192.3 jit_solution(14517619266324000870)
XLA Ops:
  0.6 2.1 %weight_chunks.1 = (bf16[16,32,128]{2,1,0:T(8,128)(2,1)}, bf16[16,32,128]{2,1,0:T(8,128)(2,1)}, bf16[16,32,128]{2,1,0:T(8,128)(2,1)}, bf16[16,32,128]{2,1,0:T(8,128)(2,1)}) custom-call(bf16[96,1024]{1,0:T(8,128)(2,1)} %bitcast.20, bf16[120,1280]{1,0:T(8,128)(2,1)} %bitcast.19), custom_call_target="tpu_custom_call" | custom-call | tf_op jit(solution)/shard_map/weight_chunks/pallas_call | solution.py:109
  2.7 2.5 %collective-permute-start = (bf16[16,32,128]{2,1,0:T(8,128)(2,1)}, bf16[16,32,128]{2,1,0:T(8,128)(2,1)S(1)}, u32[]{:S(2)}, u32[]{:S(2)}) collective-permute-start(bf16[16,32,128]{2,1,0:T(8,128)(2,1)} %get-tuple-element.19), channel_id=1, source_target_pairs={{0,8},{1,9},{2,10},{3,11},{4,12},{5,13},{6,14},{7,15},{8,16},{9,17... | collective-permute-start | bytes 393224 | tf_op jit(solution)/shard_map/ppermute | solution.py:39
  5.2 3.3 %collective-permute-start.1 = (bf16[16,32,128]{2,1,0:T(8,128)(2,1)}, bf16[16,32,128]{2,1,0:T(8,128)(2,1)S(1)}, u32[]{:S(2)}, u32[]{:S(2)}) collective-permute-start(bf16[16,32,128]{2,1,0:T(8,128)(2,1)} %get-tuple-element.20), channel_id=1, source_target_pairs={{0,16},{1,17},{2,18},{3,19},{4,20},{5,21},{6,22},{7,23},{8,24},{9,... | collective-permute-start | bytes 393224 | tf_op jit(solution)/shard_map/ppermute | solution.py:39
  8.5 0.7 collective-permute-start.2
  9.2 1.5 collective-permute-done.refs_1_
  10.7 3.7 %collective-permute-done.1.refs_2_ = bf16[16,32,128]{2,1,0:T(8,128)(2,1)S(1)} collective-permute-done((bf16[16,32,128]{2,1,0:T(8,128)(2,1)}, bf16[16,32,128]{2,1,0:T(8,128)(2,1)S(1)}, u32[]{:S(2)}, u32[]{:S(2)}) %collective-permute-start.1) | collective-permute-done | bytes 131104 | tf_op jit(solution)/shard_map/ppermute | solution.py:39
  14.4 0.6 copy-done.13
  15.1 1.9 shares.1
  17.0 2.7 %collective-permute-start.12 = (bf16[12,32,128]{2,1,0:T(8,128)(2,1)}, bf16[12,32,128]{2,1,0:T(8,128)(2,1)S(1)}, u32[]{:S(2)}, u32[]{:S(2)}) collective-permute-start(bf16[12,32,128]{2,1,0:T(8,128)(2,1)} %get-tuple-element.23), channel_id=1, source_target_pairs={{0,6},{1,7},{2,0},{3,1},{4,2},{5,3},{6,4},{7,5},{8,14},{9,15},{10,... | collective-permute-start | bytes 294920 | tf_op jit(solution)/shard_map/ppermute | solution.py:39
  19.7 0.3 collective-permute-start.11
  20.1 0.7 collective-permute-start.10
  20.8 1.0 collective-permute-done.12
  21.7 3.3 %collective-permute-done.11 = bf16[12,32,128]{2,1,0:T(8,128)(2,1)S(1)} collective-permute-done((bf16[12,32,128]{2,1,0:T(8,128)(2,1)}, bf16[12,32,128]{2,1,0:T(8,128)(2,1)S(1)}, u32[]{:S(2)}, u32[]{:S(2)}) %collective-permute-start.11) | collective-permute-done | bytes 98336 | tf_op jit(solution)/shard_map/ppermute | solution.py:39
  25.0 1.0 collective-permute-done.10
  26.0 0.9 pad_maximum_fusion.1.refs_5_
  26.9 3.9 %collective-permute-start.14 = (bf16[4,12,32,128]{3,2,1,0:T(8,128)(2,1)S(1)}, bf16[4,12,32,128]{3,2,1,0:T(8,128)(2,1)S(1)}, u32[]{:S(2)}, u32[]{:S(2)}) collective-permute-start(bf16[4,12,32,128]{3,2,1,0:T(8,128)(2,1)S(1)} %pad_maximum_fusion.1.refs_5_), channel_id=1, source_target_pairs={{0,24},{1,25},{2,26},{3,27},{4,28},{5,29},{6,30},{7,31},{8,0},{9,1... | collective-permute-start | bytes 1179656 | tf_op jit(solution)/shard_map/ppermute | solution.py:39
  30.9 1.0 collective-permute-start.4
  31.9 0.8 collective-permute-start.3
  32.6 0.9 collective-permute-start.13
  33.5 7.4 %collective-permute-done.5 = bf16[12,32,128]{2,1,0:T(8,128)(2,1)S(1)} collective-permute-done((bf16[12,32,128]{2,1,0:T(8,128)(2,1)}, bf16[12,32,128]{2,1,0:T(8,128)(2,1)S(1)}, u32[]{:S(2)}, u32[]{:S(2)}) %collective-permute-start.5) | collective-permute-done | bytes 98336 | tf_op jit(solution)/shard_map/ppermute | solution.py:39
  40.9 0.9 pad_maximum_fusion.refs_0_
  41.9 1.5 collective-permute-start.6
  43.4 4.1 %collective-permute-start.22 = (bf16[4,12,32,128]{3,2,1,0:T(8,128)(2,1)S(1)}, bf16[4,12,32,128]{3,2,1,0:T(8,128)(2,1)S(1)}, u32[]{:S(2)}, u32[]{:S(2)}) collective-permute-start(bf16[4,12,32,128]{3,2,1,0:T(8,128)(2,1)S(1)} %pad_maximum_fusion.1.refs_5_), channel_id=1, source_target_pairs={{0,1},{1,0},{2,3},{3,2},{4,5},{5,4},{6,7},{7,6},{8,9},{9,8},{10,11... | collective-permute-start | bytes 1179656 | tf_op jit(solution)/shard_map/ppermute | solution.py:39
  47.6 3.3 %collective-permute-start.16 = (bf16[2,12,32,128]{3,2,1,0:T(8,128)(2,1)S(1)}, bf16[2,12,32,128]{3,2,1,0:T(8,128)(2,1)S(1)}, u32[]{:S(2)}, u32[]{:S(2)}) collective-permute-start(bf16[2,12,32,128]{3,2,1,0:T(8,128)(2,1)S(1)} %slice.24), channel_id=1, source_target_pairs={{0,24},{1,25},{2,26},{3,27},{4,28},{5,29},{6,30},{7,31},{8,0},{9,1... | collective-permute-start | bytes 589832 | tf_op jit(solution)/shard_map/ppermute | solution.py:39
  51.0 1.3 collective-permute-start.15
  52.3 1.5 collective-permute-start.9
  53.8 0.9 slice.21
  54.8 3.8 %collective-permute-start.24 = (bf16[4,12,32,128]{3,2,1,0:T(8,128)(2,1)S(1)}, bf16[4,12,32,128]{3,2,1,0:T(8,128)(2,1)S(1)}, u32[]{:S(2)}, u32[]{:S(2)}) collective-permute-start(bf16[4,12,32,128]{3,2,1,0:T(8,128)(2,1)S(1)} %collective-permute-done.14.refs_7_), channel_id=1, source_target_pairs={{0,1},{1,0},{2,3},{3,2},{4,5},{5,4},{6,7},{7,6},{8,9},{9,8},{10,11... | collective-permute-start | bytes 1179656 | tf_op jit(solution)/shard_map/ppermute | solution.py:39
  58.6 0.2 collective-permute-start.8
  58.9 0.4 collective-permute-start.26
  59.2 1.8 collective-permute-start.23
  61.0 0.8 collective-permute-start.19
  61.8 4.4 %collective-permute-done.8.refs_3_ = bf16[2,12,32,128]{3,2,1,0:T(8,128)(2,1)} collective-permute-done((bf16[2,12,32,128]{3,2,1,0:T(8,128)(2,1)S(1)}, bf16[2,12,32,128]{3,2,1,0:T(8,128)(2,1)}, u32[]{:S(2)}, u32[]{:S(2)}) %collective-permute-start.8) | collective-permute-done | bytes 196640 | tf_op jit(solution)/shard_map/ppermute | solution.py:39
  66.3 1.0 collective-permute-start.25
  67.3 0.5 collective-permute-start.21
  67.8 0.5 collective-permute-done.25.refs_18_
  68.3 0.7 copy-done.24
  69.0 0.4 collective-permute-start.20
  69.4 9.2 %norms.1 = (bf16[2,512,1024]{2,1,0:T(8,128)(2,1)}, bf16[2,512,1280]{2,1,0:T(8,128)(2,1)}, f32[64,1024]{1,0:T(8,128)}, f32[64,1280]{1,0:T(8,128)}) custom-call(bf16[2,512,1024]{2,1,0:T(8,128)(2,1)} %wavlm.1, bf16[2,512,1280]{2,1,0:T(8,128)(2,1)} %whisper.1), custom_call_target="tpu_custom_call" | custom-call | flops 60000000 | bytes 24000000 | tf_op jit(solution)/shard_map/norms/pallas_call | solution.py:71
  78.7 16.2 %attend.1 = (bf16[4,64,640]{2,1,0:T(8,128)(2,1)}, bf16[128,512]{1,0:T(8,128)(2,1)}) custom-call(s32[64]{0:T(128)} %frames_valid.3, s32[64]{0:T(128)} %slot_clip.1, bf16[4,12,32,128]{3,2,1,0:T(8,128)(2,1)} %copy-done.7, bf16[4,12,32,128]{3,2,1,0:T(8,128)(2,1)} %collective-permute-done.6.refs_1_, bf16[4,12,32,128]{3,2,1,0:T(8,128)(2,1)} %copy-done.17, ...), custom_call_target="tpu_custom_call" | custom-call | flops 8000000000 | bytes 12000000 | tf_op jit(solution)/shard_map/attend/pallas_call | solution.py:357
  94.9 4.1 %all-to-all-start = ((bf16[4,64,640]{2,1,0:T(8,128)(2,1)}), bf16[4,64,640]{2,1,0:T(8,128)(2,1)S(1)}, u32[]{:S(2)}, u32[]{:S(2)}) async-start(bf16[4,64,640]{2,1,0:T(8,128)(2,1)} %get-tuple-element.27), calls=%async_computation | async-start | bytes 655360 | tf_op jit(solution)/shard_map/all_to_all | solution.py:558
  99.0 1.9 fusion.refs_3_
  100.9 1.0 fusion.2.refs_2_
  101.9 3.8 %all-to-all-done.parts = bf16[4,64,640]{2,1,0:T(8,128)(2,1)S(1)} async-done(((bf16[4,64,640]{2,1,0:T(8,128)(2,1)}), bf16[4,64,640]{2,1,0:T(8,128)(2,1)S(1)}, u32[]{:S(2)}, u32[]{:S(2)}) %all-to-all-start) | async-done | bytes 327712 | tf_op jit(solution)/shard_map/all_to_all | solution.py:558
  105.7 0.7 copy-done.2
  106.4 5.6 %slopes.1 = bf16[4,64,640]{2,1,0:T(8,128)(2,1)} custom-call(s32[64]{0:T(128)} %frames_valid.3, bf16[4,64,640]{2,1,0:T(8,128)(2,1)} %copy-done.2, bf16[1024,1024]{1,0:T(8,128)(2,1)} %out_a_hbm.1, bf16[1280,1280]{1,0:T(8,128)(2,1)} %out_w_hbm.1, f32[64,1024]{1,0:T(8,128)} %get-tuple-element.28.refs_0_, f32[64,1280]{1,0:T(8,128)} %get-tuple-element.29.refs_1_, ...), custom_call_target="tpu_custom_call" | custom-call | tf_op jit(solution)/shard_map/slopes/pallas_call | solution.py:430
  112.1 9.3 %all_to_all.20.refs_4_ = bf16[4,64,640]{2,1,0:T(8,128)(2,1)S(1)} all-to-all(bf16[4,64,640]{2,1,0:T(8,128)(2,1)} %slopes.1), channel_id=1, replica_groups=mesh['role'=4,'dp'=32] {'role'}, dimensions={0} | all-to-all | bytes 655360 | tf_op jit(solution)/shard_map/all_to_all | solution.py:564
  121.4 2.7 %collective-permute-start.30 = (bf16[4,64,640]{2,1,0:T(8,128)(2,1)S(1)}, bf16[4,64,640]{2,1,0:T(8,128)(2,1)S(1)}, u32[]{:S(2)}, u32[]{:S(2)}) collective-permute-start(bf16[4,64,640]{2,1,0:T(8,128)(2,1)S(1)} %all_to_all.20.refs_4_), channel_id=1, source_target_pairs={{0,1},{1,0},{2,3},{3,2},{4,5},{5,4},{6,7},{7,6},{8,9},{9,8},{10,11... | collective-permute-start | bytes 983048 | tf_op jit(solution)/shard_map/ppermute | solution.py:39
  124.1 1.6 passed.1.refs_0_
  125.7 0.9 collective-permute-start.29
  126.6 1.2 collective-permute-start.28
  127.7 3.1 %collective-permute-done.29.refs_3_ = bf16[128,512]{1,0:T(8,128)(2,1)S(1)} collective-permute-done((bf16[128,512]{1,0:T(8,128)(2,1)}, bf16[128,512]{1,0:T(8,128)(2,1)S(1)}, u32[]{:S(2)}, u32[]{:S(2)}) %collective-permute-start.29) | collective-permute-done | bytes 131104 | tf_op jit(solution)/shard_map/ppermute | solution.py:43
  130.8 2.1 %collective-permute-done.28.refs_2_ = bf16[128,512]{1,0:T(8,128)(2,1)S(1)} collective-permute-done((bf16[128,512]{1,0:T(8,128)(2,1)}, bf16[128,512]{1,0:T(8,128)(2,1)S(1)}, u32[]{:S(2)}, u32[]{:S(2)}) %collective-permute-start.28) | collective-permute-done | bytes 131104 | tf_op jit(solution)/shard_map/ppermute | solution.py:43
  132.9 3.6 %collective-permute-done.27.refs_1_ = bf16[128,512]{1,0:T(8,128)(2,1)S(1)} collective-permute-done((bf16[128,512]{1,0:T(8,128)(2,1)}, bf16[128,512]{1,0:T(8,128)(2,1)S(1)}, u32[]{:S(2)}, u32[]{:S(2)}) %collective-permute-start.27) | collective-permute-done | bytes 131104 | tf_op jit(solution)/shard_map/ppermute | solution.py:43
  136.5 0.6 copy-done.11
  137.1 0.7 copy-done.8
  137.9 2.6 %outer.1 = f32[16,16,640]{2,1,0:T(8,128)} custom-call(bf16[128,512]{1,0:T(8,128)(2,1)} %passed.1.refs_0_, bf16[128,512]{1,0:T(8,128)(2,1)} %copy-done.11, bf16[128,512]{1,0:T(8,128)(2,1)} %copy-done.10, bf16[128,512]{1,0:T(8,128)(2,1)} %copy-done.9, bf16[4,64,640]{2,1,0:T(8,128)(2,1)} %copy-done.3, bf16[4,64,640]{2,1,0:T(8,128)(2,1)} %copy-done.8), custom_call_target="tpu_custom_call" | custom-call | tf_op jit(solution)/shard_map/outer/pallas_call | solution.py:476
  140.4 16.7 %all_to_all.21.x = f32[16,16,640]{2,1,0:T(8,128)} all-to-all(f32[16,16,640]{2,1,0:T(8,128)} %outer.1), channel_id=1, replica_groups={{0,2,4,6,8,10,12,14,16,18,20,22,24,26,28,30},{1,3,5,7,9,11,13,15,17,19,..., dimensions={0} | all-to-all | bytes 1310720 | tf_op jit(solution)/shard_map/all_to_all | solution.py:569
  157.2 2.3 %reduce_parts.1 = bf16[64,16,640]{2,1,0:T(8,128)(2,1)} custom-call(f32[16,16,640]{2,1,0:T(8,128)} %all_to_all.21.x), custom_call_target="tpu_custom_call" | custom-call | tf_op jit(solution)/shard_map/reduce_parts/pallas_call | solution.py:492
  159.5 23.9 %all_to_all.22 = bf16[64,16,640]{2,1,0:T(8,128)(2,1)S(1)} all-to-all(bf16[64,16,640]{2,1,0:T(8,128)(2,1)} %reduce_parts.1), channel_id=1, replica_groups={{0,2,4,6,8,10,12,14,16,18,20,22,24,26,28,30,32,34,36,38,40,42,44,46,48,..., dimensions={0} | all-to-all | bytes 2621440 | tf_op jit(solution)/shard_map/all_to_all | solution.py:572
  183.4 3.5 %collective-permute-start.31 = (bf16[4,16,16,640]{3,2,1,0:T(8,128)(2,1)S(1)}, bf16[4,16,16,640]{3,2,1,0:T(8,128)(2,1)}, u32[]{:S(2)}, u32[]{:S(2)}) collective-permute-start(bf16[4,16,16,640]{3,2,1,0:T(8,128)(2,1)S(1)} %bitcast.15), channel_id=1, source_target_pairs={{0,1},{1,0},{2,3},{3,2},{4,5},{5,4},{6,7},{7,6},{8,9},{9,8},{10,11... | collective-permute-start | bytes 3932168 | tf_op jit(solution)/shard_map/ppermute | solution.py:39
  186.9 2.6 %place_own.1 = (f32[2,256,1024]{2,1,0:T(8,128)}, f32[2,256,1280]{2,1,0:T(8,128)}) custom-call(bf16[4,16,16,640]{3,2,1,0:T(8,128)(2,1)} %bitcast.16), custom_call_target="tpu_custom_call" | custom-call | tf_op jit(solution)/shard_map/place_own/pallas_call | solution.py:514
  189.5 0.2 collective-permute-done.31.piece
  189.7 2.6 %place_partner.1 = (f32[2,256,1024]{2,1,0:T(8,128)}, f32[2,256,1280]{2,1,0:T(8,128)}) custom-call(bf16[4,16,16,640]{3,2,1,0:T(8,128)(2,1)} %collective-permute-done.31.piece, f32[2,256,1024]{2,1,0:T(8,128)} %get-tuple-element.30.refs_0_, f32[2,256,1280]{2,1,0:T(8,128)} %get-tuple-element.31.refs_1_), custom_call_target="tpu_custom_call", output_to_operand_aliasing={{0}: (1, {}), {1}: (2, {})} | custom-call | tf_op jit(solution)/shard_map/place_partner/pallas_call | solution.py:514
  (73 shorter events, 0.6 us)
Async XLA Ops:
  0.6 98.3 %copy-start = (bf16[512,1280]{1,0:T(8,128)(2,1)S(1)}, bf16[512,1280]{1,0:T(8,128)(2,1)}, u32[]{:S(2)}) copy-start(bf16[512,1280]{1,0:T(8,128)(2,1)} %param.21) | copy-start | bytes 3932164
  2.7 8.0 %collective-permute-start = (bf16[16,32,128]{2,1,0:T(8,128)(2,1)}, bf16[16,32,128]{2,1,0:T(8,128)(2,1)S(1)}, u32[]{:S(2)}, u32[]{:S(2)}) collective-permute-start(bf16[16,32,128]{2,1,0:T(8,128)(2,1)} %get-tuple-element.19), channel_id=1, source_target_pairs={{0,8},{1,9},{2,10},{3,11},{4,12},{5,13},{6,14},{7,15},{8,16},{9,17... | collective-permute-start | bytes 393224 | tf_op jit(solution)/shard_map/ppermute | solution.py:39
  5.2 9.2 %collective-permute-start.1 = (bf16[16,32,128]{2,1,0:T(8,128)(2,1)}, bf16[16,32,128]{2,1,0:T(8,128)(2,1)S(1)}, u32[]{:S(2)}, u32[]{:S(2)}) collective-permute-start(bf16[16,32,128]{2,1,0:T(8,128)(2,1)} %get-tuple-element.20), channel_id=1, source_target_pairs={{0,16},{1,17},{2,18},{3,19},{4,20},{5,21},{6,22},{7,23},{8,24},{9,... | collective-permute-start | bytes 393224 | tf_op jit(solution)/shard_map/ppermute | solution.py:39
  8.5 5.9 %collective-permute-start.2 = (bf16[16,32,128]{2,1,0:T(8,128)(2,1)}, bf16[16,32,128]{2,1,0:T(8,128)(2,1)S(1)}, u32[]{:S(2)}, u32[]{:S(2)}) collective-permute-start(bf16[16,32,128]{2,1,0:T(8,128)(2,1)} %get-tuple-element.21), channel_id=1, source_target_pairs={{0,24},{1,25},{2,26},{3,27},{4,28},{5,29},{6,30},{7,31},{8,0},{9,1... | collective-permute-start | bytes 393224 | tf_op jit(solution)/shard_map/ppermute | solution.py:39
  10.7 3.7 %copy-start.12 = (bf16[16,32,128]{2,1,0:T(8,128)(2,1)}, bf16[16,32,128]{2,1,0:T(8,128)(2,1)S(1)}, u32[]{:S(2)}) copy-start(bf16[16,32,128]{2,1,0:T(8,128)(2,1)S(1)} %collective-permute-done.refs_1_) | copy-start | bytes 393220
  14.4 0.7 copy-start.13
  14.4 0.7 copy-start.14
  17.0 4.8 %collective-permute-start.12 = (bf16[12,32,128]{2,1,0:T(8,128)(2,1)}, bf16[12,32,128]{2,1,0:T(8,128)(2,1)S(1)}, u32[]{:S(2)}, u32[]{:S(2)}) collective-permute-start(bf16[12,32,128]{2,1,0:T(8,128)(2,1)} %get-tuple-element.23), channel_id=1, source_target_pairs={{0,6},{1,7},{2,0},{3,1},{4,2},{5,3},{6,4},{7,5},{8,14},{9,15},{10,... | collective-permute-start | bytes 294920 | tf_op jit(solution)/shard_map/ppermute | solution.py:39
  19.7 5.3 %collective-permute-start.11 = (bf16[12,32,128]{2,1,0:T(8,128)(2,1)}, bf16[12,32,128]{2,1,0:T(8,128)(2,1)S(1)}, u32[]{:S(2)}, u32[]{:S(2)}) collective-permute-start(bf16[12,32,128]{2,1,0:T(8,128)(2,1)} %get-tuple-element.23), channel_id=1, source_target_pairs={{0,4},{1,5},{2,6},{3,7},{4,0},{5,1},{6,2},{7,3},{8,12},{9,13},{10,... | collective-permute-start | bytes 294920 | tf_op jit(solution)/shard_map/ppermute | solution.py:39
  20.1 5.9 %collective-permute-start.10 = (bf16[12,32,128]{2,1,0:T(8,128)(2,1)}, bf16[12,32,128]{2,1,0:T(8,128)(2,1)S(1)}, u32[]{:S(2)}, u32[]{:S(2)}) collective-permute-start(bf16[12,32,128]{2,1,0:T(8,128)(2,1)} %get-tuple-element.23), channel_id=1, source_target_pairs={{0,2},{1,3},{2,4},{3,5},{4,6},{5,7},{6,0},{7,1},{8,10},{9,11},{10,... | collective-permute-start | bytes 294920 | tf_op jit(solution)/shard_map/ppermute | solution.py:39
  26.9 51.7 %copy-start.6 = (bf16[4,12,32,128]{3,2,1,0:T(8,128)(2,1)}, bf16[4,12,32,128]{3,2,1,0:T(8,128)(2,1)S(1)}, u32[]{:S(2)}) copy-start(bf16[4,12,32,128]{3,2,1,0:T(8,128)(2,1)S(1)} %pad_maximum_fusion.1.refs_5_) | copy-start | bytes 1179652
  26.9 20.6 %collective-permute-start.14 = (bf16[4,12,32,128]{3,2,1,0:T(8,128)(2,1)S(1)}, bf16[4,12,32,128]{3,2,1,0:T(8,128)(2,1)S(1)}, u32[]{:S(2)}, u32[]{:S(2)}) collective-permute-start(bf16[4,12,32,128]{3,2,1,0:T(8,128)(2,1)S(1)} %pad_maximum_fusion.1.refs_5_), channel_id=1, source_target_pairs={{0,24},{1,25},{2,26},{3,27},{4,28},{5,29},{6,30},{7,31},{8,0},{9,1... | collective-permute-start | bytes 1179656 | tf_op jit(solution)/shard_map/ppermute | solution.py:39
  30.8 10.1 %collective-permute-start.5 = (bf16[12,32,128]{2,1,0:T(8,128)(2,1)}, bf16[12,32,128]{2,1,0:T(8,128)(2,1)S(1)}, u32[]{:S(2)}, u32[]{:S(2)}) collective-permute-start(bf16[12,32,128]{2,1,0:T(8,128)(2,1)} %get-tuple-element.22), channel_id=1, source_target_pairs={{0,24},{1,25},{2,26},{3,27},{4,28},{5,29},{6,30},{7,31},{8,0},{9,1... | collective-permute-start | bytes 294920 | tf_op jit(solution)/shard_map/ppermute | solution.py:39
  30.9 10.0 %collective-permute-start.4 = (bf16[12,32,128]{2,1,0:T(8,128)(2,1)}, bf16[12,32,128]{2,1,0:T(8,128)(2,1)S(1)}, u32[]{:S(2)}, u32[]{:S(2)}) collective-permute-start(bf16[12,32,128]{2,1,0:T(8,128)(2,1)} %get-tuple-element.22), channel_id=1, source_target_pairs={{0,16},{1,17},{2,18},{3,19},{4,20},{5,21},{6,22},{7,23},{8,24},{9,... | collective-permute-start | bytes 294920 | tf_op jit(solution)/shard_map/ppermute | solution.py:39
  31.9 9.0 %collective-permute-start.3 = (bf16[12,32,128]{2,1,0:T(8,128)(2,1)}, bf16[12,32,128]{2,1,0:T(8,128)(2,1)S(1)}, u32[]{:S(2)}, u32[]{:S(2)}) collective-permute-start(bf16[12,32,128]{2,1,0:T(8,128)(2,1)} %get-tuple-element.22), channel_id=1, source_target_pairs={{0,8},{1,9},{2,10},{3,11},{4,12},{5,13},{6,14},{7,15},{8,16},{9,17... | collective-permute-start | bytes 294920 | tf_op jit(solution)/shard_map/ppermute | solution.py:39
  32.6 15.0 %collective-permute-start.13 = (bf16[4,12,32,128]{3,2,1,0:T(8,128)(2,1)S(1)}, bf16[4,12,32,128]{3,2,1,0:T(8,128)(2,1)S(1)}, u32[]{:S(2)}, u32[]{:S(2)}) collective-permute-start(bf16[4,12,32,128]{3,2,1,0:T(8,128)(2,1)S(1)} %pad_maximum_fusion.1.refs_5_), channel_id=1, source_target_pairs={{0,8},{1,9},{2,10},{3,11},{4,12},{5,13},{6,14},{7,15},{8,16},{9,17... | collective-permute-start | bytes 1179656 | tf_op jit(solution)/shard_map/ppermute | solution.py:39
  41.8 36.7 %copy-start.7 = (bf16[4,12,32,128]{3,2,1,0:T(8,128)(2,1)}, bf16[4,12,32,128]{3,2,1,0:T(8,128)(2,1)S(1)}, u32[]{:S(2)}) copy-start(bf16[4,12,32,128]{3,2,1,0:T(8,128)(2,1)S(1)} %pad_maximum_fusion.refs_0_) | copy-start | bytes 1179652
  41.8 9.2 %collective-permute-start.7 = (bf16[4,12,32,128]{3,2,1,0:T(8,128)(2,1)S(1)}, bf16[4,12,32,128]{3,2,1,0:T(8,128)(2,1)S(1)}, u32[]{:S(2)}, u32[]{:S(2)}) collective-permute-start(bf16[4,12,32,128]{3,2,1,0:T(8,128)(2,1)S(1)} %pad_maximum_fusion.refs_0_), channel_id=1, source_target_pairs={{0,6},{1,7},{2,0},{3,1},{4,2},{5,3},{6,4},{7,5},{8,14},{9,15},{10,... | collective-permute-start | bytes 1179656 | tf_op jit(solution)/shard_map/ppermute | solution.py:39
  41.9 10.4 %collective-permute-start.6 = (bf16[4,12,32,128]{3,2,1,0:T(8,128)(2,1)S(1)}, bf16[4,12,32,128]{3,2,1,0:T(8,128)(2,1)}, u32[]{:S(2)}, u32[]{:S(2)}) collective-permute-start(bf16[4,12,32,128]{3,2,1,0:T(8,128)(2,1)S(1)} %pad_maximum_fusion.refs_0_), channel_id=1, source_target_pairs={{0,2},{1,3},{2,4},{3,5},{4,6},{5,7},{6,0},{7,1},{8,10},{9,11},{10,... | collective-permute-start | bytes 1179656 | tf_op jit(solution)/shard_map/ppermute | solution.py:39
  43.4 11.4 %collective-permute-start.22 = (bf16[4,12,32,128]{3,2,1,0:T(8,128)(2,1)S(1)}, bf16[4,12,32,128]{3,2,1,0:T(8,128)(2,1)S(1)}, u32[]{:S(2)}, u32[]{:S(2)}) collective-permute-start(bf16[4,12,32,128]{3,2,1,0:T(8,128)(2,1)S(1)} %pad_maximum_fusion.1.refs_5_), channel_id=1, source_target_pairs={{0,1},{1,0},{2,3},{3,2},{4,5},{5,4},{6,7},{7,6},{8,9},{9,8},{10,11... | collective-permute-start | bytes 1179656 | tf_op jit(solution)/shard_map/ppermute | solution.py:39
  47.5 31.1 %copy-start.15 = (bf16[4,12,32,128]{3,2,1,0:T(8,128)(2,1)}, bf16[4,12,32,128]{3,2,1,0:T(8,128)(2,1)S(1)}, u32[]{:S(2)}) copy-start(bf16[4,12,32,128]{3,2,1,0:T(8,128)(2,1)S(1)} %collective-permute-done.14.refs_7_) | copy-start | bytes 1179652
  47.5 11.1 %collective-permute-start.17 = (bf16[4,12,32,128]{3,2,1,0:T(8,128)(2,1)S(1)}, bf16[4,12,32,128]{3,2,1,0:T(8,128)(2,1)S(1)}, u32[]{:S(2)}, u32[]{:S(2)}) collective-permute-start(bf16[4,12,32,128]{3,2,1,0:T(8,128)(2,1)S(1)} %pad_maximum_fusion.refs_0_), channel_id=1, source_target_pairs={{0,1},{1,0},{2,3},{3,2},{4,5},{5,4},{6,7},{7,6},{8,9},{9,8},{10,11... | collective-permute-start | bytes 1179656 | tf_op jit(solution)/shard_map/ppermute | solution.py:39
  47.6 31.0 %copy-start.16 = (bf16[4,12,32,128]{3,2,1,0:T(8,128)(2,1)}, bf16[4,12,32,128]{3,2,1,0:T(8,128)(2,1)S(1)}, u32[]{:S(2)}) copy-start(bf16[4,12,32,128]{3,2,1,0:T(8,128)(2,1)S(1)} %collective-permute-done.13.refs_6_) | copy-start | bytes 1179652
  47.6 11.2 %collective-permute-start.16 = (bf16[2,12,32,128]{3,2,1,0:T(8,128)(2,1)S(1)}, bf16[2,12,32,128]{3,2,1,0:T(8,128)(2,1)S(1)}, u32[]{:S(2)}, u32[]{:S(2)}) collective-permute-start(bf16[2,12,32,128]{3,2,1,0:T(8,128)(2,1)S(1)} %slice.24), channel_id=1, source_target_pairs={{0,24},{1,25},{2,26},{3,27},{4,28},{5,29},{6,30},{7,31},{8,0},{9,1... | collective-permute-start | bytes 589832 | tf_op jit(solution)/shard_map/ppermute | solution.py:39
  51.0 27.6 %copy-start.17 = (bf16[4,12,32,128]{3,2,1,0:T(8,128)(2,1)}, bf16[4,12,32,128]{3,2,1,0:T(8,128)(2,1)S(1)}, u32[]{:S(2)}) copy-start(bf16[4,12,32,128]{3,2,1,0:T(8,128)(2,1)S(1)} %collective-permute-done.7.refs_2_) | copy-start | bytes 1179652
  51.0 8.2 %collective-permute-start.15 = (bf16[2,12,32,128]{3,2,1,0:T(8,128)(2,1)S(1)}, bf16[2,12,32,128]{3,2,1,0:T(8,128)(2,1)S(1)}, u32[]{:S(2)}, u32[]{:S(2)}) collective-permute-start(bf16[2,12,32,128]{3,2,1,0:T(8,128)(2,1)S(1)} %slice.23), channel_id=1, source_target_pairs={{0,8},{1,9},{2,10},{3,11},{4,12},{5,13},{6,14},{7,15},{8,16},{9,17... | collective-permute-start | bytes 589832 | tf_op jit(solution)/shard_map/ppermute | solution.py:39
  52.3 8.7 %collective-permute-start.9 = (bf16[2,12,32,128]{3,2,1,0:T(8,128)(2,1)S(1)}, bf16[2,12,32,128]{3,2,1,0:T(8,128)(2,1)}, u32[]{:S(2)}, u32[]{:S(2)}) collective-permute-start(bf16[2,12,32,128]{3,2,1,0:T(8,128)(2,1)S(1)} %slice.22), channel_id=1, source_target_pairs={{0,6},{1,7},{2,0},{3,1},{4,2},{5,3},{6,4},{7,5},{8,14},{9,15},{10,... | collective-permute-start | bytes 589832 | tf_op jit(solution)/shard_map/ppermute | solution.py:39
  54.7 12.6 %copy-start.18 = (bf16[4,12,32,128]{3,2,1,0:T(8,128)(2,1)}, bf16[4,12,32,128]{3,2,1,0:T(8,128)(2,1)S(1)}, u32[]{:S(2)}) copy-start(bf16[4,12,32,128]{3,2,1,0:T(8,128)(2,1)S(1)} %collective-permute-done.22.refs_15_) | copy-start | bytes 1179652
  54.8 12.6 %collective-permute-start.24 = (bf16[4,12,32,128]{3,2,1,0:T(8,128)(2,1)S(1)}, bf16[4,12,32,128]{3,2,1,0:T(8,128)(2,1)S(1)}, u32[]{:S(2)}, u32[]{:S(2)}) collective-permute-start(bf16[4,12,32,128]{3,2,1,0:T(8,128)(2,1)S(1)} %collective-permute-done.14.refs_7_), channel_id=1, source_target_pairs={{0,1},{1,0},{2,3},{3,2},{4,5},{5,4},{6,7},{7,6},{8,9},{9,8},{10,11... | collective-permute-start | bytes 1179656 | tf_op jit(solution)/shard_map/ppermute | solution.py:39
  58.6 9.2 %copy-start.19 = (bf16[4,12,32,128]{3,2,1,0:T(8,128)(2,1)}, bf16[4,12,32,128]{3,2,1,0:T(8,128)(2,1)S(1)}, u32[]{:S(2)}) copy-start(bf16[4,12,32,128]{3,2,1,0:T(8,128)(2,1)S(1)} %collective-permute-done.17.refs_10_) | copy-start | bytes 1179652
  58.6 7.7 %collective-permute-start.8 = (bf16[2,12,32,128]{3,2,1,0:T(8,128)(2,1)S(1)}, bf16[2,12,32,128]{3,2,1,0:T(8,128)(2,1)}, u32[]{:S(2)}, u32[]{:S(2)}) collective-permute-start(bf16[2,12,32,128]{3,2,1,0:T(8,128)(2,1)S(1)} %slice.21), channel_id=1, source_target_pairs={{0,2},{1,3},{2,4},{3,5},{4,6},{5,7},{6,0},{7,1},{8,10},{9,11},{10,... | collective-permute-start | bytes 589832 | tf_op jit(solution)/shard_map/ppermute | solution.py:39
  58.9 19.8 %copy-start.21 = (bf16[2,12,32,128]{3,2,1,0:T(8,128)(2,1)}, bf16[2,12,32,128]{3,2,1,0:T(8,128)(2,1)S(1)}, u32[]{:S(2)}) copy-start(bf16[2,12,32,128]{3,2,1,0:T(8,128)(2,1)S(1)} %collective-permute-done.16.refs_9_) | copy-start | bytes 589828
  58.9 8.4 %collective-permute-start.26 = (bf16[2,12,32,128]{3,2,1,0:T(8,128)(2,1)S(1)}, bf16[2,12,32,128]{3,2,1,0:T(8,128)(2,1)S(1)}, u32[]{:S(2)}, u32[]{:S(2)}) collective-permute-start(bf16[2,12,32,128]{3,2,1,0:T(8,128)(2,1)S(1)} %collective-permute-done.16.refs_9_), channel_id=1, source_target_pairs={{0,1},{1,0},{2,3},{3,2},{4,5},{5,4},{6,7},{7,6},{8,9},{9,8},{10,11... | collective-permute-start | bytes 589832 | tf_op jit(solution)/shard_map/ppermute | solution.py:39
  59.2 9.1 %copy-start.22 = (bf16[2,12,32,128]{3,2,1,0:T(8,128)(2,1)}, bf16[2,12,32,128]{3,2,1,0:T(8,128)(2,1)S(1)}, u32[]{:S(2)}) copy-start(bf16[2,12,32,128]{3,2,1,0:T(8,128)(2,1)S(1)} %collective-permute-done.15.refs_8_) | copy-start | bytes 589828
  59.2 19.4 %collective-permute-start.23 = (bf16[4,12,32,128]{3,2,1,0:T(8,128)(2,1)S(1)}, bf16[4,12,32,128]{3,2,1,0:T(8,128)(2,1)}, u32[]{:S(2)}, u32[]{:S(2)}) collective-permute-start(bf16[4,12,32,128]{3,2,1,0:T(8,128)(2,1)S(1)} %collective-permute-done.13.refs_6_), channel_id=1, source_target_pairs={{0,1},{1,0},{2,3},{3,2},{4,5},{5,4},{6,7},{7,6},{8,9},{9,8},{10,11... | collective-permute-start | bytes 1179656 | tf_op jit(solution)/shard_map/ppermute | solution.py:39
  61.0 17.6 %collective-permute-start.19 = (bf16[4,12,32,128]{3,2,1,0:T(8,128)(2,1)S(1)}, bf16[4,12,32,128]{3,2,1,0:T(8,128)(2,1)}, u32[]{:S(2)}, u32[]{:S(2)}) collective-permute-start(bf16[4,12,32,128]{3,2,1,0:T(8,128)(2,1)S(1)} %collective-permute-done.7.refs_2_), channel_id=1, source_target_pairs={{0,1},{1,0},{2,3},{3,2},{4,5},{5,4},{6,7},{7,6},{8,9},{9,8},{10,11... | collective-permute-start | bytes 1179656 | tf_op jit(solution)/shard_map/ppermute | solution.py:39
  66.3 2.0 %collective-permute-start.25 = (bf16[2,12,32,128]{3,2,1,0:T(8,128)(2,1)S(1)}, bf16[2,12,32,128]{3,2,1,0:T(8,128)(2,1)S(1)}, u32[]{:S(2)}, u32[]{:S(2)}) collective-permute-start(bf16[2,12,32,128]{3,2,1,0:T(8,128)(2,1)S(1)} %collective-permute-done.15.refs_8_), channel_id=1, source_target_pairs={{0,1},{1,0},{2,3},{3,2},{4,5},{5,4},{6,7},{7,6},{8,9},{9,8},{10,11... | collective-permute-start | bytes 589832 | tf_op jit(solution)/shard_map/ppermute | solution.py:39
  67.2 1.1 copy-start.23
  67.2 11.4 %collective-permute-start.18 = (bf16[4,12,32,128]{3,2,1,0:T(8,128)(2,1)}, bf16[4,12,32,128]{3,2,1,0:T(8,128)(2,1)}, u32[]{:S(2)}, u32[]{:S(2)}) collective-permute-start(bf16[4,12,32,128]{3,2,1,0:T(8,128)(2,1)} %collective-permute-done.6.refs_1_), channel_id=1, source_target_pairs={{0,1},{1,0},{2,3},{3,2},{4,5},{5,4},{6,7},{7,6},{8,9},{9,8},{10,11... | collective-permute-start | bytes 1179656 | tf_op jit(solution)/shard_map/ppermute | solution.py:39
  67.3 1.0 copy-start.20
  67.3 11.3 %collective-permute-start.21 = (bf16[2,12,32,128]{3,2,1,0:T(8,128)(2,1)}, bf16[2,12,32,128]{3,2,1,0:T(8,128)(2,1)}, u32[]{:S(2)}, u32[]{:S(2)}) collective-permute-start(bf16[2,12,32,128]{3,2,1,0:T(8,128)(2,1)} %collective-permute-done.9.refs_4_), channel_id=1, source_target_pairs={{0,1},{1,0},{2,3},{3,2},{4,5},{5,4},{6,7},{7,6},{8,9},{9,8},{10,11... | collective-permute-start | bytes 589832 | tf_op jit(solution)/shard_map/ppermute | solution.py:39
  68.3 0.7 copy-start.24
  69.0 9.6 %collective-permute-start.20 = (bf16[2,12,32,128]{3,2,1,0:T(8,128)(2,1)}, bf16[2,12,32,128]{3,2,1,0:T(8,128)(2,1)}, u32[]{:S(2)}, u32[]{:S(2)}) collective-permute-start(bf16[2,12,32,128]{3,2,1,0:T(8,128)(2,1)} %collective-permute-done.8.refs_3_), channel_id=1, source_target_pairs={{0,1},{1,0},{2,3},{3,2},{4,5},{5,4},{6,7},{7,6},{8,9},{9,8},{10,11... | collective-permute-start | bytes 589832 | tf_op jit(solution)/shard_map/ppermute | solution.py:39
  94.8 6.0 %copy-start.4 = (bf16[512,1024]{1,0:T(8,128)(2,1)S(1)}, bf16[512,1024]{1,0:T(8,128)(2,1)}, u32[]{:S(2)}) copy-start(bf16[512,1024]{1,0:T(8,128)(2,1)} %param.20) | copy-start | bytes 3145732
  94.8 6.0 %copy-start.5 = (bf16[128,512]{1,0:T(8,128)(2,1)S(1)}, bf16[128,512]{1,0:T(8,128)(2,1)}, u32[]{:S(2)}) copy-start(bf16[128,512]{1,0:T(8,128)(2,1)} %get-tuple-element.26.x) | copy-start | bytes 393220
  94.9 10.8 %all-to-all-start = ((bf16[4,64,640]{2,1,0:T(8,128)(2,1)}), bf16[4,64,640]{2,1,0:T(8,128)(2,1)S(1)}, u32[]{:S(2)}, u32[]{:S(2)}) async-start(bf16[4,64,640]{2,1,0:T(8,128)(2,1)} %get-tuple-element.27), calls=%async_computation | async-start | bytes 655360 | tf_op jit(solution)/shard_map/all_to_all | solution.py:558
  105.7 0.7 copy-start.2
  121.4 15.1 %copy-start.3 = (bf16[4,64,640]{2,1,0:T(8,128)(2,1)}, bf16[4,64,640]{2,1,0:T(8,128)(2,1)S(1)}, u32[]{:S(2)}) copy-start(bf16[4,64,640]{2,1,0:T(8,128)(2,1)S(1)} %all_to_all.20.refs_4_) | copy-start | bytes 983044
  121.4 15.1 %collective-permute-start.30 = (bf16[4,64,640]{2,1,0:T(8,128)(2,1)S(1)}, bf16[4,64,640]{2,1,0:T(8,128)(2,1)S(1)}, u32[]{:S(2)}, u32[]{:S(2)}) collective-permute-start(bf16[4,64,640]{2,1,0:T(8,128)(2,1)S(1)} %all_to_all.20.refs_4_), channel_id=1, source_target_pairs={{0,1},{1,0},{2,3},{3,2},{4,5},{5,4},{6,7},{7,6},{8,9},{9,8},{10,11... | collective-permute-start | bytes 983048 | tf_op jit(solution)/shard_map/ppermute | solution.py:39
  125.7 5.1 %collective-permute-start.29 = (bf16[128,512]{1,0:T(8,128)(2,1)}, bf16[128,512]{1,0:T(8,128)(2,1)S(1)}, u32[]{:S(2)}, u32[]{:S(2)}) collective-permute-start(bf16[128,512]{1,0:T(8,128)(2,1)} %passed.1.refs_0_), channel_id=1, source_target_pairs={{0,96},{32,0},{64,32},{96,64},{1,97},{33,1},{65,33},{97,65},{2,98}... | collective-permute-start | bytes 393224 | tf_op jit(solution)/shard_map/ppermute | solution.py:43
  126.6 6.4 %collective-permute-start.28 = (bf16[128,512]{1,0:T(8,128)(2,1)}, bf16[128,512]{1,0:T(8,128)(2,1)S(1)}, u32[]{:S(2)}, u32[]{:S(2)}) collective-permute-start(bf16[128,512]{1,0:T(8,128)(2,1)} %passed.1.refs_0_), channel_id=1, source_target_pairs={{0,64},{32,96},{64,0},{96,32},{1,65},{33,97},{65,1},{97,33},{2,66}... | collective-permute-start | bytes 393224 | tf_op jit(solution)/shard_map/ppermute | solution.py:43
  127.7 8.8 %collective-permute-start.27 = (bf16[128,512]{1,0:T(8,128)(2,1)}, bf16[128,512]{1,0:T(8,128)(2,1)S(1)}, u32[]{:S(2)}, u32[]{:S(2)}) collective-permute-start(bf16[128,512]{1,0:T(8,128)(2,1)} %passed.1.refs_0_), channel_id=1, source_target_pairs={{0,32},{32,64},{64,96},{96,0},{1,33},{33,65},{65,97},{97,1},{2,34}... | collective-permute-start | bytes 393224 | tf_op jit(solution)/shard_map/ppermute | solution.py:43
  130.8 5.7 %copy-start.9 = (bf16[128,512]{1,0:T(8,128)(2,1)}, bf16[128,512]{1,0:T(8,128)(2,1)S(1)}, u32[]{:S(2)}) copy-start(bf16[128,512]{1,0:T(8,128)(2,1)S(1)} %collective-permute-done.29.refs_3_) | copy-start | bytes 393220
  132.9 3.6 %copy-start.10 = (bf16[128,512]{1,0:T(8,128)(2,1)}, bf16[128,512]{1,0:T(8,128)(2,1)S(1)}, u32[]{:S(2)}) copy-start(bf16[128,512]{1,0:T(8,128)(2,1)S(1)} %collective-permute-done.28.refs_2_) | copy-start | bytes 393220
  136.5 0.6 copy-start.11
  137.1 0.7 copy-start.8
  183.4 3.5 %copy-start.1 = (bf16[64,16,640]{2,1,0:T(8,128)(2,1)}, bf16[64,16,640]{2,1,0:T(8,128)(2,1)S(1)}, u32[]{:S(2)}) copy-start(bf16[64,16,640]{2,1,0:T(8,128)(2,1)S(1)} %all_to_all.22) | copy-start | bytes 3932164
  183.4 6.3 %collective-permute-start.31 = (bf16[4,16,16,640]{3,2,1,0:T(8,128)(2,1)S(1)}, bf16[4,16,16,640]{3,2,1,0:T(8,128)(2,1)}, u32[]{:S(2)}, u32[]{:S(2)}) collective-permute-start(bf16[4,16,16,640]{3,2,1,0:T(8,128)(2,1)S(1)} %bitcast.15), channel_id=1, source_target_pairs={{0,1},{1,0},{2,3},{3,2},{4,5},{5,4},{6,7},{7,6},{8,9},{9,8},{10,11... | collective-permute-start | bytes 3932168 | tf_op jit(solution)/shard_map/ppermute | solution.py:39

commit v3 on v2

--- a/solution.py
+++ b/solution.py
@@ -47,43 +47,39 @@
     return column // 8, (column // 2) % 4, column % 2
 
 
-def norm_kernel(wavlm, whisper, norm_a, norm_w, mean_a, mean_w):
+def norm_kernel(hidden, norm, mean):
     pool_mat = jnp.where(
         lax.broadcasted_iota(jnp.int32, (32, 128), 1) // POOL
         == lax.broadcasted_iota(jnp.int32, (32, 128), 0),
         1.0 / POOL,
         0.0,
     ).astype(bf16)
-    for hidden, norm, mean in ((wavlm, norm_a, mean_a), (whisper, norm_w, mean_w)):
-        rows = hidden[0].astype(f32)
-        centred = rows - jnp.mean(rows, axis=-1, keepdims=True)
-        variance = jnp.mean(centred * centred, axis=-1, keepdims=True)
-        norm[0] = (centred * lax.rsqrt(variance + epsilon_norm)).astype(bf16)
-
-        @pl.when(pl.program_id(1) == lax.axis_index("role"))
-        def _():
-            mean[...] = jnp.dot(pool_mat, hidden[0], preferred_element_type=f32)
-
-
-def norms(wavlm, whisper):
-    rows = lambda width: pl.BlockSpec((1, 128, width), lambda i, j: (i, j, 0))
-    mean = lambda width: pl.BlockSpec((32, width), lambda i, j: (i, 0))
+    rows = hidden[0].astype(f32)
+    centred = rows - jnp.mean(rows, axis=-1, keepdims=True)
+    variance = jnp.mean(centred * centred, axis=-1, keepdims=True)
+    norm[0] = (centred * lax.rsqrt(variance + epsilon_norm)).astype(bf16)
+
+    @pl.when(pl.program_id(1) == lax.axis_index("role"))
+    def _():
+        mean[...] = jnp.dot(pool_mat, hidden[0], preferred_element_type=f32)
+
+
+def norms(hidden):
+    width = hidden.shape[-1]
+    rows = pl.BlockSpec((1, 128, width), lambda i, j: (i, j, 0))
     return pl.pallas_call(
         norm_kernel,
         grid=(2, 4),
         out_shape=[
-            jax.ShapeDtypeStruct(wavlm.shape, bf16),
-            jax.ShapeDtypeStruct(whisper.shape, bf16),
-            jax.ShapeDtypeStruct((ROWS, WAVLM_D), f32),
-            jax.ShapeDtypeStruct((ROWS, WHISPER_D), f32),
+            jax.ShapeDtypeStruct(hidden.shape, bf16),
+            jax.ShapeDtypeStruct((ROWS, width), f32),
         ],
-        in_specs=[rows(WAVLM_D), rows(WHISPER_D)],
-        out_specs=[rows(WAVLM_D), rows(WHISPER_D), mean(WAVLM_D), mean(WHISPER_D)],
+        in_specs=[rows],
+        out_specs=[rows, pl.BlockSpec((32, width), lambda i, j: (i, 0))],
         cost_estimate=pl.CostEstimate(
-            flops=60_000_000, bytes_accessed=24_000_000, transcendentals=4096
+            flops=30_000_000, bytes_accessed=12_000_000, transcendentals=2048
         ),
-        name="norms",
-    )(wavlm, whisper)
+    )(hidden)
 
 
 def chunk_kernel(qkv_a, qkv_w, *refs):
@@ -165,16 +161,12 @@
 
 
 def spread_cross(first, second):
-    send_a = lambda x, k: dp_send(x, 0, k, 0)
-    send_b = lambda x, k: dp_send(x, k, 0, 0)
-    a1, b1 = send_a(first, 1), send_b(second, 1)
-    a3, b3 = send_a(first, 3), send_b(second, 3)
-    a2, b2 = send_a(a1[:2], 1), send_b(b1[:2], 1)
-    a2x, b2x = send_a(a3[2:], 3), send_b(b3[2:], 3)
-    return [first, a1, a3, a2, a2x, second, b1, b3, b2, b2x]
-
-
-CROSS = [(0, 0), (1, 0), (3, 0), (2, 0), (2, 2)]
+    got = {}
+    for k in (1, 3, 2):
+        got[k] = dp_send(first, 0, k, 0), dp_send(second, k, 0, 0)
+    return (
+        [first] + [got[k][0] for k in (1, 2, 3)] + [second] + [got[k][1] for k in (1, 2, 3)]
+    )
 
 
 def pick_latents(slot_clip, rows, slots, out):
@@ -201,10 +193,13 @@
 
 
 def attend_kernel(frames_valid, slot_clip, *refs):
-    pieces = refs[:20]
-    norm_a_hbm, norm_w_hbm, pooled, lat = refs[20:24]
+    pieces = refs[:16]
+    norm_a_hbm, norm_w_hbm, head_a_hbm, head_w_hbm = refs[16:20]
+    pooled, lat, pred_a, pred_w = refs[20:24]
     norm_a, norm_w, rows_in, qkv_a, qkv_w, proj, att_a, att_w = refs[24:32]
-    score_refs, slots, sems = refs[32:34], refs[34], refs[35]
+    score_refs, slots, head_a, head_w, sems = refs[32:34], *refs[34:38]
+    copy_head_a = pltpu.make_async_copy(head_a_hbm, head_a, sems.at[4])
+    copy_head_w = pltpu.make_async_copy(head_w_hbm, head_w, sems.at[5])
     copy_a = pltpu.make_async_copy(norm_a_hbm, norm_a, sems.at[2])
     copy_w = pltpu.make_async_copy(norm_w_hbm, norm_w, sems.at[3])
     role = lax.axis_index("role")
@@ -212,12 +207,10 @@
     z, y, c = place_of(column)
     for first, count, sem in ((0, 3, sems.at[0]), (3, 9, sems.at[1])):
         for n, piece in enumerate(pieces):
-            core = (c + n // 10) % 2
-            half = (n % 10) // 5
-            far, entry = CROSS[n % 5]
+            core = (c + n // 8) % 2
+            half, far = (n % 8) // 4, n % 4
             for e in range(piece.shape[0]):
-                near = entry + e
-                dz, dy = (near, far) if half == 0 else (far, near)
+                dz, dy = (e, far) if half == 0 else (far, e)
                 device = ((z - dz) % 4) * 8 + ((y - dy) % 4) * 2 + core
                 pltpu.make_async_copy(
                     piece.at[e, pl.ds(first, count)],
@@ -227,6 +220,8 @@
         if first == 0:
             copy_a.start()
     copy_w.start()
+    copy_head_a.start()
+    copy_head_w.start()
     wait_a = pltpu.make_async_copy(
         rows_in.at[:, pl.ds(0, 6)], rows_in.at[:, pl.ds(0, 6)], sems.at[0]
     )
@@ -315,6 +310,11 @@
 
     wait_w.wait()
     copy_w.wait()
+    copy_head_a.wait()
+    copy_head_w.wait()
+    pick_latents(slot_clip, rows_in, slots, lat)
+    pred_a[...] = jnp.dot(lat[:ROWS], head_a[...], preferred_element_type=f32)
+    pred_w[...] = jnp.dot(lat[:ROWS], head_w[...], preferred_element_type=f32)
     for clip in range(2):
         lhs = jnp.concatenate(
             [
@@ -349,20 +349,21 @@
         mean = lax.dot_general(pool_mat, rows, nt, preferred_element_type=f32).astype(bf16)
         mean = jnp.concatenate([mean, jnp.zeros((POOLED, 64), bf16)], axis=1)
         pooled[:, clip * 32 : clip * 32 + 32, A_COLS:] = mean.reshape(ROLES, 32, 384)
-    pick_latents(slot_clip, rows_in, slots, lat)
-
-
-def attend(frames_valid, slot_clip, pieces, norm_a, norm_w):
+
+
+def attend(frames_valid, slot_clip, pieces, norm_a, norm_w, head_a, head_w):
     vmem = pl.BlockSpec(memory_space=pltpu.VMEM)
     return pl.pallas_call(
         attend_kernel,
         out_shape=[
             jax.ShapeDtypeStruct((ROLES, ROWS, OUT_COLS), bf16),
             jax.ShapeDtypeStruct((2 * ROWS, STU_D), bf16),
+            jax.ShapeDtypeStruct((ROWS, WAVLM_D), f32),
+            jax.ShapeDtypeStruct((ROWS, WHISPER_D), f32),
         ],
         in_specs=[pl.BlockSpec(memory_space=pltpu.SMEM)] * 2
-        + [pl.BlockSpec(memory_space=pl.ANY)] * 22,
-        out_specs=[vmem] * 2,
+        + [pl.BlockSpec(memory_space=pl.ANY)] * 20,
+        out_specs=[vmem] * 4,
         scratch_shapes=[
             pltpu.VMEM((2, FRAMES, WAVLM_D), bf16),
             pltpu.VMEM((2, FRAMES, WHISPER_D), bf16),
@@ -375,13 +376,15 @@
             pltpu.VMEM((FRAMES, FRAMES), f32),
             pltpu.VMEM((FRAMES, FRAMES), f32),
             pltpu.SMEM((4,), jnp.int32),
-            pltpu.SemaphoreType.DMA((4,)),
+            pltpu.VMEM((STU_D, WAVLM_D), bf16),
+            pltpu.VMEM((STU_D, WHISPER_D), bf16),
+            pltpu.SemaphoreType.DMA((6,)),
         ],
         cost_estimate=pl.CostEstimate(
             flops=8_000_000_000, bytes_accessed=12_000_000, transcendentals=5_000_000
         ),
         name="attend",
-    )(frames_valid, slot_clip, *pieces, norm_a, norm_w)
+    )(frames_valid, slot_clip, *pieces, norm_a, norm_w, head_a, head_w)
 
 
 def slope_kernel(frames_valid, parts, out_a_hbm, out_w_hbm, *refs):
@@ -439,21 +442,6 @@
         ],
         name="slopes",
     )(frames_valid, parts, out_a, out_w, mean_a, mean_w, pred_a, pred_w)
-
-
-def pass_kernel(x, out):
-    out[...] = x[...]
-
-
-def passed(x):
-    vmem = pl.BlockSpec(memory_space=pltpu.VMEM)
-    return pl.pallas_call(
-        pass_kernel,
-        out_shape=jax.ShapeDtypeStruct(x.shape, x.dtype),
-        in_specs=[vmem],
-        out_specs=vmem,
-        name="passed",
-    )(x)
 
 
 def outer_kernel(*refs):
@@ -552,18 +540,18 @@
     first, second = spread_line(first, second)
     pieces = spread_cross(first, second)
     pieces = pieces + [dp_send(x, 0, 0, 1) for x in pieces]
-    norm_a, norm_w, mean_a, mean_w = norms(wavlm_hidden, whisper_hidden)
-
-    pooled, lat = attend(frames_valid, slot_clip, pieces, norm_a, norm_w)
+    norm_a, mean_a = norms(wavlm_hidden)
+    norm_w, mean_w = norms(whisper_hidden)
+
+    pooled, lat, pred_a, pred_w = attend(
+        frames_valid, slot_clip, pieces, norm_a, norm_w, wavlm_head, whisper_head
+    )
     parts = lax.all_to_all(pooled, "role", split_axis=0, concat_axis=0, tiled=True)
-    pred_a = jnp.dot(lat[:ROWS], wavlm_head, preferred_element_type=f32)
-    pred_w = jnp.dot(lat[:ROWS], whisper_head, preferred_element_type=f32)
+    lats = [lat] + [role_send(lat, k) for k in (1, 2, 3)]
     sloped = slopes(
         frames_valid, parts, wavlm_out, whisper_out, mean_a, mean_w, pred_a, pred_w
     )
     slope_own = lax.all_to_all(sloped, "role", split_axis=0, concat_axis=0, tiled=True)
-    lat = passed(lat)
-    lats = [lat] + [role_send(lat, k) for k in (1, 2, 3)]
     slope_other = dp_send(slope_own, 0, 0, 1)
     halves = outer(lats, slope_own, slope_other)
     arrived = lax.all_to_all(

time: 193 us -> 212 us (1.098)
  waiting for transfers between devices: 35.5 us -> 56.7 us
  starting transfers between devices: 50.1 us -> 37.6 us
  blocking collectives: 50 us -> 61 us
  matrix products: 2.94 us -> 0 us
  Pallas kernels: 46.4 us -> 48.7 us
    ppermute x29 -> x25, waiting for transfers between devices: 23 us -> 48.1 us  [dp_send(): return lax.ppermute(x, 'dp', pairs)]
    all_to_all x0 -> x1, blocking collectives: none -> 11 us  [per_device(): lax.all_to_all(pooled, 'role', split_axis=0, concat_axis=0, tiled=True)]
    ppermute x29 -> x25, starting transfers between devices: 43.9 us -> 35.5 us  [dp_send(): return lax.ppermute(x, 'dp', pairs)]
    pallas_call x1 -> x2, Pallas kernels: 9.19 us -> 14 us  [norms(): pl.pallas_call(norm_kernel, grid=(2, 4), out_shape=[jax.ShapeDtypeStruct(...]
    all_to_all x1 -> x0, starting transfers between devices: 4.09 us -> none  [per_device(): lax.all_to_all(pooled, 'role', split_axis=0, concat_axis=0, tiled=True)]
    all_to_all x1 -> x0, waiting for transfers between devices: 3.8 us -> none  [per_device(): lax.all_to_all(pooled, 'role', split_axis=0, concat_axis=0, tiled=True)]
    dot_general x2 -> x0, matrix products: 2.94 us -> none  [the longest x1 1.92 us: per_device(): pred_w = jnp.dot(lat[:ROWS], whisper_head, preferred_element_type=f32)]
  transfers between devices with their start and end apart: 33 -> 28, of which waited for: 13 -> 12; matrix products, arithmetic and copies ran while one was open for 3% -> 1% of each run, Pallas kernels for 7% -> 8%
where the time goes in v3:
time: 212 us; the launch traced here: 211 us
  blocking collectives  61 us (29%)
  waiting for transfers between devices  56.7 us (27%)
  Pallas kernels  48.7 us (23%)
  starting transfers between devices  37.6 us (18%)
  local copies, waits for them, and re-layouts  3.93 us (2%)
    ppermute x25, waiting for transfers between devices, dp_send(): return lax.ppermute(x, 'dp', pairs)  48.1 us
    ppermute x25, starting transfers between devices, dp_send(): return lax.ppermute(x, 'dp', pairs)  35.5 us
    all_to_all x1, blocking collectives, per_device(): lax.all_to_all(reduce_parts(arrived), ('role', 'dp'), split_axis=0, conca...  23.9 us
    all_to_all x1, blocking collectives, per_device(): lax.all_to_all(halves, 'dp', split_axis=0, concat_axis=0, tiled=True, axi...  16.8 us
    pallas_call x1, Pallas kernels, attend(): pl.pallas_call(attend_kernel, out_shape=[jax.ShapeDtypeStruct((ROLES, ROW...  15.2 us
    pallas_call x2, Pallas kernels, norms(): pl.pallas_call(norm_kernel, grid=(2, 4), out_shape=[jax.ShapeDtypeStruct(...  14 us
    all_to_all x1, blocking collectives, per_device(): lax.all_to_all(pooled, 'role', split_axis=0, concat_axis=0, tiled=True)  11 us
    all_to_all x1, blocking collectives, per_device(): lax.all_to_all(sloped, 'role', split_axis=0, concat_axis=0, tiled=True)  9.31 us
  transfers between devices with their start and end apart: 28, of which 12 were waited for; matrix products, arithmetic and copies ran while one was open for 1% of the time, Pallas kernels for 8%

profile of v3, /device:TPU:1, one launch (start us, length us, event | category | flops | bytes accessed | tf_op | source)
XLA Modules:
  0.0 210.6 jit_solution(8106215250415876585)
XLA Ops:
  0.6 1.9 weight_chunks.1
  2.6 2.5 %collective-permute-start = (bf16[16,32,128]{2,1,0:T(8,128)(2,1)}, bf16[16,32,128]{2,1,0:T(8,128)(2,1)S(1)}, u32[]{:S(2)}, u32[]{:S(2)}) collective-permute-start(bf16[16,32,128]{2,1,0:T(8,128)(2,1)} %get-tuple-element.21), channel_id=1, source_target_pairs={{0,8},{1,9},{2,10},{3,11},{4,12},{5,13},{6,14},{7,15},{8,16},{9,17... | collective-permute-start | bytes 393224 | tf_op jit(solution)/shard_map/ppermute | solution.py:39
  5.0 3.3 %collective-permute-start.1 = (bf16[16,32,128]{2,1,0:T(8,128)(2,1)}, bf16[16,32,128]{2,1,0:T(8,128)(2,1)S(1)}, u32[]{:S(2)}, u32[]{:S(2)}) collective-permute-start(bf16[16,32,128]{2,1,0:T(8,128)(2,1)} %get-tuple-element.22), channel_id=1, source_target_pairs={{0,16},{1,17},{2,18},{3,19},{4,20},{5,21},{6,22},{7,23},{8,24},{9,... | collective-permute-start | bytes 393224 | tf_op jit(solution)/shard_map/ppermute | solution.py:39
  8.3 0.7 collective-permute-start.2
  9.1 1.5 collective-permute-done.refs_1_
  10.6 3.7 %collective-permute-done.1.refs_2_ = bf16[16,32,128]{2,1,0:T(8,128)(2,1)S(1)} collective-permute-done((bf16[16,32,128]{2,1,0:T(8,128)(2,1)}, bf16[16,32,128]{2,1,0:T(8,128)(2,1)S(1)}, u32[]{:S(2)}, u32[]{:S(2)}) %collective-permute-start.1) | collective-permute-done | bytes 131104 | tf_op jit(solution)/shard_map/ppermute | solution.py:39
  14.3 0.0 collective-permute-done.2.refs_3_
  14.3 0.6 copy-done.11
  14.9 0.0 copy-done.12
  15.0 1.9 shares.1
  16.8 2.7 %collective-permute-start.11 = (bf16[12,32,128]{2,1,0:T(8,128)(2,1)}, bf16[12,32,128]{2,1,0:T(8,128)(2,1)S(1)}, u32[]{:S(2)}, u32[]{:S(2)}) collective-permute-start(bf16[12,32,128]{2,1,0:T(8,128)(2,1)} %get-tuple-element.25), channel_id=1, source_target_pairs={{0,6},{1,7},{2,0},{3,1},{4,2},{5,3},{6,4},{7,5},{8,14},{9,15},{10,... | collective-permute-start | bytes 294920 | tf_op jit(solution)/shard_map/ppermute | solution.py:39
  19.6 0.3 collective-permute-start.10
  19.9 0.7 collective-permute-start.9
  20.6 2.3 %collective-permute-start.5 = (bf16[12,32,128]{2,1,0:T(8,128)(2,1)}, bf16[12,32,128]{2,1,0:T(8,128)(2,1)S(1)}, u32[]{:S(2)}, u32[]{:S(2)}) collective-permute-start(bf16[12,32,128]{2,1,0:T(8,128)(2,1)} %get-tuple-element.24), channel_id=1, source_target_pairs={{0,24},{1,25},{2,26},{3,27},{4,28},{5,29},{6,30},{7,31},{8,0},{9,1... | collective-permute-start | bytes 294920 | tf_op jit(solution)/shard_map/ppermute | solution.py:39
  22.9 0.0 collective-permute-done.11
  22.9 2.0 collective-permute-done.10
  24.8 1.0 collective-permute-done.9
  25.8 0.9 pad_maximum_fusion.1.refs_4_
  26.8 3.0 %collective-permute-start.19 = (bf16[4,12,32,128]{3,2,1,0:T(8,128)(2,1)S(1)}, bf16[4,12,32,128]{3,2,1,0:T(8,128)(2,1)S(1)}, u32[]{:S(2)}, u32[]{:S(2)}) collective-permute-start(bf16[4,12,32,128]{3,2,1,0:T(8,128)(2,1)S(1)} %pad_maximum_fusion.1.refs_4_), channel_id=1, source_target_pairs={{0,1},{1,0},{2,3},{3,2},{4,5},{5,4},{6,7},{7,6},{8,9},{9,8},{10,11... | collective-permute-start | bytes 1179656 | tf_op jit(solution)/shard_map/ppermute | solution.py:39
  29.8 2.1 collective-permute-start.14
  31.9 0.9 collective-permute-start.13
  32.8 0.0 collective-permute-start.12
  32.8 0.0 collective-permute-done.5
  32.8 2.0 collective-permute-start.4
  34.9 19.4 %collective-permute-done.4 = bf16[12,32,128]{2,1,0:T(8,128)(2,1)S(1)} collective-permute-done((bf16[12,32,128]{2,1,0:T(8,128)(2,1)}, bf16[12,32,128]{2,1,0:T(8,128)(2,1)S(1)}, u32[]{:S(2)}, u32[]{:S(2)}) %collective-permute-start.4) | collective-permute-done | bytes 98336 | tf_op jit(solution)/shard_map/ppermute | solution.py:39
  54.3 4.9 %collective-permute-done.3 = bf16[12,32,128]{2,1,0:T(8,128)(2,1)S(1)} collective-permute-done((bf16[12,32,128]{2,1,0:T(8,128)(2,1)}, bf16[12,32,128]{2,1,0:T(8,128)(2,1)S(1)}, u32[]{:S(2)}, u32[]{:S(2)}) %collective-permute-start.3) | collective-permute-done | bytes 98336 | tf_op jit(solution)/shard_map/ppermute | solution.py:39
  59.2 0.9 pad_maximum_fusion.refs_0_
  60.1 2.4 %collective-permute-start.15 = (bf16[4,12,32,128]{3,2,1,0:T(8,128)(2,1)S(1)}, bf16[4,12,32,128]{3,2,1,0:T(8,128)(2,1)S(1)}, u32[]{:S(2)}, u32[]{:S(2)}) collective-permute-start(bf16[4,12,32,128]{3,2,1,0:T(8,128)(2,1)S(1)} %pad_maximum_fusion.refs_0_), channel_id=1, source_target_pairs={{0,1},{1,0},{2,3},{3,2},{4,5},{5,4},{6,7},{7,6},{8,9},{9,8},{10,11... | collective-permute-start | bytes 1179656 | tf_op jit(solution)/shard_map/ppermute | solution.py:39
  62.6 0.3 collective-permute-start.8
  62.9 0.3 collective-permute-start.7
  63.2 0.9 collective-permute-start.6
  64.2 0.7 collective-permute-start.22
  64.8 0.1 collective-permute-start.21
  64.9 8.3 %collective-permute-done.8.refs_3_ = bf16[4,12,32,128]{3,2,1,0:T(8,128)(2,1)S(1)} collective-permute-done((bf16[4,12,32,128]{3,2,1,0:T(8,128)(2,1)S(1)}, bf16[4,12,32,128]{3,2,1,0:T(8,128)(2,1)S(1)}, u32[]{:S(2)}, u32[]{:S(2)}) %collective-permute-start.8) | collective-permute-done | bytes 393248 | tf_op jit(solution)/shard_map/ppermute | solution.py:39
  73.3 1.4 collective-permute-start.20
  74.7 0.0 collective-permute-done.7.refs_2_
  74.7 2.1 collective-permute-start.18
  76.8 7.2 %collective-permute-done.6.refs_1_ = bf16[4,12,32,128]{3,2,1,0:T(8,128)(2,1)} collective-permute-done((bf16[4,12,32,128]{3,2,1,0:T(8,128)(2,1)S(1)}, bf16[4,12,32,128]{3,2,1,0:T(8,128)(2,1)}, u32[]{:S(2)}, u32[]{:S(2)}) %collective-permute-start.6) | collective-permute-done | bytes 393248 | tf_op jit(solution)/shard_map/ppermute | solution.py:39
  84.0 0.5 collective-permute-start.17
  84.4 0.8 copy-done.20
  85.2 0.0 collective-permute-start.16
  85.2 6.8 %shard_map.122 = (bf16[2,512,1024]{2,1,0:T(8,128)(2,1)}, f32[64,1024]{1,0:T(8,128)}) custom-call(bf16[2,512,1024]{2,1,0:T(8,128)(2,1)} %hidden.2), custom_call_target="tpu_custom_call" | custom-call | flops 30000000 | bytes 12000000 | tf_op jit(solution)/shard_map/pallas_call | solution.py:70
  92.1 7.2 %shard_map.123 = (bf16[2,512,1280]{2,1,0:T(8,128)(2,1)}, f32[64,1280]{1,0:T(8,128)}) custom-call(bf16[2,512,1280]{2,1,0:T(8,128)(2,1)} %hidden.3), custom_call_target="tpu_custom_call" | custom-call | flops 30000000 | bytes 12000000 | tf_op jit(solution)/shard_map/pallas_call | solution.py:70
  99.4 15.2 %attend.1 = (bf16[4,64,640]{2,1,0:T(8,128)(2,1)}, bf16[128,512]{1,0:T(8,128)(2,1)}, f32[64,1024]{1,0:T(8,128)}, f32[64,1280]{1,0:T(8,128)}) custom-call(s32[64]{0:T(128)} %frames_valid.3, s32[64]{0:T(128)} %slot_clip.1, bf16[4,12,32,128]{3,2,1,0:T(8,128)(2,1)} %copy-done.4, bf16[4,12,32,128]{3,2,1,0:T(8,128)(2,1)} %collective-permute-done.6.refs_1_, ...), custom_call_target="tpu_custom_call" | custom-call | flops 8000000000 | bytes 12000000 | tf_op jit(solution)/shard_map/attend/pallas_call | solution.py:356
  114.6 11.0 %all_to_all.20.parts = bf16[4,64,640]{2,1,0:T(8,128)(2,1)} all-to-all(bf16[4,64,640]{2,1,0:T(8,128)(2,1)} %get-tuple-element.29), channel_id=1, replica_groups=mesh['role'=4,'dp'=32] {'role'}, dimensions={0} | all-to-all | bytes 655360 | tf_op jit(solution)/shard_map/all_to_all | solution.py:549
  125.7 5.7 %slopes.1 = bf16[4,64,640]{2,1,0:T(8,128)(2,1)} custom-call(s32[64]{0:T(128)} %frames_valid.3, bf16[4,64,640]{2,1,0:T(8,128)(2,1)} %all_to_all.20.parts, bf16[1024,1024]{1,0:T(8,128)(2,1)} %out_a_hbm.1, bf16[1280,1280]{1,0:T(8,128)(2,1)} %out_w_hbm.1, f32[64,1024]{1,0:T(8,128)} %get-tuple-element.30.refs_0_, f32[64,1280]{1,0:T(8,128)} %get-tuple-element.31.refs_1_, ...), custom_call_target="tpu_custom_call" | custom-call | tf_op jit(solution)/shard_map/slopes/pallas_call | solution.py:433
  131.3 9.3 %all_to_all.21.refs_4_ = bf16[4,64,640]{2,1,0:T(8,128)(2,1)S(1)} all-to-all(bf16[4,64,640]{2,1,0:T(8,128)(2,1)} %slopes.1), channel_id=1, replica_groups=mesh['role'=4,'dp'=32] {'role'}, dimensions={0} | all-to-all | bytes 655360 | tf_op jit(solution)/shard_map/all_to_all | solution.py:554
  140.6 2.6 %collective-permute-start.26 = (bf16[4,64,640]{2,1,0:T(8,128)(2,1)S(1)}, bf16[4,64,640]{2,1,0:T(8,128)(2,1)S(1)}, u32[]{:S(2)}, u32[]{:S(2)}) collective-permute-start(bf16[4,64,640]{2,1,0:T(8,128)(2,1)S(1)} %all_to_all.21.refs_4_), channel_id=1, source_target_pairs={{0,1},{1,0},{2,3},{3,2},{4,5},{5,4},{6,7},{7,6},{8,9},{9,8},{10,11... | collective-permute-start | bytes 983048 | tf_op jit(solution)/shard_map/ppermute | solution.py:39
  143.3 0.9 collective-permute-start.25
  144.1 1.2 collective-permute-start.24
  145.3 2.9 %collective-permute-done.25.refs_3_ = bf16[128,512]{1,0:T(8,128)(2,1)S(1)} collective-permute-done((bf16[128,512]{1,0:T(8,128)(2,1)S(1)}, bf16[128,512]{1,0:T(8,128)(2,1)S(1)}, u32[]{:S(2)}, u32[]{:S(2)}) %collective-permute-start.25) | collective-permute-done | bytes 131104 | tf_op jit(solution)/shard_map/ppermute | solution.py:43
  148.2 2.1 %collective-permute-done.24.refs_2_ = bf16[128,512]{1,0:T(8,128)(2,1)S(1)} collective-permute-done((bf16[128,512]{1,0:T(8,128)(2,1)S(1)}, bf16[128,512]{1,0:T(8,128)(2,1)S(1)}, u32[]{:S(2)}, u32[]{:S(2)}) %collective-permute-start.24) | collective-permute-done | bytes 131104 | tf_op jit(solution)/shard_map/ppermute | solution.py:43
  150.4 3.5 %collective-permute-done.23.refs_1_ = bf16[128,512]{1,0:T(8,128)(2,1)S(1)} collective-permute-done((bf16[128,512]{1,0:T(8,128)(2,1)S(1)}, bf16[128,512]{1,0:T(8,128)(2,1)S(1)}, u32[]{:S(2)}, u32[]{:S(2)}) %collective-permute-start.23) | collective-permute-done | bytes 131104 | tf_op jit(solution)/shard_map/ppermute | solution.py:43
  153.9 0.6 copy-done.9
  154.5 0.7 copy-done.5
  155.2 2.6 %outer.1 = f32[16,16,640]{2,1,0:T(8,128)} custom-call(bf16[128,512]{1,0:T(8,128)(2,1)} %get-tuple-element.28.refs_0_, bf16[128,512]{1,0:T(8,128)(2,1)} %copy-done.9, bf16[128,512]{1,0:T(8,128)(2,1)} %copy-done.8, bf16[128,512]{1,0:T(8,128)(2,1)} %copy-done.7, bf16[4,64,640]{2,1,0:T(8,128)(2,1)} %copy-done.1, bf16[4,64,640]{2,1,0:T(8,128)(2,1)} %copy-done.5), custom_call_target="tpu_custom_call" | custom-call | tf_op jit(solution)/shard_map/outer/pallas_call | solution.py:464
  157.8 16.8 %all_to_all.22.x = f32[16,16,640]{2,1,0:T(8,128)} all-to-all(f32[16,16,640]{2,1,0:T(8,128)} %outer.1), channel_id=1, replica_groups={{0,2,4,6,8,10,12,14,16,18,20,22,24,26,28,30},{1,3,5,7,9,11,13,15,17,19,..., dimensions={0} | all-to-all | bytes 1310720 | tf_op jit(solution)/shard_map/all_to_all | solution.py:557
  174.6 2.3 %reduce_parts.1 = bf16[64,16,640]{2,1,0:T(8,128)(2,1)} custom-call(f32[16,16,640]{2,1,0:T(8,128)} %all_to_all.22.x), custom_call_target="tpu_custom_call" | custom-call | tf_op jit(solution)/shard_map/reduce_parts/pallas_call | solution.py:480
  176.9 23.9 %all_to_all.23 = bf16[64,16,640]{2,1,0:T(8,128)(2,1)S(1)} all-to-all(bf16[64,16,640]{2,1,0:T(8,128)(2,1)} %reduce_parts.1), channel_id=1, replica_groups={{0,2,4,6,8,10,12,14,16,18,20,22,24,26,28,30,32,34,36,38,40,42,44,46,48,..., dimensions={0} | all-to-all | bytes 2621440 | tf_op jit(solution)/shard_map/all_to_all | solution.py:560
  200.8 3.5 %collective-permute-start.27 = (bf16[4,16,16,640]{3,2,1,0:T(8,128)(2,1)S(1)}, bf16[4,16,16,640]{3,2,1,0:T(8,128)(2,1)S(1)}, u32[]{:S(2)}, u32[]{:S(2)}) collective-permute-start(bf16[4,16,16,640]{3,2,1,0:T(8,128)(2,1)S(1)} %bitcast.13), channel_id=1, source_target_pairs={{0,1},{1,0},{2,3},{3,2},{4,5},{5,4},{6,7},{7,6},{8,9},{9,8},{10,11... | collective-permute-start | bytes 3932168 | tf_op jit(solution)/shard_map/ppermute | solution.py:39
  204.3 2.6 %place_own.1 = (f32[2,256,1024]{2,1,0:T(8,128)}, f32[2,256,1280]{2,1,0:T(8,128)}) custom-call(bf16[4,16,16,640]{3,2,1,0:T(8,128)(2,1)} %bitcast.14), custom_call_target="tpu_custom_call" | custom-call | tf_op jit(solution)/shard_map/place_own/pallas_call | solution.py:502
  206.8 0.1 collective-permute-done.27.piece
  206.9 1.1 copy-done.2
  208.0 2.6 %place_partner.1 = (f32[2,256,1024]{2,1,0:T(8,128)}, f32[2,256,1280]{2,1,0:T(8,128)}) custom-call(bf16[4,16,16,640]{3,2,1,0:T(8,128)(2,1)} %copy-done.2, f32[2,256,1024]{2,1,0:T(8,128)} %get-tuple-element.34.refs_0_, f32[2,256,1280]{2,1,0:T(8,128)} %get-tuple-element.35.refs_1_), custom_call_target="tpu_custom_call", output_to_operand_aliasing={{0}: (1, {}), {1}: (2, {})} | custom-call | tf_op jit(solution)/shard_map/place_partner/pallas_call | solution.py:502
  (50 shorter events, 0.1 us)
Async XLA Ops:
  2.6 8.0 %collective-permute-start = (bf16[16,32,128]{2,1,0:T(8,128)(2,1)}, bf16[16,32,128]{2,1,0:T(8,128)(2,1)S(1)}, u32[]{:S(2)}, u32[]{:S(2)}) collective-permute-start(bf16[16,32,128]{2,1,0:T(8,128)(2,1)} %get-tuple-element.21), channel_id=1, source_target_pairs={{0,8},{1,9},{2,10},{3,11},{4,12},{5,13},{6,14},{7,15},{8,16},{9,17... | collective-permute-start | bytes 393224 | tf_op jit(solution)/shard_map/ppermute | solution.py:39
  5.0 9.2 %collective-permute-start.1 = (bf16[16,32,128]{2,1,0:T(8,128)(2,1)}, bf16[16,32,128]{2,1,0:T(8,128)(2,1)S(1)}, u32[]{:S(2)}, u32[]{:S(2)}) collective-permute-start(bf16[16,32,128]{2,1,0:T(8,128)(2,1)} %get-tuple-element.22), channel_id=1, source_target_pairs={{0,16},{1,17},{2,18},{3,19},{4,20},{5,21},{6,22},{7,23},{8,24},{9,... | collective-permute-start | bytes 393224 | tf_op jit(solution)/shard_map/ppermute | solution.py:39
  8.3 5.9 %collective-permute-start.2 = (bf16[16,32,128]{2,1,0:T(8,128)(2,1)}, bf16[16,32,128]{2,1,0:T(8,128)(2,1)S(1)}, u32[]{:S(2)}, u32[]{:S(2)}) collective-permute-start(bf16[16,32,128]{2,1,0:T(8,128)(2,1)} %get-tuple-element.23), channel_id=1, source_target_pairs={{0,24},{1,25},{2,26},{3,27},{4,28},{5,29},{6,30},{7,31},{8,0},{9,1... | collective-permute-start | bytes 393224 | tf_op jit(solution)/shard_map/ppermute | solution.py:39
  10.6 3.7 %copy-start.10 = (bf16[16,32,128]{2,1,0:T(8,128)(2,1)}, bf16[16,32,128]{2,1,0:T(8,128)(2,1)S(1)}, u32[]{:S(2)}) copy-start(bf16[16,32,128]{2,1,0:T(8,128)(2,1)S(1)} %collective-permute-done.refs_1_) | copy-start | bytes 393220
  14.3 0.7 copy-start.11
  14.3 0.7 copy-start.12
  16.8 6.0 %collective-permute-start.11 = (bf16[12,32,128]{2,1,0:T(8,128)(2,1)}, bf16[12,32,128]{2,1,0:T(8,128)(2,1)S(1)}, u32[]{:S(2)}, u32[]{:S(2)}) collective-permute-start(bf16[12,32,128]{2,1,0:T(8,128)(2,1)} %get-tuple-element.25), channel_id=1, source_target_pairs={{0,6},{1,7},{2,0},{3,1},{4,2},{5,3},{6,4},{7,5},{8,14},{9,15},{10,... | collective-permute-start | bytes 294920 | tf_op jit(solution)/shard_map/ppermute | solution.py:39
  19.6 5.3 %collective-permute-start.10 = (bf16[12,32,128]{2,1,0:T(8,128)(2,1)}, bf16[12,32,128]{2,1,0:T(8,128)(2,1)S(1)}, u32[]{:S(2)}, u32[]{:S(2)}) collective-permute-start(bf16[12,32,128]{2,1,0:T(8,128)(2,1)} %get-tuple-element.25), channel_id=1, source_target_pairs={{0,4},{1,5},{2,6},{3,7},{4,0},{5,1},{6,2},{7,3},{8,12},{9,13},{10,... | collective-permute-start | bytes 294920 | tf_op jit(solution)/shard_map/ppermute | solution.py:39
  19.9 5.9 %collective-permute-start.9 = (bf16[12,32,128]{2,1,0:T(8,128)(2,1)}, bf16[12,32,128]{2,1,0:T(8,128)(2,1)S(1)}, u32[]{:S(2)}, u32[]{:S(2)}) collective-permute-start(bf16[12,32,128]{2,1,0:T(8,128)(2,1)} %get-tuple-element.25), channel_id=1, source_target_pairs={{0,2},{1,3},{2,4},{3,5},{4,6},{5,7},{6,0},{7,1},{8,10},{9,11},{10,... | collective-permute-start | bytes 294920 | tf_op jit(solution)/shard_map/ppermute | solution.py:39
  20.6 12.2 %collective-permute-start.5 = (bf16[12,32,128]{2,1,0:T(8,128)(2,1)}, bf16[12,32,128]{2,1,0:T(8,128)(2,1)S(1)}, u32[]{:S(2)}, u32[]{:S(2)}) collective-permute-start(bf16[12,32,128]{2,1,0:T(8,128)(2,1)} %get-tuple-element.24), channel_id=1, source_target_pairs={{0,24},{1,25},{2,26},{3,27},{4,28},{5,29},{6,30},{7,31},{8,0},{9,1... | collective-permute-start | bytes 294920 | tf_op jit(solution)/shard_map/ppermute | solution.py:39
  26.7 72.5 %copy-start.3 = (bf16[4,12,32,128]{3,2,1,0:T(8,128)(2,1)}, bf16[4,12,32,128]{3,2,1,0:T(8,128)(2,1)S(1)}, u32[]{:S(2)}) copy-start(bf16[4,12,32,128]{3,2,1,0:T(8,128)(2,1)S(1)} %pad_maximum_fusion.1.refs_4_) | copy-start | bytes 1179652
  26.8 35.8 %collective-permute-start.19 = (bf16[4,12,32,128]{3,2,1,0:T(8,128)(2,1)S(1)}, bf16[4,12,32,128]{3,2,1,0:T(8,128)(2,1)S(1)}, u32[]{:S(2)}, u32[]{:S(2)}) collective-permute-start(bf16[4,12,32,128]{3,2,1,0:T(8,128)(2,1)S(1)} %pad_maximum_fusion.1.refs_4_), channel_id=1, source_target_pairs={{0,1},{1,0},{2,3},{3,2},{4,5},{5,4},{6,7},{7,6},{8,9},{9,8},{10,11... | collective-permute-start | bytes 1179656 | tf_op jit(solution)/shard_map/ppermute | solution.py:39
  29.8 33.1 %collective-permute-start.14 = (bf16[4,12,32,128]{3,2,1,0:T(8,128)(2,1)S(1)}, bf16[4,12,32,128]{3,2,1,0:T(8,128)(2,1)S(1)}, u32[]{:S(2)}, u32[]{:S(2)}) collective-permute-start(bf16[4,12,32,128]{3,2,1,0:T(8,128)(2,1)S(1)} %pad_maximum_fusion.1.refs_4_), channel_id=1, source_target_pairs={{0,24},{1,25},{2,26},{3,27},{4,28},{5,29},{6,30},{7,31},{8,0},{9,1... | collective-permute-start | bytes 1179656 | tf_op jit(solution)/shard_map/ppermute | solution.py:39
  31.9 31.3 %collective-permute-start.13 = (bf16[4,12,32,128]{3,2,1,0:T(8,128)(2,1)S(1)}, bf16[4,12,32,128]{3,2,1,0:T(8,128)(2,1)S(1)}, u32[]{:S(2)}, u32[]{:S(2)}) collective-permute-start(bf16[4,12,32,128]{3,2,1,0:T(8,128)(2,1)S(1)} %pad_maximum_fusion.1.refs_4_), channel_id=1, source_target_pairs={{0,16},{1,17},{2,18},{3,19},{4,20},{5,21},{6,22},{7,23},{8,24},{9,... | collective-permute-start | bytes 1179656 | tf_op jit(solution)/shard_map/ppermute | solution.py:39
  32.8 31.3 %collective-permute-start.12 = (bf16[4,12,32,128]{3,2,1,0:T(8,128)(2,1)S(1)}, bf16[4,12,32,128]{3,2,1,0:T(8,128)(2,1)S(1)}, u32[]{:S(2)}, u32[]{:S(2)}) collective-permute-start(bf16[4,12,32,128]{3,2,1,0:T(8,128)(2,1)S(1)} %pad_maximum_fusion.1.refs_4_), channel_id=1, source_target_pairs={{0,8},{1,9},{2,10},{3,11},{4,12},{5,13},{6,14},{7,15},{8,16},{9,17... | collective-permute-start | bytes 1179656 | tf_op jit(solution)/shard_map/ppermute | solution.py:39
  32.8 21.4 %collective-permute-start.4 = (bf16[12,32,128]{2,1,0:T(8,128)(2,1)}, bf16[12,32,128]{2,1,0:T(8,128)(2,1)S(1)}, u32[]{:S(2)}, u32[]{:S(2)}) collective-permute-start(bf16[12,32,128]{2,1,0:T(8,128)(2,1)} %get-tuple-element.24), channel_id=1, source_target_pairs={{0,16},{1,17},{2,18},{3,19},{4,20},{5,21},{6,22},{7,23},{8,24},{9,... | collective-permute-start | bytes 294920 | tf_op jit(solution)/shard_map/ppermute | solution.py:39
  54.3 4.9 %collective-permute-start.3 = (bf16[12,32,128]{2,1,0:T(8,128)(2,1)}, bf16[12,32,128]{2,1,0:T(8,128)(2,1)S(1)}, u32[]{:S(2)}, u32[]{:S(2)}) collective-permute-start(bf16[12,32,128]{2,1,0:T(8,128)(2,1)} %get-tuple-element.24), channel_id=1, source_target_pairs={{0,8},{1,9},{2,10},{3,11},{4,12},{5,13},{6,14},{7,15},{8,16},{9,17... | collective-permute-start | bytes 294920 | tf_op jit(solution)/shard_map/ppermute | solution.py:39
  60.1 39.1 %copy-start.4 = (bf16[4,12,32,128]{3,2,1,0:T(8,128)(2,1)}, bf16[4,12,32,128]{3,2,1,0:T(8,128)(2,1)S(1)}, u32[]{:S(2)}) copy-start(bf16[4,12,32,128]{3,2,1,0:T(8,128)(2,1)S(1)} %pad_maximum_fusion.refs_0_) | copy-start | bytes 1179652
  60.1 4.7 %collective-permute-start.15 = (bf16[4,12,32,128]{3,2,1,0:T(8,128)(2,1)S(1)}, bf16[4,12,32,128]{3,2,1,0:T(8,128)(2,1)S(1)}, u32[]{:S(2)}, u32[]{:S(2)}) collective-permute-start(bf16[4,12,32,128]{3,2,1,0:T(8,128)(2,1)S(1)} %pad_maximum_fusion.refs_0_), channel_id=1, source_target_pairs={{0,1},{1,0},{2,3},{3,2},{4,5},{5,4},{6,7},{7,6},{8,9},{9,8},{10,11... | collective-permute-start | bytes 1179656 | tf_op jit(solution)/shard_map/ppermute | solution.py:39
  62.6 36.7 %copy-start.13 = (bf16[4,12,32,128]{3,2,1,0:T(8,128)(2,1)}, bf16[4,12,32,128]{3,2,1,0:T(8,128)(2,1)S(1)}, u32[]{:S(2)}) copy-start(bf16[4,12,32,128]{3,2,1,0:T(8,128)(2,1)S(1)} %collective-permute-done.19.refs_12_) | copy-start | bytes 1179652
  62.6 10.7 %collective-permute-start.8 = (bf16[4,12,32,128]{3,2,1,0:T(8,128)(2,1)S(1)}, bf16[4,12,32,128]{3,2,1,0:T(8,128)(2,1)S(1)}, u32[]{:S(2)}, u32[]{:S(2)}) collective-permute-start(bf16[4,12,32,128]{3,2,1,0:T(8,128)(2,1)S(1)} %pad_maximum_fusion.refs_0_), channel_id=1, source_target_pairs={{0,6},{1,7},{2,0},{3,1},{4,2},{5,3},{6,4},{7,5},{8,14},{9,15},{10,... | collective-permute-start | bytes 1179656 | tf_op jit(solution)/shard_map/ppermute | solution.py:39
  62.9 36.4 %copy-start.14 = (bf16[4,12,32,128]{3,2,1,0:T(8,128)(2,1)}, bf16[4,12,32,128]{3,2,1,0:T(8,128)(2,1)S(1)}, u32[]{:S(2)}) copy-start(bf16[4,12,32,128]{3,2,1,0:T(8,128)(2,1)S(1)} %collective-permute-done.14.refs_7_) | copy-start | bytes 1179652
  62.9 11.8 %collective-permute-start.7 = (bf16[4,12,32,128]{3,2,1,0:T(8,128)(2,1)S(1)}, bf16[4,12,32,128]{3,2,1,0:T(8,128)(2,1)S(1)}, u32[]{:S(2)}, u32[]{:S(2)}) collective-permute-start(bf16[4,12,32,128]{3,2,1,0:T(8,128)(2,1)S(1)} %pad_maximum_fusion.refs_0_), channel_id=1, source_target_pairs={{0,4},{1,5},{2,6},{3,7},{4,0},{5,1},{6,2},{7,3},{8,12},{9,13},{10,... | collective-permute-start | bytes 1179656 | tf_op jit(solution)/shard_map/ppermute | solution.py:39
  63.2 36.0 %copy-start.15 = (bf16[4,12,32,128]{3,2,1,0:T(8,128)(2,1)}, bf16[4,12,32,128]{3,2,1,0:T(8,128)(2,1)S(1)}, u32[]{:S(2)}) copy-start(bf16[4,12,32,128]{3,2,1,0:T(8,128)(2,1)S(1)} %collective-permute-done.13.refs_6_) | copy-start | bytes 1179652
  63.2 20.7 %collective-permute-start.6 = (bf16[4,12,32,128]{3,2,1,0:T(8,128)(2,1)S(1)}, bf16[4,12,32,128]{3,2,1,0:T(8,128)(2,1)}, u32[]{:S(2)}, u32[]{:S(2)}) collective-permute-start(bf16[4,12,32,128]{3,2,1,0:T(8,128)(2,1)S(1)} %pad_maximum_fusion.refs_0_), channel_id=1, source_target_pairs={{0,2},{1,3},{2,4},{3,5},{4,6},{5,7},{6,0},{7,1},{8,10},{9,11},{10,... | collective-permute-start | bytes 1179656 | tf_op jit(solution)/shard_map/ppermute | solution.py:39
  64.2 35.1 %copy-start.16 = (bf16[4,12,32,128]{3,2,1,0:T(8,128)(2,1)}, bf16[4,12,32,128]{3,2,1,0:T(8,128)(2,1)S(1)}, u32[]{:S(2)}) copy-start(bf16[4,12,32,128]{3,2,1,0:T(8,128)(2,1)S(1)} %collective-permute-done.12.refs_5_) | copy-start | bytes 1179652
  64.2 20.3 %collective-permute-start.22 = (bf16[4,12,32,128]{3,2,1,0:T(8,128)(2,1)S(1)}, bf16[4,12,32,128]{3,2,1,0:T(8,128)(2,1)S(1)}, u32[]{:S(2)}, u32[]{:S(2)}) collective-permute-start(bf16[4,12,32,128]{3,2,1,0:T(8,128)(2,1)S(1)} %collective-permute-done.14.refs_7_), channel_id=1, source_target_pairs={{0,1},{1,0},{2,3},{3,2},{4,5},{5,4},{6,7},{7,6},{8,9},{9,8},{10,11... | collective-permute-start | bytes 1179656 | tf_op jit(solution)/shard_map/ppermute | solution.py:39
  64.8 34.5 %copy-start.17 = (bf16[4,12,32,128]{3,2,1,0:T(8,128)(2,1)}, bf16[4,12,32,128]{3,2,1,0:T(8,128)(2,1)S(1)}, u32[]{:S(2)}) copy-start(bf16[4,12,32,128]{3,2,1,0:T(8,128)(2,1)S(1)} %collective-permute-done.15.refs_8_) | copy-start | bytes 1179652
  64.8 34.5 %collective-permute-start.21 = (bf16[4,12,32,128]{3,2,1,0:T(8,128)(2,1)S(1)}, bf16[4,12,32,128]{3,2,1,0:T(8,128)(2,1)}, u32[]{:S(2)}, u32[]{:S(2)}) collective-permute-start(bf16[4,12,32,128]{3,2,1,0:T(8,128)(2,1)S(1)} %collective-permute-done.13.refs_6_), channel_id=1, source_target_pairs={{0,1},{1,0},{2,3},{3,2},{4,5},{5,4},{6,7},{7,6},{8,9},{9,8},{10,11... | collective-permute-start | bytes 1179656 | tf_op jit(solution)/shard_map/ppermute | solution.py:39
  73.3 26.0 %copy-start.18 = (bf16[4,12,32,128]{3,2,1,0:T(8,128)(2,1)}, bf16[4,12,32,128]{3,2,1,0:T(8,128)(2,1)S(1)}, u32[]{:S(2)}) copy-start(bf16[4,12,32,128]{3,2,1,0:T(8,128)(2,1)S(1)} %collective-permute-done.8.refs_3_) | copy-start | bytes 1179652
  73.3 26.0 %collective-permute-start.20 = (bf16[4,12,32,128]{3,2,1,0:T(8,128)(2,1)S(1)}, bf16[4,12,32,128]{3,2,1,0:T(8,128)(2,1)}, u32[]{:S(2)}, u32[]{:S(2)}) collective-permute-start(bf16[4,12,32,128]{3,2,1,0:T(8,128)(2,1)S(1)} %collective-permute-done.12.refs_5_), channel_id=1, source_target_pairs={{0,1},{1,0},{2,3},{3,2},{4,5},{5,4},{6,7},{7,6},{8,9},{9,8},{10,11... | collective-permute-start | bytes 1179656 | tf_op jit(solution)/shard_map/ppermute | solution.py:39
  74.7 24.6 %copy-start.19 = (bf16[4,12,32,128]{3,2,1,0:T(8,128)(2,1)}, bf16[4,12,32,128]{3,2,1,0:T(8,128)(2,1)S(1)}, u32[]{:S(2)}) copy-start(bf16[4,12,32,128]{3,2,1,0:T(8,128)(2,1)S(1)} %collective-permute-done.7.refs_2_) | copy-start | bytes 1179652
  74.7 24.6 %collective-permute-start.18 = (bf16[4,12,32,128]{3,2,1,0:T(8,128)(2,1)S(1)}, bf16[4,12,32,128]{3,2,1,0:T(8,128)(2,1)}, u32[]{:S(2)}, u32[]{:S(2)}) collective-permute-start(bf16[4,12,32,128]{3,2,1,0:T(8,128)(2,1)S(1)} %collective-permute-done.8.refs_3_), channel_id=1, source_target_pairs={{0,1},{1,0},{2,3},{3,2},{4,5},{5,4},{6,7},{7,6},{8,9},{9,8},{10,11... | collective-permute-start | bytes 1179656 | tf_op jit(solution)/shard_map/ppermute | solution.py:39
  84.0 15.4 %collective-permute-start.17 = (bf16[4,12,32,128]{3,2,1,0:T(8,128)(2,1)S(1)}, bf16[4,12,32,128]{3,2,1,0:T(8,128)(2,1)}, u32[]{:S(2)}, u32[]{:S(2)}) collective-permute-start(bf16[4,12,32,128]{3,2,1,0:T(8,128)(2,1)S(1)} %collective-permute-done.7.refs_2_), channel_id=1, source_target_pairs={{0,1},{1,0},{2,3},{3,2},{4,5},{5,4},{6,7},{7,6},{8,9},{9,8},{10,11... | collective-permute-start | bytes 1179656 | tf_op jit(solution)/shard_map/ppermute | solution.py:39
  84.4 0.8 copy-start.20
  85.2 14.2 %collective-permute-start.16 = (bf16[4,12,32,128]{3,2,1,0:T(8,128)(2,1)}, bf16[4,12,32,128]{3,2,1,0:T(8,128)(2,1)}, u32[]{:S(2)}, u32[]{:S(2)}) collective-permute-start(bf16[4,12,32,128]{3,2,1,0:T(8,128)(2,1)} %collective-permute-done.6.refs_1_), channel_id=1, source_target_pairs={{0,1},{1,0},{2,3},{3,2},{4,5},{5,4},{6,7},{7,6},{8,9},{9,8},{10,11... | collective-permute-start | bytes 1179656 | tf_op jit(solution)/shard_map/ppermute | solution.py:39
  125.7 17.6 %copy-start.6 = (bf16[128,512]{1,0:T(8,128)(2,1)S(1)}, bf16[128,512]{1,0:T(8,128)(2,1)}, u32[]{:S(2)}) copy-start(bf16[128,512]{1,0:T(8,128)(2,1)} %get-tuple-element.28.refs_0_) | copy-start | bytes 393220
  140.6 13.2 %copy-start.1 = (bf16[4,64,640]{2,1,0:T(8,128)(2,1)}, bf16[4,64,640]{2,1,0:T(8,128)(2,1)S(1)}, u32[]{:S(2)}) copy-start(bf16[4,64,640]{2,1,0:T(8,128)(2,1)S(1)} %all_to_all.21.refs_4_) | copy-start | bytes 983044
  140.6 13.2 %collective-permute-start.26 = (bf16[4,64,640]{2,1,0:T(8,128)(2,1)S(1)}, bf16[4,64,640]{2,1,0:T(8,128)(2,1)S(1)}, u32[]{:S(2)}, u32[]{:S(2)}) collective-permute-start(bf16[4,64,640]{2,1,0:T(8,128)(2,1)S(1)} %all_to_all.21.refs_4_), channel_id=1, source_target_pairs={{0,1},{1,0},{2,3},{3,2},{4,5},{5,4},{6,7},{7,6},{8,9},{9,8},{10,11... | collective-permute-start | bytes 983048 | tf_op jit(solution)/shard_map/ppermute | solution.py:39
  143.3 5.0 %collective-permute-start.25 = (bf16[128,512]{1,0:T(8,128)(2,1)S(1)}, bf16[128,512]{1,0:T(8,128)(2,1)S(1)}, u32[]{:S(2)}, u32[]{:S(2)}) collective-permute-start(bf16[128,512]{1,0:T(8,128)(2,1)S(1)} %copy-done.6), channel_id=1, source_target_pairs={{0,96},{32,0},{64,32},{96,64},{1,97},{33,1},{65,33},{97,65},{2,98}... | collective-permute-start | bytes 393224 | tf_op jit(solution)/shard_map/ppermute | solution.py:43
  144.1 6.2 %collective-permute-start.24 = (bf16[128,512]{1,0:T(8,128)(2,1)S(1)}, bf16[128,512]{1,0:T(8,128)(2,1)S(1)}, u32[]{:S(2)}, u32[]{:S(2)}) collective-permute-start(bf16[128,512]{1,0:T(8,128)(2,1)S(1)} %copy-done.6), channel_id=1, source_target_pairs={{0,64},{32,96},{64,0},{96,32},{1,65},{33,97},{65,1},{97,33},{2,66}... | collective-permute-start | bytes 393224 | tf_op jit(solution)/shard_map/ppermute | solution.py:43
  145.3 8.5 %collective-permute-start.23 = (bf16[128,512]{1,0:T(8,128)(2,1)S(1)}, bf16[128,512]{1,0:T(8,128)(2,1)S(1)}, u32[]{:S(2)}, u32[]{:S(2)}) collective-permute-start(bf16[128,512]{1,0:T(8,128)(2,1)S(1)} %copy-done.6), channel_id=1, source_target_pairs={{0,32},{32,64},{64,96},{96,0},{1,33},{33,65},{65,97},{97,1},{2,34}... | collective-permute-start | bytes 393224 | tf_op jit(solution)/shard_map/ppermute | solution.py:43
  148.2 5.7 %copy-start.7 = (bf16[128,512]{1,0:T(8,128)(2,1)}, bf16[128,512]{1,0:T(8,128)(2,1)S(1)}, u32[]{:S(2)}) copy-start(bf16[128,512]{1,0:T(8,128)(2,1)S(1)} %collective-permute-done.25.refs_3_) | copy-start | bytes 393220
  150.3 3.5 %copy-start.8 = (bf16[128,512]{1,0:T(8,128)(2,1)}, bf16[128,512]{1,0:T(8,128)(2,1)S(1)}, u32[]{:S(2)}) copy-start(bf16[128,512]{1,0:T(8,128)(2,1)S(1)} %collective-permute-done.24.refs_2_) | copy-start | bytes 393220
  153.9 0.6 copy-start.9
  154.5 0.7 copy-start.5
  200.8 3.5 %copy-start = (bf16[64,16,640]{2,1,0:T(8,128)(2,1)}, bf16[64,16,640]{2,1,0:T(8,128)(2,1)S(1)}, u32[]{:S(2)}) copy-start(bf16[64,16,640]{2,1,0:T(8,128)(2,1)S(1)} %all_to_all.23) | copy-start | bytes 3932164
  200.8 6.2 %collective-permute-start.27 = (bf16[4,16,16,640]{3,2,1,0:T(8,128)(2,1)S(1)}, bf16[4,16,16,640]{3,2,1,0:T(8,128)(2,1)S(1)}, u32[]{:S(2)}, u32[]{:S(2)}) collective-permute-start(bf16[4,16,16,640]{3,2,1,0:T(8,128)(2,1)S(1)} %bitcast.13), channel_id=1, source_target_pairs={{0,1},{1,0},{2,3},{3,2},{4,5},{5,4},{6,7},{7,6},{8,9},{9,8},{10,11... | collective-permute-start | bytes 3932168 | tf_op jit(solution)/shard_map/ppermute | solution.py:39
  206.9 1.1 copy-start.2

commit v4 on v3

--- a/solution.py
+++ b/solution.py
@@ -59,23 +59,22 @@
     variance = jnp.mean(centred * centred, axis=-1, keepdims=True)
     norm[0] = (centred * lax.rsqrt(variance + epsilon_norm)).astype(bf16)
 
-    @pl.when(pl.program_id(1) == lax.axis_index("role"))
-    def _():
-        mean[...] = jnp.dot(pool_mat, hidden[0], preferred_element_type=f32)
+    quarter = hidden[0, pl.ds(pl.multiple_of(lax.axis_index("role") * 128, 128), 128), :]
+    mean[...] = jnp.dot(pool_mat, quarter, preferred_element_type=f32)
 
 
 def norms(hidden):
     width = hidden.shape[-1]
-    rows = pl.BlockSpec((1, 128, width), lambda i, j: (i, j, 0))
+    rows = pl.BlockSpec((1, FRAMES, width), lambda i: (i, 0, 0))
     return pl.pallas_call(
         norm_kernel,
-        grid=(2, 4),
+        grid=(2,),
         out_shape=[
             jax.ShapeDtypeStruct(hidden.shape, bf16),
             jax.ShapeDtypeStruct((ROWS, width), f32),
         ],
         in_specs=[rows],
-        out_specs=[rows, pl.BlockSpec((32, width), lambda i, j: (i, 0))],
+        out_specs=[rows, pl.BlockSpec((32, width), lambda i: (i, 0))],
         cost_estimate=pl.CostEstimate(
             flops=30_000_000, bytes_accessed=12_000_000, transcendentals=2048
         ),
@@ -195,9 +194,9 @@
 def attend_kernel(frames_valid, slot_clip, *refs):
     pieces = refs[:16]
     norm_a_hbm, norm_w_hbm, head_a_hbm, head_w_hbm = refs[16:20]
-    pooled, lat, pred_a, pred_w = refs[20:24]
-    norm_a, norm_w, rows_in, qkv_a, qkv_w, proj, att_a, att_w = refs[24:32]
-    score_refs, slots, head_a, head_w, sems = refs[32:34], *refs[34:38]
+    outs, lat, pred_a, pred_w = refs[20:24], *refs[24:27]
+    norm_a, norm_w, rows_in, qkv_a, qkv_w, proj, att_a, att_w = refs[27:35]
+    score_refs, slots, head_a, head_w, pooled, sems = refs[35:37], *refs[37:42]
     copy_head_a = pltpu.make_async_copy(head_a_hbm, head_a, sems.at[4])
     copy_head_w = pltpu.make_async_copy(head_w_hbm, head_w, sems.at[5])
     copy_a = pltpu.make_async_copy(norm_a_hbm, norm_a, sems.at[2])
@@ -349,21 +348,23 @@
         mean = lax.dot_general(pool_mat, rows, nt, preferred_element_type=f32).astype(bf16)
         mean = jnp.concatenate([mean, jnp.zeros((POOLED, 64), bf16)], axis=1)
         pooled[:, clip * 32 : clip * 32 + 32, A_COLS:] = mean.reshape(ROLES, 32, 384)
+    for k in range(ROLES):
+        outs[k][...] = pooled[(role + k) % ROLES]
 
 
 def attend(frames_valid, slot_clip, pieces, norm_a, norm_w, head_a, head_w):
     vmem = pl.BlockSpec(memory_space=pltpu.VMEM)
     return pl.pallas_call(
         attend_kernel,
-        out_shape=[
-            jax.ShapeDtypeStruct((ROLES, ROWS, OUT_COLS), bf16),
+        out_shape=[jax.ShapeDtypeStruct((ROWS, OUT_COLS), bf16)] * ROLES
+        + [
             jax.ShapeDtypeStruct((2 * ROWS, STU_D), bf16),
             jax.ShapeDtypeStruct((ROWS, WAVLM_D), f32),
             jax.ShapeDtypeStruct((ROWS, WHISPER_D), f32),
         ],
         in_specs=[pl.BlockSpec(memory_space=pltpu.SMEM)] * 2
         + [pl.BlockSpec(memory_space=pl.ANY)] * 20,
-        out_specs=[vmem] * 4,
+        out_specs=[vmem] * 7,
         scratch_shapes=[
             pltpu.VMEM((2, FRAMES, WAVLM_D), bf16),
             pltpu.VMEM((2, FRAMES, WHISPER_D), bf16),
@@ -378,6 +379,7 @@
             pltpu.SMEM((4,), jnp.int32),
             pltpu.VMEM((STU_D, WAVLM_D), bf16),
             pltpu.VMEM((STU_D, WHISPER_D), bf16),
+            pltpu.VMEM((ROLES, ROWS, OUT_COLS), bf16),
             pltpu.SemaphoreType.DMA((6,)),
         ],
         cost_estimate=pl.CostEstimate(
@@ -387,25 +389,36 @@
     )(frames_valid, slot_clip, *pieces, norm_a, norm_w, head_a, head_w)
 
 
-def slope_kernel(frames_valid, parts, out_a_hbm, out_w_hbm, *refs):
-    mean_a, mean_w, pred_a, pred_w, grouped, out_a, out_w, sems = refs
-    copy_a = pltpu.make_async_copy(out_a_hbm, out_a, sems.at[0])
-    copy_w = pltpu.make_async_copy(out_w_hbm, out_w, sems.at[1])
-    copy_a.start()
-    copy_w.start()
+def slope_kernel(frames_valid, *refs):
+    arrived = refs[:4]
+    out_a_hbm, out_w_hbm, mean_a, mean_w, pred_a, pred_w = refs[4:10]
+    outs, parts, grouped, out_a, out_w, sems = refs[10:14], *refs[14:19]
+    copies = []
+    for source, target in ((out_a_hbm, out_a), (out_w_hbm, out_w)):
+        for start in range(0, source.shape[0], 256):
+            rows = pl.ds(start, 256)
+            copies.append(
+                pltpu.make_async_copy(source.at[rows], target.at[rows], sems.at[len(copies)])
+            )
+            copies[-1].start()
     role = lax.axis_index("role")
     clip = lax.axis_index("dp") * 2
+    for k in range(ROLES):
+        parts[(role - k + ROLES) % ROLES] = arrived[k][...]
     row = lax.broadcasted_iota(jnp.int32, (ROWS, 1), 0)
     valid = jnp.where(row < 32, frames_valid[clip], frames_valid[clip + 1]) // POOL
     keep = (row % 32 + role * 32) < valid
 
-    def slope_of(mean, copy, out, pred, cols, first):
+    def slope_of(mean, waits, out, pred, cols, first):
         width = mean.shape[-1]
         attended = jnp.concatenate(
             [parts[r, :, first : first + cols] for r in range(ROLES)], axis=1
         )
-        copy.wait()
-        total = mean[...] + jnp.dot(attended, out[...], preferred_element_type=f32)
+        total = mean[...]
+        for i, copy in enumerate(waits):
+            copy.wait()
+            rows = slice(256 * i, 256 * i + 256)
+            total = total + jnp.dot(attended[:, rows], out[rows], preferred_element_type=f32)
         target = total.astype(bf16).astype(f32)
         predicted = pred[...]
         pred_sq = jnp.sum(predicted * predicted, axis=-1, keepdims=True) + epsilon_cos
@@ -417,42 +430,45 @@
         slope = slope + (predicted - target) * (1.0 / width)
         return jnp.where(keep, slope, 0.0).astype(bf16)
 
-    slope_a = slope_of(mean_a, copy_a, out_a, pred_a, A_COLS, 0)
+    slope_a = slope_of(mean_a, copies[:4], out_a, pred_a, A_COLS, 0)
     for g in range(ROLES):
         grouped[g, :, :A_COLS] = slope_a[:, g * A_COLS : (g + 1) * A_COLS]
-    slope_w = slope_of(mean_w, copy_w, out_w, pred_w, W_COLS, A_COLS)
+    slope_w = slope_of(mean_w, copies[4:], out_w, pred_w, W_COLS, A_COLS)
     for g in range(ROLES):
         grouped[g, :, A_COLS:] = jnp.concatenate(
             [slope_w[:, g * W_COLS : (g + 1) * W_COLS], jnp.zeros((ROWS, 64), bf16)], axis=1
         )
+    for k in range(ROLES):
+        outs[k][...] = grouped[(role + k) % ROLES]
 
 
 def slopes(frames_valid, parts, out_a, out_w, mean_a, mean_w, pred_a, pred_w):
     vmem = pl.BlockSpec(memory_space=pltpu.VMEM)
-    hbm = pl.BlockSpec(memory_space=pl.ANY)
     return pl.pallas_call(
         slope_kernel,
-        out_shape=jax.ShapeDtypeStruct((ROLES, ROWS, OUT_COLS), bf16),
-        in_specs=[pl.BlockSpec(memory_space=pltpu.SMEM), vmem, hbm, hbm] + [vmem] * 4,
-        out_specs=vmem,
-        scratch_shapes=[
+        out_shape=[jax.ShapeDtypeStruct((ROWS, OUT_COLS), bf16)] * ROLES,
+        in_specs=[pl.BlockSpec(memory_space=pltpu.SMEM)]
+        + [vmem] * 4
+        + [pl.BlockSpec(memory_space=pl.ANY)] * 2
+        + [vmem] * 4,
+        out_specs=[vmem] * ROLES,
+        scratch_shapes=[pltpu.VMEM((ROLES, ROWS, OUT_COLS), bf16)] * 2
+        + [
             pltpu.VMEM((WAVLM_D, WAVLM_D), bf16),
             pltpu.VMEM((WHISPER_D, WHISPER_D), bf16),
-            pltpu.SemaphoreType.DMA((2,)),
+            pltpu.SemaphoreType.DMA((9,)),
         ],
         name="slopes",
-    )(frames_valid, parts, out_a, out_w, mean_a, mean_w, pred_a, pred_w)
+    )(frames_valid, *parts, out_a, out_w, mean_a, mean_w, pred_a, pred_w)
 
 
 def outer_kernel(*refs):
-    lats, own, other, out = refs[:4], refs[4], refs[5], refs[6]
-    role = lax.axis_index("role")
+    lats, own, other, out = refs[:4], refs[4:8], refs[8:12], refs[12]
     start = pl.multiple_of((lax.axis_index("dp") % 2) * 256, 256)
     lat = jnp.concatenate([lats[k][:, pl.ds(start, 256)] for k in range(ROLES)], axis=0)
     rows = []
     for k in range(ROLES):
-        source = (role - k + ROLES) % ROLES
-        rows += [own[source], other[source]]
+        rows += [own[k][...], other[k][...]]
     grad = lax.dot_general(
         lat, jnp.concatenate(rows, axis=0), (((0,), (0,)), ((), ())), preferred_element_type=f32
     )
@@ -464,10 +480,10 @@
     return pl.pallas_call(
         outer_kernel,
         out_shape=jax.ShapeDtypeStruct((16, 16, OUT_COLS), f32),
-        in_specs=[vmem] * 6,
+        in_specs=[vmem] * 12,
         out_specs=vmem,
         name="outer",
-    )(*lats, own, other)
+    )(*lats, *own, *other)
 
 
 def sum_kernel(x, out):
@@ -489,8 +505,9 @@
 def place_kernel(piece, *refs):
     out_a, out_w = refs[-2:]
     blocks = []
+    step = pl.program_id(0) * 8
     for g in range(ROLES):
-        block = piece[g].reshape(128, OUT_COLS).astype(f32)
+        block = piece[g, pl.ds(step, 8)].reshape(128, OUT_COLS).astype(f32)
         out_a[0, :, g * A_COLS : (g + 1) * A_COLS] = block[:, :A_COLS]
         blocks.append(block[:, A_COLS : A_COLS + W_COLS])
     out_w[0] = jnp.concatenate(blocks, axis=1)
@@ -506,7 +523,7 @@
             jax.ShapeDtypeStruct((2, 256, WAVLM_D), f32),
             jax.ShapeDtypeStruct((2, 256, WHISPER_D), f32),
         ],
-        in_specs=[pl.BlockSpec((ROLES, 8, 16, OUT_COLS), lambda i: (0, i, 0, 0))]
+        in_specs=[pl.BlockSpec(memory_space=pltpu.VMEM)]
         + [hbm] * len(held),
         out_specs=[
             pl.BlockSpec((1, 128, WAVLM_D), lambda i: (half(), i, 0)),
@@ -543,16 +560,16 @@
     norm_a, mean_a = norms(wavlm_hidden)
     norm_w, mean_w = norms(whisper_hidden)
 
-    pooled, lat, pred_a, pred_w = attend(
+    *pooled, lat, pred_a, pred_w = attend(
         frames_valid, slot_clip, pieces, norm_a, norm_w, wavlm_head, whisper_head
     )
-    parts = lax.all_to_all(pooled, "role", split_axis=0, concat_axis=0, tiled=True)
+    parts = [pooled[0]] + [role_send(pooled[k], k) for k in (1, 2, 3)]
     lats = [lat] + [role_send(lat, k) for k in (1, 2, 3)]
     sloped = slopes(
         frames_valid, parts, wavlm_out, whisper_out, mean_a, mean_w, pred_a, pred_w
     )
-    slope_own = lax.all_to_all(sloped, "role", split_axis=0, concat_axis=0, tiled=True)
-    slope_other = dp_send(slope_own, 0, 0, 1)
+    slope_own = [sloped[0]] + [role_send(sloped[k], k) for k in (1, 2, 3)]
+    slope_other = [dp_send(x, 0, 0, 1) for x in slope_own]
     halves = outer(lats, slope_own, slope_other)
     arrived = lax.all_to_all(
         halves, "dp", split_axis=0, concat_axis=0, tiled=True, axis_index_groups=PLANE

time: 212 us -> 194 us (0.915)
  blocking collectives: 61 us -> 41.2 us
  starting transfers between devices: 37.6 us -> 52.3 us
  Pallas kernels: 48.7 us -> 42.3 us
  waiting for transfers between devices: 56.7 us -> 50.8 us
    all_to_all x2 -> x0, blocking collectives: 20.4 us -> none  [the longest x1 11 us: per_device(): lax.all_to_all(pooled, 'role', split_axis=0, concat_axis=0, tiled=True)]
    ppermute x3 -> x9, starting transfers between devices: 2.08 us -> 14.1 us  [role_send(): return lax.ppermute(x, 'role', [(i, (i + k) % ROLES) for i in range(ROLES)])]
    pallas_call x4, Pallas kernels: 34.9 us -> 28 us  [the longest x1 15.3 us: attend(): pl.pallas_call(attend_kernel, out_shape=[jax.ShapeDtypeStruct((ROWS, OUT_...]
    ppermute x3 -> x9, waiting for transfers between devices: 8.53 us -> 1.68 us  [role_send(): return lax.ppermute(x, 'role', [(i, (i + k) % ROLES) for i in range(ROLES)])]
    ppermute x25 -> x28, starting transfers between devices: 35.5 us -> 38.3 us  [dp_send(): return lax.ppermute(x, 'dp', pairs)]
    ppermute x25 -> x28, waiting for transfers between devices: 48.1 us -> 49.1 us  [dp_send(): return lax.ppermute(x, 'dp', pairs)]
  transfers between devices with their start and end apart: 28 -> 37, of which waited for: 12 -> 13; matrix products, arithmetic and copies ran while one was open for 1% -> 1% of each run, Pallas kernels for 8% -> 8%
where the time goes in v4:
time: 194 us; the launch traced here: 193 us
  starting transfers between devices  52.3 us (27%)
  waiting for transfers between devices  50.8 us (26%)
  Pallas kernels  42.3 us (22%)
  blocking collectives  41.2 us (21%)
  local copies, waits for them, and re-layouts  4.1 us (2%)
    ppermute x28, waiting for transfers between devices, dp_send(): return lax.ppermute(x, 'dp', pairs)  49.1 us
    ppermute x28, starting transfers between devices, dp_send(): return lax.ppermute(x, 'dp', pairs)  38.3 us
    all_to_all x1, blocking collectives, per_device(): lax.all_to_all(reduce_parts(arrived), ('role', 'dp'), split_axis=0, conca...  25.1 us
    all_to_all x1, blocking collectives, per_device(): lax.all_to_all(halves, 'dp', split_axis=0, concat_axis=0, tiled=True, axi...  16.1 us
    pallas_call x1, Pallas kernels, attend(): pl.pallas_call(attend_kernel, out_shape=[jax.ShapeDtypeStruct((ROWS, OUT_...  15.3 us
    ppermute x9, starting transfers between devices, role_send(): return lax.ppermute(x, 'role', [(i, (i + k) % ROLES) for i in range(ROLES)])  14.1 us
    pallas_call x2, Pallas kernels, norms(): pl.pallas_call(norm_kernel, grid=(2,), out_shape=[jax.ShapeDtypeStruct(hi...  7.41 us
    pallas_call x2, Pallas kernels, place(): pl.pallas_call(place_kernel, grid=(2,), out_shape=[jax.ShapeDtypeStruct((...  5.57 us
  transfers between devices with their start and end apart: 37, of which 13 were waited for; matrix products, arithmetic and copies ran while one was open for 1% of the time, Pallas kernels for 8%

profile of v4, /device:TPU:1, one launch (start us, length us, event | category | flops | bytes accessed | tf_op | source)
XLA Modules:
  0.0 193.5 jit_solution(5597774576367714817)
XLA Ops:
  0.6 2.0 %weight_chunks.1 = (bf16[16,32,128]{2,1,0:T(8,128)(2,1)}, bf16[16,32,128]{2,1,0:T(8,128)(2,1)}, bf16[16,32,128]{2,1,0:T(8,128)(2,1)}, bf16[16,32,128]{2,1,0:T(8,128)(2,1)}) custom-call(bf16[96,1024]{1,0:T(8,128)(2,1)} %bitcast.18, bf16[120,1280]{1,0:T(8,128)(2,1)} %bitcast.17), custom_call_target="tpu_custom_call" | custom-call | tf_op jit(solution)/shard_map/weight_chunks/pallas_call | solution.py:104
  2.6 2.5 %collective-permute-start = (bf16[16,32,128]{2,1,0:T(8,128)(2,1)}, bf16[16,32,128]{2,1,0:T(8,128)(2,1)S(1)}, u32[]{:S(2)}, u32[]{:S(2)}) collective-permute-start(bf16[16,32,128]{2,1,0:T(8,128)(2,1)} %get-tuple-element.28), channel_id=1, source_target_pairs={{0,8},{1,9},{2,10},{3,11},{4,12},{5,13},{6,14},{7,15},{8,16},{9,17... | collective-permute-start | bytes 393224 | tf_op jit(solution)/shard_map/ppermute | solution.py:39
  5.0 3.3 %collective-permute-start.1 = (bf16[16,32,128]{2,1,0:T(8,128)(2,1)}, bf16[16,32,128]{2,1,0:T(8,128)(2,1)S(1)}, u32[]{:S(2)}, u32[]{:S(2)}) collective-permute-start(bf16[16,32,128]{2,1,0:T(8,128)(2,1)} %get-tuple-element.29), channel_id=1, source_target_pairs={{0,16},{1,17},{2,18},{3,19},{4,20},{5,21},{6,22},{7,23},{8,24},{9,... | collective-permute-start | bytes 393224 | tf_op jit(solution)/shard_map/ppermute | solution.py:39
  8.3 0.7 collective-permute-start.2
  9.1 1.5 collective-permute-done.refs_1_
  10.6 3.7 %collective-permute-done.1.refs_2_ = bf16[16,32,128]{2,1,0:T(8,128)(2,1)S(1)} collective-permute-done((bf16[16,32,128]{2,1,0:T(8,128)(2,1)}, bf16[16,32,128]{2,1,0:T(8,128)(2,1)S(1)}, u32[]{:S(2)}, u32[]{:S(2)}) %collective-permute-start.1) | collective-permute-done | bytes 131104 | tf_op jit(solution)/shard_map/ppermute | solution.py:39
  14.3 0.6 copy-done.9
  15.0 1.9 shares.1
  16.9 2.7 %collective-permute-start.11 = (bf16[12,32,128]{2,1,0:T(8,128)(2,1)}, bf16[12,32,128]{2,1,0:T(8,128)(2,1)S(1)}, u32[]{:S(2)}, u32[]{:S(2)}) collective-permute-start(bf16[12,32,128]{2,1,0:T(8,128)(2,1)} %get-tuple-element.32), channel_id=1, source_target_pairs={{0,6},{1,7},{2,0},{3,1},{4,2},{5,3},{6,4},{7,5},{8,14},{9,15},{10,... | collective-permute-start | bytes 294920 | tf_op jit(solution)/shard_map/ppermute | solution.py:39
  19.6 0.3 collective-permute-start.10
  20.0 0.7 collective-permute-start.9
  20.6 2.2 %collective-permute-start.5 = (bf16[12,32,128]{2,1,0:T(8,128)(2,1)}, bf16[12,32,128]{2,1,0:T(8,128)(2,1)S(1)}, u32[]{:S(2)}, u32[]{:S(2)}) collective-permute-start(bf16[12,32,128]{2,1,0:T(8,128)(2,1)} %get-tuple-element.31), channel_id=1, source_target_pairs={{0,24},{1,25},{2,26},{3,27},{4,28},{5,29},{6,30},{7,31},{8,0},{9,1... | collective-permute-start | bytes 294920 | tf_op jit(solution)/shard_map/ppermute | solution.py:39
  22.9 2.0 %collective-permute-done.10 = bf16[12,32,128]{2,1,0:T(8,128)(2,1)S(1)} collective-permute-done((bf16[12,32,128]{2,1,0:T(8,128)(2,1)}, bf16[12,32,128]{2,1,0:T(8,128)(2,1)S(1)}, u32[]{:S(2)}, u32[]{:S(2)}) %collective-permute-start.10) | collective-permute-done | bytes 98336 | tf_op jit(solution)/shard_map/ppermute | solution.py:39
  24.9 1.0 collective-permute-done.9
  25.8 0.9 pad_maximum_fusion.1.refs_4_
  26.8 3.0 %collective-permute-start.19 = (bf16[4,12,32,128]{3,2,1,0:T(8,128)(2,1)S(1)}, bf16[4,12,32,128]{3,2,1,0:T(8,128)(2,1)S(1)}, u32[]{:S(2)}, u32[]{:S(2)}) collective-permute-start(bf16[4,12,32,128]{3,2,1,0:T(8,128)(2,1)S(1)} %pad_maximum_fusion.1.refs_4_), channel_id=1, source_target_pairs={{0,1},{1,0},{2,3},{3,2},{4,5},{5,4},{6,7},{7,6},{8,9},{9,8},{10,11... | collective-permute-start | bytes 1179656 | tf_op jit(solution)/shard_map/ppermute | solution.py:39
  29.8 2.1 %collective-permute-start.14 = (bf16[4,12,32,128]{3,2,1,0:T(8,128)(2,1)S(1)}, bf16[4,12,32,128]{3,2,1,0:T(8,128)(2,1)S(1)}, u32[]{:S(2)}, u32[]{:S(2)}) collective-permute-start(bf16[4,12,32,128]{3,2,1,0:T(8,128)(2,1)S(1)} %pad_maximum_fusion.1.refs_4_), channel_id=1, source_target_pairs={{0,24},{1,25},{2,26},{3,27},{4,28},{5,29},{6,30},{7,31},{8,0},{9,1... | collective-permute-start | bytes 1179656 | tf_op jit(solution)/shard_map/ppermute | solution.py:39
  31.9 0.9 collective-permute-start.13
  32.9 2.0 %collective-permute-start.4 = (bf16[12,32,128]{2,1,0:T(8,128)(2,1)}, bf16[12,32,128]{2,1,0:T(8,128)(2,1)S(1)}, u32[]{:S(2)}, u32[]{:S(2)}) collective-permute-start(bf16[12,32,128]{2,1,0:T(8,128)(2,1)} %get-tuple-element.31), channel_id=1, source_target_pairs={{0,16},{1,17},{2,18},{3,19},{4,20},{5,21},{6,22},{7,23},{8,24},{9,... | collective-permute-start | bytes 294920 | tf_op jit(solution)/shard_map/ppermute | solution.py:39
  34.9 19.4 %collective-permute-done.4 = bf16[12,32,128]{2,1,0:T(8,128)(2,1)S(1)} collective-permute-done((bf16[12,32,128]{2,1,0:T(8,128)(2,1)}, bf16[12,32,128]{2,1,0:T(8,128)(2,1)S(1)}, u32[]{:S(2)}, u32[]{:S(2)}) %collective-permute-start.4) | collective-permute-done | bytes 98336 | tf_op jit(solution)/shard_map/ppermute | solution.py:39
  54.3 4.9 %collective-permute-done.3 = bf16[12,32,128]{2,1,0:T(8,128)(2,1)S(1)} collective-permute-done((bf16[12,32,128]{2,1,0:T(8,128)(2,1)}, bf16[12,32,128]{2,1,0:T(8,128)(2,1)S(1)}, u32[]{:S(2)}, u32[]{:S(2)}) %collective-permute-start.3) | collective-permute-done | bytes 98336 | tf_op jit(solution)/shard_map/ppermute | solution.py:39
  59.2 0.9 pad_maximum_fusion.refs_0_
  60.2 2.4 %collective-permute-start.15 = (bf16[4,12,32,128]{3,2,1,0:T(8,128)(2,1)S(1)}, bf16[4,12,32,128]{3,2,1,0:T(8,128)(2,1)S(1)}, u32[]{:S(2)}, u32[]{:S(2)}) collective-permute-start(bf16[4,12,32,128]{3,2,1,0:T(8,128)(2,1)S(1)} %pad_maximum_fusion.refs_0_), channel_id=1, source_target_pairs={{0,1},{1,0},{2,3},{3,2},{4,5},{5,4},{6,7},{7,6},{8,9},{9,8},{10,11... | collective-permute-start | bytes 1179656 | tf_op jit(solution)/shard_map/ppermute | solution.py:39
  62.6 0.3 collective-permute-start.8
  62.9 0.3 collective-permute-start.7
  63.3 0.9 collective-permute-start.6
  64.2 0.7 collective-permute-start.22
  65.0 8.3 %collective-permute-done.8.refs_3_ = bf16[4,12,32,128]{3,2,1,0:T(8,128)(2,1)S(1)} collective-permute-done((bf16[4,12,32,128]{3,2,1,0:T(8,128)(2,1)S(1)}, bf16[4,12,32,128]{3,2,1,0:T(8,128)(2,1)S(1)}, u32[]{:S(2)}, u32[]{:S(2)}) %collective-permute-start.8) | collective-permute-done | bytes 393248 | tf_op jit(solution)/shard_map/ppermute | solution.py:39
  73.3 1.4 collective-permute-start.20
  74.8 2.1 %collective-permute-start.18 = (bf16[4,12,32,128]{3,2,1,0:T(8,128)(2,1)S(1)}, bf16[4,12,32,128]{3,2,1,0:T(8,128)(2,1)}, u32[]{:S(2)}, u32[]{:S(2)}) collective-permute-start(bf16[4,12,32,128]{3,2,1,0:T(8,128)(2,1)S(1)} %collective-permute-done.8.refs_3_), channel_id=1, source_target_pairs={{0,1},{1,0},{2,3},{3,2},{4,5},{5,4},{6,7},{7,6},{8,9},{9,8},{10,11... | collective-permute-start | bytes 1179656 | tf_op jit(solution)/shard_map/ppermute | solution.py:39
  76.8 7.2 %collective-permute-done.6.refs_1_ = bf16[4,12,32,128]{3,2,1,0:T(8,128)(2,1)} collective-permute-done((bf16[4,12,32,128]{3,2,1,0:T(8,128)(2,1)S(1)}, bf16[4,12,32,128]{3,2,1,0:T(8,128)(2,1)}, u32[]{:S(2)}, u32[]{:S(2)}) %collective-permute-start.6) | collective-permute-done | bytes 393248 | tf_op jit(solution)/shard_map/ppermute | solution.py:39
  84.0 0.5 collective-permute-start.17
  84.5 0.8 copy-done.28
  85.3 3.5 %shard_map.122 = (bf16[2,512,1024]{2,1,0:T(8,128)(2,1)}, f32[64,1024]{1,0:T(8,128)}) custom-call(bf16[2,512,1024]{2,1,0:T(8,128)(2,1)} %hidden.2), custom_call_target="tpu_custom_call" | custom-call | flops 30000000 | bytes 12000000 | tf_op jit(solution)/shard_map/pallas_call | solution.py:69
  88.7 4.0 %shard_map.123 = (bf16[2,512,1280]{2,1,0:T(8,128)(2,1)}, f32[64,1280]{1,0:T(8,128)}) custom-call(bf16[2,512,1280]{2,1,0:T(8,128)(2,1)} %hidden.3), custom_call_target="tpu_custom_call" | custom-call | flops 30000000 | bytes 12000000 | tf_op jit(solution)/shard_map/pallas_call | solution.py:69
  92.8 15.3 %attend.1 = (bf16[64,640]{1,0:T(8,128)(2,1)}, bf16[64,640]{1,0:T(8,128)(2,1)}, bf16[64,640]{1,0:T(8,128)(2,1)}, bf16[64,640]{1,0:T(8,128)(2,1)}, bf16[128,512]{1...) custom-call(s32[64]{0:T(128)} %frames_valid.3, s32[64]{0:T(128)} %slot_clip.1, ...), custom_call_target="tpu_custom_call" | custom-call | flops 8000000000 | bytes 12000000 | tf_op jit(solution)/shard_map/attend/pallas_call | solution.py:357
  108.1 2.6 %collective-permute-start.25 = (bf16[128,512]{1,0:T(8,128)(2,1)}, bf16[128,512]{1,0:T(8,128)(2,1)S(1)}, u32[]{:S(2)}, u32[]{:S(2)}) collective-permute-start(bf16[128,512]{1,0:T(8,128)(2,1)} %get-tuple-element.35.refs_0_), channel_id=1, source_target_pairs={{0,96},{32,0},{64,32},{96,64},{1,97},{33,1},{65,33},{97,65},{2,98}... | collective-permute-start | bytes 393224 | tf_op jit(solution)/shard_map/ppermute | solution.py:43
  110.7 1.7 collective-permute-start.27
  112.4 0.9 collective-permute-start.28
  113.4 2.4 %collective-permute-start.24 = (bf16[128,512]{1,0:T(8,128)(2,1)}, bf16[128,512]{1,0:T(8,128)(2,1)S(1)}, u32[]{:S(2)}, u32[]{:S(2)}) collective-permute-start(bf16[128,512]{1,0:T(8,128)(2,1)} %get-tuple-element.35.refs_0_), channel_id=1, source_target_pairs={{0,64},{32,96},{64,0},{96,32},{1,65},{33,97},{65,1},{97,33},{2,66}... | collective-permute-start | bytes 393224 | tf_op jit(solution)/shard_map/ppermute | solution.py:43
  115.7 0.8 collective-permute-done.26.refs_1_
  116.5 0.4 collective-permute-done.27.refs_2_
  116.9 0.5 collective-permute-done.28.refs_3_
  117.5 0.5 copy-done.20
  118.1 5.3 %slopes.1 = (bf16[64,640]{1,0:T(8,128)(2,1)}, bf16[64,640]{1,0:T(8,128)(2,1)}, bf16[64,640]{1,0:T(8,128)(2,1)}, bf16[64,640]{1,0:T(8,128)(2,1)}) custom-call(s32[64]{0:T(128)} %frames_valid.3, bf16[64,640]{1,0:T(8,128)(2,1)} %get-tuple-element.36.refs_0_, bf16[64,640]{1,0:T(8,128)(2,1)} %copy-done.18, bf16[64,640]{1,0:T(8,128)(2,1)} %copy-done.19, ...), custom_call_target="tpu_custom_call" | custom-call | tf_op jit(solution)/shard_map/slopes/pallas_call | solution.py:447
  123.4 1.4 collective-permute-start.29
  124.8 3.5 %collective-permute-start.30 = (bf16[64,640]{1,0:T(8,128)(2,1)}, bf16[64,640]{1,0:T(8,128)(2,1)S(1)}, u32[]{:S(2)}, u32[]{:S(2)}) collective-permute-start(bf16[64,640]{1,0:T(8,128)(2,1)} %get-tuple-element.46), channel_id=1, source_target_pairs={{0,64},{32,96},{64,0},{96,32},{1,65},{33,97},{65,1},{97,33},{2,66}... | collective-permute-start | bytes 245768 | tf_op jit(solution)/shard_map/ppermute | solution.py:43
  128.3 1.5 collective-permute-start.23
  129.9 2.9 %collective-permute-start.32 = (bf16[64,640]{1,0:T(8,128)(2,1)}, bf16[64,640]{1,0:T(8,128)(2,1)S(1)}, u32[]{:S(2)}, u32[]{:S(2)}) collective-permute-start(bf16[64,640]{1,0:T(8,128)(2,1)} %get-tuple-element.44.refs_4_), channel_id=1, source_target_pairs={{0,1},{1,0},{2,3},{3,2},{4,5},{5,4},{6,7},{7,6},{8,9},{9,8},{10,11... | collective-permute-start | bytes 245768 | tf_op jit(solution)/shard_map/ppermute | solution.py:39
  132.7 0.1 collective-permute-start.33
  132.9 2.2 %collective-permute-start.34 = (bf16[64,640]{1,0:T(8,128)(2,1)S(1)}, bf16[64,640]{1,0:T(8,128)(2,1)S(1)}, u32[]{:S(2)}, u32[]{:S(2)}) collective-permute-start(bf16[64,640]{1,0:T(8,128)(2,1)S(1)} %collective-permute-done.30.refs_6_), channel_id=1, source_target_pairs={{0,1},{1,0},{2,3},{3,2},{4,5},{5,4},{6,7},{7,6},{8,9},{9,8},{10,11... | collective-permute-start | bytes 245768 | tf_op jit(solution)/shard_map/ppermute | solution.py:39
  135.1 0.2 collective-permute-start.35
  135.3 0.7 collective-permute-done.34.refs_10_
  136.0 0.4 collective-permute-done.35.refs_11_
  136.4 0.2 copy-done.16
  136.6 0.6 copy-done.17
  137.3 2.6 %outer.1 = f32[16,16,640]{2,1,0:T(8,128)} custom-call(bf16[128,512]{1,0:T(8,128)(2,1)} %get-tuple-element.35.refs_0_, bf16[128,512]{1,0:T(8,128)(2,1)} %copy-done.7, bf16[128,512]{1,0:T(8,128)(2,1)} %copy-done.6, bf16[128,512]{1,0:T(8,128)(2,1)} %copy-done.5, bf16[64,640]{1,0:T(8,128)(2,1)} %get-tuple-element.44.refs_4_, bf16[64,640]{1,0:T(8,128)(2,1)} %copy-done.11, ...), custom_call_target="tpu_custom_call" | custom-call | tf_op jit(solution)/shard_map/outer/pallas_call | solution.py:480
  139.8 16.1 %all_to_all.10.x = f32[16,16,640]{2,1,0:T(8,128)} all-to-all(f32[16,16,640]{2,1,0:T(8,128)} %outer.1), channel_id=1, replica_groups={{0,2,4,6,8,10,12,14,16,18,20,22,24,26,28,30},{1,3,5,7,9,11,13,15,17,19,..., dimensions={0} | all-to-all | bytes 1310720 | tf_op jit(solution)/shard_map/all_to_all | solution.py:574
  155.9 2.3 %reduce_parts.1 = bf16[64,16,640]{2,1,0:T(8,128)(2,1)} custom-call(f32[16,16,640]{2,1,0:T(8,128)} %all_to_all.10.x), custom_call_target="tpu_custom_call" | custom-call | tf_op jit(solution)/shard_map/reduce_parts/pallas_call | solution.py:496
  158.2 25.1 %all_to_all.11 = bf16[64,16,640]{2,1,0:T(8,128)(2,1)S(1)} all-to-all(bf16[64,16,640]{2,1,0:T(8,128)(2,1)} %reduce_parts.1), channel_id=1, replica_groups={{0,2,4,6,8,10,12,14,16,18,20,22,24,26,28,30,32,34,36,38,40,42,44,46,48,..., dimensions={0} | all-to-all | bytes 2621440 | tf_op jit(solution)/shard_map/all_to_all | solution.py:577
  183.3 3.5 %collective-permute-start.36 = (bf16[4,16,16,640]{3,2,1,0:T(8,128)(2,1)S(1)}, bf16[4,16,16,640]{3,2,1,0:T(8,128)(2,1)S(1)}, u32[]{:S(2)}, u32[]{:S(2)}) collective-permute-start(bf16[4,16,16,640]{3,2,1,0:T(8,128)(2,1)S(1)} %bitcast.13), channel_id=1, source_target_pairs={{0,1},{1,0},{2,3},{3,2},{4,5},{5,4},{6,7},{7,6},{8,9},{9,8},{10,11... | collective-permute-start | bytes 3932168 | tf_op jit(solution)/shard_map/ppermute | solution.py:39
  186.8 2.8 %place_own.1 = (f32[2,256,1024]{2,1,0:T(8,128)}, f32[2,256,1280]{2,1,0:T(8,128)}) custom-call(bf16[4,16,16,640]{3,2,1,0:T(8,128)(2,1)} %bitcast.14), custom_call_target="tpu_custom_call" | custom-call | tf_op jit(solution)/shard_map/place_own/pallas_call | solution.py:519
  189.6 1.1 copy-done.1
  190.7 2.8 %place_partner.1 = (f32[2,256,1024]{2,1,0:T(8,128)}, f32[2,256,1280]{2,1,0:T(8,128)}) custom-call(bf16[4,16,16,640]{3,2,1,0:T(8,128)(2,1)} %copy-done.1, f32[2,256,1024]{2,1,0:T(8,128)} %get-tuple-element.48.refs_0_, f32[2,256,1280]{2,1,0:T(8,128)} %get-tuple-element.49.refs_1_), custom_call_target="tpu_custom_call", output_to_operand_aliasing={{0}: (1, {}), {1}: (2, {})} | custom-call | tf_op jit(solution)/shard_map/place_partner/pallas_call | solution.py:519
  (82 shorter events, 0.5 us)
Async XLA Ops:
  2.6 8.0 %collective-permute-start = (bf16[16,32,128]{2,1,0:T(8,128)(2,1)}, bf16[16,32,128]{2,1,0:T(8,128)(2,1)S(1)}, u32[]{:S(2)}, u32[]{:S(2)}) collective-permute-start(bf16[16,32,128]{2,1,0:T(8,128)(2,1)} %get-tuple-element.28), channel_id=1, source_target_pairs={{0,8},{1,9},{2,10},{3,11},{4,12},{5,13},{6,14},{7,15},{8,16},{9,17... | collective-permute-start | bytes 393224 | tf_op jit(solution)/shard_map/ppermute | solution.py:39
  5.0 9.2 %collective-permute-start.1 = (bf16[16,32,128]{2,1,0:T(8,128)(2,1)}, bf16[16,32,128]{2,1,0:T(8,128)(2,1)S(1)}, u32[]{:S(2)}, u32[]{:S(2)}) collective-permute-start(bf16[16,32,128]{2,1,0:T(8,128)(2,1)} %get-tuple-element.29), channel_id=1, source_target_pairs={{0,16},{1,17},{2,18},{3,19},{4,20},{5,21},{6,22},{7,23},{8,24},{9,... | collective-permute-start | bytes 393224 | tf_op jit(solution)/shard_map/ppermute | solution.py:39
  8.3 5.9 %collective-permute-start.2 = (bf16[16,32,128]{2,1,0:T(8,128)(2,1)}, bf16[16,32,128]{2,1,0:T(8,128)(2,1)S(1)}, u32[]{:S(2)}, u32[]{:S(2)}) collective-permute-start(bf16[16,32,128]{2,1,0:T(8,128)(2,1)} %get-tuple-element.30), channel_id=1, source_target_pairs={{0,24},{1,25},{2,26},{3,27},{4,28},{5,29},{6,30},{7,31},{8,0},{9,1... | collective-permute-start | bytes 393224 | tf_op jit(solution)/shard_map/ppermute | solution.py:39
  10.6 3.7 %copy-start.8 = (bf16[16,32,128]{2,1,0:T(8,128)(2,1)}, bf16[16,32,128]{2,1,0:T(8,128)(2,1)S(1)}, u32[]{:S(2)}) copy-start(bf16[16,32,128]{2,1,0:T(8,128)(2,1)S(1)} %collective-permute-done.refs_1_) | copy-start | bytes 393220
  14.3 0.7 copy-start.9
  14.3 0.7 copy-start.10
  16.9 6.0 %collective-permute-start.11 = (bf16[12,32,128]{2,1,0:T(8,128)(2,1)}, bf16[12,32,128]{2,1,0:T(8,128)(2,1)S(1)}, u32[]{:S(2)}, u32[]{:S(2)}) collective-permute-start(bf16[12,32,128]{2,1,0:T(8,128)(2,1)} %get-tuple-element.32), channel_id=1, source_target_pairs={{0,6},{1,7},{2,0},{3,1},{4,2},{5,3},{6,4},{7,5},{8,14},{9,15},{10,... | collective-permute-start | bytes 294920 | tf_op jit(solution)/shard_map/ppermute | solution.py:39
  19.6 5.3 %collective-permute-start.10 = (bf16[12,32,128]{2,1,0:T(8,128)(2,1)}, bf16[12,32,128]{2,1,0:T(8,128)(2,1)S(1)}, u32[]{:S(2)}, u32[]{:S(2)}) collective-permute-start(bf16[12,32,128]{2,1,0:T(8,128)(2,1)} %get-tuple-element.32), channel_id=1, source_target_pairs={{0,4},{1,5},{2,6},{3,7},{4,0},{5,1},{6,2},{7,3},{8,12},{9,13},{10,... | collective-permute-start | bytes 294920 | tf_op jit(solution)/shard_map/ppermute | solution.py:39
  20.0 5.9 %collective-permute-start.9 = (bf16[12,32,128]{2,1,0:T(8,128)(2,1)}, bf16[12,32,128]{2,1,0:T(8,128)(2,1)S(1)}, u32[]{:S(2)}, u32[]{:S(2)}) collective-permute-start(bf16[12,32,128]{2,1,0:T(8,128)(2,1)} %get-tuple-element.32), channel_id=1, source_target_pairs={{0,2},{1,3},{2,4},{3,5},{4,6},{5,7},{6,0},{7,1},{8,10},{9,11},{10,... | collective-permute-start | bytes 294920 | tf_op jit(solution)/shard_map/ppermute | solution.py:39
  20.6 12.2 %collective-permute-start.5 = (bf16[12,32,128]{2,1,0:T(8,128)(2,1)}, bf16[12,32,128]{2,1,0:T(8,128)(2,1)S(1)}, u32[]{:S(2)}, u32[]{:S(2)}) collective-permute-start(bf16[12,32,128]{2,1,0:T(8,128)(2,1)} %get-tuple-element.31), channel_id=1, source_target_pairs={{0,24},{1,25},{2,26},{3,27},{4,28},{5,29},{6,30},{7,31},{8,0},{9,1... | collective-permute-start | bytes 294920 | tf_op jit(solution)/shard_map/ppermute | solution.py:39
  26.8 65.9 %copy-start.2 = (bf16[4,12,32,128]{3,2,1,0:T(8,128)(2,1)}, bf16[4,12,32,128]{3,2,1,0:T(8,128)(2,1)S(1)}, u32[]{:S(2)}) copy-start(bf16[4,12,32,128]{3,2,1,0:T(8,128)(2,1)S(1)} %pad_maximum_fusion.1.refs_4_) | copy-start | bytes 1179652
  26.8 35.8 %collective-permute-start.19 = (bf16[4,12,32,128]{3,2,1,0:T(8,128)(2,1)S(1)}, bf16[4,12,32,128]{3,2,1,0:T(8,128)(2,1)S(1)}, u32[]{:S(2)}, u32[]{:S(2)}) collective-permute-start(bf16[4,12,32,128]{3,2,1,0:T(8,128)(2,1)S(1)} %pad_maximum_fusion.1.refs_4_), channel_id=1, source_target_pairs={{0,1},{1,0},{2,3},{3,2},{4,5},{5,4},{6,7},{7,6},{8,9},{9,8},{10,11... | collective-permute-start | bytes 1179656 | tf_op jit(solution)/shard_map/ppermute | solution.py:39
  29.8 33.1 %collective-permute-start.14 = (bf16[4,12,32,128]{3,2,1,0:T(8,128)(2,1)S(1)}, bf16[4,12,32,128]{3,2,1,0:T(8,128)(2,1)S(1)}, u32[]{:S(2)}, u32[]{:S(2)}) collective-permute-start(bf16[4,12,32,128]{3,2,1,0:T(8,128)(2,1)S(1)} %pad_maximum_fusion.1.refs_4_), channel_id=1, source_target_pairs={{0,24},{1,25},{2,26},{3,27},{4,28},{5,29},{6,30},{7,31},{8,0},{9,1... | collective-permute-start | bytes 1179656 | tf_op jit(solution)/shard_map/ppermute | solution.py:39
  31.9 31.3 %collective-permute-start.13 = (bf16[4,12,32,128]{3,2,1,0:T(8,128)(2,1)S(1)}, bf16[4,12,32,128]{3,2,1,0:T(8,128)(2,1)S(1)}, u32[]{:S(2)}, u32[]{:S(2)}) collective-permute-start(bf16[4,12,32,128]{3,2,1,0:T(8,128)(2,1)S(1)} %pad_maximum_fusion.1.refs_4_), channel_id=1, source_target_pairs={{0,16},{1,17},{2,18},{3,19},{4,20},{5,21},{6,22},{7,23},{8,24},{9,... | collective-permute-start | bytes 1179656 | tf_op jit(solution)/shard_map/ppermute | solution.py:39
  32.9 31.3 %collective-permute-start.12 = (bf16[4,12,32,128]{3,2,1,0:T(8,128)(2,1)S(1)}, bf16[4,12,32,128]{3,2,1,0:T(8,128)(2,1)S(1)}, u32[]{:S(2)}, u32[]{:S(2)}) collective-permute-start(bf16[4,12,32,128]{3,2,1,0:T(8,128)(2,1)S(1)} %pad_maximum_fusion.1.refs_4_), channel_id=1, source_target_pairs={{0,8},{1,9},{2,10},{3,11},{4,12},{5,13},{6,14},{7,15},{8,16},{9,17... | collective-permute-start | bytes 1179656 | tf_op jit(solution)/shard_map/ppermute | solution.py:39
  32.9 21.4 %collective-permute-start.4 = (bf16[12,32,128]{2,1,0:T(8,128)(2,1)}, bf16[12,32,128]{2,1,0:T(8,128)(2,1)S(1)}, u32[]{:S(2)}, u32[]{:S(2)}) collective-permute-start(bf16[12,32,128]{2,1,0:T(8,128)(2,1)} %get-tuple-element.31), channel_id=1, source_target_pairs={{0,16},{1,17},{2,18},{3,19},{4,20},{5,21},{6,22},{7,23},{8,24},{9,... | collective-permute-start | bytes 294920 | tf_op jit(solution)/shard_map/ppermute | solution.py:39
  54.3 4.9 %collective-permute-start.3 = (bf16[12,32,128]{2,1,0:T(8,128)(2,1)}, bf16[12,32,128]{2,1,0:T(8,128)(2,1)S(1)}, u32[]{:S(2)}, u32[]{:S(2)}) collective-permute-start(bf16[12,32,128]{2,1,0:T(8,128)(2,1)} %get-tuple-element.31), channel_id=1, source_target_pairs={{0,8},{1,9},{2,10},{3,11},{4,12},{5,13},{6,14},{7,15},{8,16},{9,17... | collective-permute-start | bytes 294920 | tf_op jit(solution)/shard_map/ppermute | solution.py:39
  60.2 32.5 %copy-start.3 = (bf16[4,12,32,128]{3,2,1,0:T(8,128)(2,1)}, bf16[4,12,32,128]{3,2,1,0:T(8,128)(2,1)S(1)}, u32[]{:S(2)}) copy-start(bf16[4,12,32,128]{3,2,1,0:T(8,128)(2,1)S(1)} %pad_maximum_fusion.refs_0_) | copy-start | bytes 1179652
  60.2 4.7 %collective-permute-start.15 = (bf16[4,12,32,128]{3,2,1,0:T(8,128)(2,1)S(1)}, bf16[4,12,32,128]{3,2,1,0:T(8,128)(2,1)S(1)}, u32[]{:S(2)}, u32[]{:S(2)}) collective-permute-start(bf16[4,12,32,128]{3,2,1,0:T(8,128)(2,1)S(1)} %pad_maximum_fusion.refs_0_), channel_id=1, source_target_pairs={{0,1},{1,0},{2,3},{3,2},{4,5},{5,4},{6,7},{7,6},{8,9},{9,8},{10,11... | collective-permute-start | bytes 1179656 | tf_op jit(solution)/shard_map/ppermute | solution.py:39
  62.6 30.1 %copy-start.21 = (bf16[4,12,32,128]{3,2,1,0:T(8,128)(2,1)}, bf16[4,12,32,128]{3,2,1,0:T(8,128)(2,1)S(1)}, u32[]{:S(2)}) copy-start(bf16[4,12,32,128]{3,2,1,0:T(8,128)(2,1)S(1)} %collective-permute-done.19.refs_12_) | copy-start | bytes 1179652
  62.6 10.7 %collective-permute-start.8 = (bf16[4,12,32,128]{3,2,1,0:T(8,128)(2,1)S(1)}, bf16[4,12,32,128]{3,2,1,0:T(8,128)(2,1)S(1)}, u32[]{:S(2)}, u32[]{:S(2)}) collective-permute-start(bf16[4,12,32,128]{3,2,1,0:T(8,128)(2,1)S(1)} %pad_maximum_fusion.refs_0_), channel_id=1, source_target_pairs={{0,6},{1,7},{2,0},{3,1},{4,2},{5,3},{6,4},{7,5},{8,14},{9,15},{10,... | collective-permute-start | bytes 1179656 | tf_op jit(solution)/shard_map/ppermute | solution.py:39
  62.9 29.8 %copy-start.22 = (bf16[4,12,32,128]{3,2,1,0:T(8,128)(2,1)}, bf16[4,12,32,128]{3,2,1,0:T(8,128)(2,1)S(1)}, u32[]{:S(2)}) copy-start(bf16[4,12,32,128]{3,2,1,0:T(8,128)(2,1)S(1)} %collective-permute-done.14.refs_7_) | copy-start | bytes 1179652
  62.9 11.8 %collective-permute-start.7 = (bf16[4,12,32,128]{3,2,1,0:T(8,128)(2,1)S(1)}, bf16[4,12,32,128]{3,2,1,0:T(8,128)(2,1)S(1)}, u32[]{:S(2)}, u32[]{:S(2)}) collective-permute-start(bf16[4,12,32,128]{3,2,1,0:T(8,128)(2,1)S(1)} %pad_maximum_fusion.refs_0_), channel_id=1, source_target_pairs={{0,4},{1,5},{2,6},{3,7},{4,0},{5,1},{6,2},{7,3},{8,12},{9,13},{10,... | collective-permute-start | bytes 1179656 | tf_op jit(solution)/shard_map/ppermute | solution.py:39
  63.3 29.5 %copy-start.23 = (bf16[4,12,32,128]{3,2,1,0:T(8,128)(2,1)}, bf16[4,12,32,128]{3,2,1,0:T(8,128)(2,1)S(1)}, u32[]{:S(2)}) copy-start(bf16[4,12,32,128]{3,2,1,0:T(8,128)(2,1)S(1)} %collective-permute-done.13.refs_6_) | copy-start | bytes 1179652
  63.3 20.7 %collective-permute-start.6 = (bf16[4,12,32,128]{3,2,1,0:T(8,128)(2,1)S(1)}, bf16[4,12,32,128]{3,2,1,0:T(8,128)(2,1)}, u32[]{:S(2)}, u32[]{:S(2)}) collective-permute-start(bf16[4,12,32,128]{3,2,1,0:T(8,128)(2,1)S(1)} %pad_maximum_fusion.refs_0_), channel_id=1, source_target_pairs={{0,2},{1,3},{2,4},{3,5},{4,6},{5,7},{6,0},{7,1},{8,10},{9,11},{10,... | collective-permute-start | bytes 1179656 | tf_op jit(solution)/shard_map/ppermute | solution.py:39
  64.2 28.5 %copy-start.24 = (bf16[4,12,32,128]{3,2,1,0:T(8,128)(2,1)}, bf16[4,12,32,128]{3,2,1,0:T(8,128)(2,1)S(1)}, u32[]{:S(2)}) copy-start(bf16[4,12,32,128]{3,2,1,0:T(8,128)(2,1)S(1)} %collective-permute-done.12.refs_5_) | copy-start | bytes 1179652
  64.2 20.3 %collective-permute-start.22 = (bf16[4,12,32,128]{3,2,1,0:T(8,128)(2,1)S(1)}, bf16[4,12,32,128]{3,2,1,0:T(8,128)(2,1)S(1)}, u32[]{:S(2)}, u32[]{:S(2)}) collective-permute-start(bf16[4,12,32,128]{3,2,1,0:T(8,128)(2,1)S(1)} %collective-permute-done.14.refs_7_), channel_id=1, source_target_pairs={{0,1},{1,0},{2,3},{3,2},{4,5},{5,4},{6,7},{7,6},{8,9},{9,8},{10,11... | collective-permute-start | bytes 1179656 | tf_op jit(solution)/shard_map/ppermute | solution.py:39
  64.8 27.9 %copy-start.25 = (bf16[4,12,32,128]{3,2,1,0:T(8,128)(2,1)}, bf16[4,12,32,128]{3,2,1,0:T(8,128)(2,1)S(1)}, u32[]{:S(2)}) copy-start(bf16[4,12,32,128]{3,2,1,0:T(8,128)(2,1)S(1)} %collective-permute-done.15.refs_8_) | copy-start | bytes 1179652
  64.9 27.9 %collective-permute-start.21 = (bf16[4,12,32,128]{3,2,1,0:T(8,128)(2,1)S(1)}, bf16[4,12,32,128]{3,2,1,0:T(8,128)(2,1)}, u32[]{:S(2)}, u32[]{:S(2)}) collective-permute-start(bf16[4,12,32,128]{3,2,1,0:T(8,128)(2,1)S(1)} %collective-permute-done.13.refs_6_), channel_id=1, source_target_pairs={{0,1},{1,0},{2,3},{3,2},{4,5},{5,4},{6,7},{7,6},{8,9},{9,8},{10,11... | collective-permute-start | bytes 1179656 | tf_op jit(solution)/shard_map/ppermute | solution.py:39
  73.3 19.4 %copy-start.26 = (bf16[4,12,32,128]{3,2,1,0:T(8,128)(2,1)}, bf16[4,12,32,128]{3,2,1,0:T(8,128)(2,1)S(1)}, u32[]{:S(2)}) copy-start(bf16[4,12,32,128]{3,2,1,0:T(8,128)(2,1)S(1)} %collective-permute-done.8.refs_3_) | copy-start | bytes 1179652
  73.3 19.5 %collective-permute-start.20 = (bf16[4,12,32,128]{3,2,1,0:T(8,128)(2,1)S(1)}, bf16[4,12,32,128]{3,2,1,0:T(8,128)(2,1)}, u32[]{:S(2)}, u32[]{:S(2)}) collective-permute-start(bf16[4,12,32,128]{3,2,1,0:T(8,128)(2,1)S(1)} %collective-permute-done.12.refs_5_), channel_id=1, source_target_pairs={{0,1},{1,0},{2,3},{3,2},{4,5},{5,4},{6,7},{7,6},{8,9},{9,8},{10,11... | collective-permute-start | bytes 1179656 | tf_op jit(solution)/shard_map/ppermute | solution.py:39
  74.7 18.0 %copy-start.27 = (bf16[4,12,32,128]{3,2,1,0:T(8,128)(2,1)}, bf16[4,12,32,128]{3,2,1,0:T(8,128)(2,1)S(1)}, u32[]{:S(2)}) copy-start(bf16[4,12,32,128]{3,2,1,0:T(8,128)(2,1)S(1)} %collective-permute-done.7.refs_2_) | copy-start | bytes 1179652
  74.8 18.0 %collective-permute-start.18 = (bf16[4,12,32,128]{3,2,1,0:T(8,128)(2,1)S(1)}, bf16[4,12,32,128]{3,2,1,0:T(8,128)(2,1)}, u32[]{:S(2)}, u32[]{:S(2)}) collective-permute-start(bf16[4,12,32,128]{3,2,1,0:T(8,128)(2,1)S(1)} %collective-permute-done.8.refs_3_), channel_id=1, source_target_pairs={{0,1},{1,0},{2,3},{3,2},{4,5},{5,4},{6,7},{7,6},{8,9},{9,8},{10,11... | collective-permute-start | bytes 1179656 | tf_op jit(solution)/shard_map/ppermute | solution.py:39
  84.0 8.8 %collective-permute-start.17 = (bf16[4,12,32,128]{3,2,1,0:T(8,128)(2,1)S(1)}, bf16[4,12,32,128]{3,2,1,0:T(8,128)(2,1)}, u32[]{:S(2)}, u32[]{:S(2)}) collective-permute-start(bf16[4,12,32,128]{3,2,1,0:T(8,128)(2,1)S(1)} %collective-permute-done.7.refs_2_), channel_id=1, source_target_pairs={{0,1},{1,0},{2,3},{3,2},{4,5},{5,4},{6,7},{7,6},{8,9},{9,8},{10,11... | collective-permute-start | bytes 1179656 | tf_op jit(solution)/shard_map/ppermute | solution.py:39
  84.5 0.8 copy-start.28
  85.2 7.6 %collective-permute-start.16 = (bf16[4,12,32,128]{3,2,1,0:T(8,128)(2,1)}, bf16[4,12,32,128]{3,2,1,0:T(8,128)(2,1)}, u32[]{:S(2)}, u32[]{:S(2)}) collective-permute-start(bf16[4,12,32,128]{3,2,1,0:T(8,128)(2,1)} %collective-permute-done.6.refs_1_), channel_id=1, source_target_pairs={{0,1},{1,0},{2,3},{3,2},{4,5},{5,4},{6,7},{7,6},{8,9},{9,8},{10,11... | collective-permute-start | bytes 1179656 | tf_op jit(solution)/shard_map/ppermute | solution.py:39
  108.1 20.2 %collective-permute-start.25 = (bf16[128,512]{1,0:T(8,128)(2,1)}, bf16[128,512]{1,0:T(8,128)(2,1)S(1)}, u32[]{:S(2)}, u32[]{:S(2)}) collective-permute-start(bf16[128,512]{1,0:T(8,128)(2,1)} %get-tuple-element.35.refs_0_), channel_id=1, source_target_pairs={{0,96},{32,0},{64,32},{96,64},{1,97},{33,1},{65,33},{97,65},{2,98}... | collective-permute-start | bytes 393224 | tf_op jit(solution)/shard_map/ppermute | solution.py:43
  110.7 5.8 %collective-permute-start.26 = (bf16[64,640]{1,0:T(8,128)(2,1)}, bf16[64,640]{1,0:T(8,128)(2,1)S(1)}, u32[]{:S(2)}, u32[]{:S(2)}) collective-permute-start(bf16[64,640]{1,0:T(8,128)(2,1)} %get-tuple-element.37), channel_id=1, source_target_pairs={{0,32},{32,64},{64,96},{96,0},{1,33},{33,65},{65,97},{97,1},{2,34}... | collective-permute-start | bytes 245768 | tf_op jit(solution)/shard_map/ppermute | solution.py:43
  110.7 6.2 %collective-permute-start.27 = (bf16[64,640]{1,0:T(8,128)(2,1)}, bf16[64,640]{1,0:T(8,128)(2,1)S(1)}, u32[]{:S(2)}, u32[]{:S(2)}) collective-permute-start(bf16[64,640]{1,0:T(8,128)(2,1)} %get-tuple-element.38), channel_id=1, source_target_pairs={{0,64},{32,96},{64,0},{96,32},{1,65},{33,97},{65,1},{97,33},{2,66}... | collective-permute-start | bytes 245768 | tf_op jit(solution)/shard_map/ppermute | solution.py:43
  112.4 5.0 %collective-permute-start.28 = (bf16[64,640]{1,0:T(8,128)(2,1)}, bf16[64,640]{1,0:T(8,128)(2,1)S(1)}, u32[]{:S(2)}, u32[]{:S(2)}) collective-permute-start(bf16[64,640]{1,0:T(8,128)(2,1)} %get-tuple-element.39), channel_id=1, source_target_pairs={{0,96},{32,0},{64,32},{96,64},{1,97},{33,1},{65,33},{97,65},{2,98}... | collective-permute-start | bytes 245768 | tf_op jit(solution)/shard_map/ppermute | solution.py:43
  113.4 16.5 %collective-permute-start.24 = (bf16[128,512]{1,0:T(8,128)(2,1)}, bf16[128,512]{1,0:T(8,128)(2,1)S(1)}, u32[]{:S(2)}, u32[]{:S(2)}) collective-permute-start(bf16[128,512]{1,0:T(8,128)(2,1)} %get-tuple-element.35.refs_0_), channel_id=1, source_target_pairs={{0,64},{32,96},{64,0},{96,32},{1,65},{33,97},{65,1},{97,33},{2,66}... | collective-permute-start | bytes 393224 | tf_op jit(solution)/shard_map/ppermute | solution.py:43
  116.5 0.9 copy-start.18
  116.9 0.6 copy-start.19
  117.4 0.6 copy-start.20
  118.1 10.3 %copy-start.4 = (bf16[128,512]{1,0:T(8,128)(2,1)S(1)}, bf16[128,512]{1,0:T(8,128)(2,1)}, u32[]{:S(2)}) copy-start(bf16[128,512]{1,0:T(8,128)(2,1)} %get-tuple-element.35.refs_0_) | copy-start | bytes 393220
  123.4 9.4 %collective-permute-start.29 = (bf16[64,640]{1,0:T(8,128)(2,1)}, bf16[64,640]{1,0:T(8,128)(2,1)S(1)}, u32[]{:S(2)}, u32[]{:S(2)}) collective-permute-start(bf16[64,640]{1,0:T(8,128)(2,1)} %get-tuple-element.45), channel_id=1, source_target_pairs={{0,32},{32,64},{64,96},{96,0},{1,33},{33,65},{65,97},{97,1},{2,34}... | collective-permute-start | bytes 245768 | tf_op jit(solution)/shard_map/ppermute | solution.py:43
  124.8 8.1 %collective-permute-start.30 = (bf16[64,640]{1,0:T(8,128)(2,1)}, bf16[64,640]{1,0:T(8,128)(2,1)S(1)}, u32[]{:S(2)}, u32[]{:S(2)}) collective-permute-start(bf16[64,640]{1,0:T(8,128)(2,1)} %get-tuple-element.46), channel_id=1, source_target_pairs={{0,64},{32,96},{64,0},{96,32},{1,65},{33,97},{65,1},{97,33},{2,66}... | collective-permute-start | bytes 245768 | tf_op jit(solution)/shard_map/ppermute | solution.py:43
  128.3 6.8 %collective-permute-start.31 = (bf16[64,640]{1,0:T(8,128)(2,1)}, bf16[64,640]{1,0:T(8,128)(2,1)S(1)}, u32[]{:S(2)}, u32[]{:S(2)}) collective-permute-start(bf16[64,640]{1,0:T(8,128)(2,1)} %get-tuple-element.47), channel_id=1, source_target_pairs={{0,96},{32,0},{64,32},{96,64},{1,97},{33,1},{65,33},{97,65},{2,98}... | collective-permute-start | bytes 245768 | tf_op jit(solution)/shard_map/ppermute | solution.py:43
  128.3 8.0 %copy-start.5 = (bf16[128,512]{1,0:T(8,128)(2,1)}, bf16[128,512]{1,0:T(8,128)(2,1)S(1)}, u32[]{:S(2)}) copy-start(bf16[128,512]{1,0:T(8,128)(2,1)S(1)} %collective-permute-done.25.refs_3_) | copy-start | bytes 393220
  128.3 7.0 %collective-permute-start.23 = (bf16[128,512]{1,0:T(8,128)(2,1)S(1)}, bf16[128,512]{1,0:T(8,128)(2,1)S(1)}, u32[]{:S(2)}, u32[]{:S(2)}) collective-permute-start(bf16[128,512]{1,0:T(8,128)(2,1)S(1)} %copy-done.4), channel_id=1, source_target_pairs={{0,32},{32,64},{64,96},{96,0},{1,33},{33,65},{65,97},{97,1},{2,34}... | collective-permute-start | bytes 393224 | tf_op jit(solution)/shard_map/ppermute | solution.py:43
  129.9 6.5 %copy-start.6 = (bf16[128,512]{1,0:T(8,128)(2,1)}, bf16[128,512]{1,0:T(8,128)(2,1)S(1)}, u32[]{:S(2)}) copy-start(bf16[128,512]{1,0:T(8,128)(2,1)S(1)} %collective-permute-done.24.refs_2_) | copy-start | bytes 393220
  129.9 5.4 %collective-permute-start.32 = (bf16[64,640]{1,0:T(8,128)(2,1)}, bf16[64,640]{1,0:T(8,128)(2,1)S(1)}, u32[]{:S(2)}, u32[]{:S(2)}) collective-permute-start(bf16[64,640]{1,0:T(8,128)(2,1)} %get-tuple-element.44.refs_4_), channel_id=1, source_target_pairs={{0,1},{1,0},{2,3},{3,2},{4,5},{5,4},{6,7},{7,6},{8,9},{9,8},{10,11... | collective-permute-start | bytes 245768 | tf_op jit(solution)/shard_map/ppermute | solution.py:39
  132.7 3.6 %copy-start.11 = (bf16[64,640]{1,0:T(8,128)(2,1)}, bf16[64,640]{1,0:T(8,128)(2,1)S(1)}, u32[]{:S(2)}) copy-start(bf16[64,640]{1,0:T(8,128)(2,1)S(1)} %collective-permute-done.29.refs_5_) | copy-start | bytes 245764
  132.7 2.6 %collective-permute-start.33 = (bf16[64,640]{1,0:T(8,128)(2,1)S(1)}, bf16[64,640]{1,0:T(8,128)(2,1)S(1)}, u32[]{:S(2)}, u32[]{:S(2)}) collective-permute-start(bf16[64,640]{1,0:T(8,128)(2,1)S(1)} %collective-permute-done.29.refs_5_), channel_id=1, source_target_pairs={{0,1},{1,0},{2,3},{3,2},{4,5},{5,4},{6,7},{7,6},{8,9},{9,8},{10,11... | collective-permute-start | bytes 245768 | tf_op jit(solution)/shard_map/ppermute | solution.py:39
  132.9 3.5 %copy-start.12 = (bf16[64,640]{1,0:T(8,128)(2,1)}, bf16[64,640]{1,0:T(8,128)(2,1)S(1)}, u32[]{:S(2)}) copy-start(bf16[64,640]{1,0:T(8,128)(2,1)S(1)} %collective-permute-done.30.refs_6_) | copy-start | bytes 245764
  132.9 3.1 %collective-permute-start.34 = (bf16[64,640]{1,0:T(8,128)(2,1)S(1)}, bf16[64,640]{1,0:T(8,128)(2,1)S(1)}, u32[]{:S(2)}, u32[]{:S(2)}) collective-permute-start(bf16[64,640]{1,0:T(8,128)(2,1)S(1)} %collective-permute-done.30.refs_6_), channel_id=1, source_target_pairs={{0,1},{1,0},{2,3},{3,2},{4,5},{5,4},{6,7},{7,6},{8,9},{9,8},{10,11... | collective-permute-start | bytes 245768 | tf_op jit(solution)/shard_map/ppermute | solution.py:39
  135.1 1.3 copy-start.13
  135.1 1.3 collective-permute-start.35
  135.3 1.1 copy-start.7
  135.3 1.1 copy-start.14
  135.3 1.1 copy-start.15
  183.3 3.5 %copy-start = (bf16[64,16,640]{2,1,0:T(8,128)(2,1)}, bf16[64,16,640]{2,1,0:T(8,128)(2,1)S(1)}, u32[]{:S(2)}) copy-start(bf16[64,16,640]{2,1,0:T(8,128)(2,1)S(1)} %all_to_all.11) | copy-start | bytes 3932164
  183.3 6.3 %collective-permute-start.36 = (bf16[4,16,16,640]{3,2,1,0:T(8,128)(2,1)S(1)}, bf16[4,16,16,640]{3,2,1,0:T(8,128)(2,1)S(1)}, u32[]{:S(2)}, u32[]{:S(2)}) collective-permute-start(bf16[4,16,16,640]{3,2,1,0:T(8,128)(2,1)S(1)} %bitcast.13), channel_id=1, source_target_pairs={{0,1},{1,0},{2,3},{3,2},{4,5},{5,4},{6,7},{7,6},{8,9},{9,8},{10,11... | collective-permute-start | bytes 3932168 | tf_op jit(solution)/shard_map/ppermute | solution.py:39
  189.6 1.1 copy-start.1
  (2 other events, 1.3 us)

commit v5 on v4

--- a/solution.py
+++ b/solution.py
@@ -41,6 +41,10 @@
 
 def role_send(x, k):
     return lax.ppermute(x, "role", [(i, (i + k) % ROLES) for i in range(ROLES)])
+
+
+def near(*arrays):
+    return [pltpu.with_memory_space_constraint(x, pltpu.VMEM) for x in arrays]
 
 
 def place_of(column):
@@ -103,7 +107,7 @@
     vmem = pl.BlockSpec(memory_space=pltpu.VMEM)
     return pl.pallas_call(
         chunk_kernel,
-        out_shape=[jax.ShapeDtypeStruct((16, 32, 128), bf16)] * 4,
+        out_shape=[pltpu.VMEM((16, 32, 128), bf16)] * 4,
         in_specs=[vmem, vmem],
         out_specs=[vmem] * 4,
         scratch_shapes=[pltpu.VMEM((4, 16, 32, 128), bf16)],
@@ -138,17 +142,16 @@
 
 
 def shares(parts, latent):
-    whole = pl.BlockSpec((16, 32, 128), lambda i: (0, 0, 0))
     half = pl.BlockSpec((12, 32, 128), lambda i: (0, 0, 0))
     return pl.pallas_call(
         share_kernel,
         grid=(1,),
         out_shape=[jax.ShapeDtypeStruct((12, 32, 128), bf16)] * 2,
-        in_specs=[whole] * 4
+        in_specs=[pl.BlockSpec(memory_space=pltpu.VMEM)] * 4
         + [pl.BlockSpec((2, 1, 32, STU_D), lambda i: (0, 0, lax.axis_index("role"), 0))],
         out_specs=[half] * 2,
         name="shares",
-    )(*parts, latent)
+    )(*near(*parts), latent)
 
 
 def spread_line(first, second):
@@ -356,11 +359,11 @@
     vmem = pl.BlockSpec(memory_space=pltpu.VMEM)
     return pl.pallas_call(
         attend_kernel,
-        out_shape=[jax.ShapeDtypeStruct((ROWS, OUT_COLS), bf16)] * ROLES
+        out_shape=[pltpu.VMEM((ROWS, OUT_COLS), bf16)] * ROLES
         + [
-            jax.ShapeDtypeStruct((2 * ROWS, STU_D), bf16),
-            jax.ShapeDtypeStruct((ROWS, WAVLM_D), f32),
-            jax.ShapeDtypeStruct((ROWS, WHISPER_D), f32),
+            pltpu.VMEM((2 * ROWS, STU_D), bf16),
+            pltpu.VMEM((ROWS, WAVLM_D), f32),
+            pltpu.VMEM((ROWS, WHISPER_D), f32),
         ],
         in_specs=[pl.BlockSpec(memory_space=pltpu.SMEM)] * 2
         + [pl.BlockSpec(memory_space=pl.ANY)] * 20,
@@ -446,7 +449,7 @@
     vmem = pl.BlockSpec(memory_space=pltpu.VMEM)
     return pl.pallas_call(
         slope_kernel,
-        out_shape=[jax.ShapeDtypeStruct((ROWS, OUT_COLS), bf16)] * ROLES,
+        out_shape=[pltpu.VMEM((ROWS, OUT_COLS), bf16)] * ROLES,
         in_specs=[pl.BlockSpec(memory_space=pltpu.SMEM)]
         + [vmem] * 4
         + [pl.BlockSpec(memory_space=pl.ANY)] * 2
@@ -459,7 +462,7 @@
             pltpu.SemaphoreType.DMA((9,)),
         ],
         name="slopes",
-    )(frames_valid, *parts, out_a, out_w, mean_a, mean_w, pred_a, pred_w)
+    )(frames_valid, *near(*parts), out_a, out_w, *near(mean_a, mean_w, pred_a, pred_w))
 
 
 def outer_kernel(*refs):
@@ -479,11 +482,11 @@
     vmem = pl.BlockSpec(memory_space=pltpu.VMEM)
     return pl.pallas_call(
         outer_kernel,
-        out_shape=jax.ShapeDtypeStruct((16, 16, OUT_COLS), f32),
+        out_shape=pltpu.VMEM((16, 16, OUT_COLS), f32),
         in_specs=[vmem] * 12,
         out_specs=vmem,
         name="outer",
-    )(*lats, *own, *other)
+    )(*near(*lats, *own, *other))
 
 
 def sum_kernel(x, out):
@@ -495,11 +498,11 @@
     vmem = pl.BlockSpec(memory_space=pltpu.VMEM)
     return pl.pallas_call(
         sum_kernel,
-        out_shape=jax.ShapeDtypeStruct((64, 16, OUT_COLS), bf16),
+        out_shape=pltpu.VMEM((64, 16, OUT_COLS), bf16),
         in_specs=[vmem],
         out_specs=vmem,
         name="reduce_parts",
-    )(x)
+    )(*near(x))
 
 
 def place_kernel(piece, *refs):
@@ -531,7 +534,7 @@
         ],
         input_output_aliases={1: 0, 2: 1} if held else {},
         name="place_partner" if partner else "place_own",
-    )(piece, *held)
+    )(*near(piece), *held)
 
 
 PLANE = [[z * 8 + y * 2 + c for z in range(4) for y in range(4)] for c in range(2)]

time: 194 us -> 180 us (0.928)
  Pallas kernels: 42.3 us -> 32.2 us
  local copies, waits for them, and re-layouts: 4.1 us -> 0.81 us
    pallas_call x5, Pallas kernels: 27.4 us -> 20.2 us  [the longest x1 14.7 us: attend(): pl.pallas_call(attend_kernel, out_shape=[pltpu.VMEM((ROWS, OUT_COLS), bf1...]
    unnamed x58 -> x26, local copies, waits for them, and re-layouts: 4.1 us -> 0.81 us
    pallas_call x2, Pallas kernels: 5.57 us -> 2.94 us  [place(): pl.pallas_call(place_kernel, grid=(2,), out_shape=[jax.ShapeDtypeStruct((...]
  transfers between devices with their start and end apart: 37 -> 37, of which waited for: 13 -> 14; matrix products, arithmetic and copies ran while one was open for 1% -> 1% of each run, Pallas kernels for 8% -> 7%
where the time goes in v5:
time: 180 us; the launch traced here: 179 us
  starting transfers between devices  52.5 us (29%)
  waiting for transfers between devices  51.5 us (29%)
  blocking collectives  39.5 us (22%)
  Pallas kernels  32.2 us (18%)
  other arithmetic  1.89 us (1%)
    ppermute x28, waiting for transfers between devices, dp_send(): return lax.ppermute(x, 'dp', pairs)  49.9 us
    ppermute x28, starting transfers between devices, dp_send(): return lax.ppermute(x, 'dp', pairs)  38.6 us
    all_to_all x1, blocking collectives, per_device(): lax.all_to_all(reduce_parts(arrived), ('role', 'dp'), split_axis=0, conca...  24.9 us
    pallas_call x1, Pallas kernels, attend(): pl.pallas_call(attend_kernel, out_shape=[pltpu.VMEM((ROWS, OUT_COLS), bf1...  14.7 us
    all_to_all x1, blocking collectives, per_device(): lax.all_to_all(halves, 'dp', split_axis=0, concat_axis=0, tiled=True, axi...  14.6 us
    ppermute x9, starting transfers between devices, role_send(): return lax.ppermute(x, 'role', [(i, (i + k) % ROLES) for i in range(ROLES)])  13.9 us
    pallas_call x2, Pallas kernels, norms(): pl.pallas_call(norm_kernel, grid=(2,), out_shape=[jax.ShapeDtypeStruct(hi...  7.41 us
    pallas_call x1, Pallas kernels, slopes(): pl.pallas_call(slope_kernel, out_shape=[pltpu.VMEM((ROWS, OUT_COLS), bf16...  3.82 us
  transfers between devices with their start and end apart: 37, of which 14 were waited for; matrix products, arithmetic and copies ran while one was open for 1% of the time, Pallas kernels for 7%

profile of v5, /device:TPU:1, one launch (start us, length us, event | category | flops | bytes accessed | tf_op | source)
XLA Modules:
  0.0 179.2 jit_solution(6285254646871814694)
XLA Ops:
  0.6 1.2 weight_chunks.1
  1.8 2.5 %collective-permute-start = (bf16[16,32,128]{2,1,0:T(8,128)(2,1)S(1)}, bf16[16,32,128]{2,1,0:T(8,128)(2,1)S(1)}, u32[]{:S(2)}, u32[]{:S(2)}) collective-permute-start(bf16[16,32,128]{2,1,0:T(8,128)(2,1)S(1)} %get-tuple-element.28), channel_id=1, source_target_pairs={{0,8},{1,9},{2,10},{3,11},{4,12},{5,13},{6,14},{7,15},{8,16},{9,17... | collective-permute-start | bytes 393224 | tf_op jit(solution)/shard_map/ppermute | solution.py:39
  4.4 3.3 %collective-permute-start.1 = (bf16[16,32,128]{2,1,0:T(8,128)(2,1)S(1)}, bf16[16,32,128]{2,1,0:T(8,128)(2,1)S(1)}, u32[]{:S(2)}, u32[]{:S(2)}) collective-permute-start(bf16[16,32,128]{2,1,0:T(8,128)(2,1)S(1)} %get-tuple-element.29), channel_id=1, source_target_pairs={{0,16},{1,17},{2,18},{3,19},{4,20},{5,21},{6,22},{7,23},{8,24},{9,... | collective-permute-start | bytes 393224 | tf_op jit(solution)/shard_map/ppermute | solution.py:39
  7.7 0.7 collective-permute-start.2
  8.4 1.3 collective-permute-done.refs_1_
  9.7 3.7 %collective-permute-done.1.refs_2_ = bf16[16,32,128]{2,1,0:T(8,128)(2,1)S(1)} collective-permute-done((bf16[16,32,128]{2,1,0:T(8,128)(2,1)S(1)}, bf16[16,32,128]{2,1,0:T(8,128)(2,1)S(1)}, u32[]{:S(2)}, u32[]{:S(2)}) %collective-permute-start.1) | collective-permute-done | bytes 131104 | tf_op jit(solution)/shard_map/ppermute | solution.py:39
  13.4 1.6 shares.1
  15.0 2.7 %collective-permute-start.11 = (bf16[12,32,128]{2,1,0:T(8,128)(2,1)}, bf16[12,32,128]{2,1,0:T(8,128)(2,1)S(1)}, u32[]{:S(2)}, u32[]{:S(2)}) collective-permute-start(bf16[12,32,128]{2,1,0:T(8,128)(2,1)} %get-tuple-element.32), channel_id=1, source_target_pairs={{0,6},{1,7},{2,0},{3,1},{4,2},{5,3},{6,4},{7,5},{8,14},{9,15},{10,... | collective-permute-start | bytes 294920 | tf_op jit(solution)/shard_map/ppermute | solution.py:39
  17.7 0.3 collective-permute-start.10
  18.1 0.7 collective-permute-start.9
  18.8 2.4 %collective-permute-start.5 = (bf16[12,32,128]{2,1,0:T(8,128)(2,1)}, bf16[12,32,128]{2,1,0:T(8,128)(2,1)S(1)}, u32[]{:S(2)}, u32[]{:S(2)}) collective-permute-start(bf16[12,32,128]{2,1,0:T(8,128)(2,1)} %get-tuple-element.31), channel_id=1, source_target_pairs={{0,24},{1,25},{2,26},{3,27},{4,28},{5,29},{6,30},{7,31},{8,0},{9,1... | collective-permute-start | bytes 294920 | tf_op jit(solution)/shard_map/ppermute | solution.py:39
  21.2 1.8 %collective-permute-done.10 = bf16[12,32,128]{2,1,0:T(8,128)(2,1)S(1)} collective-permute-done((bf16[12,32,128]{2,1,0:T(8,128)(2,1)}, bf16[12,32,128]{2,1,0:T(8,128)(2,1)S(1)}, u32[]{:S(2)}, u32[]{:S(2)}) %collective-permute-start.10) | collective-permute-done | bytes 98336 | tf_op jit(solution)/shard_map/ppermute | solution.py:39
  23.0 1.0 collective-permute-done.9
  24.0 0.9 pad_maximum_fusion.1.refs_4_
  24.9 3.0 %collective-permute-start.19 = (bf16[4,12,32,128]{3,2,1,0:T(8,128)(2,1)S(1)}, bf16[4,12,32,128]{3,2,1,0:T(8,128)(2,1)S(1)}, u32[]{:S(2)}, u32[]{:S(2)}) collective-permute-start(bf16[4,12,32,128]{3,2,1,0:T(8,128)(2,1)S(1)} %pad_maximum_fusion.1.refs_4_), channel_id=1, source_target_pairs={{0,1},{1,0},{2,3},{3,2},{4,5},{5,4},{6,7},{7,6},{8,9},{9,8},{10,11... | collective-permute-start | bytes 1179656 | tf_op jit(solution)/shard_map/ppermute | solution.py:39
  28.0 2.2 %collective-permute-start.14 = (bf16[4,12,32,128]{3,2,1,0:T(8,128)(2,1)S(1)}, bf16[4,12,32,128]{3,2,1,0:T(8,128)(2,1)S(1)}, u32[]{:S(2)}, u32[]{:S(2)}) collective-permute-start(bf16[4,12,32,128]{3,2,1,0:T(8,128)(2,1)S(1)} %pad_maximum_fusion.1.refs_4_), channel_id=1, source_target_pairs={{0,24},{1,25},{2,26},{3,27},{4,28},{5,29},{6,30},{7,31},{8,0},{9,1... | collective-permute-start | bytes 1179656 | tf_op jit(solution)/shard_map/ppermute | solution.py:39
  30.2 1.0 collective-permute-start.13
  31.2 0.0 collective-permute-start.12
  31.2 1.9 %collective-permute-start.4 = (bf16[12,32,128]{2,1,0:T(8,128)(2,1)}, bf16[12,32,128]{2,1,0:T(8,128)(2,1)S(1)}, u32[]{:S(2)}, u32[]{:S(2)}) collective-permute-start(bf16[12,32,128]{2,1,0:T(8,128)(2,1)} %get-tuple-element.31), channel_id=1, source_target_pairs={{0,16},{1,17},{2,18},{3,19},{4,20},{5,21},{6,22},{7,23},{8,24},{9,... | collective-permute-start | bytes 294920 | tf_op jit(solution)/shard_map/ppermute | solution.py:39
  33.2 19.4 %collective-permute-done.4 = bf16[12,32,128]{2,1,0:T(8,128)(2,1)S(1)} collective-permute-done((bf16[12,32,128]{2,1,0:T(8,128)(2,1)}, bf16[12,32,128]{2,1,0:T(8,128)(2,1)S(1)}, u32[]{:S(2)}, u32[]{:S(2)}) %collective-permute-start.4) | collective-permute-done | bytes 98336 | tf_op jit(solution)/shard_map/ppermute | solution.py:39
  52.6 4.9 %collective-permute-done.3 = bf16[12,32,128]{2,1,0:T(8,128)(2,1)S(1)} collective-permute-done((bf16[12,32,128]{2,1,0:T(8,128)(2,1)}, bf16[12,32,128]{2,1,0:T(8,128)(2,1)S(1)}, u32[]{:S(2)}, u32[]{:S(2)}) %collective-permute-start.3) | collective-permute-done | bytes 98336 | tf_op jit(solution)/shard_map/ppermute | solution.py:39
  57.5 0.9 pad_maximum_fusion.refs_0_
  58.4 2.4 %collective-permute-start.15 = (bf16[4,12,32,128]{3,2,1,0:T(8,128)(2,1)S(1)}, bf16[4,12,32,128]{3,2,1,0:T(8,128)(2,1)S(1)}, u32[]{:S(2)}, u32[]{:S(2)}) collective-permute-start(bf16[4,12,32,128]{3,2,1,0:T(8,128)(2,1)S(1)} %pad_maximum_fusion.refs_0_), channel_id=1, source_target_pairs={{0,1},{1,0},{2,3},{3,2},{4,5},{5,4},{6,7},{7,6},{8,9},{9,8},{10,11... | collective-permute-start | bytes 1179656 | tf_op jit(solution)/shard_map/ppermute | solution.py:39
  60.9 0.3 collective-permute-start.8
  61.2 0.3 collective-permute-start.7
  61.5 0.9 collective-permute-start.6
  62.5 0.7 collective-permute-start.22
  63.1 0.1 collective-permute-start.21
  63.2 8.2 %collective-permute-done.8.refs_3_ = bf16[4,12,32,128]{3,2,1,0:T(8,128)(2,1)S(1)} collective-permute-done((bf16[4,12,32,128]{3,2,1,0:T(8,128)(2,1)S(1)}, bf16[4,12,32,128]{3,2,1,0:T(8,128)(2,1)S(1)}, u32[]{:S(2)}, u32[]{:S(2)}) %collective-permute-start.8) | collective-permute-done | bytes 393248 | tf_op jit(solution)/shard_map/ppermute | solution.py:39
  71.5 1.5 collective-permute-start.20
  73.0 0.0 collective-permute-done.7.refs_2_
  73.0 2.1 %collective-permute-start.18 = (bf16[4,12,32,128]{3,2,1,0:T(8,128)(2,1)S(1)}, bf16[4,12,32,128]{3,2,1,0:T(8,128)(2,1)}, u32[]{:S(2)}, u32[]{:S(2)}) collective-permute-start(bf16[4,12,32,128]{3,2,1,0:T(8,128)(2,1)S(1)} %collective-permute-done.8.refs_3_), channel_id=1, source_target_pairs={{0,1},{1,0},{2,3},{3,2},{4,5},{5,4},{6,7},{7,6},{8,9},{9,8},{10,11... | collective-permute-start | bytes 1179656 | tf_op jit(solution)/shard_map/ppermute | solution.py:39
  75.1 7.1 %collective-permute-done.6.refs_1_ = bf16[4,12,32,128]{3,2,1,0:T(8,128)(2,1)S(1)} collective-permute-done((bf16[4,12,32,128]{3,2,1,0:T(8,128)(2,1)S(1)}, bf16[4,12,32,128]{3,2,1,0:T(8,128)(2,1)S(1)}, u32[]{:S(2)}, u32[]{:S(2)}) %collective-permute-start.6) | collective-permute-done | bytes 393248 | tf_op jit(solution)/shard_map/ppermute | solution.py:39
  82.2 0.5 collective-permute-start.17
  82.7 0.8 copy-done.12
  83.4 0.1 collective-permute-start.16
  83.5 3.5 %shard_map.122 = (bf16[2,512,1024]{2,1,0:T(8,128)(2,1)}, f32[64,1024]{1,0:T(8,128)}) custom-call(bf16[2,512,1024]{2,1,0:T(8,128)(2,1)} %hidden.2), custom_call_target="tpu_custom_call" | custom-call | flops 30000000 | bytes 12000000 | tf_op jit(solution)/shard_map/pallas_call | solution.py:73
  87.0 4.0 %shard_map.123 = (bf16[2,512,1280]{2,1,0:T(8,128)(2,1)}, f32[64,1280]{1,0:T(8,128)}) custom-call(bf16[2,512,1280]{2,1,0:T(8,128)(2,1)} %hidden.3), custom_call_target="tpu_custom_call" | custom-call | flops 30000000 | bytes 12000000 | tf_op jit(solution)/shard_map/pallas_call | solution.py:73
  91.1 14.7 %attend.1 = (bf16[64,640]{1,0:T(8,128)(2,1)S(1)}, bf16[64,640]{1,0:T(8,128)(2,1)S(1)}, bf16[64,640]{1,0:T(8,128)(2,1)S(1)}, bf16[64,640]{1,0:T(8,128)(2,1)S(1)},...) custom-call(s32[64]{0:T(128)} %frames_valid.3, s32[64]{0:T(128)} %slot_clip.1, ...), custom_call_target="tpu_custom_call" | custom-call | flops 8000000000 | bytes 12000000 | tf_op jit(solution)/shard_map/attend/pallas_call | solution.py:360
  105.8 2.5 %collective-permute-start.25 = (bf16[128,512]{1,0:T(8,128)(2,1)S(1)}, bf16[128,512]{1,0:T(8,128)(2,1)S(1)}, u32[]{:S(2)}, u32[]{:S(2)}) collective-permute-start(bf16[128,512]{1,0:T(8,128)(2,1)S(1)} %get-tuple-element.35.refs_0_), channel_id=1, source_target_pairs={{0,96},{32,0},{64,32},{96,64},{1,97},{33,1},{65,33},{97,65},{2,98}... | collective-permute-start | bytes 393224 | tf_op jit(solution)/shard_map/ppermute | solution.py:43
  108.3 1.7 collective-permute-start.27
  110.1 0.9 collective-permute-start.28
  111.0 2.4 %collective-permute-start.24 = (bf16[128,512]{1,0:T(8,128)(2,1)S(1)}, bf16[128,512]{1,0:T(8,128)(2,1)S(1)}, u32[]{:S(2)}, u32[]{:S(2)}) collective-permute-start(bf16[128,512]{1,0:T(8,128)(2,1)S(1)} %get-tuple-element.35.refs_0_), channel_id=1, source_target_pairs={{0,64},{32,96},{64,0},{96,32},{1,65},{33,97},{65,1},{97,33},{2,66}... | collective-permute-start | bytes 393224 | tf_op jit(solution)/shard_map/ppermute | solution.py:43
  113.4 0.6 collective-permute-done.26.refs_1_
  114.0 0.3 collective-permute-done.27.refs_2_
  114.3 0.6 collective-permute-done.28.refs_3_
  114.9 3.8 %slopes.1 = (bf16[64,640]{1,0:T(8,128)(2,1)S(1)}, bf16[64,640]{1,0:T(8,128)(2,1)S(1)}, bf16[64,640]{1,0:T(8,128)(2,1)S(1)}, bf16[64,640]{1,0:T(8,128)(2,1)S(1)}) custom-call(s32[64]{0:T(128)} %frames_valid.3, bf16[64,640]{1,0:T(8,128)(2,1)S(1)} %get-tuple-element.36.refs_0_, bf16[64,640]{1,0:T(8,128)(2,1)S(1)} %collective-permute-done.26.refs_1_, ...), custom_call_target="tpu_custom_call" | custom-call | tf_op jit(solution)/shard_map/slopes/pallas_call | solution.py:450
  118.7 1.5 collective-permute-start.29
  120.2 3.4 %collective-permute-start.30 = (bf16[64,640]{1,0:T(8,128)(2,1)S(1)}, bf16[64,640]{1,0:T(8,128)(2,1)S(1)}, u32[]{:S(2)}, u32[]{:S(2)}) collective-permute-start(bf16[64,640]{1,0:T(8,128)(2,1)S(1)} %get-tuple-element.46), channel_id=1, source_target_pairs={{0,64},{32,96},{64,0},{96,32},{1,65},{33,97},{65,1},{97,33},{2,66}... | collective-permute-start | bytes 245768 | tf_op jit(solution)/shard_map/ppermute | solution.py:43
  123.6 1.5 collective-permute-start.23
  125.1 2.8 %collective-permute-start.32 = (bf16[64,640]{1,0:T(8,128)(2,1)S(1)}, bf16[64,640]{1,0:T(8,128)(2,1)S(1)}, u32[]{:S(2)}, u32[]{:S(2)}) collective-permute-start(bf16[64,640]{1,0:T(8,128)(2,1)S(1)} %get-tuple-element.44.refs_4_), channel_id=1, source_target_pairs={{0,1},{1,0},{2,3},{3,2},{4,5},{5,4},{6,7},{7,6},{8,9},{9,8},{10,11... | collective-permute-start | bytes 245768 | tf_op jit(solution)/shard_map/ppermute | solution.py:39
  127.9 1.2 collective-permute-start.33
  129.1 1.2 collective-permute-start.34
  130.3 0.0 collective-permute-start.35
  130.3 0.9 collective-permute-done.34.refs_10_
  131.2 0.4 collective-permute-done.35.refs_11_
  131.6 0.4 outer.1
  132.0 14.6 %all_to_all.10.x = f32[16,16,640]{2,1,0:T(8,128)S(1)} all-to-all(f32[16,16,640]{2,1,0:T(8,128)S(1)} %outer.1), channel_id=1, replica_groups={{0,2,4,6,8,10,12,14,16,18,20,22,24,26,28,30},{1,3,5,7,9,11,13,15,17,19,..., dimensions={0} | all-to-all | bytes 1310720 | tf_op jit(solution)/shard_map/all_to_all | solution.py:577
  146.6 0.1 reduce_parts.1
  146.7 24.9 %all_to_all.11 = bf16[64,16,640]{2,1,0:T(8,128)(2,1)S(1)} all-to-all(bf16[64,16,640]{2,1,0:T(8,128)(2,1)S(1)} %reduce_parts.1), channel_id=1, replica_groups={{0,2,4,6,8,10,12,14,16,18,20,22,24,26,28,30,32,34,36,38,40,42,44,46,48,..., dimensions={0} | all-to-all | bytes 2621440 | tf_op jit(solution)/shard_map/all_to_all | solution.py:580
  171.6 3.5 %collective-permute-start.36 = (bf16[4,16,16,640]{3,2,1,0:T(8,128)(2,1)S(1)}, bf16[4,16,16,640]{3,2,1,0:T(8,128)(2,1)S(1)}, u32[]{:S(2)}, u32[]{:S(2)}) collective-permute-start(bf16[4,16,16,640]{3,2,1,0:T(8,128)(2,1)S(1)} %bitcast.13), channel_id=1, source_target_pairs={{0,1},{1,0},{2,3},{3,2},{4,5},{5,4},{6,7},{7,6},{8,9},{9,8},{10,11... | collective-permute-start | bytes 3932168 | tf_op jit(solution)/shard_map/ppermute | solution.py:39
  175.1 1.5 place_own.1
  176.5 1.2 collective-permute-done.36.piece
  177.7 1.5 place_partner.1
  (50 shorter events, 0.1 us)
Async XLA Ops:
  1.8 7.8 %collective-permute-start = (bf16[16,32,128]{2,1,0:T(8,128)(2,1)S(1)}, bf16[16,32,128]{2,1,0:T(8,128)(2,1)S(1)}, u32[]{:S(2)}, u32[]{:S(2)}) collective-permute-start(bf16[16,32,128]{2,1,0:T(8,128)(2,1)S(1)} %get-tuple-element.28), channel_id=1, source_target_pairs={{0,8},{1,9},{2,10},{3,11},{4,12},{5,13},{6,14},{7,15},{8,16},{9,17... | collective-permute-start | bytes 393224 | tf_op jit(solution)/shard_map/ppermute | solution.py:39
  4.4 9.0 %collective-permute-start.1 = (bf16[16,32,128]{2,1,0:T(8,128)(2,1)S(1)}, bf16[16,32,128]{2,1,0:T(8,128)(2,1)S(1)}, u32[]{:S(2)}, u32[]{:S(2)}) collective-permute-start(bf16[16,32,128]{2,1,0:T(8,128)(2,1)S(1)} %get-tuple-element.29), channel_id=1, source_target_pairs={{0,16},{1,17},{2,18},{3,19},{4,20},{5,21},{6,22},{7,23},{8,24},{9,... | collective-permute-start | bytes 393224 | tf_op jit(solution)/shard_map/ppermute | solution.py:39
  7.7 5.7 %collective-permute-start.2 = (bf16[16,32,128]{2,1,0:T(8,128)(2,1)S(1)}, bf16[16,32,128]{2,1,0:T(8,128)(2,1)S(1)}, u32[]{:S(2)}, u32[]{:S(2)}) collective-permute-start(bf16[16,32,128]{2,1,0:T(8,128)(2,1)S(1)} %get-tuple-element.30), channel_id=1, source_target_pairs={{0,24},{1,25},{2,26},{3,27},{4,28},{5,29},{6,30},{7,31},{8,0},{9,1... | collective-permute-start | bytes 393224 | tf_op jit(solution)/shard_map/ppermute | solution.py:39
  15.0 6.2 %collective-permute-start.11 = (bf16[12,32,128]{2,1,0:T(8,128)(2,1)}, bf16[12,32,128]{2,1,0:T(8,128)(2,1)S(1)}, u32[]{:S(2)}, u32[]{:S(2)}) collective-permute-start(bf16[12,32,128]{2,1,0:T(8,128)(2,1)} %get-tuple-element.32), channel_id=1, source_target_pairs={{0,6},{1,7},{2,0},{3,1},{4,2},{5,3},{6,4},{7,5},{8,14},{9,15},{10,... | collective-permute-start | bytes 294920 | tf_op jit(solution)/shard_map/ppermute | solution.py:39
  17.7 5.3 %collective-permute-start.10 = (bf16[12,32,128]{2,1,0:T(8,128)(2,1)}, bf16[12,32,128]{2,1,0:T(8,128)(2,1)S(1)}, u32[]{:S(2)}, u32[]{:S(2)}) collective-permute-start(bf16[12,32,128]{2,1,0:T(8,128)(2,1)} %get-tuple-element.32), channel_id=1, source_target_pairs={{0,4},{1,5},{2,6},{3,7},{4,0},{5,1},{6,2},{7,3},{8,12},{9,13},{10,... | collective-permute-start | bytes 294920 | tf_op jit(solution)/shard_map/ppermute | solution.py:39
  18.1 5.9 %collective-permute-start.9 = (bf16[12,32,128]{2,1,0:T(8,128)(2,1)}, bf16[12,32,128]{2,1,0:T(8,128)(2,1)S(1)}, u32[]{:S(2)}, u32[]{:S(2)}) collective-permute-start(bf16[12,32,128]{2,1,0:T(8,128)(2,1)} %get-tuple-element.32), channel_id=1, source_target_pairs={{0,2},{1,3},{2,4},{3,5},{4,6},{5,7},{6,0},{7,1},{8,10},{9,11},{10,... | collective-permute-start | bytes 294920 | tf_op jit(solution)/shard_map/ppermute | solution.py:39
  18.8 12.5 %collective-permute-start.5 = (bf16[12,32,128]{2,1,0:T(8,128)(2,1)}, bf16[12,32,128]{2,1,0:T(8,128)(2,1)S(1)}, u32[]{:S(2)}, u32[]{:S(2)}) collective-permute-start(bf16[12,32,128]{2,1,0:T(8,128)(2,1)} %get-tuple-element.31), channel_id=1, source_target_pairs={{0,24},{1,25},{2,26},{3,27},{4,28},{5,29},{6,30},{7,31},{8,0},{9,1... | collective-permute-start | bytes 294920 | tf_op jit(solution)/shard_map/ppermute | solution.py:39
  24.9 66.0 %copy-start.2 = (bf16[4,12,32,128]{3,2,1,0:T(8,128)(2,1)}, bf16[4,12,32,128]{3,2,1,0:T(8,128)(2,1)S(1)}, u32[]{:S(2)}) copy-start(bf16[4,12,32,128]{3,2,1,0:T(8,128)(2,1)S(1)} %pad_maximum_fusion.1.refs_4_) | copy-start | bytes 1179652
  24.9 36.0 %collective-permute-start.19 = (bf16[4,12,32,128]{3,2,1,0:T(8,128)(2,1)S(1)}, bf16[4,12,32,128]{3,2,1,0:T(8,128)(2,1)S(1)}, u32[]{:S(2)}, u32[]{:S(2)}) collective-permute-start(bf16[4,12,32,128]{3,2,1,0:T(8,128)(2,1)S(1)} %pad_maximum_fusion.1.refs_4_), channel_id=1, source_target_pairs={{0,1},{1,0},{2,3},{3,2},{4,5},{5,4},{6,7},{7,6},{8,9},{9,8},{10,11... | collective-permute-start | bytes 1179656 | tf_op jit(solution)/shard_map/ppermute | solution.py:39
  28.0 33.2 %collective-permute-start.14 = (bf16[4,12,32,128]{3,2,1,0:T(8,128)(2,1)S(1)}, bf16[4,12,32,128]{3,2,1,0:T(8,128)(2,1)S(1)}, u32[]{:S(2)}, u32[]{:S(2)}) collective-permute-start(bf16[4,12,32,128]{3,2,1,0:T(8,128)(2,1)S(1)} %pad_maximum_fusion.1.refs_4_), channel_id=1, source_target_pairs={{0,24},{1,25},{2,26},{3,27},{4,28},{5,29},{6,30},{7,31},{8,0},{9,1... | collective-permute-start | bytes 1179656 | tf_op jit(solution)/shard_map/ppermute | solution.py:39
  30.2 31.3 %collective-permute-start.13 = (bf16[4,12,32,128]{3,2,1,0:T(8,128)(2,1)S(1)}, bf16[4,12,32,128]{3,2,1,0:T(8,128)(2,1)S(1)}, u32[]{:S(2)}, u32[]{:S(2)}) collective-permute-start(bf16[4,12,32,128]{3,2,1,0:T(8,128)(2,1)S(1)} %pad_maximum_fusion.1.refs_4_), channel_id=1, source_target_pairs={{0,16},{1,17},{2,18},{3,19},{4,20},{5,21},{6,22},{7,23},{8,24},{9,... | collective-permute-start | bytes 1179656 | tf_op jit(solution)/shard_map/ppermute | solution.py:39
  31.2 31.2 %collective-permute-start.12 = (bf16[4,12,32,128]{3,2,1,0:T(8,128)(2,1)S(1)}, bf16[4,12,32,128]{3,2,1,0:T(8,128)(2,1)S(1)}, u32[]{:S(2)}, u32[]{:S(2)}) collective-permute-start(bf16[4,12,32,128]{3,2,1,0:T(8,128)(2,1)S(1)} %pad_maximum_fusion.1.refs_4_), channel_id=1, source_target_pairs={{0,8},{1,9},{2,10},{3,11},{4,12},{5,13},{6,14},{7,15},{8,16},{9,17... | collective-permute-start | bytes 1179656 | tf_op jit(solution)/shard_map/ppermute | solution.py:39
  31.2 21.4 %collective-permute-start.4 = (bf16[12,32,128]{2,1,0:T(8,128)(2,1)}, bf16[12,32,128]{2,1,0:T(8,128)(2,1)S(1)}, u32[]{:S(2)}, u32[]{:S(2)}) collective-permute-start(bf16[12,32,128]{2,1,0:T(8,128)(2,1)} %get-tuple-element.31), channel_id=1, source_target_pairs={{0,16},{1,17},{2,18},{3,19},{4,20},{5,21},{6,22},{7,23},{8,24},{9,... | collective-permute-start | bytes 294920 | tf_op jit(solution)/shard_map/ppermute | solution.py:39
  52.6 4.9 %collective-permute-start.3 = (bf16[12,32,128]{2,1,0:T(8,128)(2,1)}, bf16[12,32,128]{2,1,0:T(8,128)(2,1)S(1)}, u32[]{:S(2)}, u32[]{:S(2)}) collective-permute-start(bf16[12,32,128]{2,1,0:T(8,128)(2,1)} %get-tuple-element.31), channel_id=1, source_target_pairs={{0,8},{1,9},{2,10},{3,11},{4,12},{5,13},{6,14},{7,15},{8,16},{9,17... | collective-permute-start | bytes 294920 | tf_op jit(solution)/shard_map/ppermute | solution.py:39
  58.4 32.5 %copy-start.3 = (bf16[4,12,32,128]{3,2,1,0:T(8,128)(2,1)}, bf16[4,12,32,128]{3,2,1,0:T(8,128)(2,1)S(1)}, u32[]{:S(2)}) copy-start(bf16[4,12,32,128]{3,2,1,0:T(8,128)(2,1)S(1)} %pad_maximum_fusion.refs_0_) | copy-start | bytes 1179652
  58.4 4.7 %collective-permute-start.15 = (bf16[4,12,32,128]{3,2,1,0:T(8,128)(2,1)S(1)}, bf16[4,12,32,128]{3,2,1,0:T(8,128)(2,1)S(1)}, u32[]{:S(2)}, u32[]{:S(2)}) collective-permute-start(bf16[4,12,32,128]{3,2,1,0:T(8,128)(2,1)S(1)} %pad_maximum_fusion.refs_0_), channel_id=1, source_target_pairs={{0,1},{1,0},{2,3},{3,2},{4,5},{5,4},{6,7},{7,6},{8,9},{9,8},{10,11... | collective-permute-start | bytes 1179656 | tf_op jit(solution)/shard_map/ppermute | solution.py:39
  60.9 21.3 %copy-start.4 = (bf16[4,12,32,128]{3,2,1,0:T(8,128)(2,1)}, bf16[4,12,32,128]{3,2,1,0:T(8,128)(2,1)S(1)}, u32[]{:S(2)}) copy-start(bf16[4,12,32,128]{3,2,1,0:T(8,128)(2,1)S(1)} %collective-permute-done.19.refs_12_) | copy-start | bytes 1179652
  60.9 10.6 %collective-permute-start.8 = (bf16[4,12,32,128]{3,2,1,0:T(8,128)(2,1)S(1)}, bf16[4,12,32,128]{3,2,1,0:T(8,128)(2,1)S(1)}, u32[]{:S(2)}, u32[]{:S(2)}) collective-permute-start(bf16[4,12,32,128]{3,2,1,0:T(8,128)(2,1)S(1)} %pad_maximum_fusion.refs_0_), channel_id=1, source_target_pairs={{0,6},{1,7},{2,0},{3,1},{4,2},{5,3},{6,4},{7,5},{8,14},{9,15},{10,... | collective-permute-start | bytes 1179656 | tf_op jit(solution)/shard_map/ppermute | solution.py:39
  61.2 21.5 %copy-start.5 = (bf16[4,12,32,128]{3,2,1,0:T(8,128)(2,1)}, bf16[4,12,32,128]{3,2,1,0:T(8,128)(2,1)S(1)}, u32[]{:S(2)}) copy-start(bf16[4,12,32,128]{3,2,1,0:T(8,128)(2,1)S(1)} %collective-permute-done.14.refs_7_) | copy-start | bytes 1179652
  61.2 11.8 %collective-permute-start.7 = (bf16[4,12,32,128]{3,2,1,0:T(8,128)(2,1)S(1)}, bf16[4,12,32,128]{3,2,1,0:T(8,128)(2,1)S(1)}, u32[]{:S(2)}, u32[]{:S(2)}) collective-permute-start(bf16[4,12,32,128]{3,2,1,0:T(8,128)(2,1)S(1)} %pad_maximum_fusion.refs_0_), channel_id=1, source_target_pairs={{0,4},{1,5},{2,6},{3,7},{4,0},{5,1},{6,2},{7,3},{8,12},{9,13},{10,... | collective-permute-start | bytes 1179656 | tf_op jit(solution)/shard_map/ppermute | solution.py:39
  61.5 29.4 %copy-start.6 = (bf16[4,12,32,128]{3,2,1,0:T(8,128)(2,1)}, bf16[4,12,32,128]{3,2,1,0:T(8,128)(2,1)S(1)}, u32[]{:S(2)}) copy-start(bf16[4,12,32,128]{3,2,1,0:T(8,128)(2,1)S(1)} %collective-permute-done.13.refs_6_) | copy-start | bytes 1179652
  61.5 20.6 %collective-permute-start.6 = (bf16[4,12,32,128]{3,2,1,0:T(8,128)(2,1)S(1)}, bf16[4,12,32,128]{3,2,1,0:T(8,128)(2,1)S(1)}, u32[]{:S(2)}, u32[]{:S(2)}) collective-permute-start(bf16[4,12,32,128]{3,2,1,0:T(8,128)(2,1)S(1)} %pad_maximum_fusion.refs_0_), channel_id=1, source_target_pairs={{0,2},{1,3},{2,4},{3,5},{4,6},{5,7},{6,0},{7,1},{8,10},{9,11},{10,... | collective-permute-start | bytes 1179656 | tf_op jit(solution)/shard_map/ppermute | solution.py:39
  62.5 28.5 %copy-start.7 = (bf16[4,12,32,128]{3,2,1,0:T(8,128)(2,1)}, bf16[4,12,32,128]{3,2,1,0:T(8,128)(2,1)S(1)}, u32[]{:S(2)}) copy-start(bf16[4,12,32,128]{3,2,1,0:T(8,128)(2,1)S(1)} %collective-permute-done.12.refs_5_) | copy-start | bytes 1179652
  62.5 20.2 %collective-permute-start.22 = (bf16[4,12,32,128]{3,2,1,0:T(8,128)(2,1)S(1)}, bf16[4,12,32,128]{3,2,1,0:T(8,128)(2,1)S(1)}, u32[]{:S(2)}, u32[]{:S(2)}) collective-permute-start(bf16[4,12,32,128]{3,2,1,0:T(8,128)(2,1)S(1)} %collective-permute-done.14.refs_7_), channel_id=1, source_target_pairs={{0,1},{1,0},{2,3},{3,2},{4,5},{5,4},{6,7},{7,6},{8,9},{9,8},{10,11... | collective-permute-start | bytes 1179656 | tf_op jit(solution)/shard_map/ppermute | solution.py:39
  63.1 27.8 %copy-start.8 = (bf16[4,12,32,128]{3,2,1,0:T(8,128)(2,1)}, bf16[4,12,32,128]{3,2,1,0:T(8,128)(2,1)S(1)}, u32[]{:S(2)}) copy-start(bf16[4,12,32,128]{3,2,1,0:T(8,128)(2,1)S(1)} %collective-permute-done.15.refs_8_) | copy-start | bytes 1179652
  63.1 27.9 %collective-permute-start.21 = (bf16[4,12,32,128]{3,2,1,0:T(8,128)(2,1)S(1)}, bf16[4,12,32,128]{3,2,1,0:T(8,128)(2,1)}, u32[]{:S(2)}, u32[]{:S(2)}) collective-permute-start(bf16[4,12,32,128]{3,2,1,0:T(8,128)(2,1)S(1)} %collective-permute-done.13.refs_6_), channel_id=1, source_target_pairs={{0,1},{1,0},{2,3},{3,2},{4,5},{5,4},{6,7},{7,6},{8,9},{9,8},{10,11... | collective-permute-start | bytes 1179656 | tf_op jit(solution)/shard_map/ppermute | solution.py:39
  71.5 19.5 %copy-start.9 = (bf16[4,12,32,128]{3,2,1,0:T(8,128)(2,1)}, bf16[4,12,32,128]{3,2,1,0:T(8,128)(2,1)S(1)}, u32[]{:S(2)}) copy-start(bf16[4,12,32,128]{3,2,1,0:T(8,128)(2,1)S(1)} %collective-permute-done.8.refs_3_) | copy-start | bytes 1179652
  71.5 19.6 %collective-permute-start.20 = (bf16[4,12,32,128]{3,2,1,0:T(8,128)(2,1)S(1)}, bf16[4,12,32,128]{3,2,1,0:T(8,128)(2,1)}, u32[]{:S(2)}, u32[]{:S(2)}) collective-permute-start(bf16[4,12,32,128]{3,2,1,0:T(8,128)(2,1)S(1)} %collective-permute-done.12.refs_5_), channel_id=1, source_target_pairs={{0,1},{1,0},{2,3},{3,2},{4,5},{5,4},{6,7},{7,6},{8,9},{9,8},{10,11... | collective-permute-start | bytes 1179656 | tf_op jit(solution)/shard_map/ppermute | solution.py:39
  73.0 18.0 %copy-start.10 = (bf16[4,12,32,128]{3,2,1,0:T(8,128)(2,1)}, bf16[4,12,32,128]{3,2,1,0:T(8,128)(2,1)S(1)}, u32[]{:S(2)}) copy-start(bf16[4,12,32,128]{3,2,1,0:T(8,128)(2,1)S(1)} %collective-permute-done.7.refs_2_) | copy-start | bytes 1179652
  73.0 18.0 %collective-permute-start.18 = (bf16[4,12,32,128]{3,2,1,0:T(8,128)(2,1)S(1)}, bf16[4,12,32,128]{3,2,1,0:T(8,128)(2,1)}, u32[]{:S(2)}, u32[]{:S(2)}) collective-permute-start(bf16[4,12,32,128]{3,2,1,0:T(8,128)(2,1)S(1)} %collective-permute-done.8.refs_3_), channel_id=1, source_target_pairs={{0,1},{1,0},{2,3},{3,2},{4,5},{5,4},{6,7},{7,6},{8,9},{9,8},{10,11... | collective-permute-start | bytes 1179656 | tf_op jit(solution)/shard_map/ppermute | solution.py:39
  82.2 8.8 %copy-start.11 = (bf16[4,12,32,128]{3,2,1,0:T(8,128)(2,1)}, bf16[4,12,32,128]{3,2,1,0:T(8,128)(2,1)S(1)}, u32[]{:S(2)}) copy-start(bf16[4,12,32,128]{3,2,1,0:T(8,128)(2,1)S(1)} %collective-permute-done.6.refs_1_) | copy-start | bytes 1179652
  82.2 8.9 %collective-permute-start.17 = (bf16[4,12,32,128]{3,2,1,0:T(8,128)(2,1)S(1)}, bf16[4,12,32,128]{3,2,1,0:T(8,128)(2,1)}, u32[]{:S(2)}, u32[]{:S(2)}) collective-permute-start(bf16[4,12,32,128]{3,2,1,0:T(8,128)(2,1)S(1)} %collective-permute-done.7.refs_2_), channel_id=1, source_target_pairs={{0,1},{1,0},{2,3},{3,2},{4,5},{5,4},{6,7},{7,6},{8,9},{9,8},{10,11... | collective-permute-start | bytes 1179656 | tf_op jit(solution)/shard_map/ppermute | solution.py:39
  82.7 0.8 copy-start.12
  83.4 7.6 %collective-permute-start.16 = (bf16[4,12,32,128]{3,2,1,0:T(8,128)(2,1)S(1)}, bf16[4,12,32,128]{3,2,1,0:T(8,128)(2,1)}, u32[]{:S(2)}, u32[]{:S(2)}) collective-permute-start(bf16[4,12,32,128]{3,2,1,0:T(8,128)(2,1)S(1)} %collective-permute-done.6.refs_1_), channel_id=1, source_target_pairs={{0,1},{1,0},{2,3},{3,2},{4,5},{5,4},{6,7},{7,6},{8,9},{9,8},{10,11... | collective-permute-start | bytes 1179656 | tf_op jit(solution)/shard_map/ppermute | solution.py:39
  91.1 23.8 %copy-start = (f32[64,1280]{1,0:T(8,128)S(1)}, f32[64,1280]{1,0:T(8,128)}, u32[]{:S(2)}) copy-start(f32[64,1280]{1,0:T(8,128)} %get-tuple-element.41.refs_7_) | copy-start | bytes 983044
  91.1 23.8 %copy-start.1 = (f32[64,1024]{1,0:T(8,128)S(1)}, f32[64,1024]{1,0:T(8,128)}, u32[]{:S(2)}) copy-start(f32[64,1024]{1,0:T(8,128)} %get-tuple-element.40.refs_6_) | copy-start | bytes 786436
  105.8 17.8 %collective-permute-start.25 = (bf16[128,512]{1,0:T(8,128)(2,1)S(1)}, bf16[128,512]{1,0:T(8,128)(2,1)S(1)}, u32[]{:S(2)}, u32[]{:S(2)}) collective-permute-start(bf16[128,512]{1,0:T(8,128)(2,1)S(1)} %get-tuple-element.35.refs_0_), channel_id=1, source_target_pairs={{0,96},{32,0},{64,32},{96,64},{1,97},{33,1},{65,33},{97,65},{2,98}... | collective-permute-start | bytes 393224 | tf_op jit(solution)/shard_map/ppermute | solution.py:43
  108.3 5.7 %collective-permute-start.26 = (bf16[64,640]{1,0:T(8,128)(2,1)S(1)}, bf16[64,640]{1,0:T(8,128)(2,1)S(1)}, u32[]{:S(2)}, u32[]{:S(2)}) collective-permute-start(bf16[64,640]{1,0:T(8,128)(2,1)S(1)} %get-tuple-element.37), channel_id=1, source_target_pairs={{0,32},{32,64},{64,96},{96,0},{1,33},{33,65},{65,97},{97,1},{2,34}... | collective-permute-start | bytes 245768 | tf_op jit(solution)/shard_map/ppermute | solution.py:43
  108.3 6.0 %collective-permute-start.27 = (bf16[64,640]{1,0:T(8,128)(2,1)S(1)}, bf16[64,640]{1,0:T(8,128)(2,1)S(1)}, u32[]{:S(2)}, u32[]{:S(2)}) collective-permute-start(bf16[64,640]{1,0:T(8,128)(2,1)S(1)} %get-tuple-element.38), channel_id=1, source_target_pairs={{0,64},{32,96},{64,0},{96,32},{1,65},{33,97},{65,1},{97,33},{2,66}... | collective-permute-start | bytes 245768 | tf_op jit(solution)/shard_map/ppermute | solution.py:43
  110.1 4.8 %collective-permute-start.28 = (bf16[64,640]{1,0:T(8,128)(2,1)S(1)}, bf16[64,640]{1,0:T(8,128)(2,1)S(1)}, u32[]{:S(2)}, u32[]{:S(2)}) collective-permute-start(bf16[64,640]{1,0:T(8,128)(2,1)S(1)} %get-tuple-element.39), channel_id=1, source_target_pairs={{0,96},{32,0},{64,32},{96,64},{1,97},{33,1},{65,33},{97,65},{2,98}... | collective-permute-start | bytes 245768 | tf_op jit(solution)/shard_map/ppermute | solution.py:43
  111.0 14.1 %collective-permute-start.24 = (bf16[128,512]{1,0:T(8,128)(2,1)S(1)}, bf16[128,512]{1,0:T(8,128)(2,1)S(1)}, u32[]{:S(2)}, u32[]{:S(2)}) collective-permute-start(bf16[128,512]{1,0:T(8,128)(2,1)S(1)} %get-tuple-element.35.refs_0_), channel_id=1, source_target_pairs={{0,64},{32,96},{64,0},{96,32},{1,65},{33,97},{65,1},{97,33},{2,66}... | collective-permute-start | bytes 393224 | tf_op jit(solution)/shard_map/ppermute | solution.py:43
  118.7 9.2 %collective-permute-start.29 = (bf16[64,640]{1,0:T(8,128)(2,1)S(1)}, bf16[64,640]{1,0:T(8,128)(2,1)S(1)}, u32[]{:S(2)}, u32[]{:S(2)}) collective-permute-start(bf16[64,640]{1,0:T(8,128)(2,1)S(1)} %get-tuple-element.45), channel_id=1, source_target_pairs={{0,32},{32,64},{64,96},{96,0},{1,33},{33,65},{65,97},{97,1},{2,34}... | collective-permute-start | bytes 245768 | tf_op jit(solution)/shard_map/ppermute | solution.py:43
  120.2 8.9 %collective-permute-start.30 = (bf16[64,640]{1,0:T(8,128)(2,1)S(1)}, bf16[64,640]{1,0:T(8,128)(2,1)S(1)}, u32[]{:S(2)}, u32[]{:S(2)}) collective-permute-start(bf16[64,640]{1,0:T(8,128)(2,1)S(1)} %get-tuple-element.46), channel_id=1, source_target_pairs={{0,64},{32,96},{64,0},{96,32},{1,65},{33,97},{65,1},{97,33},{2,66}... | collective-permute-start | bytes 245768 | tf_op jit(solution)/shard_map/ppermute | solution.py:43
  123.6 6.7 %collective-permute-start.31 = (bf16[64,640]{1,0:T(8,128)(2,1)S(1)}, bf16[64,640]{1,0:T(8,128)(2,1)S(1)}, u32[]{:S(2)}, u32[]{:S(2)}) collective-permute-start(bf16[64,640]{1,0:T(8,128)(2,1)S(1)} %get-tuple-element.47), channel_id=1, source_target_pairs={{0,96},{32,0},{64,32},{96,64},{1,97},{33,1},{65,33},{97,65},{2,98}... | collective-permute-start | bytes 245768 | tf_op jit(solution)/shard_map/ppermute | solution.py:43
  123.6 6.7 %collective-permute-start.23 = (bf16[128,512]{1,0:T(8,128)(2,1)S(1)}, bf16[128,512]{1,0:T(8,128)(2,1)S(1)}, u32[]{:S(2)}, u32[]{:S(2)}) collective-permute-start(bf16[128,512]{1,0:T(8,128)(2,1)S(1)} %get-tuple-element.35.refs_0_), channel_id=1, source_target_pairs={{0,32},{32,64},{64,96},{96,0},{1,33},{33,65},{65,97},{97,1},{2,34}... | collective-permute-start | bytes 393224 | tf_op jit(solution)/shard_map/ppermute | solution.py:43
  125.1 5.2 %collective-permute-start.32 = (bf16[64,640]{1,0:T(8,128)(2,1)S(1)}, bf16[64,640]{1,0:T(8,128)(2,1)S(1)}, u32[]{:S(2)}, u32[]{:S(2)}) collective-permute-start(bf16[64,640]{1,0:T(8,128)(2,1)S(1)} %get-tuple-element.44.refs_4_), channel_id=1, source_target_pairs={{0,1},{1,0},{2,3},{3,2},{4,5},{5,4},{6,7},{7,6},{8,9},{9,8},{10,11... | collective-permute-start | bytes 245768 | tf_op jit(solution)/shard_map/ppermute | solution.py:39
  127.9 2.4 %collective-permute-start.33 = (bf16[64,640]{1,0:T(8,128)(2,1)S(1)}, bf16[64,640]{1,0:T(8,128)(2,1)S(1)}, u32[]{:S(2)}, u32[]{:S(2)}) collective-permute-start(bf16[64,640]{1,0:T(8,128)(2,1)S(1)} %collective-permute-done.29.refs_5_), channel_id=1, source_target_pairs={{0,1},{1,0},{2,3},{3,2},{4,5},{5,4},{6,7},{7,6},{8,9},{9,8},{10,11... | collective-permute-start | bytes 245768 | tf_op jit(solution)/shard_map/ppermute | solution.py:39
  129.1 2.1 %collective-permute-start.34 = (bf16[64,640]{1,0:T(8,128)(2,1)S(1)}, bf16[64,640]{1,0:T(8,128)(2,1)S(1)}, u32[]{:S(2)}, u32[]{:S(2)}) collective-permute-start(bf16[64,640]{1,0:T(8,128)(2,1)S(1)} %collective-permute-done.30.refs_6_), channel_id=1, source_target_pairs={{0,1},{1,0},{2,3},{3,2},{4,5},{5,4},{6,7},{7,6},{8,9},{9,8},{10,11... | collective-permute-start | bytes 245768 | tf_op jit(solution)/shard_map/ppermute | solution.py:39
  130.3 1.3 collective-permute-start.35
  171.6 6.2 %collective-permute-start.36 = (bf16[4,16,16,640]{3,2,1,0:T(8,128)(2,1)S(1)}, bf16[4,16,16,640]{3,2,1,0:T(8,128)(2,1)S(1)}, u32[]{:S(2)}, u32[]{:S(2)}) collective-permute-start(bf16[4,16,16,640]{3,2,1,0:T(8,128)(2,1)S(1)} %bitcast.13), channel_id=1, source_target_pairs={{0,1},{1,0},{2,3},{3,2},{4,5},{5,4},{6,7},{7,6},{8,9},{9,8},{10,11... | collective-permute-start | bytes 3932168 | tf_op jit(solution)/shard_map/ppermute | solution.py:39

commit v6 on v5

--- a/solution.py
+++ b/solution.py
@@ -475,14 +475,17 @@
     grad = lax.dot_general(
         lat, jnp.concatenate(rows, axis=0), (((0,), (0,)), ((), ())), preferred_element_type=f32
     )
-    out[...] = grad.reshape(16, 16, OUT_COLS)
+    grad = grad.reshape(16, 16, OUT_COLS)
+    for t in range(4):
+        out[:, 16 * t : 16 * t + 16] = grad[:, :, 128 * t : 128 * t + 128]
+    out[:, 64:] = jnp.concatenate([grad[:, :8, 512:576], grad[:, 8:, 512:576]], axis=-1)
 
 
 def outer(lats, own, other):
     vmem = pl.BlockSpec(memory_space=pltpu.VMEM)
     return pl.pallas_call(
         outer_kernel,
-        out_shape=pltpu.VMEM((16, 16, OUT_COLS), f32),
+        out_shape=pltpu.VMEM((16, 72, 128), f32),
         in_specs=[vmem] * 12,
         out_specs=vmem,
         name="outer",
@@ -498,7 +501,7 @@
     vmem = pl.BlockSpec(memory_space=pltpu.VMEM)
     return pl.pallas_call(
         sum_kernel,
-        out_shape=pltpu.VMEM((64, 16, OUT_COLS), bf16),
+        out_shape=pltpu.VMEM((64, 72, 128), bf16),
         in_specs=[vmem],
         out_specs=vmem,
         name="reduce_parts",
@@ -510,9 +513,14 @@
     blocks = []
     step = pl.program_id(0) * 8
     for g in range(ROLES):
-        block = piece[g, pl.ds(step, 8)].reshape(128, OUT_COLS).astype(f32)
-        out_a[0, :, g * A_COLS : (g + 1) * A_COLS] = block[:, :A_COLS]
-        blocks.append(block[:, A_COLS : A_COLS + W_COLS])
+        block = piece[g, pl.ds(step, 8)].astype(f32)
+        for t in range(2):
+            lane = g * A_COLS + 128 * t
+            out_a[0, :, lane : lane + 128] = block[:, 16 * t : 16 * t + 16].reshape(128, 128)
+            blocks.append(block[:, 32 + 16 * t : 48 + 16 * t].reshape(128, 128))
+        last = block[:, 64:]
+        last = jnp.concatenate([last[:, :, :64], last[:, :, 64:]], axis=1)
+        blocks.append(last.reshape(128, 64))
     out_w[0] = jnp.concatenate(blocks, axis=1)
 
 
@@ -584,7 +592,7 @@
         concat_axis=0,
         tiled=True,
         axis_index_groups=SLICE,
-    ).reshape(ROLES, 16, 16, OUT_COLS)
+    ).reshape(ROLES, 16, 72, 128)
     partner = dp_send(summed, 0, 0, 1)
     held = place(summed, 0)
     grad_a, grad_w = place(partner, 1, held)

time: 180 us -> 177 us (0.983)
  blocking collectives: 39.5 us -> 37 us
where the time goes in v6:
time: 177 us
  starting transfers between devices  52.9 us (30%)
  waiting for transfers between devices  51.1 us (29%)
  blocking collectives  37 us (21%)
  Pallas kernels  32.4 us (18%)
  other arithmetic  1.89 us (1%)
    ppermute x28, waiting for transfers between devices, dp_send(): return lax.ppermute(x, 'dp', pairs)  49.6 us
    ppermute x28, starting transfers between devices, dp_send(): return lax.ppermute(x, 'dp', pairs)  38.8 us
    all_to_all x1, blocking collectives, per_device(): lax.all_to_all(reduce_parts(arrived), ('role', 'dp'), split_axis=0, conca...  23.1 us
    pallas_call x1, Pallas kernels, attend(): pl.pallas_call(attend_kernel, out_shape=[pltpu.VMEM((ROWS, OUT_COLS), bf1...  14.7 us
    ppermute x9, starting transfers between devices, role_send(): return lax.ppermute(x, 'role', [(i, (i + k) % ROLES) for i in range(ROLES)])  14 us
    all_to_all x1, blocking collectives, per_device(): lax.all_to_all(halves, 'dp', split_axis=0, concat_axis=0, tiled=True, axi...  13.9 us
    pallas_call x2, Pallas kernels, norms(): pl.pallas_call(norm_kernel, grid=(2,), out_shape=[jax.ShapeDtypeStruct(hi...  7.41 us
    pallas_call x1, Pallas kernels, slopes(): pl.pallas_call(slope_kernel, out_shape=[pltpu.VMEM((ROWS, OUT_COLS), bf16...  3.82 us
  transfers between devices with their start and end apart: 37, of which 14 were waited for; matrix products, arithmetic and copies ran while one was open for 1% of the time, Pallas kernels for 7%

profile of v6, /device:TPU:1, one launch (start us, length us, event | category | flops | bytes accessed | tf_op | source)
XLA Modules:
  0.0 176.9 jit_solution(10504757626849098662)
XLA Ops:
  0.6 1.2 weight_chunks.1
  1.8 2.5 %collective-permute-start = (bf16[16,32,128]{2,1,0:T(8,128)(2,1)S(1)}, bf16[16,32,128]{2,1,0:T(8,128)(2,1)S(1)}, u32[]{:S(2)}, u32[]{:S(2)}) collective-permute-start(bf16[16,32,128]{2,1,0:T(8,128)(2,1)S(1)} %get-tuple-element.28), channel_id=1, source_target_pairs={{0,8},{1,9},{2,10},{3,11},{4,12},{5,13},{6,14},{7,15},{8,16},{9,17... | collective-permute-start | bytes 393224 | tf_op jit(solution)/shard_map/ppermute | solution.py:39
  4.4 3.3 %collective-permute-start.1 = (bf16[16,32,128]{2,1,0:T(8,128)(2,1)S(1)}, bf16[16,32,128]{2,1,0:T(8,128)(2,1)S(1)}, u32[]{:S(2)}, u32[]{:S(2)}) collective-permute-start(bf16[16,32,128]{2,1,0:T(8,128)(2,1)S(1)} %get-tuple-element.29), channel_id=1, source_target_pairs={{0,16},{1,17},{2,18},{3,19},{4,20},{5,21},{6,22},{7,23},{8,24},{9,... | collective-permute-start | bytes 393224 | tf_op jit(solution)/shard_map/ppermute | solution.py:39
  7.7 0.7 collective-permute-start.2
  8.4 1.3 collective-permute-done.refs_1_
  9.7 3.7 %collective-permute-done.1.refs_2_ = bf16[16,32,128]{2,1,0:T(8,128)(2,1)S(1)} collective-permute-done((bf16[16,32,128]{2,1,0:T(8,128)(2,1)S(1)}, bf16[16,32,128]{2,1,0:T(8,128)(2,1)S(1)}, u32[]{:S(2)}, u32[]{:S(2)}) %collective-permute-start.1) | collective-permute-done | bytes 131104 | tf_op jit(solution)/shard_map/ppermute | solution.py:39
  13.4 1.6 shares.1
  15.0 2.7 %collective-permute-start.11 = (bf16[12,32,128]{2,1,0:T(8,128)(2,1)}, bf16[12,32,128]{2,1,0:T(8,128)(2,1)S(1)}, u32[]{:S(2)}, u32[]{:S(2)}) collective-permute-start(bf16[12,32,128]{2,1,0:T(8,128)(2,1)} %get-tuple-element.32), channel_id=1, source_target_pairs={{0,6},{1,7},{2,0},{3,1},{4,2},{5,3},{6,4},{7,5},{8,14},{9,15},{10,... | collective-permute-start | bytes 294920 | tf_op jit(solution)/shard_map/ppermute | solution.py:39
  17.7 0.3 collective-permute-start.10
  18.1 0.7 collective-permute-start.9
  18.8 2.4 %collective-permute-start.5 = (bf16[12,32,128]{2,1,0:T(8,128)(2,1)}, bf16[12,32,128]{2,1,0:T(8,128)(2,1)S(1)}, u32[]{:S(2)}, u32[]{:S(2)}) collective-permute-start(bf16[12,32,128]{2,1,0:T(8,128)(2,1)} %get-tuple-element.31), channel_id=1, source_target_pairs={{0,24},{1,25},{2,26},{3,27},{4,28},{5,29},{6,30},{7,31},{8,0},{9,1... | collective-permute-start | bytes 294920 | tf_op jit(solution)/shard_map/ppermute | solution.py:39
  21.2 1.8 %collective-permute-done.10 = bf16[12,32,128]{2,1,0:T(8,128)(2,1)S(1)} collective-permute-done((bf16[12,32,128]{2,1,0:T(8,128)(2,1)}, bf16[12,32,128]{2,1,0:T(8,128)(2,1)S(1)}, u32[]{:S(2)}, u32[]{:S(2)}) %collective-permute-start.10) | collective-permute-done | bytes 98336 | tf_op jit(solution)/shard_map/ppermute | solution.py:39
  23.0 1.0 collective-permute-done.9
  24.0 0.9 pad_maximum_fusion.1.refs_4_
  24.9 3.0 %collective-permute-start.19 = (bf16[4,12,32,128]{3,2,1,0:T(8,128)(2,1)S(1)}, bf16[4,12,32,128]{3,2,1,0:T(8,128)(2,1)S(1)}, u32[]{:S(2)}, u32[]{:S(2)}) collective-permute-start(bf16[4,12,32,128]{3,2,1,0:T(8,128)(2,1)S(1)} %pad_maximum_fusion.1.refs_4_), channel_id=1, source_target_pairs={{0,1},{1,0},{2,3},{3,2},{4,5},{5,4},{6,7},{7,6},{8,9},{9,8},{10,11... | collective-permute-start | bytes 1179656 | tf_op jit(solution)/shard_map/ppermute | solution.py:39
  28.0 2.2 %collective-permute-start.14 = (bf16[4,12,32,128]{3,2,1,0:T(8,128)(2,1)S(1)}, bf16[4,12,32,128]{3,2,1,0:T(8,128)(2,1)S(1)}, u32[]{:S(2)}, u32[]{:S(2)}) collective-permute-start(bf16[4,12,32,128]{3,2,1,0:T(8,128)(2,1)S(1)} %pad_maximum_fusion.1.refs_4_), channel_id=1, source_target_pairs={{0,24},{1,25},{2,26},{3,27},{4,28},{5,29},{6,30},{7,31},{8,0},{9,1... | collective-permute-start | bytes 1179656 | tf_op jit(solution)/shard_map/ppermute | solution.py:39
  30.2 1.0 collective-permute-start.13
  31.2 0.0 collective-permute-start.12
  31.2 1.9 %collective-permute-start.4 = (bf16[12,32,128]{2,1,0:T(8,128)(2,1)}, bf16[12,32,128]{2,1,0:T(8,128)(2,1)S(1)}, u32[]{:S(2)}, u32[]{:S(2)}) collective-permute-start(bf16[12,32,128]{2,1,0:T(8,128)(2,1)} %get-tuple-element.31), channel_id=1, source_target_pairs={{0,16},{1,17},{2,18},{3,19},{4,20},{5,21},{6,22},{7,23},{8,24},{9,... | collective-permute-start | bytes 294920 | tf_op jit(solution)/shard_map/ppermute | solution.py:39
  33.2 19.4 %collective-permute-done.4 = bf16[12,32,128]{2,1,0:T(8,128)(2,1)S(1)} collective-permute-done((bf16[12,32,128]{2,1,0:T(8,128)(2,1)}, bf16[12,32,128]{2,1,0:T(8,128)(2,1)S(1)}, u32[]{:S(2)}, u32[]{:S(2)}) %collective-permute-start.4) | collective-permute-done | bytes 98336 | tf_op jit(solution)/shard_map/ppermute | solution.py:39
  52.6 4.9 %collective-permute-done.3 = bf16[12,32,128]{2,1,0:T(8,128)(2,1)S(1)} collective-permute-done((bf16[12,32,128]{2,1,0:T(8,128)(2,1)}, bf16[12,32,128]{2,1,0:T(8,128)(2,1)S(1)}, u32[]{:S(2)}, u32[]{:S(2)}) %collective-permute-start.3) | collective-permute-done | bytes 98336 | tf_op jit(solution)/shard_map/ppermute | solution.py:39
  57.5 0.9 pad_maximum_fusion.refs_0_
  58.4 2.4 %collective-permute-start.15 = (bf16[4,12,32,128]{3,2,1,0:T(8,128)(2,1)S(1)}, bf16[4,12,32,128]{3,2,1,0:T(8,128)(2,1)S(1)}, u32[]{:S(2)}, u32[]{:S(2)}) collective-permute-start(bf16[4,12,32,128]{3,2,1,0:T(8,128)(2,1)S(1)} %pad_maximum_fusion.refs_0_), channel_id=1, source_target_pairs={{0,1},{1,0},{2,3},{3,2},{4,5},{5,4},{6,7},{7,6},{8,9},{9,8},{10,11... | collective-permute-start | bytes 1179656 | tf_op jit(solution)/shard_map/ppermute | solution.py:39
  60.9 0.3 collective-permute-start.8
  61.2 0.3 collective-permute-start.7
  61.5 0.9 collective-permute-start.6
  62.5 0.7 collective-permute-start.22
  63.1 0.1 collective-permute-start.21
  63.2 8.3 %collective-permute-done.8.refs_3_ = bf16[4,12,32,128]{3,2,1,0:T(8,128)(2,1)} collective-permute-done((bf16[4,12,32,128]{3,2,1,0:T(8,128)(2,1)S(1)}, bf16[4,12,32,128]{3,2,1,0:T(8,128)(2,1)}, u32[]{:S(2)}, u32[]{:S(2)}) %collective-permute-start.8) | collective-permute-done | bytes 393248 | tf_op jit(solution)/shard_map/ppermute | solution.py:39
  71.6 1.5 collective-permute-start.20
  73.1 0.0 collective-permute-done.7.refs_2_
  73.1 2.1 %collective-permute-start.18 = (bf16[4,12,32,128]{3,2,1,0:T(8,128)(2,1)}, bf16[4,12,32,128]{3,2,1,0:T(8,128)(2,1)}, u32[]{:S(2)}, u32[]{:S(2)}) collective-permute-start(bf16[4,12,32,128]{3,2,1,0:T(8,128)(2,1)} %collective-permute-done.8.refs_3_), channel_id=1, source_target_pairs={{0,1},{1,0},{2,3},{3,2},{4,5},{5,4},{6,7},{7,6},{8,9},{9,8},{10,11... | collective-permute-start | bytes 1179656 | tf_op jit(solution)/shard_map/ppermute | solution.py:39
  75.2 7.1 %collective-permute-done.6.refs_1_ = bf16[4,12,32,128]{3,2,1,0:T(8,128)(2,1)} collective-permute-done((bf16[4,12,32,128]{3,2,1,0:T(8,128)(2,1)S(1)}, bf16[4,12,32,128]{3,2,1,0:T(8,128)(2,1)}, u32[]{:S(2)}, u32[]{:S(2)}) %collective-permute-start.6) | collective-permute-done | bytes 393248 | tf_op jit(solution)/shard_map/ppermute | solution.py:39
  82.3 0.5 collective-permute-start.17
  82.8 0.8 copy-done.9
  83.5 0.0 collective-permute-start.16
  83.5 3.5 %shard_map.122 = (bf16[2,512,1024]{2,1,0:T(8,128)(2,1)}, f32[64,1024]{1,0:T(8,128)}) custom-call(bf16[2,512,1024]{2,1,0:T(8,128)(2,1)} %hidden.2), custom_call_target="tpu_custom_call" | custom-call | flops 30000000 | bytes 12000000 | tf_op jit(solution)/shard_map/pallas_call | solution.py:73
  87.0 4.0 %shard_map.123 = (bf16[2,512,1280]{2,1,0:T(8,128)(2,1)}, f32[64,1280]{1,0:T(8,128)}) custom-call(bf16[2,512,1280]{2,1,0:T(8,128)(2,1)} %hidden.3), custom_call_target="tpu_custom_call" | custom-call | flops 30000000 | bytes 12000000 | tf_op jit(solution)/shard_map/pallas_call | solution.py:73
  91.1 14.7 %attend.1 = (bf16[64,640]{1,0:T(8,128)(2,1)S(1)}, bf16[64,640]{1,0:T(8,128)(2,1)S(1)}, bf16[64,640]{1,0:T(8,128)(2,1)S(1)}, bf16[64,640]{1,0:T(8,128)(2,1)S(1)},...) custom-call(s32[64]{0:T(128)} %frames_valid.3, s32[64]{0:T(128)} %slot_clip.1, ...), custom_call_target="tpu_custom_call" | custom-call | flops 8000000000 | bytes 12000000 | tf_op jit(solution)/shard_map/attend/pallas_call | solution.py:360
  105.8 2.6 %collective-permute-start.25 = (bf16[128,512]{1,0:T(8,128)(2,1)S(1)}, bf16[128,512]{1,0:T(8,128)(2,1)S(1)}, u32[]{:S(2)}, u32[]{:S(2)}) collective-permute-start(bf16[128,512]{1,0:T(8,128)(2,1)S(1)} %get-tuple-element.35.refs_0_), channel_id=1, source_target_pairs={{0,96},{32,0},{64,32},{96,64},{1,97},{33,1},{65,33},{97,65},{2,98}... | collective-permute-start | bytes 393224 | tf_op jit(solution)/shard_map/ppermute | solution.py:43
  108.3 1.7 collective-permute-start.27
  110.1 0.9 collective-permute-start.28
  111.0 2.4 %collective-permute-start.24 = (bf16[128,512]{1,0:T(8,128)(2,1)S(1)}, bf16[128,512]{1,0:T(8,128)(2,1)S(1)}, u32[]{:S(2)}, u32[]{:S(2)}) collective-permute-start(bf16[128,512]{1,0:T(8,128)(2,1)S(1)} %get-tuple-element.35.refs_0_), channel_id=1, source_target_pairs={{0,64},{32,96},{64,0},{96,32},{1,65},{33,97},{65,1},{97,33},{2,66}... | collective-permute-start | bytes 393224 | tf_op jit(solution)/shard_map/ppermute | solution.py:43
  113.4 0.6 collective-permute-done.26.refs_1_
  113.9 0.4 collective-permute-done.27.refs_2_
  114.3 0.5 collective-permute-done.28.refs_3_
  114.8 3.8 %slopes.1 = (bf16[64,640]{1,0:T(8,128)(2,1)S(1)}, bf16[64,640]{1,0:T(8,128)(2,1)S(1)}, bf16[64,640]{1,0:T(8,128)(2,1)S(1)}, bf16[64,640]{1,0:T(8,128)(2,1)S(1)}) custom-call(s32[64]{0:T(128)} %frames_valid.3, bf16[64,640]{1,0:T(8,128)(2,1)S(1)} %get-tuple-element.36.refs_0_, bf16[64,640]{1,0:T(8,128)(2,1)S(1)} %collective-permute-done.26.refs_1_, ...), custom_call_target="tpu_custom_call" | custom-call | tf_op jit(solution)/shard_map/slopes/pallas_call | solution.py:450
  118.7 1.4 collective-permute-start.29
  120.1 3.5 %collective-permute-start.30 = (bf16[64,640]{1,0:T(8,128)(2,1)S(1)}, bf16[64,640]{1,0:T(8,128)(2,1)S(1)}, u32[]{:S(2)}, u32[]{:S(2)}) collective-permute-start(bf16[64,640]{1,0:T(8,128)(2,1)S(1)} %get-tuple-element.46), channel_id=1, source_target_pairs={{0,64},{32,96},{64,0},{96,32},{1,65},{33,97},{65,1},{97,33},{2,66}... | collective-permute-start | bytes 245768 | tf_op jit(solution)/shard_map/ppermute | solution.py:43
  123.6 1.5 collective-permute-start.23
  125.1 2.9 %collective-permute-start.32 = (bf16[64,640]{1,0:T(8,128)(2,1)S(1)}, bf16[64,640]{1,0:T(8,128)(2,1)S(1)}, u32[]{:S(2)}, u32[]{:S(2)}) collective-permute-start(bf16[64,640]{1,0:T(8,128)(2,1)S(1)} %get-tuple-element.44.refs_4_), channel_id=1, source_target_pairs={{0,1},{1,0},{2,3},{3,2},{4,5},{5,4},{6,7},{7,6},{8,9},{9,8},{10,11... | collective-permute-start | bytes 245768 | tf_op jit(solution)/shard_map/ppermute | solution.py:39
  128.0 0.1 collective-permute-start.33
  128.1 2.2 %collective-permute-start.34 = (bf16[64,640]{1,0:T(8,128)(2,1)S(1)}, bf16[64,640]{1,0:T(8,128)(2,1)S(1)}, u32[]{:S(2)}, u32[]{:S(2)}) collective-permute-start(bf16[64,640]{1,0:T(8,128)(2,1)S(1)} %collective-permute-done.30.refs_6_), channel_id=1, source_target_pairs={{0,1},{1,0},{2,3},{3,2},{4,5},{5,4},{6,7},{7,6},{8,9},{9,8},{10,11... | collective-permute-start | bytes 245768 | tf_op jit(solution)/shard_map/ppermute | solution.py:39
  130.2 0.2 collective-permute-start.35
  130.4 0.8 collective-permute-done.34.refs_10_
  131.1 0.4 collective-permute-done.35.refs_11_
  131.5 0.5 outer.1
  132.0 13.9 %all_to_all.10.x = f32[16,72,128]{2,1,0:T(8,128)S(1)} all-to-all(f32[16,72,128]{2,1,0:T(8,128)S(1)} %outer.1), channel_id=1, replica_groups={{0,2,4,6,8,10,12,14,16,18,20,22,24,26,28,30},{1,3,5,7,9,11,13,15,17,19,..., dimensions={0} | all-to-all | bytes 1179648 | tf_op jit(solution)/shard_map/all_to_all | solution.py:585
  145.9 0.1 reduce_parts.1
  146.0 23.1 %all_to_all.11 = bf16[64,72,128]{2,1,0:T(8,128)(2,1)S(1)} all-to-all(bf16[64,72,128]{2,1,0:T(8,128)(2,1)S(1)} %reduce_parts.1), channel_id=1, replica_groups={{0,2,4,6,8,10,12,14,16,18,20,22,24,26,28,30,32,34,36,38,40,42,44,46,48,..., dimensions={0} | all-to-all | bytes 2359296 | tf_op jit(solution)/shard_map/all_to_all | solution.py:588
  169.1 3.7 %collective-permute-start.36 = (bf16[4,16,72,128]{3,2,1,0:T(8,128)(2,1)S(1)}, bf16[4,16,72,128]{3,2,1,0:T(8,128)(2,1)S(1)}, u32[]{:S(2)}, u32[]{:S(2)}) collective-permute-start(bf16[4,16,72,128]{3,2,1,0:T(8,128)(2,1)S(1)} %bitcast.13), channel_id=1, source_target_pairs={{0,1},{1,0},{2,3},{3,2},{4,5},{5,4},{6,7},{7,6},{8,9},{9,8},{10,11... | collective-permute-start | bytes 3538952 | tf_op jit(solution)/shard_map/ppermute | solution.py:39
  172.9 1.5 place_own.1
  174.4 0.9 collective-permute-done.36.piece
  175.3 1.5 place_partner.1
  (44 shorter events, 0.1 us)
Async XLA Ops:
  1.8 7.8 %collective-permute-start = (bf16[16,32,128]{2,1,0:T(8,128)(2,1)S(1)}, bf16[16,32,128]{2,1,0:T(8,128)(2,1)S(1)}, u32[]{:S(2)}, u32[]{:S(2)}) collective-permute-start(bf16[16,32,128]{2,1,0:T(8,128)(2,1)S(1)} %get-tuple-element.28), channel_id=1, source_target_pairs={{0,8},{1,9},{2,10},{3,11},{4,12},{5,13},{6,14},{7,15},{8,16},{9,17... | collective-permute-start | bytes 393224 | tf_op jit(solution)/shard_map/ppermute | solution.py:39
  4.4 9.0 %collective-permute-start.1 = (bf16[16,32,128]{2,1,0:T(8,128)(2,1)S(1)}, bf16[16,32,128]{2,1,0:T(8,128)(2,1)S(1)}, u32[]{:S(2)}, u32[]{:S(2)}) collective-permute-start(bf16[16,32,128]{2,1,0:T(8,128)(2,1)S(1)} %get-tuple-element.29), channel_id=1, source_target_pairs={{0,16},{1,17},{2,18},{3,19},{4,20},{5,21},{6,22},{7,23},{8,24},{9,... | collective-permute-start | bytes 393224 | tf_op jit(solution)/shard_map/ppermute | solution.py:39
  7.7 5.7 %collective-permute-start.2 = (bf16[16,32,128]{2,1,0:T(8,128)(2,1)S(1)}, bf16[16,32,128]{2,1,0:T(8,128)(2,1)S(1)}, u32[]{:S(2)}, u32[]{:S(2)}) collective-permute-start(bf16[16,32,128]{2,1,0:T(8,128)(2,1)S(1)} %get-tuple-element.30), channel_id=1, source_target_pairs={{0,24},{1,25},{2,26},{3,27},{4,28},{5,29},{6,30},{7,31},{8,0},{9,1... | collective-permute-start | bytes 393224 | tf_op jit(solution)/shard_map/ppermute | solution.py:39
  15.0 6.2 %collective-permute-start.11 = (bf16[12,32,128]{2,1,0:T(8,128)(2,1)}, bf16[12,32,128]{2,1,0:T(8,128)(2,1)S(1)}, u32[]{:S(2)}, u32[]{:S(2)}) collective-permute-start(bf16[12,32,128]{2,1,0:T(8,128)(2,1)} %get-tuple-element.32), channel_id=1, source_target_pairs={{0,6},{1,7},{2,0},{3,1},{4,2},{5,3},{6,4},{7,5},{8,14},{9,15},{10,... | collective-permute-start | bytes 294920 | tf_op jit(solution)/shard_map/ppermute | solution.py:39
  17.7 5.3 %collective-permute-start.10 = (bf16[12,32,128]{2,1,0:T(8,128)(2,1)}, bf16[12,32,128]{2,1,0:T(8,128)(2,1)S(1)}, u32[]{:S(2)}, u32[]{:S(2)}) collective-permute-start(bf16[12,32,128]{2,1,0:T(8,128)(2,1)} %get-tuple-element.32), channel_id=1, source_target_pairs={{0,4},{1,5},{2,6},{3,7},{4,0},{5,1},{6,2},{7,3},{8,12},{9,13},{10,... | collective-permute-start | bytes 294920 | tf_op jit(solution)/shard_map/ppermute | solution.py:39
  18.1 5.9 %collective-permute-start.9 = (bf16[12,32,128]{2,1,0:T(8,128)(2,1)}, bf16[12,32,128]{2,1,0:T(8,128)(2,1)S(1)}, u32[]{:S(2)}, u32[]{:S(2)}) collective-permute-start(bf16[12,32,128]{2,1,0:T(8,128)(2,1)} %get-tuple-element.32), channel_id=1, source_target_pairs={{0,2},{1,3},{2,4},{3,5},{4,6},{5,7},{6,0},{7,1},{8,10},{9,11},{10,... | collective-permute-start | bytes 294920 | tf_op jit(solution)/shard_map/ppermute | solution.py:39
  18.8 12.5 %collective-permute-start.5 = (bf16[12,32,128]{2,1,0:T(8,128)(2,1)}, bf16[12,32,128]{2,1,0:T(8,128)(2,1)S(1)}, u32[]{:S(2)}, u32[]{:S(2)}) collective-permute-start(bf16[12,32,128]{2,1,0:T(8,128)(2,1)} %get-tuple-element.31), channel_id=1, source_target_pairs={{0,24},{1,25},{2,26},{3,27},{4,28},{5,29},{6,30},{7,31},{8,0},{9,1... | collective-permute-start | bytes 294920 | tf_op jit(solution)/shard_map/ppermute | solution.py:39
  24.9 66.0 %copy-start.2 = (bf16[4,12,32,128]{3,2,1,0:T(8,128)(2,1)}, bf16[4,12,32,128]{3,2,1,0:T(8,128)(2,1)S(1)}, u32[]{:S(2)}) copy-start(bf16[4,12,32,128]{3,2,1,0:T(8,128)(2,1)S(1)} %pad_maximum_fusion.1.refs_4_) | copy-start | bytes 1179652
  24.9 36.0 %collective-permute-start.19 = (bf16[4,12,32,128]{3,2,1,0:T(8,128)(2,1)S(1)}, bf16[4,12,32,128]{3,2,1,0:T(8,128)(2,1)S(1)}, u32[]{:S(2)}, u32[]{:S(2)}) collective-permute-start(bf16[4,12,32,128]{3,2,1,0:T(8,128)(2,1)S(1)} %pad_maximum_fusion.1.refs_4_), channel_id=1, source_target_pairs={{0,1},{1,0},{2,3},{3,2},{4,5},{5,4},{6,7},{7,6},{8,9},{9,8},{10,11... | collective-permute-start | bytes 1179656 | tf_op jit(solution)/shard_map/ppermute | solution.py:39
  28.0 33.2 %collective-permute-start.14 = (bf16[4,12,32,128]{3,2,1,0:T(8,128)(2,1)S(1)}, bf16[4,12,32,128]{3,2,1,0:T(8,128)(2,1)S(1)}, u32[]{:S(2)}, u32[]{:S(2)}) collective-permute-start(bf16[4,12,32,128]{3,2,1,0:T(8,128)(2,1)S(1)} %pad_maximum_fusion.1.refs_4_), channel_id=1, source_target_pairs={{0,24},{1,25},{2,26},{3,27},{4,28},{5,29},{6,30},{7,31},{8,0},{9,1... | collective-permute-start | bytes 1179656 | tf_op jit(solution)/shard_map/ppermute | solution.py:39
  30.2 31.3 %collective-permute-start.13 = (bf16[4,12,32,128]{3,2,1,0:T(8,128)(2,1)S(1)}, bf16[4,12,32,128]{3,2,1,0:T(8,128)(2,1)S(1)}, u32[]{:S(2)}, u32[]{:S(2)}) collective-permute-start(bf16[4,12,32,128]{3,2,1,0:T(8,128)(2,1)S(1)} %pad_maximum_fusion.1.refs_4_), channel_id=1, source_target_pairs={{0,16},{1,17},{2,18},{3,19},{4,20},{5,21},{6,22},{7,23},{8,24},{9,... | collective-permute-start | bytes 1179656 | tf_op jit(solution)/shard_map/ppermute | solution.py:39
  31.2 31.2 %collective-permute-start.12 = (bf16[4,12,32,128]{3,2,1,0:T(8,128)(2,1)S(1)}, bf16[4,12,32,128]{3,2,1,0:T(8,128)(2,1)S(1)}, u32[]{:S(2)}, u32[]{:S(2)}) collective-permute-start(bf16[4,12,32,128]{3,2,1,0:T(8,128)(2,1)S(1)} %pad_maximum_fusion.1.refs_4_), channel_id=1, source_target_pairs={{0,8},{1,9},{2,10},{3,11},{4,12},{5,13},{6,14},{7,15},{8,16},{9,17... | collective-permute-start | bytes 1179656 | tf_op jit(solution)/shard_map/ppermute | solution.py:39
  31.2 21.4 %collective-permute-start.4 = (bf16[12,32,128]{2,1,0:T(8,128)(2,1)}, bf16[12,32,128]{2,1,0:T(8,128)(2,1)S(1)}, u32[]{:S(2)}, u32[]{:S(2)}) collective-permute-start(bf16[12,32,128]{2,1,0:T(8,128)(2,1)} %get-tuple-element.31), channel_id=1, source_target_pairs={{0,16},{1,17},{2,18},{3,19},{4,20},{5,21},{6,22},{7,23},{8,24},{9,... | collective-permute-start | bytes 294920 | tf_op jit(solution)/shard_map/ppermute | solution.py:39
  52.6 4.9 %collective-permute-start.3 = (bf16[12,32,128]{2,1,0:T(8,128)(2,1)}, bf16[12,32,128]{2,1,0:T(8,128)(2,1)S(1)}, u32[]{:S(2)}, u32[]{:S(2)}) collective-permute-start(bf16[12,32,128]{2,1,0:T(8,128)(2,1)} %get-tuple-element.31), channel_id=1, source_target_pairs={{0,8},{1,9},{2,10},{3,11},{4,12},{5,13},{6,14},{7,15},{8,16},{9,17... | collective-permute-start | bytes 294920 | tf_op jit(solution)/shard_map/ppermute | solution.py:39
  58.4 32.5 %copy-start.3 = (bf16[4,12,32,128]{3,2,1,0:T(8,128)(2,1)}, bf16[4,12,32,128]{3,2,1,0:T(8,128)(2,1)S(1)}, u32[]{:S(2)}) copy-start(bf16[4,12,32,128]{3,2,1,0:T(8,128)(2,1)S(1)} %pad_maximum_fusion.refs_0_) | copy-start | bytes 1179652
  58.4 4.7 %collective-permute-start.15 = (bf16[4,12,32,128]{3,2,1,0:T(8,128)(2,1)S(1)}, bf16[4,12,32,128]{3,2,1,0:T(8,128)(2,1)S(1)}, u32[]{:S(2)}, u32[]{:S(2)}) collective-permute-start(bf16[4,12,32,128]{3,2,1,0:T(8,128)(2,1)S(1)} %pad_maximum_fusion.refs_0_), channel_id=1, source_target_pairs={{0,1},{1,0},{2,3},{3,2},{4,5},{5,4},{6,7},{7,6},{8,9},{9,8},{10,11... | collective-permute-start | bytes 1179656 | tf_op jit(solution)/shard_map/ppermute | solution.py:39
  60.9 30.1 %copy-start.4 = (bf16[4,12,32,128]{3,2,1,0:T(8,128)(2,1)}, bf16[4,12,32,128]{3,2,1,0:T(8,128)(2,1)S(1)}, u32[]{:S(2)}) copy-start(bf16[4,12,32,128]{3,2,1,0:T(8,128)(2,1)S(1)} %collective-permute-done.19.refs_12_) | copy-start | bytes 1179652
  60.9 10.7 %collective-permute-start.8 = (bf16[4,12,32,128]{3,2,1,0:T(8,128)(2,1)S(1)}, bf16[4,12,32,128]{3,2,1,0:T(8,128)(2,1)}, u32[]{:S(2)}, u32[]{:S(2)}) collective-permute-start(bf16[4,12,32,128]{3,2,1,0:T(8,128)(2,1)S(1)} %pad_maximum_fusion.refs_0_), channel_id=1, source_target_pairs={{0,6},{1,7},{2,0},{3,1},{4,2},{5,3},{6,4},{7,5},{8,14},{9,15},{10,... | collective-permute-start | bytes 1179656 | tf_op jit(solution)/shard_map/ppermute | solution.py:39
  61.2 29.8 %copy-start.5 = (bf16[4,12,32,128]{3,2,1,0:T(8,128)(2,1)}, bf16[4,12,32,128]{3,2,1,0:T(8,128)(2,1)S(1)}, u32[]{:S(2)}) copy-start(bf16[4,12,32,128]{3,2,1,0:T(8,128)(2,1)S(1)} %collective-permute-done.14.refs_7_) | copy-start | bytes 1179652
  61.2 11.9 %collective-permute-start.7 = (bf16[4,12,32,128]{3,2,1,0:T(8,128)(2,1)S(1)}, bf16[4,12,32,128]{3,2,1,0:T(8,128)(2,1)}, u32[]{:S(2)}, u32[]{:S(2)}) collective-permute-start(bf16[4,12,32,128]{3,2,1,0:T(8,128)(2,1)S(1)} %pad_maximum_fusion.refs_0_), channel_id=1, source_target_pairs={{0,4},{1,5},{2,6},{3,7},{4,0},{5,1},{6,2},{7,3},{8,12},{9,13},{10,... | collective-permute-start | bytes 1179656 | tf_op jit(solution)/shard_map/ppermute | solution.py:39
  61.5 29.5 %copy-start.6 = (bf16[4,12,32,128]{3,2,1,0:T(8,128)(2,1)}, bf16[4,12,32,128]{3,2,1,0:T(8,128)(2,1)S(1)}, u32[]{:S(2)}) copy-start(bf16[4,12,32,128]{3,2,1,0:T(8,128)(2,1)S(1)} %collective-permute-done.13.refs_6_) | copy-start | bytes 1179652
  61.5 20.7 %collective-permute-start.6 = (bf16[4,12,32,128]{3,2,1,0:T(8,128)(2,1)S(1)}, bf16[4,12,32,128]{3,2,1,0:T(8,128)(2,1)}, u32[]{:S(2)}, u32[]{:S(2)}) collective-permute-start(bf16[4,12,32,128]{3,2,1,0:T(8,128)(2,1)S(1)} %pad_maximum_fusion.refs_0_), channel_id=1, source_target_pairs={{0,2},{1,3},{2,4},{3,5},{4,6},{5,7},{6,0},{7,1},{8,10},{9,11},{10,... | collective-permute-start | bytes 1179656 | tf_op jit(solution)/shard_map/ppermute | solution.py:39
  62.5 28.5 %copy-start.7 = (bf16[4,12,32,128]{3,2,1,0:T(8,128)(2,1)}, bf16[4,12,32,128]{3,2,1,0:T(8,128)(2,1)S(1)}, u32[]{:S(2)}) copy-start(bf16[4,12,32,128]{3,2,1,0:T(8,128)(2,1)S(1)} %collective-permute-done.12.refs_5_) | copy-start | bytes 1179652
  62.5 20.3 %collective-permute-start.22 = (bf16[4,12,32,128]{3,2,1,0:T(8,128)(2,1)S(1)}, bf16[4,12,32,128]{3,2,1,0:T(8,128)(2,1)S(1)}, u32[]{:S(2)}, u32[]{:S(2)}) collective-permute-start(bf16[4,12,32,128]{3,2,1,0:T(8,128)(2,1)S(1)} %collective-permute-done.14.refs_7_), channel_id=1, source_target_pairs={{0,1},{1,0},{2,3},{3,2},{4,5},{5,4},{6,7},{7,6},{8,9},{9,8},{10,11... | collective-permute-start | bytes 1179656 | tf_op jit(solution)/shard_map/ppermute | solution.py:39
  63.1 27.9 %copy-start.8 = (bf16[4,12,32,128]{3,2,1,0:T(8,128)(2,1)}, bf16[4,12,32,128]{3,2,1,0:T(8,128)(2,1)S(1)}, u32[]{:S(2)}) copy-start(bf16[4,12,32,128]{3,2,1,0:T(8,128)(2,1)S(1)} %collective-permute-done.15.refs_8_) | copy-start | bytes 1179652
  63.1 27.9 %collective-permute-start.21 = (bf16[4,12,32,128]{3,2,1,0:T(8,128)(2,1)S(1)}, bf16[4,12,32,128]{3,2,1,0:T(8,128)(2,1)}, u32[]{:S(2)}, u32[]{:S(2)}) collective-permute-start(bf16[4,12,32,128]{3,2,1,0:T(8,128)(2,1)S(1)} %collective-permute-done.13.refs_6_), channel_id=1, source_target_pairs={{0,1},{1,0},{2,3},{3,2},{4,5},{5,4},{6,7},{7,6},{8,9},{9,8},{10,11... | collective-permute-start | bytes 1179656 | tf_op jit(solution)/shard_map/ppermute | solution.py:39
  71.6 19.5 %collective-permute-start.20 = (bf16[4,12,32,128]{3,2,1,0:T(8,128)(2,1)S(1)}, bf16[4,12,32,128]{3,2,1,0:T(8,128)(2,1)}, u32[]{:S(2)}, u32[]{:S(2)}) collective-permute-start(bf16[4,12,32,128]{3,2,1,0:T(8,128)(2,1)S(1)} %collective-permute-done.12.refs_5_), channel_id=1, source_target_pairs={{0,1},{1,0},{2,3},{3,2},{4,5},{5,4},{6,7},{7,6},{8,9},{9,8},{10,11... | collective-permute-start | bytes 1179656 | tf_op jit(solution)/shard_map/ppermute | solution.py:39
  73.1 17.9 %collective-permute-start.18 = (bf16[4,12,32,128]{3,2,1,0:T(8,128)(2,1)}, bf16[4,12,32,128]{3,2,1,0:T(8,128)(2,1)}, u32[]{:S(2)}, u32[]{:S(2)}) collective-permute-start(bf16[4,12,32,128]{3,2,1,0:T(8,128)(2,1)} %collective-permute-done.8.refs_3_), channel_id=1, source_target_pairs={{0,1},{1,0},{2,3},{3,2},{4,5},{5,4},{6,7},{7,6},{8,9},{9,8},{10,11... | collective-permute-start | bytes 1179656 | tf_op jit(solution)/shard_map/ppermute | solution.py:39
  82.3 8.8 %collective-permute-start.17 = (bf16[4,12,32,128]{3,2,1,0:T(8,128)(2,1)}, bf16[4,12,32,128]{3,2,1,0:T(8,128)(2,1)}, u32[]{:S(2)}, u32[]{:S(2)}) collective-permute-start(bf16[4,12,32,128]{3,2,1,0:T(8,128)(2,1)} %collective-permute-done.7.refs_2_), channel_id=1, source_target_pairs={{0,1},{1,0},{2,3},{3,2},{4,5},{5,4},{6,7},{7,6},{8,9},{9,8},{10,11... | collective-permute-start | bytes 1179656 | tf_op jit(solution)/shard_map/ppermute | solution.py:39
  82.8 0.8 copy-start.9
  83.5 7.6 %collective-permute-start.16 = (bf16[4,12,32,128]{3,2,1,0:T(8,128)(2,1)}, bf16[4,12,32,128]{3,2,1,0:T(8,128)(2,1)}, u32[]{:S(2)}, u32[]{:S(2)}) collective-permute-start(bf16[4,12,32,128]{3,2,1,0:T(8,128)(2,1)} %collective-permute-done.6.refs_1_), channel_id=1, source_target_pairs={{0,1},{1,0},{2,3},{3,2},{4,5},{5,4},{6,7},{7,6},{8,9},{9,8},{10,11... | collective-permute-start | bytes 1179656 | tf_op jit(solution)/shard_map/ppermute | solution.py:39
  91.1 23.8 %copy-start = (f32[64,1280]{1,0:T(8,128)S(1)}, f32[64,1280]{1,0:T(8,128)}, u32[]{:S(2)}) copy-start(f32[64,1280]{1,0:T(8,128)} %get-tuple-element.41.refs_7_) | copy-start | bytes 983044
  91.1 23.8 %copy-start.1 = (f32[64,1024]{1,0:T(8,128)S(1)}, f32[64,1024]{1,0:T(8,128)}, u32[]{:S(2)}) copy-start(f32[64,1024]{1,0:T(8,128)} %get-tuple-element.40.refs_6_) | copy-start | bytes 786436
  105.8 17.9 %collective-permute-start.25 = (bf16[128,512]{1,0:T(8,128)(2,1)S(1)}, bf16[128,512]{1,0:T(8,128)(2,1)S(1)}, u32[]{:S(2)}, u32[]{:S(2)}) collective-permute-start(bf16[128,512]{1,0:T(8,128)(2,1)S(1)} %get-tuple-element.35.refs_0_), channel_id=1, source_target_pairs={{0,96},{32,0},{64,32},{96,64},{1,97},{33,1},{65,33},{97,65},{2,98}... | collective-permute-start | bytes 393224 | tf_op jit(solution)/shard_map/ppermute | solution.py:43
  108.3 5.6 %collective-permute-start.26 = (bf16[64,640]{1,0:T(8,128)(2,1)S(1)}, bf16[64,640]{1,0:T(8,128)(2,1)S(1)}, u32[]{:S(2)}, u32[]{:S(2)}) collective-permute-start(bf16[64,640]{1,0:T(8,128)(2,1)S(1)} %get-tuple-element.37), channel_id=1, source_target_pairs={{0,32},{32,64},{64,96},{96,0},{1,33},{33,65},{65,97},{97,1},{2,34}... | collective-permute-start | bytes 245768 | tf_op jit(solution)/shard_map/ppermute | solution.py:43
  108.3 6.0 %collective-permute-start.27 = (bf16[64,640]{1,0:T(8,128)(2,1)S(1)}, bf16[64,640]{1,0:T(8,128)(2,1)S(1)}, u32[]{:S(2)}, u32[]{:S(2)}) collective-permute-start(bf16[64,640]{1,0:T(8,128)(2,1)S(1)} %get-tuple-element.38), channel_id=1, source_target_pairs={{0,64},{32,96},{64,0},{96,32},{1,65},{33,97},{65,1},{97,33},{2,66}... | collective-permute-start | bytes 245768 | tf_op jit(solution)/shard_map/ppermute | solution.py:43
  110.1 4.8 %collective-permute-start.28 = (bf16[64,640]{1,0:T(8,128)(2,1)S(1)}, bf16[64,640]{1,0:T(8,128)(2,1)S(1)}, u32[]{:S(2)}, u32[]{:S(2)}) collective-permute-start(bf16[64,640]{1,0:T(8,128)(2,1)S(1)} %get-tuple-element.39), channel_id=1, source_target_pairs={{0,96},{32,0},{64,32},{96,64},{1,97},{33,1},{65,33},{97,65},{2,98}... | collective-permute-start | bytes 245768 | tf_op jit(solution)/shard_map/ppermute | solution.py:43
  111.0 14.1 %collective-permute-start.24 = (bf16[128,512]{1,0:T(8,128)(2,1)S(1)}, bf16[128,512]{1,0:T(8,128)(2,1)S(1)}, u32[]{:S(2)}, u32[]{:S(2)}) collective-permute-start(bf16[128,512]{1,0:T(8,128)(2,1)S(1)} %get-tuple-element.35.refs_0_), channel_id=1, source_target_pairs={{0,64},{32,96},{64,0},{96,32},{1,65},{33,97},{65,1},{97,33},{2,66}... | collective-permute-start | bytes 393224 | tf_op jit(solution)/shard_map/ppermute | solution.py:43
  118.7 9.3 %collective-permute-start.29 = (bf16[64,640]{1,0:T(8,128)(2,1)S(1)}, bf16[64,640]{1,0:T(8,128)(2,1)S(1)}, u32[]{:S(2)}, u32[]{:S(2)}) collective-permute-start(bf16[64,640]{1,0:T(8,128)(2,1)S(1)} %get-tuple-element.45), channel_id=1, source_target_pairs={{0,32},{32,64},{64,96},{96,0},{1,33},{33,65},{65,97},{97,1},{2,34}... | collective-permute-start | bytes 245768 | tf_op jit(solution)/shard_map/ppermute | solution.py:43
  120.1 8.0 %collective-permute-start.30 = (bf16[64,640]{1,0:T(8,128)(2,1)S(1)}, bf16[64,640]{1,0:T(8,128)(2,1)S(1)}, u32[]{:S(2)}, u32[]{:S(2)}) collective-permute-start(bf16[64,640]{1,0:T(8,128)(2,1)S(1)} %get-tuple-element.46), channel_id=1, source_target_pairs={{0,64},{32,96},{64,0},{96,32},{1,65},{33,97},{65,1},{97,33},{2,66}... | collective-permute-start | bytes 245768 | tf_op jit(solution)/shard_map/ppermute | solution.py:43
  123.6 6.6 %collective-permute-start.31 = (bf16[64,640]{1,0:T(8,128)(2,1)S(1)}, bf16[64,640]{1,0:T(8,128)(2,1)S(1)}, u32[]{:S(2)}, u32[]{:S(2)}) collective-permute-start(bf16[64,640]{1,0:T(8,128)(2,1)S(1)} %get-tuple-element.47), channel_id=1, source_target_pairs={{0,96},{32,0},{64,32},{96,64},{1,97},{33,1},{65,33},{97,65},{2,98}... | collective-permute-start | bytes 245768 | tf_op jit(solution)/shard_map/ppermute | solution.py:43
  123.6 6.8 %collective-permute-start.23 = (bf16[128,512]{1,0:T(8,128)(2,1)S(1)}, bf16[128,512]{1,0:T(8,128)(2,1)S(1)}, u32[]{:S(2)}, u32[]{:S(2)}) collective-permute-start(bf16[128,512]{1,0:T(8,128)(2,1)S(1)} %get-tuple-element.35.refs_0_), channel_id=1, source_target_pairs={{0,32},{32,64},{64,96},{96,0},{1,33},{33,65},{65,97},{97,1},{2,34}... | collective-permute-start | bytes 393224 | tf_op jit(solution)/shard_map/ppermute | solution.py:43
  125.1 5.3 %collective-permute-start.32 = (bf16[64,640]{1,0:T(8,128)(2,1)S(1)}, bf16[64,640]{1,0:T(8,128)(2,1)S(1)}, u32[]{:S(2)}, u32[]{:S(2)}) collective-permute-start(bf16[64,640]{1,0:T(8,128)(2,1)S(1)} %get-tuple-element.44.refs_4_), channel_id=1, source_target_pairs={{0,1},{1,0},{2,3},{3,2},{4,5},{5,4},{6,7},{7,6},{8,9},{9,8},{10,11... | collective-permute-start | bytes 245768 | tf_op jit(solution)/shard_map/ppermute | solution.py:39
  128.0 2.4 %collective-permute-start.33 = (bf16[64,640]{1,0:T(8,128)(2,1)S(1)}, bf16[64,640]{1,0:T(8,128)(2,1)S(1)}, u32[]{:S(2)}, u32[]{:S(2)}) collective-permute-start(bf16[64,640]{1,0:T(8,128)(2,1)S(1)} %collective-permute-done.29.refs_5_), channel_id=1, source_target_pairs={{0,1},{1,0},{2,3},{3,2},{4,5},{5,4},{6,7},{7,6},{8,9},{9,8},{10,11... | collective-permute-start | bytes 245768 | tf_op jit(solution)/shard_map/ppermute | solution.py:39
  128.1 3.1 %collective-permute-start.34 = (bf16[64,640]{1,0:T(8,128)(2,1)S(1)}, bf16[64,640]{1,0:T(8,128)(2,1)S(1)}, u32[]{:S(2)}, u32[]{:S(2)}) collective-permute-start(bf16[64,640]{1,0:T(8,128)(2,1)S(1)} %collective-permute-done.30.refs_6_), channel_id=1, source_target_pairs={{0,1},{1,0},{2,3},{3,2},{4,5},{5,4},{6,7},{7,6},{8,9},{9,8},{10,11... | collective-permute-start | bytes 245768 | tf_op jit(solution)/shard_map/ppermute | solution.py:39
  130.2 1.3 collective-permute-start.35
  169.1 6.2 %collective-permute-start.36 = (bf16[4,16,72,128]{3,2,1,0:T(8,128)(2,1)S(1)}, bf16[4,16,72,128]{3,2,1,0:T(8,128)(2,1)S(1)}, u32[]{:S(2)}, u32[]{:S(2)}) collective-permute-start(bf16[4,16,72,128]{3,2,1,0:T(8,128)(2,1)S(1)} %bitcast.13), channel_id=1, source_target_pairs={{0,1},{1,0},{2,3},{3,2},{4,5},{5,4},{6,7},{7,6},{8,9},{9,8},{10,11... | collective-permute-start | bytes 3538952 | tf_op jit(solution)/shard_map/ppermute | solution.py:39

commit v7 on v6

--- a/solution.py
+++ b/solution.py
@@ -85,7 +85,7 @@
     )(hidden)
 
 
-def chunk_kernel(qkv_a, qkv_w, *refs):
+def chunk_kernel(qkv_a, qkv_w, latent, raw, *refs):
     outs, chunks = refs[:4], refs[4]
     z = place_of(lax.axis_index("dp"))[0]
     for part in range(4):
@@ -94,72 +94,118 @@
             chunks[part, 8 * t : 8 * t + 3] = qkv_a[:, lane : lane + 128].reshape(3, 32, 128)
         for t in range(10):
             if part < 3:
-                chunks[part, 3 + t + 3 * (t // 5)] = qkv_w[32 * part : 32 * part + 32, 128 * t : 128 * t + 128]
+                rows = qkv_w[32 * part : 32 * part + 32, 128 * t : 128 * t + 128]
             else:
-                chunks[part, 3 + t + 3 * (t // 5)] = jnp.concatenate(
+                rows = jnp.concatenate(
                     [qkv_w[96:120, 128 * t : 128 * t + 128], jnp.zeros((8, 128), bf16)], axis=0
                 )
+            chunks[part, 3 + t + 3 * (t // 5)] = rows
+        raw[8 * part : 8 * part + 8] = chunks[part, :8]
+    for t in range(4):
+        raw[32 + t] = latent[0, 0, :, 128 * t : 128 * t + 128]
     for k in range(4):
-        outs[k][...] = chunks[(z + k) % 4]
-
-
-def weight_chunks(qkv_a, qkv_w):
-    vmem = pl.BlockSpec(memory_space=pltpu.VMEM)
+        outs[k][...] = chunks[(z + k) % 4, pl.ds(8, 8)]
+
+
+def weight_chunks(qkv_a, qkv_w, latent):
+    block = lambda shape: pl.BlockSpec(shape, lambda i: (0,) * len(shape))
     return pl.pallas_call(
         chunk_kernel,
-        out_shape=[pltpu.VMEM((16, 32, 128), bf16)] * 4,
-        in_specs=[vmem, vmem],
-        out_specs=[vmem] * 4,
+        grid=(1,),
+        out_shape=[pltpu.VMEM((36, 32, 128), bf16)] + [pltpu.VMEM((8, 32, 128), bf16)] * 4,
+        in_specs=[
+            block((96, WAVLM_D)),
+            block((120, WHISPER_D)),
+            pl.BlockSpec((1, 1, 32, STU_D), lambda i: (0, 0, lax.axis_index("role"), 0)),
+        ],
+        out_specs=[pl.BlockSpec(memory_space=pltpu.VMEM)] * 5,
         scratch_shapes=[pltpu.VMEM((4, 16, 32, 128), bf16)],
         name="weight_chunks",
-    )(qkv_a, qkv_w)
-
-
-def share_kernel(*refs):
-    parts, latent, outs = refs[:4], refs[4], refs[5:]
+    )(qkv_a, qkv_w, latent)
+
+
+def needed_source(group, part):
     role = lax.axis_index("role")
-    z, y, c = place_of(lax.axis_index("dp"))
+    _, y, c = place_of(lax.axis_index("dp"))
     row = lax.broadcasted_iota(jnp.int32, (32, 128), 0)
     sources = [(role + 4 * ((s - role + 6) % 3)) // 3 for s in range(3)]
-    for g in range(4):
-        if g < 3:
-            column, width = 96 * (2 * y + c) + 32 * g + row, A_COLS
-        else:
-            column, width = 120 * (2 * y + c) + 32 * z + row, W_COLS
-        source = jnp.where(
-            column < width, sources[0], jnp.where(column < 2 * width, sources[1], sources[2])
-        )
-        for half in range(2):
-            for group in (g,) if g < 3 else range(3, 8):
-                value = parts[0][8 * half + group].astype(f32)
-                for k in range(1, 4):
-                    other = parts[k][8 * half + group].astype(f32)
-                    value = jnp.where(source == (z - k + 4) % 4, other, value)
-                outs[half][group] = value.astype(bf16)
-    for half in range(2):
-        for t in range(4):
-            outs[half][8 + t] = latent[half, 0, :, 128 * t : 128 * t + 128]
-
-
-def shares(parts, latent):
-    half = pl.BlockSpec((12, 32, 128), lambda i: (0, 0, 0))
-    return pl.pallas_call(
-        share_kernel,
+    if group < 3:
+        column, width = 96 * (2 * y + c) + 32 * group + row, A_COLS
+    else:
+        column, width = 120 * (2 * y + c) + 32 * part + row, W_COLS
+    return jnp.where(
+        column < width, sources[0], jnp.where(column < 2 * width, sources[1], sources[2])
+    )
+
+
+def choose(parts, index, source, z):
+    value = parts[0][index].astype(f32)
+    for k in range(1, 4):
+        value = jnp.where(source == (z - k + 4) % 4, parts[k][index].astype(f32), value)
+    return value.astype(bf16)
+
+
+def first_kernel(*refs):
+    parts, out = refs[:4], refs[4]
+    z = place_of(lax.axis_index("dp"))[0]
+    for e in range(4):
+        part = (z - e + 4) % 4
+        for group in range(8):
+            if group < 4:
+                source = needed_source(group, part)
+            out[e, group] = choose(parts, 8 * part + group, source, z)
+        out[e, 8:] = parts[e][32:]
+
+
+def second_kernel(*refs):
+    parts, latent, out = refs[:4], refs[4], refs[5]
+    z = place_of(lax.axis_index("dp"))[0]
+    for group in range(8):
+        if group < 4:
+            source = needed_source(group, z)
+        out[group] = choose(parts, group, source, z)
+    for t in range(4):
+        out[8 + t] = latent[0, 0, :, 128 * t : 128 * t + 128]
+
+
+def first_shares(parts):
+    vmem = pl.BlockSpec(memory_space=pltpu.VMEM)
+    return pl.pallas_call(
+        first_kernel,
+        out_shape=pltpu.VMEM((4, 12, 32, 128), bf16),
+        in_specs=[vmem] * 4,
+        out_specs=vmem,
+        name="first_shares",
+    )(*near(*parts))
+
+
+def second_shares(parts, latent):
+    vmem = pl.BlockSpec(memory_space=pltpu.VMEM)
+    return pl.pallas_call(
+        second_kernel,
         grid=(1,),
-        out_shape=[jax.ShapeDtypeStruct((12, 32, 128), bf16)] * 2,
-        in_specs=[pl.BlockSpec(memory_space=pltpu.VMEM)] * 4
-        + [pl.BlockSpec((2, 1, 32, STU_D), lambda i: (0, 0, lax.axis_index("role"), 0))],
-        out_specs=[half] * 2,
-        name="shares",
+        out_shape=pltpu.VMEM((12, 32, 128), bf16),
+        in_specs=[vmem] * 4
+        + [pl.BlockSpec((1, 1, 32, STU_D), lambda i: (1, 0, lax.axis_index("role"), 0))],
+        out_specs=vmem,
+        name="second_shares",
     )(*near(*parts), latent)
 
 
-def spread_line(first, second):
-    got = {}
-    for k in (1, 3, 2):
-        got[k] = dp_send(first, k, 0, 0), dp_send(second, 0, k, 0)
-    lines = [first] + [got[k][0] for k in (1, 2, 3)], [second] + [got[k][1] for k in (1, 2, 3)]
-    return jnp.stack(lines[0]), jnp.stack(lines[1])
+def stack_kernel(*refs):
+    for k in range(4):
+        refs[4][k] = refs[k][...]
+
+
+def stacked(parts):
+    vmem = pl.BlockSpec(memory_space=pltpu.VMEM)
+    return pl.pallas_call(
+        stack_kernel,
+        out_shape=pltpu.VMEM((4,) + parts[0].shape, bf16),
+        in_specs=[vmem] * 4,
+        out_specs=vmem,
+        name="stacked",
+    )(*near(*parts))
 
 
 def spread_cross(first, second):
@@ -562,10 +608,13 @@
     wavlm_head,
     whisper_head,
 ):
-    chunks = weight_chunks(wavlm_qkv.T, whisper_qkv.T)
+    raw, *chunks = weight_chunks(wavlm_qkv.T, whisper_qkv.T, latent)
     chunks = [chunks[0]] + [dp_send(chunks[k], k, 0, 0) for k in (1, 2, 3)]
-    first, second = shares(chunks, latent)
-    first, second = spread_line(first, second)
+    raws = [raw] + [dp_send(raw, k, 0, 0) for k in (1, 2, 3)]
+    second = second_shares(chunks, latent)
+    seconds = [second] + [dp_send(second, 0, k, 0) for k in (1, 2, 3)]
+    first = first_shares(raws)
+    second = stacked(seconds)
     pieces = spread_cross(first, second)
     pieces = pieces + [dp_send(x, 0, 0, 1) for x in pieces]
     norm_a, mean_a = norms(wavlm_hidden)

time: 177 us -> 181 us (1.023)
  waiting for transfers between devices: 51.1 us -> 57.7 us
  other arithmetic: 1.89 us -> 0 us
    ppermute x28, waiting for transfers between devices: 49.6 us -> 56.2 us  [dp_send(): return lax.ppermute(x, 'dp', pairs)]
    another operation x2 -> x0, other arithmetic: 1.89 us -> none  [spread_line(): return (jnp.stack(lines[0]), jnp.stack(lines[1]))]
  transfers between devices with their start and end apart: 37 -> 37, of which waited for: 14 -> 16; matrix products, arithmetic and copies ran while one was open for 1% -> 0% of each run, Pallas kernels for 7% -> 8%
where the time goes in v7:
time: 181 us
  waiting for transfers between devices  57.7 us (32%)
  starting transfers between devices  53.1 us (29%)
  blocking collectives  36.9 us (20%)
  Pallas kernels  31.8 us (18%)
    ppermute x28, waiting for transfers between devices, dp_send(): return lax.ppermute(x, 'dp', pairs)  56.2 us
    ppermute x28, starting transfers between devices, dp_send(): return lax.ppermute(x, 'dp', pairs)  39.1 us
    all_to_all x1, blocking collectives, per_device(): lax.all_to_all(reduce_parts(arrived), ('role', 'dp'), split_axis=0, conca...  22.7 us
    pallas_call x1, Pallas kernels, attend(): pl.pallas_call(attend_kernel, out_shape=[pltpu.VMEM((ROWS, OUT_COLS), bf1...  14.7 us
    all_to_all x1, blocking collectives, per_device(): lax.all_to_all(halves, 'dp', split_axis=0, concat_axis=0, tiled=True, axi...  14.2 us
    ppermute x9, starting transfers between devices, role_send(): return lax.ppermute(x, 'role', [(i, (i + k) % ROLES) for i in range(ROLES)])  14 us
    pallas_call x2, Pallas kernels, norms(): pl.pallas_call(norm_kernel, grid=(2,), out_shape=[jax.ShapeDtypeStruct(hi...  7.41 us
    pallas_call x1, Pallas kernels, slopes(): pl.pallas_call(slope_kernel, out_shape=[pltpu.VMEM((ROWS, OUT_COLS), bf16...  3.83 us
  transfers between devices with their start and end apart: 37, of which 16 were waited for; matrix products, arithmetic and copies ran while one was open for 0% of the time, Pallas kernels for 8%

profile of v7, /device:TPU:1, one launch (start us, length us, event | category | flops | bytes accessed | tf_op | source)
XLA Modules:
  0.0 181.1 jit_solution(7182450562210775330)
XLA Ops:
  0.6 1.2 weight_chunks.1
  1.8 4.6 %collective-permute-start.2 = (bf16[36,32,128]{2,1,0:T(8,128)(2,1)S(1)}, bf16[36,32,128]{2,1,0:T(8,128)(2,1)S(1)}, u32[]{:S(2)}, u32[]{:S(2)}) collective-permute-start(bf16[36,32,128]{2,1,0:T(8,128)(2,1)S(1)} %get-tuple-element.26.refs_0_), channel_id=1, source_target_pairs={{0,24},{1,25},{2,26},{3,27},{4,28},{5,29},{6,30},{7,31},{8,0},{9,1... | collective-permute-start | bytes 884744 | tf_op jit(solution)/shard_map/ppermute | solution.py:39
  6.4 0.0 collective-permute-start.1
  6.4 0.7 collective-permute-start.6
  7.1 2.3 %collective-permute-start.7 = (bf16[8,32,128]{2,1,0:T(8,128)(2,1)S(1)}, bf16[8,32,128]{2,1,0:T(8,128)(2,1)S(1)}, u32[]{:S(2)}, u32[]{:S(2)}) collective-permute-start(bf16[8,32,128]{2,1,0:T(8,128)(2,1)S(1)} %get-tuple-element.29), channel_id=1, source_target_pairs={{0,16},{1,17},{2,18},{3,19},{4,20},{5,21},{6,22},{7,23},{8,24},{9,... | collective-permute-start | bytes 196616 | tf_op jit(solution)/shard_map/ppermute | solution.py:39
  9.4 2.1 %collective-permute-start.8 = (bf16[8,32,128]{2,1,0:T(8,128)(2,1)S(1)}, bf16[8,32,128]{2,1,0:T(8,128)(2,1)S(1)}, u32[]{:S(2)}, u32[]{:S(2)}) collective-permute-start(bf16[8,32,128]{2,1,0:T(8,128)(2,1)S(1)} %get-tuple-element.30), channel_id=1, source_target_pairs={{0,24},{1,25},{2,26},{3,27},{4,28},{5,29},{6,30},{7,31},{8,0},{9,1... | collective-permute-start | bytes 196616 | tf_op jit(solution)/shard_map/ppermute | solution.py:39
  11.5 5.5 %collective-permute-done.6.refs_1_ = bf16[8,32,128]{2,1,0:T(8,128)(2,1)S(1)} collective-permute-done((bf16[8,32,128]{2,1,0:T(8,128)(2,1)S(1)}, bf16[8,32,128]{2,1,0:T(8,128)(2,1)S(1)}, u32[]{:S(2)}, u32[]{:S(2)}) %collective-permute-start.6) | collective-permute-done | bytes 65568 | tf_op jit(solution)/shard_map/ppermute | solution.py:39
  17.0 1.4 collective-permute-done.7.refs_2_
  18.4 2.9 %collective-permute-done.8.refs_3_ = bf16[8,32,128]{2,1,0:T(8,128)(2,1)S(1)} collective-permute-done((bf16[8,32,128]{2,1,0:T(8,128)(2,1)S(1)}, bf16[8,32,128]{2,1,0:T(8,128)(2,1)S(1)}, u32[]{:S(2)}, u32[]{:S(2)}) %collective-permute-start.8) | collective-permute-done | bytes 65568 | tf_op jit(solution)/shard_map/ppermute | solution.py:39
  21.3 0.9 second_shares.1.refs_0_
  22.1 2.8 %collective-permute-start.11 = (bf16[12,32,128]{2,1,0:T(8,128)(2,1)S(1)}, bf16[12,32,128]{2,1,0:T(8,128)(2,1)S(1)}, u32[]{:S(2)}, u32[]{:S(2)}) collective-permute-start(bf16[12,32,128]{2,1,0:T(8,128)(2,1)S(1)} %second_shares.1.refs_0_), channel_id=1, source_target_pairs={{0,6},{1,7},{2,0},{3,1},{4,2},{5,3},{6,4},{7,5},{8,14},{9,15},{10,... | collective-permute-start | bytes 294920 | tf_op jit(solution)/shard_map/ppermute | solution.py:39
  24.9 0.3 collective-permute-start.10
  25.3 0.7 collective-permute-start.9
  26.0 0.7 collective-permute-done.11.refs_3_
  26.6 3.4 %collective-permute-done.10.refs_2_ = bf16[12,32,128]{2,1,0:T(8,128)(2,1)S(1)} collective-permute-done((bf16[12,32,128]{2,1,0:T(8,128)(2,1)S(1)}, bf16[12,32,128]{2,1,0:T(8,128)(2,1)S(1)}, u32[]{:S(2)}, u32[]{:S(2)}) %collective-permute-start.10) | collective-permute-done | bytes 98336 | tf_op jit(solution)/shard_map/ppermute | solution.py:39
  30.0 1.0 collective-permute-done.9.refs_1_
  31.0 3.0 %collective-permute-start.19 = (bf16[4,12,32,128]{3,2,1,0:T(8,128)(2,1)S(1)}, bf16[4,12,32,128]{3,2,1,0:T(8,128)(2,1)S(1)}, u32[]{:S(2)}, u32[]{:S(2)}) collective-permute-start(bf16[4,12,32,128]{3,2,1,0:T(8,128)(2,1)S(1)} %stacked.1.refs_4_), channel_id=1, source_target_pairs={{0,1},{1,0},{2,3},{3,2},{4,5},{5,4},{6,7},{7,6},{8,9},{9,8},{10,11... | collective-permute-start | bytes 1179656 | tf_op jit(solution)/shard_map/ppermute | solution.py:39
  34.0 3.4 %collective-permute-start.14 = (bf16[4,12,32,128]{3,2,1,0:T(8,128)(2,1)S(1)}, bf16[4,12,32,128]{3,2,1,0:T(8,128)(2,1)S(1)}, u32[]{:S(2)}, u32[]{:S(2)}) collective-permute-start(bf16[4,12,32,128]{3,2,1,0:T(8,128)(2,1)S(1)} %stacked.1.refs_4_), channel_id=1, source_target_pairs={{0,24},{1,25},{2,26},{3,27},{4,28},{5,29},{6,30},{7,31},{8,0},{9,1... | collective-permute-start | bytes 1179656 | tf_op jit(solution)/shard_map/ppermute | solution.py:39
  37.4 0.6 collective-permute-start.12
  38.0 2.1 %collective-permute-start = (bf16[36,32,128]{2,1,0:T(8,128)(2,1)S(1)}, bf16[36,32,128]{2,1,0:T(8,128)(2,1)S(1)}, u32[]{:S(2)}, u32[]{:S(2)}) collective-permute-start(bf16[36,32,128]{2,1,0:T(8,128)(2,1)S(1)} %get-tuple-element.26.refs_0_), channel_id=1, source_target_pairs={{0,8},{1,9},{2,10},{3,11},{4,12},{5,13},{6,14},{7,15},{8,16},{9,17... | collective-permute-start | bytes 884744 | tf_op jit(solution)/shard_map/ppermute | solution.py:39
  40.1 24.1 %collective-permute-done.refs_1_ = bf16[36,32,128]{2,1,0:T(8,128)(2,1)S(1)} collective-permute-done((bf16[36,32,128]{2,1,0:T(8,128)(2,1)S(1)}, bf16[36,32,128]{2,1,0:T(8,128)(2,1)S(1)}, u32[]{:S(2)}, u32[]{:S(2)}) %collective-permute-start) | collective-permute-done | bytes 294944 | tf_op jit(solution)/shard_map/ppermute | solution.py:39
  64.1 0.2 first_shares.1.refs_0_
  64.4 0.9 collective-permute-start.15
  65.2 0.3 collective-permute-start.5
  65.5 0.5 collective-permute-start.4
  66.0 0.8 collective-permute-start.3
  66.8 0.9 collective-permute-start.22
  67.7 0.1 collective-permute-start.21
  67.8 8.1 %collective-permute-done.5.refs_3_ = bf16[4,12,32,128]{3,2,1,0:T(8,128)(2,1)S(1)} collective-permute-done((bf16[4,12,32,128]{3,2,1,0:T(8,128)(2,1)S(1)}, bf16[4,12,32,128]{3,2,1,0:T(8,128)(2,1)S(1)}, u32[]{:S(2)}, u32[]{:S(2)}) %collective-permute-start.5) | collective-permute-done | bytes 393248 | tf_op jit(solution)/shard_map/ppermute | solution.py:39
  75.9 1.4 collective-permute-start.20
  77.3 0.2 collective-permute-done.4.refs_2_
  77.5 2.1 %collective-permute-start.18 = (bf16[4,12,32,128]{3,2,1,0:T(8,128)(2,1)S(1)}, bf16[4,12,32,128]{3,2,1,0:T(8,128)(2,1)}, u32[]{:S(2)}, u32[]{:S(2)}) collective-permute-start(bf16[4,12,32,128]{3,2,1,0:T(8,128)(2,1)S(1)} %collective-permute-done.5.refs_3_), channel_id=1, source_target_pairs={{0,1},{1,0},{2,3},{3,2},{4,5},{5,4},{6,7},{7,6},{8,9},{9,8},{10,11... | collective-permute-start | bytes 1179656 | tf_op jit(solution)/shard_map/ppermute | solution.py:39
  79.5 7.1 %collective-permute-done.3.refs_1_ = bf16[4,12,32,128]{3,2,1,0:T(8,128)(2,1)} collective-permute-done((bf16[4,12,32,128]{3,2,1,0:T(8,128)(2,1)S(1)}, bf16[4,12,32,128]{3,2,1,0:T(8,128)(2,1)}, u32[]{:S(2)}, u32[]{:S(2)}) %collective-permute-start.3) | collective-permute-done | bytes 393248 | tf_op jit(solution)/shard_map/ppermute | solution.py:39
  86.6 0.5 collective-permute-start.17
  87.1 0.7 copy-done.9
  87.8 0.0 collective-permute-start.16
  87.9 3.5 %shard_map.122 = (bf16[2,512,1024]{2,1,0:T(8,128)(2,1)}, f32[64,1024]{1,0:T(8,128)}) custom-call(bf16[2,512,1024]{2,1,0:T(8,128)(2,1)} %hidden.2), custom_call_target="tpu_custom_call" | custom-call | flops 30000000 | bytes 12000000 | tf_op jit(solution)/shard_map/pallas_call | solution.py:73
  91.3 4.0 %shard_map.123 = (bf16[2,512,1280]{2,1,0:T(8,128)(2,1)}, f32[64,1280]{1,0:T(8,128)}) custom-call(bf16[2,512,1280]{2,1,0:T(8,128)(2,1)} %hidden.3), custom_call_target="tpu_custom_call" | custom-call | flops 30000000 | bytes 12000000 | tf_op jit(solution)/shard_map/pallas_call | solution.py:73
  95.4 14.7 %attend.1 = (bf16[64,640]{1,0:T(8,128)(2,1)S(1)}, bf16[64,640]{1,0:T(8,128)(2,1)S(1)}, bf16[64,640]{1,0:T(8,128)(2,1)S(1)}, bf16[64,640]{1,0:T(8,128)(2,1)S(1)},...) custom-call(s32[64]{0:T(128)} %frames_valid.3, s32[64]{0:T(128)} %slot_clip.1, ...), custom_call_target="tpu_custom_call" | custom-call | flops 8000000000 | bytes 12000000 | tf_op jit(solution)/shard_map/attend/pallas_call | solution.py:406
  110.1 2.5 %collective-permute-start.25 = (bf16[128,512]{1,0:T(8,128)(2,1)S(1)}, bf16[128,512]{1,0:T(8,128)(2,1)S(1)}, u32[]{:S(2)}, u32[]{:S(2)}) collective-permute-start(bf16[128,512]{1,0:T(8,128)(2,1)S(1)} %get-tuple-element.33.refs_0_), channel_id=1, source_target_pairs={{0,96},{32,0},{64,32},{96,64},{1,97},{33,1},{65,33},{97,65},{2,98}... | collective-permute-start | bytes 393224 | tf_op jit(solution)/shard_map/ppermute | solution.py:43
  112.6 1.7 collective-permute-start.27
  114.4 0.9 collective-permute-start.28
  115.3 2.4 %collective-permute-start.24 = (bf16[128,512]{1,0:T(8,128)(2,1)S(1)}, bf16[128,512]{1,0:T(8,128)(2,1)S(1)}, u32[]{:S(2)}, u32[]{:S(2)}) collective-permute-start(bf16[128,512]{1,0:T(8,128)(2,1)S(1)} %get-tuple-element.33.refs_0_), channel_id=1, source_target_pairs={{0,64},{32,96},{64,0},{96,32},{1,65},{33,97},{65,1},{97,33},{2,66}... | collective-permute-start | bytes 393224 | tf_op jit(solution)/shard_map/ppermute | solution.py:43
  117.7 0.6 collective-permute-done.26.refs_1_
  118.2 0.4 collective-permute-done.27.refs_2_
  118.6 0.5 collective-permute-done.28.refs_3_
  119.1 3.8 %slopes.1 = (bf16[64,640]{1,0:T(8,128)(2,1)S(1)}, bf16[64,640]{1,0:T(8,128)(2,1)S(1)}, bf16[64,640]{1,0:T(8,128)(2,1)S(1)}, bf16[64,640]{1,0:T(8,128)(2,1)S(1)}) custom-call(s32[64]{0:T(128)} %frames_valid.3, bf16[64,640]{1,0:T(8,128)(2,1)S(1)} %get-tuple-element.34.refs_0_, bf16[64,640]{1,0:T(8,128)(2,1)S(1)} %collective-permute-done.26.refs_1_, ...), custom_call_target="tpu_custom_call" | custom-call | tf_op jit(solution)/shard_map/slopes/pallas_call | solution.py:496
  123.0 1.5 collective-permute-start.29
  124.4 3.5 %collective-permute-start.30 = (bf16[64,640]{1,0:T(8,128)(2,1)S(1)}, bf16[64,640]{1,0:T(8,128)(2,1)S(1)}, u32[]{:S(2)}, u32[]{:S(2)}) collective-permute-start(bf16[64,640]{1,0:T(8,128)(2,1)S(1)} %get-tuple-element.44), channel_id=1, source_target_pairs={{0,64},{32,96},{64,0},{96,32},{1,65},{33,97},{65,1},{97,33},{2,66}... | collective-permute-start | bytes 245768 | tf_op jit(solution)/shard_map/ppermute | solution.py:43
  127.9 1.5 collective-permute-start.23
  129.4 2.9 %collective-permute-start.32 = (bf16[64,640]{1,0:T(8,128)(2,1)S(1)}, bf16[64,640]{1,0:T(8,128)(2,1)S(1)}, u32[]{:S(2)}, u32[]{:S(2)}) collective-permute-start(bf16[64,640]{1,0:T(8,128)(2,1)S(1)} %get-tuple-element.42.refs_4_), channel_id=1, source_target_pairs={{0,1},{1,0},{2,3},{3,2},{4,5},{5,4},{6,7},{7,6},{8,9},{9,8},{10,11... | collective-permute-start | bytes 245768 | tf_op jit(solution)/shard_map/ppermute | solution.py:39
  132.3 0.1 collective-permute-start.33
  132.4 2.2 %collective-permute-start.34 = (bf16[64,640]{1,0:T(8,128)(2,1)S(1)}, bf16[64,640]{1,0:T(8,128)(2,1)S(1)}, u32[]{:S(2)}, u32[]{:S(2)}) collective-permute-start(bf16[64,640]{1,0:T(8,128)(2,1)S(1)} %collective-permute-done.30.refs_6_), channel_id=1, source_target_pairs={{0,1},{1,0},{2,3},{3,2},{4,5},{5,4},{6,7},{7,6},{8,9},{9,8},{10,11... | collective-permute-start | bytes 245768 | tf_op jit(solution)/shard_map/ppermute | solution.py:39
  134.5 0.2 collective-permute-start.35
  134.7 0.8 collective-permute-done.34.refs_10_
  135.5 0.4 collective-permute-done.35.refs_11_
  135.8 0.5 outer.1
  136.3 14.2 %all_to_all.10.x = f32[16,72,128]{2,1,0:T(8,128)S(1)} all-to-all(f32[16,72,128]{2,1,0:T(8,128)S(1)} %outer.1), channel_id=1, replica_groups={{0,2,4,6,8,10,12,14,16,18,20,22,24,26,28,30},{1,3,5,7,9,11,13,15,17,19,..., dimensions={0} | all-to-all | bytes 1179648 | tf_op jit(solution)/shard_map/all_to_all | solution.py:634
  150.5 0.1 reduce_parts.1
  150.6 22.7 %all_to_all.11 = bf16[64,72,128]{2,1,0:T(8,128)(2,1)S(1)} all-to-all(bf16[64,72,128]{2,1,0:T(8,128)(2,1)S(1)} %reduce_parts.1), channel_id=1, replica_groups={{0,2,4,6,8,10,12,14,16,18,20,22,24,26,28,30,32,34,36,38,40,42,44,46,48,..., dimensions={0} | all-to-all | bytes 2359296 | tf_op jit(solution)/shard_map/all_to_all | solution.py:637
  173.3 3.8 %collective-permute-start.36 = (bf16[4,16,72,128]{3,2,1,0:T(8,128)(2,1)S(1)}, bf16[4,16,72,128]{3,2,1,0:T(8,128)(2,1)S(1)}, u32[]{:S(2)}, u32[]{:S(2)}) collective-permute-start(bf16[4,16,72,128]{3,2,1,0:T(8,128)(2,1)S(1)} %bitcast.5), channel_id=1, source_target_pairs={{0,1},{1,0},{2,3},{3,2},{4,5},{5,4},{6,7},{7,6},{8,9},{9,8},{10,11... | collective-permute-start | bytes 3538952 | tf_op jit(solution)/shard_map/ppermute | solution.py:39
  177.1 1.5 place_own.1
  178.6 0.9 collective-permute-done.36.piece
  179.6 1.5 place_partner.1
  (44 shorter events, 0.1 us)
Async XLA Ops:
  1.8 35.6 %collective-permute-start.2 = (bf16[36,32,128]{2,1,0:T(8,128)(2,1)S(1)}, bf16[36,32,128]{2,1,0:T(8,128)(2,1)S(1)}, u32[]{:S(2)}, u32[]{:S(2)}) collective-permute-start(bf16[36,32,128]{2,1,0:T(8,128)(2,1)S(1)} %get-tuple-element.26.refs_0_), channel_id=1, source_target_pairs={{0,24},{1,25},{2,26},{3,27},{4,28},{5,29},{6,30},{7,31},{8,0},{9,1... | collective-permute-start | bytes 884744 | tf_op jit(solution)/shard_map/ppermute | solution.py:39
  6.4 31.6 %collective-permute-start.1 = (bf16[36,32,128]{2,1,0:T(8,128)(2,1)S(1)}, bf16[36,32,128]{2,1,0:T(8,128)(2,1)S(1)}, u32[]{:S(2)}, u32[]{:S(2)}) collective-permute-start(bf16[36,32,128]{2,1,0:T(8,128)(2,1)S(1)} %get-tuple-element.26.refs_0_), channel_id=1, source_target_pairs={{0,16},{1,17},{2,18},{3,19},{4,20},{5,21},{6,22},{7,23},{8,24},{9,... | collective-permute-start | bytes 884744 | tf_op jit(solution)/shard_map/ppermute | solution.py:39
  6.4 10.6 %collective-permute-start.6 = (bf16[8,32,128]{2,1,0:T(8,128)(2,1)S(1)}, bf16[8,32,128]{2,1,0:T(8,128)(2,1)S(1)}, u32[]{:S(2)}, u32[]{:S(2)}) collective-permute-start(bf16[8,32,128]{2,1,0:T(8,128)(2,1)S(1)} %get-tuple-element.28), channel_id=1, source_target_pairs={{0,8},{1,9},{2,10},{3,11},{4,12},{5,13},{6,14},{7,15},{8,16},{9,17... | collective-permute-start | bytes 196616 | tf_op jit(solution)/shard_map/ppermute | solution.py:39
  7.1 11.2 %collective-permute-start.7 = (bf16[8,32,128]{2,1,0:T(8,128)(2,1)S(1)}, bf16[8,32,128]{2,1,0:T(8,128)(2,1)S(1)}, u32[]{:S(2)}, u32[]{:S(2)}) collective-permute-start(bf16[8,32,128]{2,1,0:T(8,128)(2,1)S(1)} %get-tuple-element.29), channel_id=1, source_target_pairs={{0,16},{1,17},{2,18},{3,19},{4,20},{5,21},{6,22},{7,23},{8,24},{9,... | collective-permute-start | bytes 196616 | tf_op jit(solution)/shard_map/ppermute | solution.py:39
  9.4 11.8 %collective-permute-start.8 = (bf16[8,32,128]{2,1,0:T(8,128)(2,1)S(1)}, bf16[8,32,128]{2,1,0:T(8,128)(2,1)S(1)}, u32[]{:S(2)}, u32[]{:S(2)}) collective-permute-start(bf16[8,32,128]{2,1,0:T(8,128)(2,1)S(1)} %get-tuple-element.30), channel_id=1, source_target_pairs={{0,24},{1,25},{2,26},{3,27},{4,28},{5,29},{6,30},{7,31},{8,0},{9,1... | collective-permute-start | bytes 196616 | tf_op jit(solution)/shard_map/ppermute | solution.py:39
  22.1 4.5 %collective-permute-start.11 = (bf16[12,32,128]{2,1,0:T(8,128)(2,1)S(1)}, bf16[12,32,128]{2,1,0:T(8,128)(2,1)S(1)}, u32[]{:S(2)}, u32[]{:S(2)}) collective-permute-start(bf16[12,32,128]{2,1,0:T(8,128)(2,1)S(1)} %second_shares.1.refs_0_), channel_id=1, source_target_pairs={{0,6},{1,7},{2,0},{3,1},{4,2},{5,3},{6,4},{7,5},{8,14},{9,15},{10,... | collective-permute-start | bytes 294920 | tf_op jit(solution)/shard_map/ppermute | solution.py:39
  24.9 5.1 %collective-permute-start.10 = (bf16[12,32,128]{2,1,0:T(8,128)(2,1)S(1)}, bf16[12,32,128]{2,1,0:T(8,128)(2,1)S(1)}, u32[]{:S(2)}, u32[]{:S(2)}) collective-permute-start(bf16[12,32,128]{2,1,0:T(8,128)(2,1)S(1)} %second_shares.1.refs_0_), channel_id=1, source_target_pairs={{0,4},{1,5},{2,6},{3,7},{4,0},{5,1},{6,2},{7,3},{8,12},{9,13},{10,... | collective-permute-start | bytes 294920 | tf_op jit(solution)/shard_map/ppermute | solution.py:39
  25.3 5.7 %collective-permute-start.9 = (bf16[12,32,128]{2,1,0:T(8,128)(2,1)S(1)}, bf16[12,32,128]{2,1,0:T(8,128)(2,1)S(1)}, u32[]{:S(2)}, u32[]{:S(2)}) collective-permute-start(bf16[12,32,128]{2,1,0:T(8,128)(2,1)S(1)} %second_shares.1.refs_0_), channel_id=1, source_target_pairs={{0,2},{1,3},{2,4},{3,5},{4,6},{5,7},{6,0},{7,1},{8,10},{9,11},{10,... | collective-permute-start | bytes 294920 | tf_op jit(solution)/shard_map/ppermute | solution.py:39
  31.0 64.3 %copy-start = (bf16[4,12,32,128]{3,2,1,0:T(8,128)(2,1)}, bf16[4,12,32,128]{3,2,1,0:T(8,128)(2,1)S(1)}, u32[]{:S(2)}) copy-start(bf16[4,12,32,128]{3,2,1,0:T(8,128)(2,1)S(1)} %stacked.1.refs_4_) | copy-start | bytes 1179652
  31.0 34.2 %collective-permute-start.19 = (bf16[4,12,32,128]{3,2,1,0:T(8,128)(2,1)S(1)}, bf16[4,12,32,128]{3,2,1,0:T(8,128)(2,1)S(1)}, u32[]{:S(2)}, u32[]{:S(2)}) collective-permute-start(bf16[4,12,32,128]{3,2,1,0:T(8,128)(2,1)S(1)} %stacked.1.refs_4_), channel_id=1, source_target_pairs={{0,1},{1,0},{2,3},{3,2},{4,5},{5,4},{6,7},{7,6},{8,9},{9,8},{10,11... | collective-permute-start | bytes 1179656 | tf_op jit(solution)/shard_map/ppermute | solution.py:39
  34.0 31.5 %collective-permute-start.14 = (bf16[4,12,32,128]{3,2,1,0:T(8,128)(2,1)S(1)}, bf16[4,12,32,128]{3,2,1,0:T(8,128)(2,1)S(1)}, u32[]{:S(2)}, u32[]{:S(2)}) collective-permute-start(bf16[4,12,32,128]{3,2,1,0:T(8,128)(2,1)S(1)} %stacked.1.refs_4_), channel_id=1, source_target_pairs={{0,24},{1,25},{2,26},{3,27},{4,28},{5,29},{6,30},{7,31},{8,0},{9,1... | collective-permute-start | bytes 1179656 | tf_op jit(solution)/shard_map/ppermute | solution.py:39
  37.4 28.6 %collective-permute-start.13 = (bf16[4,12,32,128]{3,2,1,0:T(8,128)(2,1)S(1)}, bf16[4,12,32,128]{3,2,1,0:T(8,128)(2,1)S(1)}, u32[]{:S(2)}, u32[]{:S(2)}) collective-permute-start(bf16[4,12,32,128]{3,2,1,0:T(8,128)(2,1)S(1)} %stacked.1.refs_4_), channel_id=1, source_target_pairs={{0,16},{1,17},{2,18},{3,19},{4,20},{5,21},{6,22},{7,23},{8,24},{9,... | collective-permute-start | bytes 1179656 | tf_op jit(solution)/shard_map/ppermute | solution.py:39
  37.4 29.4 %collective-permute-start.12 = (bf16[4,12,32,128]{3,2,1,0:T(8,128)(2,1)S(1)}, bf16[4,12,32,128]{3,2,1,0:T(8,128)(2,1)}, u32[]{:S(2)}, u32[]{:S(2)}) collective-permute-start(bf16[4,12,32,128]{3,2,1,0:T(8,128)(2,1)S(1)} %stacked.1.refs_4_), channel_id=1, source_target_pairs={{0,8},{1,9},{2,10},{3,11},{4,12},{5,13},{6,14},{7,15},{8,16},{9,17... | collective-permute-start | bytes 1179656 | tf_op jit(solution)/shard_map/ppermute | solution.py:39
  38.0 26.1 %collective-permute-start = (bf16[36,32,128]{2,1,0:T(8,128)(2,1)S(1)}, bf16[36,32,128]{2,1,0:T(8,128)(2,1)S(1)}, u32[]{:S(2)}, u32[]{:S(2)}) collective-permute-start(bf16[36,32,128]{2,1,0:T(8,128)(2,1)S(1)} %get-tuple-element.26.refs_0_), channel_id=1, source_target_pairs={{0,8},{1,9},{2,10},{3,11},{4,12},{5,13},{6,14},{7,15},{8,16},{9,17... | collective-permute-start | bytes 884744 | tf_op jit(solution)/shard_map/ppermute | solution.py:39
  64.4 30.9 %copy-start.1 = (bf16[4,12,32,128]{3,2,1,0:T(8,128)(2,1)}, bf16[4,12,32,128]{3,2,1,0:T(8,128)(2,1)S(1)}, u32[]{:S(2)}) copy-start(bf16[4,12,32,128]{3,2,1,0:T(8,128)(2,1)S(1)} %first_shares.1.refs_0_) | copy-start | bytes 1179652
  64.4 3.4 %collective-permute-start.15 = (bf16[4,12,32,128]{3,2,1,0:T(8,128)(2,1)S(1)}, bf16[4,12,32,128]{3,2,1,0:T(8,128)(2,1)S(1)}, u32[]{:S(2)}, u32[]{:S(2)}) collective-permute-start(bf16[4,12,32,128]{3,2,1,0:T(8,128)(2,1)S(1)} %first_shares.1.refs_0_), channel_id=1, source_target_pairs={{0,1},{1,0},{2,3},{3,2},{4,5},{5,4},{6,7},{7,6},{8,9},{9,8},{10,11... | collective-permute-start | bytes 1179656 | tf_op jit(solution)/shard_map/ppermute | solution.py:39
  65.2 30.1 %copy-start.4 = (bf16[4,12,32,128]{3,2,1,0:T(8,128)(2,1)}, bf16[4,12,32,128]{3,2,1,0:T(8,128)(2,1)S(1)}, u32[]{:S(2)}) copy-start(bf16[4,12,32,128]{3,2,1,0:T(8,128)(2,1)S(1)} %collective-permute-done.19.refs_12_) | copy-start | bytes 1179652
  65.2 10.7 %collective-permute-start.5 = (bf16[4,12,32,128]{3,2,1,0:T(8,128)(2,1)S(1)}, bf16[4,12,32,128]{3,2,1,0:T(8,128)(2,1)S(1)}, u32[]{:S(2)}, u32[]{:S(2)}) collective-permute-start(bf16[4,12,32,128]{3,2,1,0:T(8,128)(2,1)S(1)} %first_shares.1.refs_0_), channel_id=1, source_target_pairs={{0,6},{1,7},{2,0},{3,1},{4,2},{5,3},{6,4},{7,5},{8,14},{9,15},{10,... | collective-permute-start | bytes 1179656 | tf_op jit(solution)/shard_map/ppermute | solution.py:39
  65.5 29.8 %copy-start.5 = (bf16[4,12,32,128]{3,2,1,0:T(8,128)(2,1)}, bf16[4,12,32,128]{3,2,1,0:T(8,128)(2,1)S(1)}, u32[]{:S(2)}) copy-start(bf16[4,12,32,128]{3,2,1,0:T(8,128)(2,1)S(1)} %collective-permute-done.14.refs_7_) | copy-start | bytes 1179652
  65.5 11.9 %collective-permute-start.4 = (bf16[4,12,32,128]{3,2,1,0:T(8,128)(2,1)S(1)}, bf16[4,12,32,128]{3,2,1,0:T(8,128)(2,1)}, u32[]{:S(2)}, u32[]{:S(2)}) collective-permute-start(bf16[4,12,32,128]{3,2,1,0:T(8,128)(2,1)S(1)} %first_shares.1.refs_0_), channel_id=1, source_target_pairs={{0,4},{1,5},{2,6},{3,7},{4,0},{5,1},{6,2},{7,3},{8,12},{9,13},{10,... | collective-permute-start | bytes 1179656 | tf_op jit(solution)/shard_map/ppermute | solution.py:39
  66.0 29.3 %copy-start.6 = (bf16[4,12,32,128]{3,2,1,0:T(8,128)(2,1)}, bf16[4,12,32,128]{3,2,1,0:T(8,128)(2,1)S(1)}, u32[]{:S(2)}) copy-start(bf16[4,12,32,128]{3,2,1,0:T(8,128)(2,1)S(1)} %collective-permute-done.13.refs_6_) | copy-start | bytes 1179652
  66.0 20.6 %collective-permute-start.3 = (bf16[4,12,32,128]{3,2,1,0:T(8,128)(2,1)S(1)}, bf16[4,12,32,128]{3,2,1,0:T(8,128)(2,1)}, u32[]{:S(2)}, u32[]{:S(2)}) collective-permute-start(bf16[4,12,32,128]{3,2,1,0:T(8,128)(2,1)S(1)} %first_shares.1.refs_0_), channel_id=1, source_target_pairs={{0,2},{1,3},{2,4},{3,5},{4,6},{5,7},{6,0},{7,1},{8,10},{9,11},{10,... | collective-permute-start | bytes 1179656 | tf_op jit(solution)/shard_map/ppermute | solution.py:39
  66.8 20.3 %collective-permute-start.22 = (bf16[4,12,32,128]{3,2,1,0:T(8,128)(2,1)S(1)}, bf16[4,12,32,128]{3,2,1,0:T(8,128)(2,1)S(1)}, u32[]{:S(2)}, u32[]{:S(2)}) collective-permute-start(bf16[4,12,32,128]{3,2,1,0:T(8,128)(2,1)S(1)} %collective-permute-done.14.refs_7_), channel_id=1, source_target_pairs={{0,1},{1,0},{2,3},{3,2},{4,5},{5,4},{6,7},{7,6},{8,9},{9,8},{10,11... | collective-permute-start | bytes 1179656 | tf_op jit(solution)/shard_map/ppermute | solution.py:39
  67.7 27.6 %copy-start.7 = (bf16[4,12,32,128]{3,2,1,0:T(8,128)(2,1)}, bf16[4,12,32,128]{3,2,1,0:T(8,128)(2,1)S(1)}, u32[]{:S(2)}) copy-start(bf16[4,12,32,128]{3,2,1,0:T(8,128)(2,1)S(1)} %collective-permute-done.15.refs_8_) | copy-start | bytes 1179652
  67.7 27.6 %collective-permute-start.21 = (bf16[4,12,32,128]{3,2,1,0:T(8,128)(2,1)S(1)}, bf16[4,12,32,128]{3,2,1,0:T(8,128)(2,1)}, u32[]{:S(2)}, u32[]{:S(2)}) collective-permute-start(bf16[4,12,32,128]{3,2,1,0:T(8,128)(2,1)S(1)} %collective-permute-done.13.refs_6_), channel_id=1, source_target_pairs={{0,1},{1,0},{2,3},{3,2},{4,5},{5,4},{6,7},{7,6},{8,9},{9,8},{10,11... | collective-permute-start | bytes 1179656 | tf_op jit(solution)/shard_map/ppermute | solution.py:39
  75.9 19.4 %copy-start.8 = (bf16[4,12,32,128]{3,2,1,0:T(8,128)(2,1)}, bf16[4,12,32,128]{3,2,1,0:T(8,128)(2,1)S(1)}, u32[]{:S(2)}) copy-start(bf16[4,12,32,128]{3,2,1,0:T(8,128)(2,1)S(1)} %collective-permute-done.5.refs_3_) | copy-start | bytes 1179652
  75.9 19.4 %collective-permute-start.20 = (bf16[4,12,32,128]{3,2,1,0:T(8,128)(2,1)}, bf16[4,12,32,128]{3,2,1,0:T(8,128)(2,1)}, u32[]{:S(2)}, u32[]{:S(2)}) collective-permute-start(bf16[4,12,32,128]{3,2,1,0:T(8,128)(2,1)} %collective-permute-done.12.refs_5_), channel_id=1, source_target_pairs={{0,1},{1,0},{2,3},{3,2},{4,5},{5,4},{6,7},{7,6},{8,9},{9,8},{10,11... | collective-permute-start | bytes 1179656 | tf_op jit(solution)/shard_map/ppermute | solution.py:39
  77.5 17.9 %collective-permute-start.18 = (bf16[4,12,32,128]{3,2,1,0:T(8,128)(2,1)S(1)}, bf16[4,12,32,128]{3,2,1,0:T(8,128)(2,1)}, u32[]{:S(2)}, u32[]{:S(2)}) collective-permute-start(bf16[4,12,32,128]{3,2,1,0:T(8,128)(2,1)S(1)} %collective-permute-done.5.refs_3_), channel_id=1, source_target_pairs={{0,1},{1,0},{2,3},{3,2},{4,5},{5,4},{6,7},{7,6},{8,9},{9,8},{10,11... | collective-permute-start | bytes 1179656 | tf_op jit(solution)/shard_map/ppermute | solution.py:39
  86.6 8.8 %collective-permute-start.17 = (bf16[4,12,32,128]{3,2,1,0:T(8,128)(2,1)}, bf16[4,12,32,128]{3,2,1,0:T(8,128)(2,1)}, u32[]{:S(2)}, u32[]{:S(2)}) collective-permute-start(bf16[4,12,32,128]{3,2,1,0:T(8,128)(2,1)} %collective-permute-done.4.refs_2_), channel_id=1, source_target_pairs={{0,1},{1,0},{2,3},{3,2},{4,5},{5,4},{6,7},{7,6},{8,9},{9,8},{10,11... | collective-permute-start | bytes 1179656 | tf_op jit(solution)/shard_map/ppermute | solution.py:39
  87.1 0.7 copy-start.9
  87.8 7.6 %collective-permute-start.16 = (bf16[4,12,32,128]{3,2,1,0:T(8,128)(2,1)}, bf16[4,12,32,128]{3,2,1,0:T(8,128)(2,1)}, u32[]{:S(2)}, u32[]{:S(2)}) collective-permute-start(bf16[4,12,32,128]{3,2,1,0:T(8,128)(2,1)} %collective-permute-done.3.refs_1_), channel_id=1, source_target_pairs={{0,1},{1,0},{2,3},{3,2},{4,5},{5,4},{6,7},{7,6},{8,9},{9,8},{10,11... | collective-permute-start | bytes 1179656 | tf_op jit(solution)/shard_map/ppermute | solution.py:39
  95.4 23.7 %copy-start.2 = (f32[64,1280]{1,0:T(8,128)S(1)}, f32[64,1280]{1,0:T(8,128)}, u32[]{:S(2)}) copy-start(f32[64,1280]{1,0:T(8,128)} %get-tuple-element.39.refs_7_) | copy-start | bytes 983044
  95.4 23.7 %copy-start.3 = (f32[64,1024]{1,0:T(8,128)S(1)}, f32[64,1024]{1,0:T(8,128)}, u32[]{:S(2)}) copy-start(f32[64,1024]{1,0:T(8,128)} %get-tuple-element.38.refs_6_) | copy-start | bytes 786436
  110.1 17.9 %collective-permute-start.25 = (bf16[128,512]{1,0:T(8,128)(2,1)S(1)}, bf16[128,512]{1,0:T(8,128)(2,1)S(1)}, u32[]{:S(2)}, u32[]{:S(2)}) collective-permute-start(bf16[128,512]{1,0:T(8,128)(2,1)S(1)} %get-tuple-element.33.refs_0_), channel_id=1, source_target_pairs={{0,96},{32,0},{64,32},{96,64},{1,97},{33,1},{65,33},{97,65},{2,98}... | collective-permute-start | bytes 393224 | tf_op jit(solution)/shard_map/ppermute | solution.py:43
  112.6 5.6 %collective-permute-start.26 = (bf16[64,640]{1,0:T(8,128)(2,1)S(1)}, bf16[64,640]{1,0:T(8,128)(2,1)S(1)}, u32[]{:S(2)}, u32[]{:S(2)}) collective-permute-start(bf16[64,640]{1,0:T(8,128)(2,1)S(1)} %get-tuple-element.35), channel_id=1, source_target_pairs={{0,32},{32,64},{64,96},{96,0},{1,33},{33,65},{65,97},{97,1},{2,34}... | collective-permute-start | bytes 245768 | tf_op jit(solution)/shard_map/ppermute | solution.py:43
  112.6 6.0 %collective-permute-start.27 = (bf16[64,640]{1,0:T(8,128)(2,1)S(1)}, bf16[64,640]{1,0:T(8,128)(2,1)S(1)}, u32[]{:S(2)}, u32[]{:S(2)}) collective-permute-start(bf16[64,640]{1,0:T(8,128)(2,1)S(1)} %get-tuple-element.36), channel_id=1, source_target_pairs={{0,64},{32,96},{64,0},{96,32},{1,65},{33,97},{65,1},{97,33},{2,66}... | collective-permute-start | bytes 245768 | tf_op jit(solution)/shard_map/ppermute | solution.py:43
  114.4 4.8 %collective-permute-start.28 = (bf16[64,640]{1,0:T(8,128)(2,1)S(1)}, bf16[64,640]{1,0:T(8,128)(2,1)S(1)}, u32[]{:S(2)}, u32[]{:S(2)}) collective-permute-start(bf16[64,640]{1,0:T(8,128)(2,1)S(1)} %get-tuple-element.37), channel_id=1, source_target_pairs={{0,96},{32,0},{64,32},{96,64},{1,97},{33,1},{65,33},{97,65},{2,98}... | collective-permute-start | bytes 245768 | tf_op jit(solution)/shard_map/ppermute | solution.py:43
  115.3 14.1 %collective-permute-start.24 = (bf16[128,512]{1,0:T(8,128)(2,1)S(1)}, bf16[128,512]{1,0:T(8,128)(2,1)S(1)}, u32[]{:S(2)}, u32[]{:S(2)}) collective-permute-start(bf16[128,512]{1,0:T(8,128)(2,1)S(1)} %get-tuple-element.33.refs_0_), channel_id=1, source_target_pairs={{0,64},{32,96},{64,0},{96,32},{1,65},{33,97},{65,1},{97,33},{2,66}... | collective-permute-start | bytes 393224 | tf_op jit(solution)/shard_map/ppermute | solution.py:43
  123.0 9.3 %collective-permute-start.29 = (bf16[64,640]{1,0:T(8,128)(2,1)S(1)}, bf16[64,640]{1,0:T(8,128)(2,1)S(1)}, u32[]{:S(2)}, u32[]{:S(2)}) collective-permute-start(bf16[64,640]{1,0:T(8,128)(2,1)S(1)} %get-tuple-element.43), channel_id=1, source_target_pairs={{0,32},{32,64},{64,96},{96,0},{1,33},{33,65},{65,97},{97,1},{2,34}... | collective-permute-start | bytes 245768 | tf_op jit(solution)/shard_map/ppermute | solution.py:43
  124.4 8.0 %collective-permute-start.30 = (bf16[64,640]{1,0:T(8,128)(2,1)S(1)}, bf16[64,640]{1,0:T(8,128)(2,1)S(1)}, u32[]{:S(2)}, u32[]{:S(2)}) collective-permute-start(bf16[64,640]{1,0:T(8,128)(2,1)S(1)} %get-tuple-element.44), channel_id=1, source_target_pairs={{0,64},{32,96},{64,0},{96,32},{1,65},{33,97},{65,1},{97,33},{2,66}... | collective-permute-start | bytes 245768 | tf_op jit(solution)/shard_map/ppermute | solution.py:43
  127.9 6.6 %collective-permute-start.31 = (bf16[64,640]{1,0:T(8,128)(2,1)S(1)}, bf16[64,640]{1,0:T(8,128)(2,1)S(1)}, u32[]{:S(2)}, u32[]{:S(2)}) collective-permute-start(bf16[64,640]{1,0:T(8,128)(2,1)S(1)} %get-tuple-element.45), channel_id=1, source_target_pairs={{0,96},{32,0},{64,32},{96,64},{1,97},{33,1},{65,33},{97,65},{2,98}... | collective-permute-start | bytes 245768 | tf_op jit(solution)/shard_map/ppermute | solution.py:43
  127.9 6.8 %collective-permute-start.23 = (bf16[128,512]{1,0:T(8,128)(2,1)S(1)}, bf16[128,512]{1,0:T(8,128)(2,1)S(1)}, u32[]{:S(2)}, u32[]{:S(2)}) collective-permute-start(bf16[128,512]{1,0:T(8,128)(2,1)S(1)} %get-tuple-element.33.refs_0_), channel_id=1, source_target_pairs={{0,32},{32,64},{64,96},{96,0},{1,33},{33,65},{65,97},{97,1},{2,34}... | collective-permute-start | bytes 393224 | tf_op jit(solution)/shard_map/ppermute | solution.py:43
  129.4 5.3 %collective-permute-start.32 = (bf16[64,640]{1,0:T(8,128)(2,1)S(1)}, bf16[64,640]{1,0:T(8,128)(2,1)S(1)}, u32[]{:S(2)}, u32[]{:S(2)}) collective-permute-start(bf16[64,640]{1,0:T(8,128)(2,1)S(1)} %get-tuple-element.42.refs_4_), channel_id=1, source_target_pairs={{0,1},{1,0},{2,3},{3,2},{4,5},{5,4},{6,7},{7,6},{8,9},{9,8},{10,11... | collective-permute-start | bytes 245768 | tf_op jit(solution)/shard_map/ppermute | solution.py:39
  132.3 2.4 %collective-permute-start.33 = (bf16[64,640]{1,0:T(8,128)(2,1)S(1)}, bf16[64,640]{1,0:T(8,128)(2,1)S(1)}, u32[]{:S(2)}, u32[]{:S(2)}) collective-permute-start(bf16[64,640]{1,0:T(8,128)(2,1)S(1)} %collective-permute-done.29.refs_5_), channel_id=1, source_target_pairs={{0,1},{1,0},{2,3},{3,2},{4,5},{5,4},{6,7},{7,6},{8,9},{9,8},{10,11... | collective-permute-start | bytes 245768 | tf_op jit(solution)/shard_map/ppermute | solution.py:39
  132.4 3.1 %collective-permute-start.34 = (bf16[64,640]{1,0:T(8,128)(2,1)S(1)}, bf16[64,640]{1,0:T(8,128)(2,1)S(1)}, u32[]{:S(2)}, u32[]{:S(2)}) collective-permute-start(bf16[64,640]{1,0:T(8,128)(2,1)S(1)} %collective-permute-done.30.refs_6_), channel_id=1, source_target_pairs={{0,1},{1,0},{2,3},{3,2},{4,5},{5,4},{6,7},{7,6},{8,9},{9,8},{10,11... | collective-permute-start | bytes 245768 | tf_op jit(solution)/shard_map/ppermute | solution.py:39
  134.5 1.3 collective-permute-start.35
  173.3 6.3 %collective-permute-start.36 = (bf16[4,16,72,128]{3,2,1,0:T(8,128)(2,1)S(1)}, bf16[4,16,72,128]{3,2,1,0:T(8,128)(2,1)S(1)}, u32[]{:S(2)}, u32[]{:S(2)}) collective-permute-start(bf16[4,16,72,128]{3,2,1,0:T(8,128)(2,1)S(1)} %bitcast.5), channel_id=1, source_target_pairs={{0,1},{1,0},{2,3},{3,2},{4,5},{5,4},{6,7},{7,6},{8,9},{9,8},{10,11... | collective-permute-start | bytes 3538952 | tf_op jit(solution)/shard_map/ppermute | solution.py:39

commit v8 on v7

--- a/solution.py
+++ b/solution.py
@@ -217,21 +217,8 @@
     )
 
 
-def pick_latents(slot_clip, rows, slots, out):
-    column = lax.axis_index("dp")
-    c = column % 2
-    base = (column // 2) * 4
-
-    def find(s, carry):
-        local = slot_clip[s] - base
-
-        @pl.when((local >= 0) & (local < 4))
-        def _():
-            slots[jnp.clip(local, 0, 3)] = s
-
-        return carry
-
-    lax.fori_loop(0, CLIPS, find, 0)
+def pick_latents(slots, rows, out):
+    c = lax.axis_index("dp") % 2
     for i in range(4):
         slot = slots[(2 * c + i) % 4]
         h, j = slot // 32, slot % 32
@@ -240,16 +227,20 @@
         )
 
 
-def attend_kernel(frames_valid, slot_clip, *refs):
+def attend_kernel(frames_valid, slots, *refs):
     pieces = refs[:16]
     norm_a_hbm, norm_w_hbm, head_a_hbm, head_w_hbm = refs[16:20]
     outs, lat, pred_a, pred_w = refs[20:24], *refs[24:27]
     norm_a, norm_w, rows_in, qkv_a, qkv_w, proj, att_a, att_w = refs[27:35]
-    score_refs, slots, head_a, head_w, pooled, sems = refs[35:37], *refs[37:42]
+    score_refs, head_a, head_w, pooled, sems = refs[35:37], *refs[37:41]
     copy_head_a = pltpu.make_async_copy(head_a_hbm, head_a, sems.at[4])
     copy_head_w = pltpu.make_async_copy(head_w_hbm, head_w, sems.at[5])
-    copy_a = pltpu.make_async_copy(norm_a_hbm, norm_a, sems.at[2])
-    copy_w = pltpu.make_async_copy(norm_w_hbm, norm_w, sems.at[3])
+    copy_a = [
+        pltpu.make_async_copy(norm_a_hbm.at[i], norm_a.at[i], sems.at[2 + i]) for i in range(2)
+    ]
+    copy_w = [
+        pltpu.make_async_copy(norm_w_hbm.at[i], norm_w.at[i], sems.at[6 + i]) for i in range(2)
+    ]
     role = lax.axis_index("role")
     column = lax.axis_index("dp")
     z, y, c = place_of(column)
@@ -266,8 +257,10 @@
                     sem,
                 ).start()
         if first == 0:
-            copy_a.start()
-    copy_w.start()
+            copy_a[0].start()
+            copy_a[1].start()
+    copy_w[0].start()
+    copy_w[1].start()
     copy_head_a.start()
     copy_head_w.start()
     wait_a = pltpu.make_async_copy(
@@ -327,8 +320,8 @@
             top = next_top
 
     wait_a.wait()
-    copy_a.wait()
     for clip in range(2):
+        copy_a[clip].wait()
         lhs = jnp.concatenate(
             [
                 jnp.concatenate(
@@ -357,13 +350,13 @@
         pooled[:, clip * 32 : clip * 32 + 32, :A_COLS] = mean.reshape(ROLES, 32, A_COLS)
 
     wait_w.wait()
-    copy_w.wait()
     copy_head_a.wait()
     copy_head_w.wait()
-    pick_latents(slot_clip, rows_in, slots, lat)
+    pick_latents(slots, rows_in, lat)
     pred_a[...] = jnp.dot(lat[:ROWS], head_a[...], preferred_element_type=f32)
     pred_w[...] = jnp.dot(lat[:ROWS], head_w[...], preferred_element_type=f32)
     for clip in range(2):
+        copy_w[clip].wait()
         lhs = jnp.concatenate(
             [
                 jnp.concatenate(
@@ -401,7 +394,7 @@
         outs[k][...] = pooled[(role + k) % ROLES]
 
 
-def attend(frames_valid, slot_clip, pieces, norm_a, norm_w, head_a, head_w):
+def attend(frames_valid, slots, pieces, norm_a, norm_w, head_a, head_w):
     vmem = pl.BlockSpec(memory_space=pltpu.VMEM)
     return pl.pallas_call(
         attend_kernel,
@@ -425,17 +418,16 @@
             pltpu.VMEM((2, W_HEADS, HEAD, FRAMES), bf16),
             pltpu.VMEM((FRAMES, FRAMES), f32),
             pltpu.VMEM((FRAMES, FRAMES), f32),
-            pltpu.SMEM((4,), jnp.int32),
             pltpu.VMEM((STU_D, WAVLM_D), bf16),
             pltpu.VMEM((STU_D, WHISPER_D), bf16),
             pltpu.VMEM((ROLES, ROWS, OUT_COLS), bf16),
-            pltpu.SemaphoreType.DMA((6,)),
+            pltpu.SemaphoreType.DMA((8,)),
         ],
         cost_estimate=pl.CostEstimate(
             flops=8_000_000_000, bytes_accessed=12_000_000, transcendentals=5_000_000
         ),
         name="attend",
-    )(frames_valid, slot_clip, *pieces, norm_a, norm_w, head_a, head_w)
+    )(frames_valid, slots, *pieces, norm_a, norm_w, head_a, head_w)
 
 
 def slope_kernel(frames_valid, *refs):
@@ -608,6 +600,9 @@
     wavlm_head,
     whisper_head,
 ):
+    chip_clips = lax.axis_index("dp") // 2 * 4 + jnp.arange(4)
+    match = slot_clip[None, :] == chip_clips[:, None]
+    slots = jnp.sum(jnp.where(match, jnp.arange(CLIPS)[None, :], 0), axis=1).astype(jnp.int32)
     raw, *chunks = weight_chunks(wavlm_qkv.T, whisper_qkv.T, latent)
     chunks = [chunks[0]] + [dp_send(chunks[k], k, 0, 0) for k in (1, 2, 3)]
     raws = [raw] + [dp_send(raw, k, 0, 0) for k in (1, 2, 3)]
@@ -621,7 +616,7 @@
     norm_w, mean_w = norms(whisper_hidden)
 
     *pooled, lat, pred_a, pred_w = attend(
-        frames_valid, slot_clip, pieces, norm_a, norm_w, wavlm_head, whisper_head
+        frames_valid, slots, pieces, norm_a, norm_w, wavlm_head, whisper_head
     )
     parts = [pooled[0]] + [role_send(pooled[k], k) for k in (1, 2, 3)]
     lats = [lat] + [role_send(lat, k) for k in (1, 2, 3)]

time: 181 us -> 183 us (1.011)
  no operation moved by 1% of the time
where the time goes in v8:
time: 183 us; the launch traced here: 182 us
  waiting for transfers between devices  57.6 us (31%)
  starting transfers between devices  53.2 us (29%)
  blocking collectives  36.9 us (20%)
  Pallas kernels  32.2 us (18%)
    ppermute x28, waiting for transfers between devices, dp_send(): return lax.ppermute(x, 'dp', pairs)  56.2 us
    ppermute x28, starting transfers between devices, dp_send(): return lax.ppermute(x, 'dp', pairs)  39.1 us
    all_to_all x1, blocking collectives, per_device(): lax.all_to_all(reduce_parts(arrived), ('role', 'dp'), split_axis=0, conca...  22.7 us
    pallas_call x1, Pallas kernels, attend(): pl.pallas_call(attend_kernel, out_shape=[pltpu.VMEM((ROWS, OUT_COLS), bf1...  15 us
    all_to_all x1, blocking collectives, per_device(): lax.all_to_all(halves, 'dp', split_axis=0, concat_axis=0, tiled=True, axi...  14.2 us
    ppermute x9, starting transfers between devices, role_send(): return lax.ppermute(x, 'role', [(i, (i + k) % ROLES) for i in range(ROLES)])  14 us
    pallas_call x2, Pallas kernels, norms(): pl.pallas_call(norm_kernel, grid=(2,), out_shape=[jax.ShapeDtypeStruct(hi...  7.43 us
    pallas_call x1, Pallas kernels, slopes(): pl.pallas_call(slope_kernel, out_shape=[pltpu.VMEM((ROWS, OUT_COLS), bf16...  3.83 us
  transfers between devices with their start and end apart: 37, of which 16 were waited for; matrix products, arithmetic and copies ran while one was open for 0% of the time, Pallas kernels for 8%

profile of v8, /device:TPU:1, one launch (start us, length us, event | category | flops | bytes accessed | tf_op | source)
XLA Modules:
  0.0 182.2 jit_solution(7747899034463029943)
XLA Ops:
  0.6 1.2 weight_chunks.1
  1.8 4.6 %collective-permute-start.2 = (bf16[36,32,128]{2,1,0:T(8,128)(2,1)S(1)}, bf16[36,32,128]{2,1,0:T(8,128)(2,1)S(1)}, u32[]{:S(2)}, u32[]{:S(2)}) collective-permute-start(bf16[36,32,128]{2,1,0:T(8,128)(2,1)S(1)} %get-tuple-element.26.refs_0_), channel_id=1, source_target_pairs={{0,24},{1,25},{2,26},{3,27},{4,28},{5,29},{6,30},{7,31},{8,0},{9,1... | collective-permute-start | bytes 884744 | tf_op jit(solution)/shard_map/ppermute | solution.py:39
  6.4 0.7 collective-permute-start.6
  7.1 2.3 %collective-permute-start.7 = (bf16[8,32,128]{2,1,0:T(8,128)(2,1)S(1)}, bf16[8,32,128]{2,1,0:T(8,128)(2,1)S(1)}, u32[]{:S(2)}, u32[]{:S(2)}) collective-permute-start(bf16[8,32,128]{2,1,0:T(8,128)(2,1)S(1)} %get-tuple-element.29), channel_id=1, source_target_pairs={{0,16},{1,17},{2,18},{3,19},{4,20},{5,21},{6,22},{7,23},{8,24},{9,... | collective-permute-start | bytes 196616 | tf_op jit(solution)/shard_map/ppermute | solution.py:39
  9.4 2.1 %collective-permute-start.8 = (bf16[8,32,128]{2,1,0:T(8,128)(2,1)S(1)}, bf16[8,32,128]{2,1,0:T(8,128)(2,1)S(1)}, u32[]{:S(2)}, u32[]{:S(2)}) collective-permute-start(bf16[8,32,128]{2,1,0:T(8,128)(2,1)S(1)} %get-tuple-element.30), channel_id=1, source_target_pairs={{0,24},{1,25},{2,26},{3,27},{4,28},{5,29},{6,30},{7,31},{8,0},{9,1... | collective-permute-start | bytes 196616 | tf_op jit(solution)/shard_map/ppermute | solution.py:39
  11.5 5.5 %collective-permute-done.6.refs_1_ = bf16[8,32,128]{2,1,0:T(8,128)(2,1)S(1)} collective-permute-done((bf16[8,32,128]{2,1,0:T(8,128)(2,1)S(1)}, bf16[8,32,128]{2,1,0:T(8,128)(2,1)S(1)}, u32[]{:S(2)}, u32[]{:S(2)}) %collective-permute-start.6) | collective-permute-done | bytes 65568 | tf_op jit(solution)/shard_map/ppermute | solution.py:39
  17.0 1.4 collective-permute-done.7.refs_2_
  18.4 2.9 %collective-permute-done.8.refs_3_ = bf16[8,32,128]{2,1,0:T(8,128)(2,1)S(1)} collective-permute-done((bf16[8,32,128]{2,1,0:T(8,128)(2,1)S(1)}, bf16[8,32,128]{2,1,0:T(8,128)(2,1)S(1)}, u32[]{:S(2)}, u32[]{:S(2)}) %collective-permute-start.8) | collective-permute-done | bytes 65568 | tf_op jit(solution)/shard_map/ppermute | solution.py:39
  21.3 0.9 second_shares.1.refs_0_
  22.1 2.8 %collective-permute-start.11 = (bf16[12,32,128]{2,1,0:T(8,128)(2,1)S(1)}, bf16[12,32,128]{2,1,0:T(8,128)(2,1)S(1)}, u32[]{:S(2)}, u32[]{:S(2)}) collective-permute-start(bf16[12,32,128]{2,1,0:T(8,128)(2,1)S(1)} %second_shares.1.refs_0_), channel_id=1, source_target_pairs={{0,6},{1,7},{2,0},{3,1},{4,2},{5,3},{6,4},{7,5},{8,14},{9,15},{10,... | collective-permute-start | bytes 294920 | tf_op jit(solution)/shard_map/ppermute | solution.py:39
  24.9 0.3 collective-permute-start.10
  25.3 0.7 collective-permute-start.9
  26.0 0.7 collective-permute-done.11.refs_3_
  26.6 3.4 %collective-permute-done.10.refs_2_ = bf16[12,32,128]{2,1,0:T(8,128)(2,1)S(1)} collective-permute-done((bf16[12,32,128]{2,1,0:T(8,128)(2,1)S(1)}, bf16[12,32,128]{2,1,0:T(8,128)(2,1)S(1)}, u32[]{:S(2)}, u32[]{:S(2)}) %collective-permute-start.10) | collective-permute-done | bytes 98336 | tf_op jit(solution)/shard_map/ppermute | solution.py:39
  30.0 1.0 collective-permute-done.9.refs_1_
  31.0 3.0 %collective-permute-start.19 = (bf16[4,12,32,128]{3,2,1,0:T(8,128)(2,1)S(1)}, bf16[4,12,32,128]{3,2,1,0:T(8,128)(2,1)S(1)}, u32[]{:S(2)}, u32[]{:S(2)}) collective-permute-start(bf16[4,12,32,128]{3,2,1,0:T(8,128)(2,1)S(1)} %stacked.1.refs_4_), channel_id=1, source_target_pairs={{0,1},{1,0},{2,3},{3,2},{4,5},{5,4},{6,7},{7,6},{8,9},{9,8},{10,11... | collective-permute-start | bytes 1179656 | tf_op jit(solution)/shard_map/ppermute | solution.py:39
  34.0 3.4 %collective-permute-start.14 = (bf16[4,12,32,128]{3,2,1,0:T(8,128)(2,1)S(1)}, bf16[4,12,32,128]{3,2,1,0:T(8,128)(2,1)S(1)}, u32[]{:S(2)}, u32[]{:S(2)}) collective-permute-start(bf16[4,12,32,128]{3,2,1,0:T(8,128)(2,1)S(1)} %stacked.1.refs_4_), channel_id=1, source_target_pairs={{0,24},{1,25},{2,26},{3,27},{4,28},{5,29},{6,30},{7,31},{8,0},{9,1... | collective-permute-start | bytes 1179656 | tf_op jit(solution)/shard_map/ppermute | solution.py:39
  37.4 0.6 collective-permute-start.12
  38.0 2.1 %collective-permute-start = (bf16[36,32,128]{2,1,0:T(8,128)(2,1)S(1)}, bf16[36,32,128]{2,1,0:T(8,128)(2,1)S(1)}, u32[]{:S(2)}, u32[]{:S(2)}) collective-permute-start(bf16[36,32,128]{2,1,0:T(8,128)(2,1)S(1)} %get-tuple-element.26.refs_0_), channel_id=1, source_target_pairs={{0,8},{1,9},{2,10},{3,11},{4,12},{5,13},{6,14},{7,15},{8,16},{9,17... | collective-permute-start | bytes 884744 | tf_op jit(solution)/shard_map/ppermute | solution.py:39
  40.1 24.1 %collective-permute-done.refs_1_ = bf16[36,32,128]{2,1,0:T(8,128)(2,1)S(1)} collective-permute-done((bf16[36,32,128]{2,1,0:T(8,128)(2,1)S(1)}, bf16[36,32,128]{2,1,0:T(8,128)(2,1)S(1)}, u32[]{:S(2)}, u32[]{:S(2)}) %collective-permute-start) | collective-permute-done | bytes 294944 | tf_op jit(solution)/shard_map/ppermute | solution.py:39
  64.1 0.2 first_shares.1.refs_0_
  64.4 0.9 collective-permute-start.15
  65.2 0.3 collective-permute-start.5
  65.5 0.5 collective-permute-start.4
  66.0 0.8 collective-permute-start.3
  66.8 0.9 collective-permute-start.22
  67.7 0.1 collective-permute-start.21
  67.8 8.1 %collective-permute-done.5.refs_3_ = bf16[4,12,32,128]{3,2,1,0:T(8,128)(2,1)S(1)} collective-permute-done((bf16[4,12,32,128]{3,2,1,0:T(8,128)(2,1)S(1)}, bf16[4,12,32,128]{3,2,1,0:T(8,128)(2,1)S(1)}, u32[]{:S(2)}, u32[]{:S(2)}) %collective-permute-start.5) | collective-permute-done | bytes 393248 | tf_op jit(solution)/shard_map/ppermute | solution.py:39
  75.9 1.4 collective-permute-start.20
  77.3 0.2 collective-permute-done.4.refs_2_
  77.5 2.1 %collective-permute-start.18 = (bf16[4,12,32,128]{3,2,1,0:T(8,128)(2,1)S(1)}, bf16[4,12,32,128]{3,2,1,0:T(8,128)(2,1)}, u32[]{:S(2)}, u32[]{:S(2)}) collective-permute-start(bf16[4,12,32,128]{3,2,1,0:T(8,128)(2,1)S(1)} %collective-permute-done.5.refs_3_), channel_id=1, source_target_pairs={{0,1},{1,0},{2,3},{3,2},{4,5},{5,4},{6,7},{7,6},{8,9},{9,8},{10,11... | collective-permute-start | bytes 1179656 | tf_op jit(solution)/shard_map/ppermute | solution.py:39
  79.5 7.1 %collective-permute-done.3.refs_1_ = bf16[4,12,32,128]{3,2,1,0:T(8,128)(2,1)} collective-permute-done((bf16[4,12,32,128]{3,2,1,0:T(8,128)(2,1)S(1)}, bf16[4,12,32,128]{3,2,1,0:T(8,128)(2,1)}, u32[]{:S(2)}, u32[]{:S(2)}) %collective-permute-start.3) | collective-permute-done | bytes 393248 | tf_op jit(solution)/shard_map/ppermute | solution.py:39
  86.6 0.5 collective-permute-start.17
  87.1 0.7 copy-done.9
  87.8 0.0 collective-permute-start.16
  87.9 3.5 %shard_map.122 = (bf16[2,512,1024]{2,1,0:T(8,128)(2,1)}, f32[64,1024]{1,0:T(8,128)}) custom-call(bf16[2,512,1024]{2,1,0:T(8,128)(2,1)} %hidden.2), custom_call_target="tpu_custom_call" | custom-call | flops 30000000 | bytes 12000000 | tf_op jit(solution)/shard_map/pallas_call | solution.py:73
  91.3 4.0 %shard_map.123 = (bf16[2,512,1280]{2,1,0:T(8,128)(2,1)}, f32[64,1280]{1,0:T(8,128)}) custom-call(bf16[2,512,1280]{2,1,0:T(8,128)(2,1)} %hidden.3), custom_call_target="tpu_custom_call" | custom-call | flops 30000000 | bytes 12000000 | tf_op jit(solution)/shard_map/pallas_call | solution.py:73
  95.4 0.7 select_reduce_fusion.slots
  96.2 15.0 %attend.1 = (bf16[64,640]{1,0:T(8,128)(2,1)S(1)}, bf16[64,640]{1,0:T(8,128)(2,1)S(1)}, bf16[64,640]{1,0:T(8,128)(2,1)S(1)}, bf16[64,640]{1,0:T(8,128)(2,1)S(1)},...) custom-call(s32[64]{0:T(128)} %frames_valid.3, s32[4]{0:T(128)} %select_reduce_fusion.slots, ...), custom_call_target="tpu_custom_call" | custom-call | flops 8000000000 | bytes 12000000 | tf_op jit(solution)/shard_map/attend/pallas_call | solution.py:399
  111.2 2.5 %collective-permute-start.25 = (bf16[128,512]{1,0:T(8,128)(2,1)S(1)}, bf16[128,512]{1,0:T(8,128)(2,1)S(1)}, u32[]{:S(2)}, u32[]{:S(2)}) collective-permute-start(bf16[128,512]{1,0:T(8,128)(2,1)S(1)} %get-tuple-element.33.refs_0_), channel_id=1, source_target_pairs={{0,96},{32,0},{64,32},{96,64},{1,97},{33,1},{65,33},{97,65},{2,98}... | collective-permute-start | bytes 393224 | tf_op jit(solution)/shard_map/ppermute | solution.py:43
  113.7 1.7 collective-permute-start.27
  115.5 0.9 collective-permute-start.28
  116.4 2.4 %collective-permute-start.24 = (bf16[128,512]{1,0:T(8,128)(2,1)S(1)}, bf16[128,512]{1,0:T(8,128)(2,1)S(1)}, u32[]{:S(2)}, u32[]{:S(2)}) collective-permute-start(bf16[128,512]{1,0:T(8,128)(2,1)S(1)} %get-tuple-element.33.refs_0_), channel_id=1, source_target_pairs={{0,64},{32,96},{64,0},{96,32},{1,65},{33,97},{65,1},{97,33},{2,66}... | collective-permute-start | bytes 393224 | tf_op jit(solution)/shard_map/ppermute | solution.py:43
  118.8 0.5 collective-permute-done.26.refs_1_
  119.3 0.4 collective-permute-done.27.refs_2_
  119.7 0.5 collective-permute-done.28.refs_3_
  120.2 3.8 %slopes.1 = (bf16[64,640]{1,0:T(8,128)(2,1)S(1)}, bf16[64,640]{1,0:T(8,128)(2,1)S(1)}, bf16[64,640]{1,0:T(8,128)(2,1)S(1)}, bf16[64,640]{1,0:T(8,128)(2,1)S(1)}) custom-call(s32[64]{0:T(128)} %frames_valid.3, bf16[64,640]{1,0:T(8,128)(2,1)S(1)} %get-tuple-element.34.refs_0_, bf16[64,640]{1,0:T(8,128)(2,1)S(1)} %collective-permute-done.26.refs_1_, ...), custom_call_target="tpu_custom_call" | custom-call | tf_op jit(solution)/shard_map/slopes/pallas_call | solution.py:488
  124.1 1.5 collective-permute-start.29
  125.5 3.5 %collective-permute-start.30 = (bf16[64,640]{1,0:T(8,128)(2,1)S(1)}, bf16[64,640]{1,0:T(8,128)(2,1)S(1)}, u32[]{:S(2)}, u32[]{:S(2)}) collective-permute-start(bf16[64,640]{1,0:T(8,128)(2,1)S(1)} %get-tuple-element.44), channel_id=1, source_target_pairs={{0,64},{32,96},{64,0},{96,32},{1,65},{33,97},{65,1},{97,33},{2,66}... | collective-permute-start | bytes 245768 | tf_op jit(solution)/shard_map/ppermute | solution.py:43
  129.0 1.5 collective-permute-start.23
  130.5 2.9 %collective-permute-start.32 = (bf16[64,640]{1,0:T(8,128)(2,1)S(1)}, bf16[64,640]{1,0:T(8,128)(2,1)S(1)}, u32[]{:S(2)}, u32[]{:S(2)}) collective-permute-start(bf16[64,640]{1,0:T(8,128)(2,1)S(1)} %get-tuple-element.42.refs_4_), channel_id=1, source_target_pairs={{0,1},{1,0},{2,3},{3,2},{4,5},{5,4},{6,7},{7,6},{8,9},{9,8},{10,11... | collective-permute-start | bytes 245768 | tf_op jit(solution)/shard_map/ppermute | solution.py:39
  133.4 0.1 collective-permute-start.33
  133.5 2.1 %collective-permute-start.34 = (bf16[64,640]{1,0:T(8,128)(2,1)S(1)}, bf16[64,640]{1,0:T(8,128)(2,1)S(1)}, u32[]{:S(2)}, u32[]{:S(2)}) collective-permute-start(bf16[64,640]{1,0:T(8,128)(2,1)S(1)} %collective-permute-done.30.refs_6_), channel_id=1, source_target_pairs={{0,1},{1,0},{2,3},{3,2},{4,5},{5,4},{6,7},{7,6},{8,9},{9,8},{10,11... | collective-permute-start | bytes 245768 | tf_op jit(solution)/shard_map/ppermute | solution.py:39
  135.6 0.2 collective-permute-start.35
  135.8 0.7 collective-permute-done.34.refs_10_
  136.6 0.4 collective-permute-done.35.refs_11_
  136.9 0.5 outer.1
  137.4 14.2 %all_to_all.10.x = f32[16,72,128]{2,1,0:T(8,128)S(1)} all-to-all(f32[16,72,128]{2,1,0:T(8,128)S(1)} %outer.1), channel_id=1, replica_groups={{0,2,4,6,8,10,12,14,16,18,20,22,24,26,28,30},{1,3,5,7,9,11,13,15,17,19,..., dimensions={0} | all-to-all | bytes 1179648 | tf_op jit(solution)/shard_map/all_to_all | solution.py:629
  151.6 0.1 reduce_parts.1
  151.7 22.7 %all_to_all.11 = bf16[64,72,128]{2,1,0:T(8,128)(2,1)S(1)} all-to-all(bf16[64,72,128]{2,1,0:T(8,128)(2,1)S(1)} %reduce_parts.1), channel_id=1, replica_groups={{0,2,4,6,8,10,12,14,16,18,20,22,24,26,28,30,32,34,36,38,40,42,44,46,48,..., dimensions={0} | all-to-all | bytes 2359296 | tf_op jit(solution)/shard_map/all_to_all | solution.py:632
  174.4 3.8 %collective-permute-start.36 = (bf16[4,16,72,128]{3,2,1,0:T(8,128)(2,1)S(1)}, bf16[4,16,72,128]{3,2,1,0:T(8,128)(2,1)S(1)}, u32[]{:S(2)}, u32[]{:S(2)}) collective-permute-start(bf16[4,16,72,128]{3,2,1,0:T(8,128)(2,1)S(1)} %bitcast.5), channel_id=1, source_target_pairs={{0,1},{1,0},{2,3},{3,2},{4,5},{5,4},{6,7},{7,6},{8,9},{9,8},{10,11... | collective-permute-start | bytes 3538952 | tf_op jit(solution)/shard_map/ppermute | solution.py:39
  178.2 1.5 place_own.1
  179.7 0.9 collective-permute-done.36.piece
  180.7 1.5 place_partner.1
  (48 shorter events, 0.1 us)
Async XLA Ops:
  1.8 35.6 %collective-permute-start.2 = (bf16[36,32,128]{2,1,0:T(8,128)(2,1)S(1)}, bf16[36,32,128]{2,1,0:T(8,128)(2,1)S(1)}, u32[]{:S(2)}, u32[]{:S(2)}) collective-permute-start(bf16[36,32,128]{2,1,0:T(8,128)(2,1)S(1)} %get-tuple-element.26.refs_0_), channel_id=1, source_target_pairs={{0,24},{1,25},{2,26},{3,27},{4,28},{5,29},{6,30},{7,31},{8,0},{9,1... | collective-permute-start | bytes 884744 | tf_op jit(solution)/shard_map/ppermute | solution.py:39
  6.4 31.6 %collective-permute-start.1 = (bf16[36,32,128]{2,1,0:T(8,128)(2,1)S(1)}, bf16[36,32,128]{2,1,0:T(8,128)(2,1)S(1)}, u32[]{:S(2)}, u32[]{:S(2)}) collective-permute-start(bf16[36,32,128]{2,1,0:T(8,128)(2,1)S(1)} %get-tuple-element.26.refs_0_), channel_id=1, source_target_pairs={{0,16},{1,17},{2,18},{3,19},{4,20},{5,21},{6,22},{7,23},{8,24},{9,... | collective-permute-start | bytes 884744 | tf_op jit(solution)/shard_map/ppermute | solution.py:39
  6.4 10.6 %collective-permute-start.6 = (bf16[8,32,128]{2,1,0:T(8,128)(2,1)S(1)}, bf16[8,32,128]{2,1,0:T(8,128)(2,1)S(1)}, u32[]{:S(2)}, u32[]{:S(2)}) collective-permute-start(bf16[8,32,128]{2,1,0:T(8,128)(2,1)S(1)} %get-tuple-element.28), channel_id=1, source_target_pairs={{0,8},{1,9},{2,10},{3,11},{4,12},{5,13},{6,14},{7,15},{8,16},{9,17... | collective-permute-start | bytes 196616 | tf_op jit(solution)/shard_map/ppermute | solution.py:39
  7.1 11.2 %collective-permute-start.7 = (bf16[8,32,128]{2,1,0:T(8,128)(2,1)S(1)}, bf16[8,32,128]{2,1,0:T(8,128)(2,1)S(1)}, u32[]{:S(2)}, u32[]{:S(2)}) collective-permute-start(bf16[8,32,128]{2,1,0:T(8,128)(2,1)S(1)} %get-tuple-element.29), channel_id=1, source_target_pairs={{0,16},{1,17},{2,18},{3,19},{4,20},{5,21},{6,22},{7,23},{8,24},{9,... | collective-permute-start | bytes 196616 | tf_op jit(solution)/shard_map/ppermute | solution.py:39
  9.4 11.8 %collective-permute-start.8 = (bf16[8,32,128]{2,1,0:T(8,128)(2,1)S(1)}, bf16[8,32,128]{2,1,0:T(8,128)(2,1)S(1)}, u32[]{:S(2)}, u32[]{:S(2)}) collective-permute-start(bf16[8,32,128]{2,1,0:T(8,128)(2,1)S(1)} %get-tuple-element.30), channel_id=1, source_target_pairs={{0,24},{1,25},{2,26},{3,27},{4,28},{5,29},{6,30},{7,31},{8,0},{9,1... | collective-permute-start | bytes 196616 | tf_op jit(solution)/shard_map/ppermute | solution.py:39
  22.1 4.5 %collective-permute-start.11 = (bf16[12,32,128]{2,1,0:T(8,128)(2,1)S(1)}, bf16[12,32,128]{2,1,0:T(8,128)(2,1)S(1)}, u32[]{:S(2)}, u32[]{:S(2)}) collective-permute-start(bf16[12,32,128]{2,1,0:T(8,128)(2,1)S(1)} %second_shares.1.refs_0_), channel_id=1, source_target_pairs={{0,6},{1,7},{2,0},{3,1},{4,2},{5,3},{6,4},{7,5},{8,14},{9,15},{10,... | collective-permute-start | bytes 294920 | tf_op jit(solution)/shard_map/ppermute | solution.py:39
  24.9 5.1 %collective-permute-start.10 = (bf16[12,32,128]{2,1,0:T(8,128)(2,1)S(1)}, bf16[12,32,128]{2,1,0:T(8,128)(2,1)S(1)}, u32[]{:S(2)}, u32[]{:S(2)}) collective-permute-start(bf16[12,32,128]{2,1,0:T(8,128)(2,1)S(1)} %second_shares.1.refs_0_), channel_id=1, source_target_pairs={{0,4},{1,5},{2,6},{3,7},{4,0},{5,1},{6,2},{7,3},{8,12},{9,13},{10,... | collective-permute-start | bytes 294920 | tf_op jit(solution)/shard_map/ppermute | solution.py:39
  25.3 5.7 %collective-permute-start.9 = (bf16[12,32,128]{2,1,0:T(8,128)(2,1)S(1)}, bf16[12,32,128]{2,1,0:T(8,128)(2,1)S(1)}, u32[]{:S(2)}, u32[]{:S(2)}) collective-permute-start(bf16[12,32,128]{2,1,0:T(8,128)(2,1)S(1)} %second_shares.1.refs_0_), channel_id=1, source_target_pairs={{0,2},{1,3},{2,4},{3,5},{4,6},{5,7},{6,0},{7,1},{8,10},{9,11},{10,... | collective-permute-start | bytes 294920 | tf_op jit(solution)/shard_map/ppermute | solution.py:39
  31.0 64.3 %copy-start = (bf16[4,12,32,128]{3,2,1,0:T(8,128)(2,1)}, bf16[4,12,32,128]{3,2,1,0:T(8,128)(2,1)S(1)}, u32[]{:S(2)}) copy-start(bf16[4,12,32,128]{3,2,1,0:T(8,128)(2,1)S(1)} %stacked.1.refs_4_) | copy-start | bytes 1179652
  31.0 34.2 %collective-permute-start.19 = (bf16[4,12,32,128]{3,2,1,0:T(8,128)(2,1)S(1)}, bf16[4,12,32,128]{3,2,1,0:T(8,128)(2,1)S(1)}, u32[]{:S(2)}, u32[]{:S(2)}) collective-permute-start(bf16[4,12,32,128]{3,2,1,0:T(8,128)(2,1)S(1)} %stacked.1.refs_4_), channel_id=1, source_target_pairs={{0,1},{1,0},{2,3},{3,2},{4,5},{5,4},{6,7},{7,6},{8,9},{9,8},{10,11... | collective-permute-start | bytes 1179656 | tf_op jit(solution)/shard_map/ppermute | solution.py:39
  34.0 31.5 %collective-permute-start.14 = (bf16[4,12,32,128]{3,2,1,0:T(8,128)(2,1)S(1)}, bf16[4,12,32,128]{3,2,1,0:T(8,128)(2,1)S(1)}, u32[]{:S(2)}, u32[]{:S(2)}) collective-permute-start(bf16[4,12,32,128]{3,2,1,0:T(8,128)(2,1)S(1)} %stacked.1.refs_4_), channel_id=1, source_target_pairs={{0,24},{1,25},{2,26},{3,27},{4,28},{5,29},{6,30},{7,31},{8,0},{9,1... | collective-permute-start | bytes 1179656 | tf_op jit(solution)/shard_map/ppermute | solution.py:39
  37.4 28.6 %collective-permute-start.13 = (bf16[4,12,32,128]{3,2,1,0:T(8,128)(2,1)S(1)}, bf16[4,12,32,128]{3,2,1,0:T(8,128)(2,1)S(1)}, u32[]{:S(2)}, u32[]{:S(2)}) collective-permute-start(bf16[4,12,32,128]{3,2,1,0:T(8,128)(2,1)S(1)} %stacked.1.refs_4_), channel_id=1, source_target_pairs={{0,16},{1,17},{2,18},{3,19},{4,20},{5,21},{6,22},{7,23},{8,24},{9,... | collective-permute-start | bytes 1179656 | tf_op jit(solution)/shard_map/ppermute | solution.py:39
  37.4 29.4 %collective-permute-start.12 = (bf16[4,12,32,128]{3,2,1,0:T(8,128)(2,1)S(1)}, bf16[4,12,32,128]{3,2,1,0:T(8,128)(2,1)}, u32[]{:S(2)}, u32[]{:S(2)}) collective-permute-start(bf16[4,12,32,128]{3,2,1,0:T(8,128)(2,1)S(1)} %stacked.1.refs_4_), channel_id=1, source_target_pairs={{0,8},{1,9},{2,10},{3,11},{4,12},{5,13},{6,14},{7,15},{8,16},{9,17... | collective-permute-start | bytes 1179656 | tf_op jit(solution)/shard_map/ppermute | solution.py:39
  38.0 26.1 %collective-permute-start = (bf16[36,32,128]{2,1,0:T(8,128)(2,1)S(1)}, bf16[36,32,128]{2,1,0:T(8,128)(2,1)S(1)}, u32[]{:S(2)}, u32[]{:S(2)}) collective-permute-start(bf16[36,32,128]{2,1,0:T(8,128)(2,1)S(1)} %get-tuple-element.26.refs_0_), channel_id=1, source_target_pairs={{0,8},{1,9},{2,10},{3,11},{4,12},{5,13},{6,14},{7,15},{8,16},{9,17... | collective-permute-start | bytes 884744 | tf_op jit(solution)/shard_map/ppermute | solution.py:39
  64.4 31.0 %copy-start.1 = (bf16[4,12,32,128]{3,2,1,0:T(8,128)(2,1)}, bf16[4,12,32,128]{3,2,1,0:T(8,128)(2,1)S(1)}, u32[]{:S(2)}) copy-start(bf16[4,12,32,128]{3,2,1,0:T(8,128)(2,1)S(1)} %first_shares.1.refs_0_) | copy-start | bytes 1179652
  64.4 3.4 %collective-permute-start.15 = (bf16[4,12,32,128]{3,2,1,0:T(8,128)(2,1)S(1)}, bf16[4,12,32,128]{3,2,1,0:T(8,128)(2,1)S(1)}, u32[]{:S(2)}, u32[]{:S(2)}) collective-permute-start(bf16[4,12,32,128]{3,2,1,0:T(8,128)(2,1)S(1)} %first_shares.1.refs_0_), channel_id=1, source_target_pairs={{0,1},{1,0},{2,3},{3,2},{4,5},{5,4},{6,7},{7,6},{8,9},{9,8},{10,11... | collective-permute-start | bytes 1179656 | tf_op jit(solution)/shard_map/ppermute | solution.py:39
  65.2 30.1 %copy-start.4 = (bf16[4,12,32,128]{3,2,1,0:T(8,128)(2,1)}, bf16[4,12,32,128]{3,2,1,0:T(8,128)(2,1)S(1)}, u32[]{:S(2)}) copy-start(bf16[4,12,32,128]{3,2,1,0:T(8,128)(2,1)S(1)} %collective-permute-done.19.refs_12_) | copy-start | bytes 1179652
  65.2 10.7 %collective-permute-start.5 = (bf16[4,12,32,128]{3,2,1,0:T(8,128)(2,1)S(1)}, bf16[4,12,32,128]{3,2,1,0:T(8,128)(2,1)S(1)}, u32[]{:S(2)}, u32[]{:S(2)}) collective-permute-start(bf16[4,12,32,128]{3,2,1,0:T(8,128)(2,1)S(1)} %first_shares.1.refs_0_), channel_id=1, source_target_pairs={{0,6},{1,7},{2,0},{3,1},{4,2},{5,3},{6,4},{7,5},{8,14},{9,15},{10,... | collective-permute-start | bytes 1179656 | tf_op jit(solution)/shard_map/ppermute | solution.py:39
  65.5 29.8 %copy-start.5 = (bf16[4,12,32,128]{3,2,1,0:T(8,128)(2,1)}, bf16[4,12,32,128]{3,2,1,0:T(8,128)(2,1)S(1)}, u32[]{:S(2)}) copy-start(bf16[4,12,32,128]{3,2,1,0:T(8,128)(2,1)S(1)} %collective-permute-done.14.refs_7_) | copy-start | bytes 1179652
  65.5 11.9 %collective-permute-start.4 = (bf16[4,12,32,128]{3,2,1,0:T(8,128)(2,1)S(1)}, bf16[4,12,32,128]{3,2,1,0:T(8,128)(2,1)}, u32[]{:S(2)}, u32[]{:S(2)}) collective-permute-start(bf16[4,12,32,128]{3,2,1,0:T(8,128)(2,1)S(1)} %first_shares.1.refs_0_), channel_id=1, source_target_pairs={{0,4},{1,5},{2,6},{3,7},{4,0},{5,1},{6,2},{7,3},{8,12},{9,13},{10,... | collective-permute-start | bytes 1179656 | tf_op jit(solution)/shard_map/ppermute | solution.py:39
  66.0 29.3 %copy-start.6 = (bf16[4,12,32,128]{3,2,1,0:T(8,128)(2,1)}, bf16[4,12,32,128]{3,2,1,0:T(8,128)(2,1)S(1)}, u32[]{:S(2)}) copy-start(bf16[4,12,32,128]{3,2,1,0:T(8,128)(2,1)S(1)} %collective-permute-done.13.refs_6_) | copy-start | bytes 1179652
  66.0 20.6 %collective-permute-start.3 = (bf16[4,12,32,128]{3,2,1,0:T(8,128)(2,1)S(1)}, bf16[4,12,32,128]{3,2,1,0:T(8,128)(2,1)}, u32[]{:S(2)}, u32[]{:S(2)}) collective-permute-start(bf16[4,12,32,128]{3,2,1,0:T(8,128)(2,1)S(1)} %first_shares.1.refs_0_), channel_id=1, source_target_pairs={{0,2},{1,3},{2,4},{3,5},{4,6},{5,7},{6,0},{7,1},{8,10},{9,11},{10,... | collective-permute-start | bytes 1179656 | tf_op jit(solution)/shard_map/ppermute | solution.py:39
  66.8 20.3 %collective-permute-start.22 = (bf16[4,12,32,128]{3,2,1,0:T(8,128)(2,1)S(1)}, bf16[4,12,32,128]{3,2,1,0:T(8,128)(2,1)S(1)}, u32[]{:S(2)}, u32[]{:S(2)}) collective-permute-start(bf16[4,12,32,128]{3,2,1,0:T(8,128)(2,1)S(1)} %collective-permute-done.14.refs_7_), channel_id=1, source_target_pairs={{0,1},{1,0},{2,3},{3,2},{4,5},{5,4},{6,7},{7,6},{8,9},{9,8},{10,11... | collective-permute-start | bytes 1179656 | tf_op jit(solution)/shard_map/ppermute | solution.py:39
  67.7 27.6 %copy-start.7 = (bf16[4,12,32,128]{3,2,1,0:T(8,128)(2,1)}, bf16[4,12,32,128]{3,2,1,0:T(8,128)(2,1)S(1)}, u32[]{:S(2)}) copy-start(bf16[4,12,32,128]{3,2,1,0:T(8,128)(2,1)S(1)} %collective-permute-done.15.refs_8_) | copy-start | bytes 1179652
  67.7 28.4 %collective-permute-start.21 = (bf16[4,12,32,128]{3,2,1,0:T(8,128)(2,1)S(1)}, bf16[4,12,32,128]{3,2,1,0:T(8,128)(2,1)}, u32[]{:S(2)}, u32[]{:S(2)}) collective-permute-start(bf16[4,12,32,128]{3,2,1,0:T(8,128)(2,1)S(1)} %collective-permute-done.13.refs_6_), channel_id=1, source_target_pairs={{0,1},{1,0},{2,3},{3,2},{4,5},{5,4},{6,7},{7,6},{8,9},{9,8},{10,11... | collective-permute-start | bytes 1179656 | tf_op jit(solution)/shard_map/ppermute | solution.py:39
  75.9 19.4 %copy-start.8 = (bf16[4,12,32,128]{3,2,1,0:T(8,128)(2,1)}, bf16[4,12,32,128]{3,2,1,0:T(8,128)(2,1)S(1)}, u32[]{:S(2)}) copy-start(bf16[4,12,32,128]{3,2,1,0:T(8,128)(2,1)S(1)} %collective-permute-done.5.refs_3_) | copy-start | bytes 1179652
  75.9 20.2 %collective-permute-start.20 = (bf16[4,12,32,128]{3,2,1,0:T(8,128)(2,1)}, bf16[4,12,32,128]{3,2,1,0:T(8,128)(2,1)}, u32[]{:S(2)}, u32[]{:S(2)}) collective-permute-start(bf16[4,12,32,128]{3,2,1,0:T(8,128)(2,1)} %collective-permute-done.12.refs_5_), channel_id=1, source_target_pairs={{0,1},{1,0},{2,3},{3,2},{4,5},{5,4},{6,7},{7,6},{8,9},{9,8},{10,11... | collective-permute-start | bytes 1179656 | tf_op jit(solution)/shard_map/ppermute | solution.py:39
  77.5 18.6 %collective-permute-start.18 = (bf16[4,12,32,128]{3,2,1,0:T(8,128)(2,1)S(1)}, bf16[4,12,32,128]{3,2,1,0:T(8,128)(2,1)}, u32[]{:S(2)}, u32[]{:S(2)}) collective-permute-start(bf16[4,12,32,128]{3,2,1,0:T(8,128)(2,1)S(1)} %collective-permute-done.5.refs_3_), channel_id=1, source_target_pairs={{0,1},{1,0},{2,3},{3,2},{4,5},{5,4},{6,7},{7,6},{8,9},{9,8},{10,11... | collective-permute-start | bytes 1179656 | tf_op jit(solution)/shard_map/ppermute | solution.py:39
  86.6 9.5 %collective-permute-start.17 = (bf16[4,12,32,128]{3,2,1,0:T(8,128)(2,1)}, bf16[4,12,32,128]{3,2,1,0:T(8,128)(2,1)}, u32[]{:S(2)}, u32[]{:S(2)}) collective-permute-start(bf16[4,12,32,128]{3,2,1,0:T(8,128)(2,1)} %collective-permute-done.4.refs_2_), channel_id=1, source_target_pairs={{0,1},{1,0},{2,3},{3,2},{4,5},{5,4},{6,7},{7,6},{8,9},{9,8},{10,11... | collective-permute-start | bytes 1179656 | tf_op jit(solution)/shard_map/ppermute | solution.py:39
  87.1 0.7 copy-start.9
  87.8 8.3 %collective-permute-start.16 = (bf16[4,12,32,128]{3,2,1,0:T(8,128)(2,1)}, bf16[4,12,32,128]{3,2,1,0:T(8,128)(2,1)}, u32[]{:S(2)}, u32[]{:S(2)}) collective-permute-start(bf16[4,12,32,128]{3,2,1,0:T(8,128)(2,1)} %collective-permute-done.3.refs_1_), channel_id=1, source_target_pairs={{0,1},{1,0},{2,3},{3,2},{4,5},{5,4},{6,7},{7,6},{8,9},{9,8},{10,11... | collective-permute-start | bytes 1179656 | tf_op jit(solution)/shard_map/ppermute | solution.py:39
  87.9 7.5 %copy-start.10 = (s32[64]{0:T(128)S(1)}, s32[64]{0:T(128)}, u32[]{:S(2)}) copy-start(s32[64]{0:T(128)} %param.18) | copy-start | bytes 772
  96.1 24.1 %copy-start.2 = (f32[64,1280]{1,0:T(8,128)S(1)}, f32[64,1280]{1,0:T(8,128)}, u32[]{:S(2)}) copy-start(f32[64,1280]{1,0:T(8,128)} %get-tuple-element.39.refs_7_) | copy-start | bytes 983044
  96.2 24.1 %copy-start.3 = (f32[64,1024]{1,0:T(8,128)S(1)}, f32[64,1024]{1,0:T(8,128)}, u32[]{:S(2)}) copy-start(f32[64,1024]{1,0:T(8,128)} %get-tuple-element.38.refs_6_) | copy-start | bytes 786436
  111.2 17.9 %collective-permute-start.25 = (bf16[128,512]{1,0:T(8,128)(2,1)S(1)}, bf16[128,512]{1,0:T(8,128)(2,1)S(1)}, u32[]{:S(2)}, u32[]{:S(2)}) collective-permute-start(bf16[128,512]{1,0:T(8,128)(2,1)S(1)} %get-tuple-element.33.refs_0_), channel_id=1, source_target_pairs={{0,96},{32,0},{64,32},{96,64},{1,97},{33,1},{65,33},{97,65},{2,98}... | collective-permute-start | bytes 393224 | tf_op jit(solution)/shard_map/ppermute | solution.py:43
  113.7 5.6 %collective-permute-start.26 = (bf16[64,640]{1,0:T(8,128)(2,1)S(1)}, bf16[64,640]{1,0:T(8,128)(2,1)S(1)}, u32[]{:S(2)}, u32[]{:S(2)}) collective-permute-start(bf16[64,640]{1,0:T(8,128)(2,1)S(1)} %get-tuple-element.35), channel_id=1, source_target_pairs={{0,32},{32,64},{64,96},{96,0},{1,33},{33,65},{65,97},{97,1},{2,34}... | collective-permute-start | bytes 245768 | tf_op jit(solution)/shard_map/ppermute | solution.py:43
  113.7 6.0 %collective-permute-start.27 = (bf16[64,640]{1,0:T(8,128)(2,1)S(1)}, bf16[64,640]{1,0:T(8,128)(2,1)S(1)}, u32[]{:S(2)}, u32[]{:S(2)}) collective-permute-start(bf16[64,640]{1,0:T(8,128)(2,1)S(1)} %get-tuple-element.36), channel_id=1, source_target_pairs={{0,64},{32,96},{64,0},{96,32},{1,65},{33,97},{65,1},{97,33},{2,66}... | collective-permute-start | bytes 245768 | tf_op jit(solution)/shard_map/ppermute | solution.py:43
  115.5 4.8 %collective-permute-start.28 = (bf16[64,640]{1,0:T(8,128)(2,1)S(1)}, bf16[64,640]{1,0:T(8,128)(2,1)S(1)}, u32[]{:S(2)}, u32[]{:S(2)}) collective-permute-start(bf16[64,640]{1,0:T(8,128)(2,1)S(1)} %get-tuple-element.37), channel_id=1, source_target_pairs={{0,96},{32,0},{64,32},{96,64},{1,97},{33,1},{65,33},{97,65},{2,98}... | collective-permute-start | bytes 245768 | tf_op jit(solution)/shard_map/ppermute | solution.py:43
  116.4 14.1 %collective-permute-start.24 = (bf16[128,512]{1,0:T(8,128)(2,1)S(1)}, bf16[128,512]{1,0:T(8,128)(2,1)S(1)}, u32[]{:S(2)}, u32[]{:S(2)}) collective-permute-start(bf16[128,512]{1,0:T(8,128)(2,1)S(1)} %get-tuple-element.33.refs_0_), channel_id=1, source_target_pairs={{0,64},{32,96},{64,0},{96,32},{1,65},{33,97},{65,1},{97,33},{2,66}... | collective-permute-start | bytes 393224 | tf_op jit(solution)/shard_map/ppermute | solution.py:43
  124.1 9.3 %collective-permute-start.29 = (bf16[64,640]{1,0:T(8,128)(2,1)S(1)}, bf16[64,640]{1,0:T(8,128)(2,1)S(1)}, u32[]{:S(2)}, u32[]{:S(2)}) collective-permute-start(bf16[64,640]{1,0:T(8,128)(2,1)S(1)} %get-tuple-element.43), channel_id=1, source_target_pairs={{0,32},{32,64},{64,96},{96,0},{1,33},{33,65},{65,97},{97,1},{2,34}... | collective-permute-start | bytes 245768 | tf_op jit(solution)/shard_map/ppermute | solution.py:43
  125.5 8.0 %collective-permute-start.30 = (bf16[64,640]{1,0:T(8,128)(2,1)S(1)}, bf16[64,640]{1,0:T(8,128)(2,1)S(1)}, u32[]{:S(2)}, u32[]{:S(2)}) collective-permute-start(bf16[64,640]{1,0:T(8,128)(2,1)S(1)} %get-tuple-element.44), channel_id=1, source_target_pairs={{0,64},{32,96},{64,0},{96,32},{1,65},{33,97},{65,1},{97,33},{2,66}... | collective-permute-start | bytes 245768 | tf_op jit(solution)/shard_map/ppermute | solution.py:43
  129.0 6.6 %collective-permute-start.31 = (bf16[64,640]{1,0:T(8,128)(2,1)S(1)}, bf16[64,640]{1,0:T(8,128)(2,1)S(1)}, u32[]{:S(2)}, u32[]{:S(2)}) collective-permute-start(bf16[64,640]{1,0:T(8,128)(2,1)S(1)} %get-tuple-element.45), channel_id=1, source_target_pairs={{0,96},{32,0},{64,32},{96,64},{1,97},{33,1},{65,33},{97,65},{2,98}... | collective-permute-start | bytes 245768 | tf_op jit(solution)/shard_map/ppermute | solution.py:43
  129.0 6.8 %collective-permute-start.23 = (bf16[128,512]{1,0:T(8,128)(2,1)S(1)}, bf16[128,512]{1,0:T(8,128)(2,1)S(1)}, u32[]{:S(2)}, u32[]{:S(2)}) collective-permute-start(bf16[128,512]{1,0:T(8,128)(2,1)S(1)} %get-tuple-element.33.refs_0_), channel_id=1, source_target_pairs={{0,32},{32,64},{64,96},{96,0},{1,33},{33,65},{65,97},{97,1},{2,34}... | collective-permute-start | bytes 393224 | tf_op jit(solution)/shard_map/ppermute | solution.py:43
  130.5 5.3 %collective-permute-start.32 = (bf16[64,640]{1,0:T(8,128)(2,1)S(1)}, bf16[64,640]{1,0:T(8,128)(2,1)S(1)}, u32[]{:S(2)}, u32[]{:S(2)}) collective-permute-start(bf16[64,640]{1,0:T(8,128)(2,1)S(1)} %get-tuple-element.42.refs_4_), channel_id=1, source_target_pairs={{0,1},{1,0},{2,3},{3,2},{4,5},{5,4},{6,7},{7,6},{8,9},{9,8},{10,11... | collective-permute-start | bytes 245768 | tf_op jit(solution)/shard_map/ppermute | solution.py:39
  133.4 2.4 %collective-permute-start.33 = (bf16[64,640]{1,0:T(8,128)(2,1)S(1)}, bf16[64,640]{1,0:T(8,128)(2,1)S(1)}, u32[]{:S(2)}, u32[]{:S(2)}) collective-permute-start(bf16[64,640]{1,0:T(8,128)(2,1)S(1)} %collective-permute-done.29.refs_5_), channel_id=1, source_target_pairs={{0,1},{1,0},{2,3},{3,2},{4,5},{5,4},{6,7},{7,6},{8,9},{9,8},{10,11... | collective-permute-start | bytes 245768 | tf_op jit(solution)/shard_map/ppermute | solution.py:39
  133.5 3.1 %collective-permute-start.34 = (bf16[64,640]{1,0:T(8,128)(2,1)S(1)}, bf16[64,640]{1,0:T(8,128)(2,1)S(1)}, u32[]{:S(2)}, u32[]{:S(2)}) collective-permute-start(bf16[64,640]{1,0:T(8,128)(2,1)S(1)} %collective-permute-done.30.refs_6_), channel_id=1, source_target_pairs={{0,1},{1,0},{2,3},{3,2},{4,5},{5,4},{6,7},{7,6},{8,9},{9,8},{10,11... | collective-permute-start | bytes 245768 | tf_op jit(solution)/shard_map/ppermute | solution.py:39
  135.6 1.3 collective-permute-start.35
  174.4 6.3 %collective-permute-start.36 = (bf16[4,16,72,128]{3,2,1,0:T(8,128)(2,1)S(1)}, bf16[4,16,72,128]{3,2,1,0:T(8,128)(2,1)S(1)}, u32[]{:S(2)}, u32[]{:S(2)}) collective-permute-start(bf16[4,16,72,128]{3,2,1,0:T(8,128)(2,1)S(1)} %bitcast.5), channel_id=1, source_target_pairs={{0,1},{1,0},{2,3},{3,2},{4,5},{5,4},{6,7},{7,6},{8,9},{9,8},{10,11... | collective-permute-start | bytes 3538952 | tf_op jit(solution)/shard_map/ppermute | solution.py:39
